TPU v7x, 128 devices: a whole 4x4x4 slice. The times are simulated.
128 devices in a mesh: ctx: 64 (over z_lo, x, y, core), fsdp: 2 (over z_hi).
Axes of the slice: x: 4, y: 4, z: 4 (z_hi: 2, z_lo: 2; z = z_hi * 2 + z_lo), core: 2. Of those that a mesh axis runs over, the one named last changes fastest.
Arguments:
- block_in: bfloat16 [2, 8192, 768], P('fsdp', 'ctx'), may hold values from -70 to 70
- out_grad: bfloat16 [2, 8192, 768], P('fsdp', 'ctx'), may hold values from -6 to 6
- ln1_gain: bfloat16 [768], P('fsdp'), may hold values from 0.5 to 1.5
- ln1_bias: bfloat16 [768], P('fsdp'), may hold values from -3 to 3
- w_qkv: bfloat16 [768, 2304], P('fsdp'), may hold values from -2 to 2
- q_bias: bfloat16 [768], P('fsdp'), may hold values from -3 to 3
- v_bias: bfloat16 [768], P('fsdp'), may hold values from -3 to 3
- w_proj: bfloat16 [768, 768], P('fsdp'), may hold values from -2 to 2
- b_proj: bfloat16 [768], P('fsdp'), may hold values from -3 to 3
- ln2_gain: bfloat16 [768], P('fsdp'), may hold values from 0.5 to 1.5
- ln2_bias: bfloat16 [768], P('fsdp'), may hold values from -3 to 3
- w_fc: bfloat16 [768, 3072], P('fsdp'), may hold values from -0.21875 to 0.21875
- b_fc: bfloat16 [3072], P('fsdp'), may hold values from -3 to 3
- w_out: bfloat16 [3072, 768], P('fsdp'), may hold values from -0.109375 to 0.109375
- b_out: bfloat16 [768], P('fsdp'), may hold values from -3 to 3
Outputs:
- block_out: bfloat16 [2, 8192, 768], P('fsdp', 'ctx')
- input_grad: float32 [2, 8192, 768], P('fsdp', 'ctx')
- grad_ln1_gain: float32 [768], P('fsdp')
- grad_ln1_bias: float32 [768], P('fsdp')
- grad_w_qkv: float32 [768, 2304], P('fsdp')
- grad_q_bias: float32 [768], P('fsdp')
- grad_v_bias: float32 [768], P('fsdp')
- grad_w_proj: float32 [768, 768], P('fsdp')
- grad_b_proj: float32 [768], P('fsdp')
- grad_ln2_gain: float32 [768], P('fsdp')
- grad_ln2_bias: float32 [768], P('fsdp')
- grad_w_fc: float32 [768, 3072], P('fsdp')
- grad_b_fc: float32 [3072], P('fsdp')
- grad_w_out: float32 [3072, 768], P('fsdp')
- grad_b_out: float32 [768], P('fsdp')
All inputs are finite; a program needn't handle non-finite values.
Results may differ from a plain program's by a relative error of at most 0.025.
The roundings to bfloat16 on the way count: a program that leaves them out, or rounds other values in their place, can miss the bound.
Values may be sent and summed in bfloat16 or wider, within the bound.
No kernel may reach another device: no remote copies, remote signals or barrier semaphores. Data moves between devices by JAX's collectives and lax.ppermute only.
A program may use at most 256 MiB of HBM per device.

v0:
```python
import math

import jax
import jax.numpy as jnp
from jax import lax
from jax.sharding import PartitionSpec as P

HEADS = 12


norm_epsilon = 1e-05
gelu_factor = 0.7978845608028654
gelu_cubic = 0.044715
masked_score = -1e30


def layer_norm(values, gain, offset):
    center = jnp.mean(values, axis=-1, keepdims=True)
    centered = values - center
    spread = jnp.mean(centered * centered, axis=-1, keepdims=True)
    return centered * lax.rsqrt(spread + norm_epsilon) * gain + offset


def gelu_tanh(values):
    return (
        0.5
        * values
        * (1.0 + jnp.tanh(gelu_factor * (values + gelu_cubic * values * values * values)))
    )


def score_grads(
    query_rows, grad_rows, lse_rows, delta_rows, key_rows, value_rows, allowed, score_scale
):
    scores = (
        jnp.einsum("thd,shd->hts", query_rows, key_rows, preferred_element_type=jnp.float32)
        * score_scale
    )
    scores = jnp.where(allowed[None], scores, masked_score)
    probabilities = jnp.where(allowed[None], jnp.exp(scores - lse_rows[:, :, None]), 0.0)
    grad_probs = jnp.einsum(
        "thd,shd->hts", grad_rows, value_rows, preferred_element_type=jnp.float32
    )
    grad_scores = (probabilities * (grad_probs - delta_rows[:, :, None]) * score_scale).astype(
        jnp.bfloat16
    )
    return (grad_scores, probabilities)


def body(
    block_in,
    out_grad,
    ln1_gain,
    ln1_bias,
    w_qkv,
    q_bias,
    v_bias,
    w_proj,
    b_proj,
    ln2_gain,
    ln2_bias,
    w_fc,
    b_fc,
    w_out,
    b_out,
):
    gathered = (
        lax.all_gather(ln1_gain, "fsdp", axis=0, tiled=True),
        lax.all_gather(ln1_bias, "fsdp", axis=0, tiled=True),
        lax.all_gather(w_qkv, "fsdp", axis=0, tiled=True),
        lax.all_gather(q_bias, "fsdp", axis=0, tiled=True),
        lax.all_gather(v_bias, "fsdp", axis=0, tiled=True),
        lax.all_gather(w_proj, "fsdp", axis=0, tiled=True),
        lax.all_gather(b_proj, "fsdp", axis=0, tiled=True),
        lax.all_gather(ln2_gain, "fsdp", axis=0, tiled=True),
        lax.all_gather(ln2_bias, "fsdp", axis=0, tiled=True),
        lax.all_gather(w_fc, "fsdp", axis=0, tiled=True),
        lax.all_gather(b_fc, "fsdp", axis=0, tiled=True),
        lax.all_gather(w_out, "fsdp", axis=0, tiled=True),
        lax.all_gather(b_out, "fsdp", axis=0, tiled=True),
    )
    gain_one = gathered[0].astype(jnp.float32)
    shift_one = gathered[1].astype(jnp.float32)
    qkv_weight = gathered[2]
    query_bias = gathered[3].astype(jnp.float32)
    value_bias = gathered[4].astype(jnp.float32)
    proj_weight = gathered[5]
    proj_bias = gathered[6].astype(jnp.float32)
    gain_two = gathered[7].astype(jnp.float32)
    shift_two = gathered[8].astype(jnp.float32)
    fc_weight = gathered[9]
    fc_bias = gathered[10].astype(jnp.float32)
    out_weight = gathered[11]
    out_bias = gathered[12].astype(jnp.float32)
    row_count = block_in.shape[1]
    width = block_in.shape[2]
    head_count = HEADS
    head_width = width // head_count
    score_scale = 1.0 / math.sqrt(head_width)
    row_total = row_count * lax.axis_size("ctx")
    first_query = lax.axis_index("ctx") * row_count
    query_pos = first_query + jnp.arange(row_count, dtype=jnp.int32)
    last_query = first_query + row_count - 1
    inputs_wide = block_in[0].astype(jnp.float32)
    normed_one = layer_norm(inputs_wide, gain_one, shift_one).astype(jnp.bfloat16)
    projected = jnp.dot(normed_one, qkv_weight, preferred_element_type=jnp.float32)
    queries = (projected[:, :width] + query_bias).astype(jnp.bfloat16)
    keys_local = projected[:, width : 2 * width].astype(jnp.bfloat16)
    values_local = (projected[:, 2 * width :] + value_bias).astype(jnp.bfloat16)
    query_heads = queries.reshape(row_count, head_count, head_width)
    initial = (
        jnp.full((head_count, row_count), masked_score, jnp.float32),
        jnp.zeros((head_count, row_count), jnp.float32),
        jnp.zeros((row_count, head_count, head_width), jnp.float32),
    )
    key_span = lax.all_gather(keys_local, "ctx", axis=0, tiled=True)
    value_span = lax.all_gather(values_local, "ctx", axis=0, tiled=True)
    span_total = key_span.shape[0]
    attend_span_rows = math.gcd(span_total, 512)

    def one_step(step_index, inner):
        offset = step_index * attend_span_rows
        key_rows = lax.dynamic_slice_in_dim(key_span, offset, attend_span_rows, 0).reshape(
            attend_span_rows, head_count, head_width
        )
        value_rows = lax.dynamic_slice_in_dim(value_span, offset, attend_span_rows, 0).reshape(
            attend_span_rows, head_count, head_width
        )

        def one_computed(state):
            maximum, denominator, accumulated = state
            key_pos = offset + jnp.arange(attend_span_rows, dtype=jnp.int32)
            allowed = key_pos[None, :] <= query_pos[:, None]
            scores = (
                jnp.einsum(
                    "thd,shd->hts", query_heads, key_rows, preferred_element_type=jnp.float32
                )
                * score_scale
            )
            scores = jnp.where(allowed[None], scores, masked_score)
            new_max = jnp.maximum(maximum, jnp.max(scores, axis=2))
            weights = jnp.where(allowed[None], jnp.exp(scores - new_max[:, :, None]), 0.0)
            factor = jnp.exp(maximum - new_max)
            denominator = denominator * factor + jnp.sum(weights, axis=2)
            accumulated = accumulated * jnp.transpose(factor)[:, :, None] + jnp.einsum(
                "hts,shd->thd",
                weights.astype(jnp.bfloat16),
                value_rows,
                preferred_element_type=jnp.float32,
            )
            return (new_max, denominator, accumulated)

        return lax.cond(offset > last_query, lambda state: state, one_computed, inner)

    maximum, denominator, accumulated = lax.fori_loop(
        0, span_total // attend_span_rows, one_step, initial
    )
    log_sums = maximum + jnp.log(denominator)
    attended = accumulated / jnp.transpose(denominator)[:, :, None]
    attn_rows = lax.optimization_barrier(attended.reshape(row_count, width).astype(jnp.bfloat16))
    residual_one = (
        jnp.dot(attn_rows, proj_weight, preferred_element_type=jnp.float32)
        + proj_bias
        + inputs_wide
    )
    normed_two = layer_norm(residual_one, gain_two, shift_two).astype(jnp.bfloat16)
    hidden_pre = jnp.dot(normed_two, fc_weight, preferred_element_type=jnp.float32) + fc_bias
    activated = gelu_tanh(hidden_pre).astype(jnp.bfloat16)
    output = (
        jnp.dot(activated, out_weight, preferred_element_type=jnp.float32) + out_bias + residual_one
    ).astype(jnp.bfloat16)
    cotangent = out_grad[0]
    grad_wide = cotangent.astype(jnp.float32)
    grad_out_weight = jnp.einsum(
        "tf,td->fd", activated, cotangent, preferred_element_type=jnp.float32
    )
    grad_out_bias = jnp.sum(grad_wide, axis=0)
    grad_activated = jnp.einsum(
        "td,fd->tf", cotangent, out_weight, preferred_element_type=jnp.float32
    )
    unused, gelu_back = jax.vjp(gelu_tanh, hidden_pre)
    grad_hidden = gelu_back(grad_activated)[0]
    grad_hidden_low = grad_hidden.astype(jnp.bfloat16)
    grad_fc_weight = jnp.einsum(
        "td,tf->df", normed_two, grad_hidden_low, preferred_element_type=jnp.float32
    )
    grad_fc_bias = jnp.sum(grad_hidden, axis=0)
    grad_normed_two = jnp.einsum(
        "tf,df->td", grad_hidden_low, fc_weight, preferred_element_type=jnp.float32
    )
    unused, norm_back_two = jax.vjp(layer_norm, residual_one, gain_two, shift_two)
    grad_residual, grad_gain_two, grad_shift_two = norm_back_two(grad_normed_two)
    grad_residual = grad_residual + grad_wide
    grad_residual_low = grad_residual.astype(jnp.bfloat16)
    grad_proj_weight = jnp.einsum(
        "td,te->de", attn_rows, grad_residual_low, preferred_element_type=jnp.float32
    )
    grad_proj_bias = jnp.sum(grad_residual, axis=0)
    grad_attn = lax.optimization_barrier(
        jnp.einsum(
            "te,de->td", grad_residual_low, proj_weight, preferred_element_type=jnp.float32
        ).astype(jnp.bfloat16)
    )
    grad_heads = grad_attn.reshape(row_count, head_count, head_width)
    delta_sums = jnp.transpose(
        jnp.sum(
            grad_heads.astype(jnp.float32)
            * attn_rows.reshape(row_count, head_count, head_width).astype(jnp.float32),
            axis=2,
        )
    )
    keys_all, values_all = (
        lax.all_gather(keys_local, "ctx", axis=0, tiled=True),
        lax.all_gather(values_local, "ctx", axis=0, tiled=True),
    )
    span_rows = math.gcd(row_total, 512)
    span_count = row_total // span_rows
    key_blocks = keys_all.reshape(span_count, span_rows, head_count, head_width)
    value_blocks = values_all.reshape(span_count, span_rows, head_count, head_width)
    zero_query = jnp.zeros((row_count, head_count, head_width), jnp.float32)

    def back_step(grad_query, inputs):
        key_rows, value_rows, step_index = inputs
        start_pos = step_index * span_rows

        def back_computed(running):
            key_pos = start_pos + jnp.arange(span_rows, dtype=jnp.int32)
            allowed = key_pos[None, :] <= query_pos[:, None]
            grad_scores, probabilities = score_grads(
                query_heads,
                grad_heads,
                log_sums,
                delta_sums,
                key_rows,
                value_rows,
                allowed,
                score_scale,
            )
            rounded = probabilities.astype(jnp.bfloat16)
            grad_key = jnp.einsum(
                "hts,thd->shd", grad_scores, query_heads, preferred_element_type=jnp.float32
            )
            grad_value = jnp.einsum(
                "hts,thd->shd", rounded, grad_heads, preferred_element_type=jnp.float32
            )
            updated = running + jnp.einsum(
                "hts,shd->thd", grad_scores, key_rows, preferred_element_type=jnp.float32
            )
            return (
                updated,
                jnp.concatenate(
                    [grad_key.reshape(span_rows, width), grad_value.reshape(span_rows, width)],
                    axis=1,
                ),
            )

        def skipped(running):
            return (running, jnp.zeros((span_rows, 2 * width), jnp.float32))

        return lax.cond(start_pos > last_query, skipped, back_computed, grad_query)

    grad_query, key_terms = lax.scan(
        back_step, zero_query, (key_blocks, value_blocks, jnp.arange(span_count, dtype=jnp.int32))
    )
    own_terms = lax.psum_scatter(
        key_terms.reshape(row_total, 2 * width), "ctx", scatter_dimension=0, tiled=True
    )
    grad_keys = own_terms[:, :width]
    grad_values = own_terms[:, width:]
    grad_query = grad_query.reshape(row_count, width)
    grad_query_bias = jnp.sum(grad_query, axis=0)
    grad_value_bias = jnp.sum(grad_values, axis=0)
    grad_projected = jnp.concatenate([grad_query, grad_keys, grad_values], axis=1).astype(
        jnp.bfloat16
    )
    grad_qkv_weight = jnp.einsum(
        "td,te->de", normed_one, grad_projected, preferred_element_type=jnp.float32
    )
    grad_normed_one = jnp.einsum(
        "te,de->td", grad_projected, qkv_weight, preferred_element_type=jnp.float32
    )
    unused, norm_back_one = jax.vjp(layer_norm, inputs_wide, gain_one, shift_one)
    grad_inputs, grad_gain_one, grad_shift_one = norm_back_one(grad_normed_one)
    grad_inputs = grad_inputs + grad_residual
    shards = (
        lax.psum_scatter(
            grad_gain_one.astype(jnp.bfloat16), "fsdp", scatter_dimension=0, tiled=True
        ).astype(jnp.float32),
        lax.psum_scatter(
            grad_shift_one.astype(jnp.bfloat16), "fsdp", scatter_dimension=0, tiled=True
        ).astype(jnp.float32),
        lax.psum_scatter(
            grad_qkv_weight.astype(jnp.bfloat16), "fsdp", scatter_dimension=0, tiled=True
        ).astype(jnp.float32),
        lax.psum_scatter(
            grad_query_bias.astype(jnp.bfloat16), "fsdp", scatter_dimension=0, tiled=True
        ).astype(jnp.float32),
        lax.psum_scatter(
            grad_value_bias.astype(jnp.bfloat16), "fsdp", scatter_dimension=0, tiled=True
        ).astype(jnp.float32),
        lax.psum_scatter(
            grad_proj_weight.astype(jnp.bfloat16), "fsdp", scatter_dimension=0, tiled=True
        ).astype(jnp.float32),
        lax.psum_scatter(
            grad_proj_bias.astype(jnp.bfloat16), "fsdp", scatter_dimension=0, tiled=True
        ).astype(jnp.float32),
        lax.psum_scatter(
            grad_gain_two.astype(jnp.bfloat16), "fsdp", scatter_dimension=0, tiled=True
        ).astype(jnp.float32),
        lax.psum_scatter(
            grad_shift_two.astype(jnp.bfloat16), "fsdp", scatter_dimension=0, tiled=True
        ).astype(jnp.float32),
        lax.psum_scatter(
            grad_fc_weight.astype(jnp.bfloat16), "fsdp", scatter_dimension=0, tiled=True
        ).astype(jnp.float32),
        lax.psum_scatter(
            grad_fc_bias.astype(jnp.bfloat16), "fsdp", scatter_dimension=0, tiled=True
        ).astype(jnp.float32),
        lax.psum_scatter(
            grad_out_weight.astype(jnp.bfloat16), "fsdp", scatter_dimension=0, tiled=True
        ).astype(jnp.float32),
        lax.psum_scatter(
            grad_out_bias.astype(jnp.bfloat16), "fsdp", scatter_dimension=0, tiled=True
        ).astype(jnp.float32),
    )
    totals = lax.psum(
        (
            shards[0],
            shards[1],
            shards[2],
            shards[3],
            shards[4],
            shards[5],
            shards[6],
            shards[7],
            shards[8],
            shards[9],
            shards[10],
            shards[11],
            shards[12],
        ),
        "ctx",
    )
    return (
        output[None],
        grad_inputs[None],
        totals[0],
        totals[1],
        totals[2],
        totals[3],
        totals[4],
        totals[5],
        totals[6],
        totals[7],
        totals[8],
        totals[9],
        totals[10],
        totals[11],
        totals[12],
    )


def solution(mesh):
    in_specs = (
        P("fsdp", "ctx", None),
        P("fsdp", "ctx", None),
        P("fsdp"),
        P("fsdp"),
        P("fsdp", None),
        P("fsdp"),
        P("fsdp"),
        P("fsdp", None),
        P("fsdp"),
        P("fsdp"),
        P("fsdp"),
        P("fsdp", None),
        P("fsdp"),
        P("fsdp", None),
        P("fsdp"),
    )
    out_specs = (
        P("fsdp", "ctx", None),
        P("fsdp", "ctx", None),
        P("fsdp"),
        P("fsdp"),
        P("fsdp", None),
        P("fsdp"),
        P("fsdp"),
        P("fsdp", None),
        P("fsdp"),
        P("fsdp"),
        P("fsdp"),
        P("fsdp", None),
        P("fsdp"),
        P("fsdp", None),
        P("fsdp"),
    )
    return jax.shard_map(body, mesh=mesh, in_specs=in_specs, out_specs=out_specs, check_vma=False)
```

profile of v0, /device:TPU:1, one launch (start us, length us, event | category | flops | bytes accessed | tf_op | source)
XLA Modules:
  0.0 1728.8 jit_solution(4564429500221950973)
XLA Ops:
  8.7 6.1 all-gather.1
  15.5 4.7 all-gather
  23.0 43.4 %all-gather.16.cloned.1.call-done = bf16[768,2304]{1,0:T(8,128)(2,1)} async-done(((bf16[384,2304]{1,0:T(8,128)(2,1)}), bf16[768,2304]{1,0:T(8,128)(2,1)}) %all-gather.16.cloned.1.call-update) | async-done | bytes 3538960 | tf_op jit(solution)/shard_map/all_gather | solution.py:70
  70.1 4.7 all-gather.3
  74.8 4.7 all-gather.2
  82.2 4.7 all-gather.4
  87.0 4.8 all-gather.7
  91.8 4.7 all-gather.6
  96.6 4.7 all-gather.5
  101.5 86.3 %all-gather.18.cloned.1.call-done = bf16[8192,768]{1,0:T(8,128)(2,1)} async-done(((bf16[128,768]{1,0:T(8,128)(2,1)}), bf16[8192,768]{1,0:T(8,128)(2,1)}) %all-gather.18.cloned.1.call-update) | async-done | bytes 12582928 | tf_op jit(solution)/shard_map/all_gather | solution.py:116
  187.8 16.4 copy.76
  204.2 103.2 %all-gather.20.cloned.1.call-done = bf16[8192,768]{1,0:T(8,128)(2,1)} async-done(((bf16[128,768]{1,0:T(8,128)(2,1)}), bf16[8192,768]{1,0:T(8,128)(2,1)}) %all-gather.20.cloned.1.call-update) | async-done | bytes 12582928 | tf_op jit(solution)/shard_map/all_gather | solution.py:117
  307.4 15.8 copy.77
  323.2 5.7 while.34
  323.3 4.4 conditional.6
  329.0 5.8 all-gather.22.cloned.1.call-done
  336.8 65.6 %all-gather.24.cloned.1.call-done = bf16[768,3072]{1,0:T(8,128)(2,1)} async-done(((bf16[384,3072]{1,0:T(8,128)(2,1)}), bf16[768,3072]{1,0:T(8,128)(2,1)}) %all-gather.24.cloned.1.call-update) | async-done | bytes 4718608 | tf_op jit(solution)/shard_map/all_gather | solution.py:77
  405.7 64.3 %all-gather.26.cloned.1.call-done = bf16[3072,768]{1,0:T(8,128)(2,1)} async-done(((bf16[1536,768]{1,0:T(8,128)(2,1)}), bf16[3072,768]{1,0:T(8,128)(2,1)}) %all-gather.26.cloned.1.call-update) | async-done | bytes 4718608 | tf_op jit(solution)/shard_map/all_gather | solution.py:79
  470.0 5.4 fusion.95
  478.0 9.5 copy.108
  487.6 18.8 %copy.81 = bf16[16,512,12,64]{1,3,2,0:T(8,128)(2,1)} copy(bf16[16,512,12,64]{1,0,3,2:T(8,128)(2,1)S(1)} %bitcast.175) | data formatting | bytes 25165824
  507.0 4.6 copy.109
  511.6 18.6 %copy.82 = bf16[16,512,12,64]{1,3,2,0:T(8,128)(2,1)} copy(bf16[16,512,12,64]{1,0,3,2:T(8,128)(2,1)S(1)} %bitcast.176) | data formatting | bytes 25165824
  533.4 134.6 %while.35 = (s32[]{:T(128)}, f32[128,12,64]{0,2,1:T(8,128)}, f32[16,512,1536]{2,1,0:T(8,128)}, s32[16]{0:T(128)S(1)}, s32[]{:T(128)}, /*index=5*/bf16[16,512,12,...) while((s32[]{:T(128)}, f32[128,12,64]{0,2,1:T(8,128)}, ...), condition=%wide.region_16.17_spmd.clone, body=%wide.region_13.16_spmd.clone.sunk | while | flops 514491008 | bytes 40333600 | solution.py:262
  534.6 10.1 conditional.7
  547.1 3.7 constant_dynamic-update-slice_fusion.2
  554.9 3.8 constant_dynamic-update-slice_fusion.2
  562.7 3.8 constant_dynamic-update-slice_fusion.2
  570.5 3.7 constant_dynamic-update-slice_fusion.2
  578.3 3.7 constant_dynamic-update-slice_fusion.2
  586.1 3.7 constant_dynamic-update-slice_fusion.2
  593.9 3.8 constant_dynamic-update-slice_fusion.2
  601.7 3.8 constant_dynamic-update-slice_fusion.2
  609.5 3.8 constant_dynamic-update-slice_fusion.2
  617.3 3.8 constant_dynamic-update-slice_fusion.2
  632.9 3.8 constant_dynamic-update-slice_fusion.2
  648.6 3.8 constant_dynamic-update-slice_fusion.2
  656.4 3.8 constant_dynamic-update-slice_fusion.2
  675.9 3.8 convolution_convert_fusion
  681.3 498.5 %reduce-scatter.6.cloned.1.call-done = f32[128,1536]{1,0:T(8,128)} async-done(((f32[8192,1536]{1,0:T(8,128)}), f32[128,1536]{1,0:T(8,128)}) %reduce-scatter.6.cloned.1.call-update) | async-done | bytes 786448 | tf_op jit(solution)/shard_map/reduce_scatter | solution.py:265
  1185.3 4.8 all-gather.8
  1193.9 4.2 fusion.55
  1198.0 12.9 reduce-scatter.10.cloned.1.call-done
  1210.9 66.5 %reduce-scatter.12.cloned.1.call-done = bf16[384,3072]{1,0:T(8,128)(2,1)} async-done(((bf16[768,3072]{1,0:T(8,128)(2,1)}), bf16[384,3072]{1,0:T(8,128)(2,1)}) %reduce-scatter.12.cloned.1.call-update) | async-done | bytes 2359312 | tf_op jit(solution)/shard_map/reduce_scatter | solution.py:313
  1277.5 66.2 %reduce-scatter.14.cloned.1.call-done = bf16[1536,768]{1,0:T(8,128)(2,1)} async-done(((bf16[3072,768]{1,0:T(8,128)(2,1)}), bf16[1536,768]{1,0:T(8,128)(2,1)}) %reduce-scatter.14.cloned.1.call-update) | async-done | bytes 2359312 | tf_op jit(solution)/shard_map/reduce_scatter | solution.py:319
  1348.8 7.0 all-reduce.10
  1356.2 41.6 %reduce-scatter.8.cloned.1.call-done = bf16[384,2304]{1,0:T(8,128)(2,1)} async-done(((bf16[768,2304]{1,0:T(8,128)(2,1)}), bf16[384,2304]{1,0:T(8,128)(2,1)}) %reduce-scatter.8.cloned.1.call-update) | async-done | bytes 1769488 | tf_op jit(solution)/shard_map/reduce_scatter | solution.py:292
  1397.8 324.4 %all-reduce.12 = (f32[384]{0:T(512)}, f32[384]{0:T(512)}, f32[384,2304]{1,0:T(8,128)}, f32[384]{0:T(512)}, f32[384]{0:T(512)}, /*index=5*/f32[384,768]{1,0:T(8,1...) all-reduce(f32[384]{0:T(512)S(1)} %get-tuple-element.680, ...), channel_id=1, replica_groups=mesh['ctx'=64,'fsdp'=2] {'ctx'}, use_global_device_ids=true, to_apply=%region_22.23 | all-reduce | flops 3543552 | bytes 21270528 | tf_op jit(solution)/shard_map/psum | solution.py:326
  (380 shorter events, 131.0 us)
Async XLA Ops:
  7.2 59.3 %all-gather.16.cloned.1.call-start = ((), (), s32[]{:S(2)}) async-start(), calls=%async_computation.5 | async-start | bytes 5308416 | tf_op jit(solution)/shard_map/all_gather | solution.py:70
  7.9 62.1 %copy-start.47 = (bf16[384]{0:T(512)(128)(2,1)S(1)}, bf16[384]{0:T(512)(128)(2,1)}, u32[]{:S(2)}) copy-start(bf16[384]{0:T(512)(128)(2,1)} %param.29) | copy-start | bytes 2308
  7.9 66.9 %copy-start.48 = (bf16[384]{0:T(512)(128)(2,1)S(1)}, bf16[384]{0:T(512)(128)(2,1)}, u32[]{:S(2)}) copy-start(bf16[384]{0:T(512)(128)(2,1)} %param.28) | copy-start | bytes 2308
  7.9 179.8 %all-gather.18.cloned.1.call-start = ((), (), s32[]{:S(2)}) async-start(), calls=%async_computation.6 | async-start | bytes 12779520 | tf_op jit(solution)/shard_map/all_gather | solution.py:116
  14.8 64.7 %copy-start.26 = (f32[768]{0:T(1024)}, f32[768]{0:T(1024)S(1)}, u32[]{:S(2)}) copy-start(f32[768]{0:T(1024)S(1)} %reshape.253) | copy-start | bytes 9220
  20.2 59.3 %copy-start.19 = (f32[768]{0:T(1024)}, f32[768]{0:T(1024)S(1)}, u32[]{:S(2)}) copy-start(f32[768]{0:T(1024)S(1)} %reshape.252) | copy-start | bytes 9220
  21.3 58.3 %copy-start.31 = (f32[128]{0:T(128)}, f32[128]{0:T(128)S(1)}, u32[]{:S(2)}) copy-start(f32[128]{0:T(128)S(1)} %broadcast_multiply_fusion.1) | copy-start | bytes 1540
  23.0 56.5 %copy-start.36 = (f32[128]{0:T(128)}, f32[128]{0:T(128)S(1)}, u32[]{:S(2)}) copy-start(f32[128]{0:T(128)S(1)} %fusion.82) | copy-start | bytes 1540
  70.0 237.4 %all-gather.20.cloned.1.call-start = ((), (), s32[]{:S(2)}) async-start(), calls=%async_computation.7 | async-start | bytes 12779520 | tf_op jit(solution)/shard_map/all_gather | solution.py:117
  79.6 7.4 copy-start.46
  79.6 12.2 copy-start.50
  79.6 16.9 copy-start.51
  80.4 254.4 %all-gather.22.cloned.1.call-start = ((), (), s32[]{:S(2)}) async-start(), calls=%async_computation.8 | async-start | bytes 1769472 | tf_op jit(solution)/shard_map/all_gather | solution.py:73
  81.0 321.4 %all-gather.24.cloned.1.call-start = ((), (), s32[]{:S(2)}) async-start(), calls=%async_computation.9 | async-start | bytes 7077888 | tf_op jit(solution)/shard_map/all_gather | solution.py:77
  81.5 388.4 %all-gather.26.cloned.1.call-start = ((), (), s32[]{:S(2)}) async-start(), calls=%async_computation.10 | async-start | bytes 7077888 | tf_op jit(solution)/shard_map/all_gather | solution.py:79
  82.1 1097.7 %reduce-scatter.6.cloned.1.call-start = ((), (), s32[]{:S(2)}) async-start(), calls=%async_computation.11 | async-start | bytes 51118080 | tf_op jit(solution)/shard_map/reduce_scatter | solution.py:265
  96.5 305.9 %copy-start.24 = (f32[768]{0:T(1024)}, f32[768]{0:T(1024)S(1)}, u32[]{:S(2)}) copy-start(f32[768]{0:T(1024)S(1)} %reshape.258) | copy-start | bytes 9220
  101.3 301.1 %copy-start.21 = (f32[768]{0:T(1024)}, f32[768]{0:T(1024)S(1)}, u32[]{:S(2)}) copy-start(f32[768]{0:T(1024)S(1)} %reshape.257) | copy-start | bytes 9220
  323.2 11.6 copy-start.5
  329.0 202.6 %copy-start.11 = (bf16[128,12,64]{0,2,1:T(8,128)(2,1)}, bf16[128,12,64]{0,2,1:T(8,128)(2,1)S(1)}, u32[]{:S(2)}) copy-start(bf16[128,12,64]{0,2,1:T(8,128)(2,1)S(1)} %divide_convert_fusion) | copy-start | bytes 589828
  336.5 141.2 %copy-start.1 = (f32[128,768]{1,0:T(8,128)}, f32[128,768]{1,0:T(8,128)S(1)}, u32[]{:S(2)}) copy-start(f32[128,768]{1,0:T(8,128)S(1)} %get-tuple-element.668) | copy-start | bytes 1179652
  336.6 69.1 %copy-start.28 = (f32[128]{0:T(128)}, f32[128]{0:T(128)S(1)}, u32[]{:S(2)}) copy-start(f32[128]{0:T(128)S(1)} %broadcast_multiply_fusion) | copy-start | bytes 1540
  336.8 68.9 %copy-start.55 = (f32[128]{0:T(128)}, f32[128]{0:T(128)S(1)}, u32[]{:S(2)}) copy-start(f32[128]{0:T(128)S(1)} %multiply_reduce_fusion.2) | copy-start | bytes 1540
  336.8 68.9 %copy-start.33 = (f32[128]{0:T(128)}, f32[128]{0:T(128)S(1)}, u32[]{:S(2)}) copy-start(f32[128]{0:T(128)S(1)} %fusion.83) | copy-start | bytes 1540
  402.4 67.6 %copy-start.8 = (bf16[1,128,768]{2,1,0:T(8,128)(2,1)S(1)}, bf16[1,128,768]{2,1,0:T(8,128)(2,1)}, u32[]{:S(2)}) copy-start(bf16[1,128,768]{2,1,0:T(8,128)(2,1)} %param.24) | copy-start | bytes 589828
  405.7 69.7 %copy-start.3 = (f32[128,3072]{1,0:T(8,128)}, f32[128,3072]{1,0:T(8,128)S(1)}, u32[]{:S(2)}) copy-start(f32[128,3072]{1,0:T(8,128)S(1)} %convolution_add_fusion) | copy-start | bytes 4718596
  470.0 5.4 copy-start.29
  470.0 5.4 copy-start.34
  478.0 52.2 %copy-start.6 = (f32[128,768]{1,0:T(8,128)}, f32[128,768]{1,0:T(8,128)S(1)}, u32[]{:S(2)}) copy-start(f32[128,768]{1,0:T(8,128)S(1)} %get-tuple-element.656) | copy-start | bytes 1179652
  478.0 52.2 %copy-start.43 = (f32[128]{0:T(128)}, f32[128]{0:T(128)S(1)}, u32[]{:S(2)}) copy-start(f32[128]{0:T(128)S(1)} %negate_multiply_fusion.1) | copy-start | bytes 1540
  487.6 19.4 %slice-start = ((s8[12582912]{0:T(1024)(128)(4,1)}), s8[4194304]{0:T(1024)(128)(4,1)S(1)}, s32[]{:S(2)}) async-start(s8[12582912]{0:T(1024)(128)(4,1)} %bitcast.169), calls=%async_computation.16 | async-start | bytes 8388608
  487.6 19.4 %slice-start.1 = ((s8[12582912]{0:T(1024)(128)(4,1)}), s8[4194304]{0:T(1024)(128)(4,1)S(1)}, s32[]{:S(2)}) async-start(s8[12582912]{0:T(1024)(128)(4,1)} %bitcast.169), calls=%async_computation.17 | async-start | bytes 8388608
  487.6 19.4 %slice-start.2 = ((s8[12582912]{0:T(1024)(128)(4,1)}), s8[4194304]{0:T(1024)(128)(4,1)S(1)}, s32[]{:S(2)}) async-start(s8[12582912]{0:T(1024)(128)(4,1)} %bitcast.169), calls=%async_computation.18 | async-start | bytes 8388608
  511.6 18.6 %copy-start.10 = (bf16[768,768]{1,0:T(8,128)(2,1)S(1)}, bf16[768,768]{1,0:T(8,128)(2,1)}, u32[]{:S(2)}) copy-start(bf16[768,768]{1,0:T(8,128)(2,1)} %all-gather.22.cloned.1.call-done) | copy-start | bytes 3538948
  668.1 542.8 %reduce-scatter.10.cloned.1.call-start = ((), (), s32[]{:S(2)}) async-start(), calls=%async_computation.13 | async-start | bytes 1769472 | tf_op jit(solution)/shard_map/reduce_scatter | solution.py:301
  670.7 606.8 %reduce-scatter.12.cloned.1.call-start = ((), (), s32[]{:S(2)}) async-start(), calls=%async_computation.14 | async-start | bytes 7077888 | tf_op jit(solution)/shard_map/reduce_scatter | solution.py:313
  674.5 669.2 %reduce-scatter.14.cloned.1.call-start = ((), (), s32[]{:S(2)}) async-start(), calls=%async_computation.15 | async-start | bytes 7077888 | tf_op jit(solution)/shard_map/reduce_scatter | solution.py:319
  679.7 501.3 %copy-start.20 = (f32[768]{0:T(1024)S(1)}, f32[768]{0:T(1024)}, u32[]{:S(2)}) copy-start(f32[768]{0:T(1024)} %copy-done.19) | copy-start | bytes 9220
  679.7 501.3 %copy-start.27 = (f32[768]{0:T(1024)S(1)}, f32[768]{0:T(1024)}, u32[]{:S(2)}) copy-start(f32[768]{0:T(1024)} %copy-done.26) | copy-start | bytes 9220
  679.7 501.3 %copy-start.32 = (f32[128]{0:T(128)S(1)}, f32[128]{0:T(128)}, u32[]{:S(2)}) copy-start(f32[128]{0:T(128)} %copy-done.31) | copy-start | bytes 1540
  679.8 718.1 %reduce-scatter.8.cloned.1.call-start = ((), (), s32[]{:S(2)}) async-start(), calls=%async_computation.12 | async-start | bytes 5308416 | tf_op jit(solution)/shard_map/reduce_scatter | solution.py:292
  681.2 503.4 %copy-start.17 = (bf16[128,768]{1,0:T(8,128)(2,1)}, bf16[128,768]{1,0:T(8,128)(2,1)S(1)}, u32[]{:S(2)}) copy-start(bf16[128,768]{1,0:T(8,128)(2,1)S(1)} %copy.84) | copy-start | bytes 589828
  1184.6 6.7 copy-start.57
  1193.9 149.8 %copy-start.15 = (f32[128,1536]{1,0:T(8,128)S(1)}, f32[128,1536]{1,0:T(8,128)}, u32[]{:S(2)}) copy-start(f32[128,1536]{1,0:T(8,128)} %reduce-scatter.6.cloned.1.call-done) | copy-start | bytes 2359300
  1198.0 149.5 %copy-start.54 = (f32[128]{0:T(128)S(1)}, f32[128]{0:T(128)}, u32[]{:S(2)}) copy-start(f32[128]{0:T(128)} %copy-done.53) | copy-start | bytes 1540
  1198.0 149.5 %copy-start.37 = (f32[128]{0:T(128)S(1)}, f32[128]{0:T(128)}, u32[]{:S(2)}) copy-start(f32[128]{0:T(128)} %copy-done.36) | copy-start | bytes 1540
  1198.0 149.8 %copy-start.45 = (f32[128]{0:T(128)S(1)}, f32[128]{0:T(128)}, u32[]{:S(2)}) copy-start(f32[128]{0:T(128)} %copy-done.43) | copy-start | bytes 1540
  1343.8 54.0 %copy-start.18 = (bf16[384,768]{1,0:T(8,128)(2,1)S(1)}, bf16[384,768]{1,0:T(8,128)(2,1)}, u32[]{:S(2)}) copy-start(bf16[384,768]{1,0:T(8,128)(2,1)} %reduce-scatter.10.cloned.1.call-done) | copy-start | bytes 1769476
  (24 other events, 70.4 us)
Sparse Core Ops, SparseCore 0:
  9.7 56.7 all-gather.15
  70.1 117.5 all-gather.17
  190.1 117.2 all-gather.19
  308.9 25.8 all-gather.21
  336.3 66.0 all-gather.23
  403.9 66.0 all-gather.25
  668.1 511.6 reduce-scatter.5
  1182.7 28.1 reduce-scatter.9
  1214.0 63.3 reduce-scatter.11
  1280.3 63.3 reduce-scatter.13
  1346.7 51.0 reduce-scatter.7
where the time goes:
time: 1740 us; the launch traced here: 1730 us
  waiting for transfers between devices  1060 us (61%)
  blocking collectives  375 us (22%)
  local copies, waits for them, and re-layouts  208 us (12%)
  matrix products  48 us (3%)
    reduce_scatter x1, waiting for transfers between devices, body(): lax.psum_scatter(key_terms.reshape(row_total, 2 * width), 'ctx', scatter_...  499 us
    psum x1, blocking collectives, body(): lax.psum((shards[0], shards[1], shards[2], shards[3], shards[4], shards[5...  324 us
    all_gather x1, waiting for transfers between devices, body(): value_span = lax.all_gather(values_local, 'ctx', axis=0, tiled=True)  103 us
    dynamic_update_slice x32, local copies, waits for them, and re-layouts, body(): lax.scan(back_step, zero_query, (key_blocks, value_blocks, jnp.arange(spa...  98.1 us
    unnamed x138, local copies, waits for them, and re-layouts  89.3 us
    all_gather x1, waiting for transfers between devices, body(): key_span = lax.all_gather(keys_local, 'ctx', axis=0, tiled=True)  86.3 us
    reduce_scatter x1, waiting for transfers between devices, body(): lax.psum_scatter(grad_fc_weight.astype(jnp.bfloat16), 'fsdp', scatter_dim...  66.5 us
    reduce_scatter x1, waiting for transfers between devices, body(): lax.psum_scatter(grad_out_weight.astype(jnp.bfloat16), 'fsdp', scatter_di...  66.2 us
  transfers between devices with their start and end apart: 11, of which 11 were waited for; matrix products, arithmetic and copies ran while one was open for 4% of the time, Pallas kernels for 0%

commit v1 on v0

v1 whole, which is shorter than its diff:
```python
import jax
import jax.numpy as jnp
from jax import lax
from jax.experimental import pallas as pl
from jax.experimental.pallas import tpu as pltpu
from jax.sharding import Mesh, PartitionSpec as P

TP = ("zl", "xh")
SEQ_AXES = ("xl", "yh", "yl", "core")
CTX = TP + SEQ_AXES
EPS = 1e-05
GELU_F = 0.7978845608028654
GELU_C = 0.044715
NEG = -1e30
F32 = jnp.float32
BF16 = jnp.bfloat16
NT = (((1,), (1,)), ((), ()))
VMEM_LIMIT = 56 * 1024 * 1024


def lane_half(shape):
    return lax.broadcasted_iota(jnp.int32, shape, len(shape) - 1) >= 64


def slot_only(values, slot):
    lane = lax.broadcasted_iota(jnp.int32, values.shape, 1)
    keep = jnp.logical_and(lane >= 64 * slot, lane < 64 * slot + 64)
    return jnp.where(keep, values, jnp.zeros_like(values))


def wide(values):
    return jnp.concatenate([values] * 4, axis=1)


def pieces(values):
    high = values.astype(BF16)
    rest = values - high.astype(F32)
    middle = rest.astype(BF16)
    low = (rest - middle.astype(F32)).astype(BF16)
    return (high, middle, low)


def chunk_rows(ref, rank, chunk):
    rows = ref[pl.ds(4 * lax.rem(chunk, 4), 4), rank ^ (chunk // 4)]
    return rows.reshape(512, rows.shape[-1])


def causal(scores, first_query, first_key, keys_in_rows):
    rows = lax.broadcasted_iota(jnp.int32, (128, 512), 0)
    cols = lax.broadcasted_iota(jnp.int32, (128, 512), 1)
    if keys_in_rows:
        allowed = first_key + rows <= first_query + cols
    else:
        allowed = first_key + cols <= first_query + rows
    return jnp.concatenate(
        [jnp.where(allowed, scores[128 * h : 128 * h + 128], NEG) for h in range(3)], axis=0
    )


def value_halves(product):
    return jnp.concatenate([product[:256, 128:], product[256:, :128]], axis=0)


def row_halves(product):
    return jnp.concatenate([product[:256, :128], product[256:, 128:]], axis=0)


def forward_kernel(pos_ref, q_ref, kv_ref, attn_ref, qaug_ref, lse_ref, m_ref, l_ref, acc_ref):
    seq = pos_ref[0]
    rank = pos_ref[1]

    def tile(k, carry):
        slot = rank ^ k
        block = k * 16 + seq
        q_rows = q_ref[slot]
        queries = jnp.concatenate([slot_only(q_rows, h) for h in range(3)], axis=0)
        m_ref[...] = jnp.full(m_ref.shape, NEG, F32)
        l_ref[...] = jnp.zeros(l_ref.shape, F32)
        acc_ref[...] = jnp.zeros(acc_ref.shape, F32)

        def step(chunk, masked):
            kv = chunk_rows(kv_ref, rank, chunk)
            scores = lax.dot_general(queries, kv[:, :256], NT, preferred_element_type=F32)
            if masked:
                scores = causal(scores, block * 128, chunk * 512, False)
            before = m_ref[...]
            after = jnp.maximum(before, jnp.max(scores, axis=1, keepdims=True))
            weights = jnp.exp(scores - wide(after))
            factor = jnp.exp(before - after)
            m_ref[...] = after
            partial = (weights[:, :128] + weights[:, 128:256]) + (
                weights[:, 256:384] + weights[:, 384:]
            )
            l_ref[...] = l_ref[...] * factor + partial
            acc_ref[...] = acc_ref[...] * factor + value_halves(
                jnp.dot(weights.astype(BF16), kv[:, 128:], preferred_element_type=F32)
            )

        last = block // 4

        def full(chunk, inner):
            step(chunk, False)
            return inner

        lax.fori_loop(0, last, full, 0)
        step(last, True)
        lane = lax.broadcasted_iota(jnp.int32, (128, 128), 1)
        extra = jnp.zeros((128, 128), BF16)
        total = jnp.sum(l_ref[...], axis=1, keepdims=True)
        log_sum = m_ref[...] + jnp.log(total)
        lse_ref[slot] = log_sum
        outs = acc_ref[...] / total
        for p, part in enumerate(pieces(-log_sum)):
            for h in range(3):
                extra = jnp.where(
                    lane == 64 + 3 * h + p, part[128 * h : 128 * h + 128], extra
                )
        attn_ref[slot, :, :128] = jnp.where(lane < 64, outs[:128], outs[128:256]).astype(BF16)
        attn_ref[slot, :, 128:] = jnp.where(lane < 64, 0.0, outs[256:]).astype(BF16)
        qaug_ref[slot, :, :128] = q_rows[:, :128]
        qaug_ref[slot, :, 128:] = jnp.where(lane < 64, q_rows[:, 128:], extra)
        return carry

    lax.fori_loop(0, 4, tile, 0)


def vmem_spec():
    return pl.BlockSpec(memory_space=pltpu.VMEM)


def forward_attention(pos, q, kv):
    return pl.pallas_call(
        forward_kernel,
        out_shape=(
            jax.ShapeDtypeStruct((4, 128, 256), BF16),
            jax.ShapeDtypeStruct((4, 128, 256), BF16),
            jax.ShapeDtypeStruct((4, 384, 128), F32),
        ),
        in_specs=[pl.BlockSpec(memory_space=pltpu.SMEM), vmem_spec(), vmem_spec()],
        out_specs=(vmem_spec(), vmem_spec(), vmem_spec()),
        scratch_shapes=[pltpu.VMEM((384, 128), F32)] * 3,
        compiler_params=pltpu.CompilerParams(vmem_limit_bytes=VMEM_LIMIT),
        cost_estimate=pl.CostEstimate(
            flops=3 * 512 * 4096 * 512, transcendentals=3 * 512 * 4096, bytes_accessed=8 * 2**20
        ),
        name="attention_forward",
    )(pos, q, kv)


def grad_rows_kernel(dr_ref, w_ref, attn_ref, do_ref, delta_ref):
    lane = lax.broadcasted_iota(jnp.int32, (512, 128), 1)
    grads = lax.dot_general(dr_ref[...], w_ref[...], NT, preferred_element_type=F32).astype(BF16)
    attn = attn_ref[...].reshape(512, 256).astype(F32)
    product = grads.astype(F32) * attn
    extra = jnp.zeros((512, 128), BF16)
    for h, run in enumerate((0, 1, 3)):
        delta = jnp.sum(slot_only(product, run), axis=1, keepdims=True)
        delta = jnp.broadcast_to(delta, (512, 128))
        for k in range(4):
            delta_ref[k, 128 * h : 128 * h + 128] = delta[128 * k : 128 * k + 128]
        for p, piece in enumerate(pieces(-delta)):
            extra = jnp.where(lane == 3 * h + p, piece, extra)
    do_ref[:, :, :128] = grads[:, :128].reshape(4, 128, 128)
    do_ref[:, :, 128:] = jnp.where(lane < 64, extra, grads[:, 128:]).reshape(4, 128, 128)


def grad_rows(dr_low, w_rows, attn):
    return pl.pallas_call(
        grad_rows_kernel,
        out_shape=(
            jax.ShapeDtypeStruct((4, 128, 256), BF16),
            jax.ShapeDtypeStruct((4, 384, 128), F32),
        ),
        in_specs=[vmem_spec(), vmem_spec(), vmem_spec()],
        out_specs=(vmem_spec(), vmem_spec()),
        compiler_params=pltpu.CompilerParams(vmem_limit_bytes=VMEM_LIMIT),
        name="attention_grad_rows",
    )(dr_low, w_rows, attn)


def query_grad_kernel(pos_ref, q_ref, do_ref, lse_ref, delta_ref, kv_ref, dq_ref, acc_ref):
    seq = pos_ref[0]
    rank = pos_ref[1]

    def tile(k, carry):
        slot = rank ^ k
        block = k * 16 + seq
        q_rows = q_ref[slot]
        do_rows = do_ref[slot]
        queries = jnp.concatenate([slot_only(q_rows, h) for h in range(3)], axis=0)
        turned = jnp.concatenate([do_rows[:, 128:], do_rows[:, :128]], axis=1)
        grads = jnp.concatenate([slot_only(turned, run) for run in (2, 3, 1)], axis=0)
        acc_ref[...] = jnp.zeros(acc_ref.shape, F32)

        def step(chunk, masked):
            kv = chunk_rows(kv_ref, rank, chunk)
            scores = lax.dot_general(queries, kv[:, :256], NT, preferred_element_type=F32)
            scores = scores - wide(lse_ref[slot])
            if masked:
                scores = causal(scores, block * 128, chunk * 512, False)
            weights = jnp.exp(scores)
            grad_weights = lax.dot_general(grads, kv[:, 128:], NT, preferred_element_type=F32)
            grad_scores = (weights * (grad_weights - wide(delta_ref[slot]))).astype(BF16)
            acc_ref[...] += row_halves(
                jnp.dot(grad_scores, kv[:, :256], preferred_element_type=F32)
            )

        last = block // 4

        def full(chunk, inner):
            step(chunk, False)
            return inner

        lax.fori_loop(0, last, full, 0)
        step(last, True)
        lane = lax.broadcasted_iota(jnp.int32, (128, 128), 1)
        acc = acc_ref[...] * 0.125
        dq_ref[slot, :, :128] = jnp.where(lane < 64, acc[:128], acc[128:256])
        dq_ref[slot, :, 128:] = jnp.where(lane < 64, acc[256:], 0.0)
        return carry

    lax.fori_loop(0, 4, tile, 0)


def query_grad(pos, q, do, lse, delta, kv):
    return pl.pallas_call(
        query_grad_kernel,
        out_shape=jax.ShapeDtypeStruct((4, 128, 256), F32),
        in_specs=[pl.BlockSpec(memory_space=pltpu.SMEM)] + [vmem_spec()] * 5,
        out_specs=vmem_spec(),
        scratch_shapes=[pltpu.VMEM((384, 128), F32)],
        compiler_params=pltpu.CompilerParams(vmem_limit_bytes=VMEM_LIMIT),
        cost_estimate=pl.CostEstimate(
            flops=3 * 512 * 4096 * 768, transcendentals=3 * 512 * 4096, bytes_accessed=8 * 2**20
        ),
        name="attention_query_grad",
    )(pos, q, do, lse, delta, kv)


def key_grad_kernel(pos_ref, kv_ref, qg_ref, dog_ref, dkv_ref, dk_ref, dv_ref):
    seq = pos_ref[0]
    rank = pos_ref[1]

    def tile(k, carry):
        slot = rank ^ k
        block = k * 16 + seq
        rows = kv_ref[slot]
        lane = lax.broadcasted_iota(jnp.int32, (128, 256), 1)
        key_rows = rows[:, :256]
        value_rows = jnp.concatenate([rows[:, 256:], rows[:, 128:256]], axis=1)
        keys = []
        values = []
        for h, run in enumerate((0, 1, 3)):
            key_ones = jnp.logical_and(lane >= 192 + 3 * h, lane < 195 + 3 * h)
            value_ones = jnp.logical_and(lane >= 128 + 3 * h, lane < 131 + 3 * h)
            keys.append(jnp.where(key_ones, 1.0, slot_only(key_rows, h)).astype(BF16))
            values.append(jnp.where(value_ones, 1.0, slot_only(value_rows, run)).astype(BF16))
        keys = jnp.concatenate(keys, axis=0)
        values = jnp.concatenate(values, axis=0)
        dk_ref[...] = jnp.zeros(dk_ref.shape, F32)
        dv_ref[...] = jnp.zeros(dv_ref.shape, F32)

        def step(chunk, masked):
            q_rows = chunk_rows(qg_ref, rank, chunk)
            do_rows = chunk_rows(dog_ref, rank, chunk)
            scores = lax.dot_general(keys, q_rows, NT, preferred_element_type=F32)
            if masked:
                scores = causal(scores, chunk * 512, block * 128, True)
            weights = jnp.exp(scores)
            grad_weights = lax.dot_general(values, do_rows, NT, preferred_element_type=F32)
            grad_scores = (weights * grad_weights).astype(BF16)
            dv_ref[...] += row_halves(
                jnp.dot(weights.astype(BF16), do_rows, preferred_element_type=F32)
            )
            dk_ref[...] += row_halves(jnp.dot(grad_scores, q_rows, preferred_element_type=F32))

        first = block // 4

        def full(chunk, inner):
            step(chunk, False)
            return inner

        step(first, True)
        lax.fori_loop(first + 1, 16, full, 0)
        half = lax.broadcasted_iota(jnp.int32, (128, 128), 1) < 64
        dkv_ref[slot, :, :128] = jnp.where(half, dk_ref[:128], dk_ref[128:256])
        dkv_ref[slot, :, 128:256] = jnp.where(half, dk_ref[256:], dv_ref[256:])
        dkv_ref[slot, :, 256:] = jnp.where(half, dv_ref[:128], dv_ref[128:256])
        return carry

    lax.fori_loop(0, 4, tile, 0)


def key_grad(pos, kv_own, q_all, do_all):
    return pl.pallas_call(
        key_grad_kernel,
        out_shape=jax.ShapeDtypeStruct((4, 128, 384), F32),
        in_specs=[pl.BlockSpec(memory_space=pltpu.SMEM)] + [vmem_spec()] * 3,
        out_specs=vmem_spec(),
        scratch_shapes=[pltpu.VMEM((384, 128), F32), pltpu.VMEM((384, 128), F32)],
        compiler_params=pltpu.CompilerParams(vmem_limit_bytes=VMEM_LIMIT),
        cost_estimate=pl.CostEstimate(
            flops=3 * 512 * 4096 * 1024, transcendentals=3 * 512 * 4096, bytes_accessed=10 * 2**20
        ),
        name="attention_key_grad",
    )(pos, kv_own, q_all, do_all)


def unpack_mlp_kernel(in_ref, out_w_ref, fc_w_ref):
    step = pl.program_id(0)

    @pl.when(step < 8)
    def _():
        for g in range(4):
            out_w_ref[g, 0] = in_ref[0, g, :48].astype(F32)

    @pl.when(step >= 8)
    def _():
        for g in range(4):
            rows = in_ref[0, g, :48].astype(F32)
            fc_w_ref[0, :, 384 * g : 384 * g + 384] = rows[:, :384]
            fc_w_ref[0, :, 1536 + 384 * g : 1920 + 384 * g] = rows[:, 384:]


def unpack_mlp(early):
    out_w, fc_w = pl.pallas_call(
        unpack_mlp_kernel,
        grid=(16,),
        out_shape=(
            jax.ShapeDtypeStruct((4, 8, 48, 768), F32),
            jax.ShapeDtypeStruct((8, 48, 3072), F32),
        ),
        in_specs=[pl.BlockSpec((1, 4, 64, 768), lambda s: (s, 0, 0, 0))],
        out_specs=(
            pl.BlockSpec((4, 1, 48, 768), lambda s: (0, jnp.minimum(s, 7), 0, 0)),
            pl.BlockSpec((1, 48, 3072), lambda s: (jnp.maximum(s - 8, 0), 0, 0)),
        ),
        name="unpack_mlp",
    )(early)
    return out_w.reshape(1536, 768), fc_w.reshape(384, 3072)


def unpack_qkv_kernel(in_ref, out_ref):
    rows = [in_ref[0, g, :24].astype(F32) for g in range(4)]
    out_ref[0, :, :768] = jnp.concatenate([r[:, :192] for r in rows], axis=1)
    out_ref[0, :, 768:1536] = jnp.concatenate([r[:, 256:448] for r in rows], axis=1)
    out_ref[0, :, 1536:] = jnp.concatenate(
        [part for r in rows for part in (r[:, 512:], r[:, 448:512])], axis=1
    )


def unpack_qkv(late):
    rows = late.shape[2]
    return pl.pallas_call(
        unpack_qkv_kernel,
        grid=(16,),
        out_shape=jax.ShapeDtypeStruct((16, 24, 2304), F32),
        in_specs=[pl.BlockSpec((1, 4, rows, 640), lambda s: (s, 0, 0, 0))],
        out_specs=pl.BlockSpec((1, 24, 2304), lambda s: (s, 0, 0)),
        name="unpack_qkv",
    )(late).reshape(384, 2304)


def swap(values, axis):
    return lax.ppermute(values, axis, [(0, 1), (1, 0)])


def to_rank(values, offset):
    return lax.ppermute(values, TP, [(a, a ^ offset) for a in range(4)])


def gather_ranks(values):
    return [values] + [to_rank(values, r) for r in (1, 2, 3)]


def sum_ranks(partial):
    total = partial[0]
    for r in (1, 2, 3):
        total = total + to_rank(partial[r], r)
    return total


def pick(values, index, axis=0):
    return lax.dynamic_index_in_dim(values, index, axis, keepdims=False)


def normalize(values):
    center = jnp.mean(values, axis=-1, keepdims=True)
    centered = values - center
    scale = lax.rsqrt(jnp.mean(centered * centered, axis=-1, keepdims=True) + EPS)
    return (centered * scale, scale)


def norm_back(grad, normed, scale, gain):
    grad_normed = grad * gain
    first = jnp.mean(grad_normed, axis=-1, keepdims=True)
    second = jnp.mean(grad_normed * normed, axis=-1, keepdims=True)
    return scale * (grad_normed - first - normed * second)


def dot(a, b):
    return jnp.dot(a, b, preferred_element_type=F32)


def dot_nt(a, b):
    return jnp.einsum("ab,cb->ac", a, b, preferred_element_type=F32)


def dot_tn(a, b):
    return jnp.einsum("ta,tb->ab", a, b, preferred_element_type=F32)


def both_shards(own, fs):
    peer = swap(own, "fsdp")
    first = jnp.where(fs == 0, own, peer)
    second = jnp.where(fs == 0, peer, own)
    return jnp.stack([first, second])


def both_shards_by_core(own, fs):
    core = lax.axis_index("core")
    half = own.shape[0] // 2
    part = swap(lax.dynamic_slice_in_dim(own, half * core, half, 0), "fsdp")
    other = swap(part, "core")
    peer = jnp.concatenate(
        [jnp.where(core == 0, part, other), jnp.where(core == 0, other, part)], axis=0
    )
    first = jnp.where(fs == 0, own, peer)
    second = jnp.where(fs == 0, peer, own)
    return jnp.stack([first, second])


def after(values, *earlier):
    return lax.optimization_barrier((values, *earlier))[0]


def reduce_pieces(blocks, shared, fs, by_permute):
    half = blocks.shape[1] // 2
    local = jnp.concatenate([blocks, shared], axis=1)
    rows, width = local.shape[1:]
    if by_permute:
        part = local.reshape(2, 2, 2, 2, rows, width)
        for axis, dim in (("core", 3), ("yl", 2), ("yh", 1), ("xl", 0)):
            bit = lax.axis_index(axis)
            part = pick(part, bit, dim) + swap(pick(part, 1 - bit, dim), axis)
    else:
        part = lax.psum_scatter(local, SEQ_AXES, scatter_dimension=0, tiled=False)
    part = part.reshape(rows, width)
    rest = part[2 * half :]
    own = lax.dynamic_slice_in_dim(part, fs * half, half, 0)
    other = lax.dynamic_slice_in_dim(part, (1 - fs) * half, half, 0)
    total = jnp.concatenate([own, rest], axis=0) + swap(
        jnp.concatenate([other, rest], axis=0), "fsdp"
    )
    total = total.astype(BF16)
    rank = lax.axis_index(TP)
    ranks = jnp.stack(gather_ranks(total))
    ranks = jnp.stack([pick(ranks, rank ^ k) for k in range(4)])
    if by_permute:
        out = ranks[None]
        for axis in ("xl", "yh", "yl", "core"):
            peer = swap(out, axis)
            bit = lax.axis_index(axis)
            pair = jnp.stack([jnp.where(bit == 0, out, peer), jnp.where(bit == 0, peer, out)])
            out = jnp.moveaxis(pair, 0, 1).reshape((-1,) + ranks.shape)
        return out
    return lax.all_gather(ranks, SEQ_AXES, axis=0, tiled=False)


def body(
    block_in,
    out_grad,
    ln1_gain,
    ln1_bias,
    w_qkv,
    q_bias,
    v_bias,
    w_proj,
    b_proj,
    ln2_gain,
    ln2_bias,
    w_fc,
    b_fc,
    w_out,
    b_out,
):
    rank = lax.axis_index(TP)
    seq = lax.axis_index(SEQ_AXES)
    fs = lax.axis_index("fsdp")
    pos = jnp.stack([seq, rank]).astype(jnp.int32)

    x_low = jnp.concatenate(gather_ranks(block_in[0]), axis=0)
    w_q = lax.dynamic_slice_in_dim(w_qkv, 192 * rank, 192, 1)
    w_k = lax.dynamic_slice_in_dim(w_qkv, 768 + 192 * rank, 192, 1)
    w_v = lax.dynamic_slice_in_dim(w_qkv, 1536 + 192 * rank, 192, 1)
    qkv_shard = jnp.concatenate(
        [w_q, jnp.zeros((384, 64), BF16), w_k, w_v[:, 128:], w_v[:, :128]], axis=1
    )
    w_cols = both_shards(qkv_shard, fs).reshape(768, 640)
    small = jnp.concatenate(
        [ln1_gain, ln1_bias, q_bias, v_bias, b_proj, ln2_gain, ln2_bias, b_out, b_fc]
    )
    small = both_shards(small.reshape(36, 128), fs).reshape(2, 4608).astype(F32)
    wide = small[:, :3072].reshape(2, 8, 384).transpose(1, 0, 2).reshape(8, 768)
    gain_one, shift_one, query_bias, value_bias, proj_bias, gain_two, shift_two, out_bias = wide
    fc_bias = lax.dynamic_slice_in_dim(small[:, 3072:], 384 * rank, 384, 1).reshape(768)
    q_own = lax.dynamic_slice_in_dim(query_bias, 192 * rank, 192, 0)
    v_own = lax.dynamic_slice_in_dim(value_bias, 192 * rank, 192, 0)
    qkv_bias = jnp.concatenate(
        [q_own, jnp.zeros((64 + 192,), F32), v_own[128:], v_own[:128]], axis=0
    )
    proj_rows = both_shards_by_core(w_proj, fs).reshape(4, 3, 64, 768)
    proj_rows = jnp.concatenate(
        [proj_rows[:, :2], jnp.zeros((4, 1, 64, 768), BF16), proj_rows[:, 2:]], axis=1
    ).reshape(4, 256, 768)
    proj_ranks = [pick(proj_rows, rank ^ r) for r in range(4)]
    fc_halves = w_fc.reshape(384, 2, 1536)
    fc_shard = lax.dynamic_slice_in_dim(fc_halves, 384 * rank, 384, 2).reshape(384, 768)
    fc_cols = both_shards_by_core(fc_shard, fs).reshape(768, 768)
    out_shard = lax.dynamic_slice_in_dim(w_out, 384 * rank, 384, 0)
    out_rows = both_shards_by_core(out_shard, fs).reshape(768, 768)

    x = x_low.astype(F32)
    x_normed, x_scale = normalize(x)
    normed_one = (x_normed * gain_one + shift_one).astype(BF16)
    projected = dot(normed_one, w_cols) + qkv_bias
    q_scaled = (projected[:, :256].astype(BF16) * 0.125).astype(BF16).reshape(4, 128, 256)
    kv_own = projected[:, 256:].astype(BF16).reshape(4, 128, 384)
    kv_all = lax.all_gather(kv_own, SEQ_AXES, axis=0, tiled=False)
    attn, q_aug, lse = forward_attention(pos, q_scaled, kv_all)
    q_all = lax.all_gather(q_aug, SEQ_AXES, axis=0, tiled=False)

    attn_ranks = gather_ranks(attn)
    residual = x + proj_bias
    attn_full = jnp.concatenate(
        [
            jnp.concatenate([attn_ranks[r][k ^ r] for k in range(4)], axis=0) for r in range(4)
        ],
        axis=1,
    )
    residual = residual + dot(attn_full, jnp.concatenate(proj_ranks, axis=0))

    r_normed, r_scale = normalize(residual)
    normed_two = (r_normed * gain_two + shift_two).astype(BF16)
    hidden = dot(normed_two, fc_cols) + fc_bias
    cot_low = jnp.concatenate(gather_ranks(out_grad[0]), axis=0)
    grad_act = dot_nt(cot_low, out_rows)
    inner = GELU_F * (hidden + GELU_C * hidden * hidden * hidden)
    tanh = jnp.tanh(inner)
    activated = (0.5 * hidden * (1.0 + tanh)).astype(BF16)
    slope = 0.5 * (1.0 + tanh) + 0.5 * hidden * (1.0 - tanh * tanh) * GELU_F * (
        1.0 + 3.0 * GELU_C * hidden * hidden
    )
    grad_hidden = grad_act * slope
    grad_hidden_low = grad_hidden.astype(BF16)
    grad_normed_two = sum_ranks(dot_nt(grad_hidden_low, fc_cols).reshape(4, 128, 768))

    cot_own = out_grad[0].astype(F32)
    grad_residual = (
        norm_back(grad_normed_two, r_normed[:128], r_scale[:128], gain_two) + cot_own
    )
    grad_residual_low = jnp.concatenate(gather_ranks(grad_residual.astype(BF16)), axis=0)
    do_aug, delta = grad_rows(grad_residual_low, proj_ranks[0], attn)
    do_all = lax.all_gather(after(do_aug, q_all), SEQ_AXES, axis=0, tiled=False)
    grad_q = query_grad(pos, q_aug, do_aug, lse, delta, kv_all)

    activated, normed_two, grad_hidden_low, attn_late, grad_q, do_all = lax.optimization_barrier(
        (activated, normed_two, grad_hidden_low, attn, grad_q, do_all)
    )
    output = (
        sum_ranks(dot(activated, out_rows).reshape(4, 128, 768)) + out_bias + residual[:128]
    ).astype(BF16)
    grad_out_w = dot_tn(activated, cot_low).reshape(2, 384, 768)
    grad_fc_w = dot_tn(normed_two, grad_hidden_low).reshape(2, 384, 768)
    grad_proj_w = dot_tn(attn_late.reshape(512, 256), grad_residual_low)
    grad_proj_w = jnp.concatenate([grad_proj_w[:128], grad_proj_w[192:]], axis=0)
    extra = jnp.stack(
        [
            jnp.sum(grad_normed_two * r_normed[:128], axis=0),
            jnp.sum(grad_normed_two, axis=0),
            jnp.sum(grad_residual, axis=0),
            jnp.sum(cot_own, axis=0),
            jnp.sum(grad_hidden, axis=0),
        ]
        + [jnp.zeros((768,), F32)] * 11
    )
    early = reduce_pieces(
        jnp.concatenate([grad_out_w, grad_fc_w], axis=1)
        .reshape(2, 16, 48, 768)
        .transpose(1, 0, 2, 3)
        .reshape(16, 96, 768),
        jnp.concatenate(
            [grad_proj_w.reshape(16, 12, 768), extra[:, None], jnp.zeros((16, 3, 768), F32)], axis=1
        ),
        fs,
        False,
    )

    grad_kv = key_grad(pos, kv_own, q_all, do_all)
    grad_cols = jnp.concatenate([grad_q, grad_kv], axis=2).reshape(512, 640)
    grad_cols_low = grad_cols.astype(BF16)
    grad_qkv_w = dot_tn(normed_one, grad_cols_low).reshape(2, 16, 24, 640)
    partial_one = dot_nt(grad_cols_low, w_cols)
    late_extra = jnp.concatenate(
        [
            jnp.sum(grad_cols, axis=0),
            jnp.sum(partial_one * x_normed, axis=0),
            jnp.sum(partial_one, axis=0),
            jnp.zeros((640 * 15 - 1536,), F32),
        ]
    ).reshape(16, 1, 640)
    late = reduce_pieces(
        grad_qkv_w.transpose(1, 0, 2, 3).reshape(16, 48, 640), late_extra, fs, True
    )
    grad_normed_one = sum_ranks(partial_one.reshape(4, 128, 768))
    input_grad = (
        norm_back(grad_normed_one, x_normed[:128], x_scale[:128], gain_one) + grad_residual
    )

    def own_half(values):
        return lax.dynamic_slice_in_dim(values, 384 * fs, 384, 0)

    g_w_out, g_w_fc = unpack_mlp(early)
    early = early[:, :, 48:61].astype(F32)
    g_w_proj = lax.dynamic_slice_in_dim(early[:, :, :12], 2 * fs, 2, 1)
    g_w_proj = g_w_proj.transpose(1, 0, 2, 3).reshape(384, 768)
    sums = jnp.sum(early[:4, :, 12], axis=1)
    g_b_fc = pick(early[4, :, 12].reshape(4, 2, 384), fs, 1).reshape(1536)
    g_w_qkv = unpack_qkv(late)
    late = late[:4, :, 24].astype(F32)
    bias_row = late[0]
    g_q_bias = own_half(bias_row[:, :192].reshape(768))
    g_v_bias = own_half(
        jnp.concatenate([bias_row[:, 512:], bias_row[:, 448:512]], axis=1).reshape(768)
    )
    ln_one = jnp.sum(late[1:4], axis=1).reshape(1920)
    return (
        output[None],
        input_grad[None],
        own_half(ln_one[:768]),
        own_half(ln_one[768:1536]),
        g_w_qkv,
        g_q_bias,
        g_v_bias,
        g_w_proj,
        own_half(sums[2]),
        own_half(sums[0]),
        own_half(sums[1]),
        g_w_fc,
        g_b_fc,
        g_w_out,
        own_half(sums[3]),
    )


def solution(mesh):
    split = Mesh(
        mesh.devices.reshape(2, 2, 2, 2, 2, 2, 2),
        ("zl", "xh", "xl", "yh", "yl", "core", "fsdp"),
    )
    tokens = P("fsdp", CTX, None)
    vector = P("fsdp")
    matrix = P("fsdp", None)
    in_specs = (
        tokens,
        tokens,
        vector,
        vector,
        matrix,
        vector,
        vector,
        matrix,
        vector,
        vector,
        vector,
        matrix,
        vector,
        matrix,
        vector,
    )
    out_specs = (
        tokens,
        tokens,
        vector,
        vector,
        matrix,
        vector,
        vector,
        matrix,
        vector,
        vector,
        vector,
        matrix,
        vector,
        matrix,
        vector,
    )
    return jax.shard_map(body, mesh=split, in_specs=in_specs, out_specs=out_specs, check_vma=False)
```

time: 1740 us -> 543 us (0.31)
  waiting for transfers between devices: 1060 us -> 242 us
  blocking collectives: 375 us -> 0 us
  local copies, waits for them, and re-layouts: 208 us -> 52.1 us
  Pallas kernels: 0 us -> 94.9 us
  starting transfers between devices: 0.66 us -> 74.1 us
  matrix products: 48 us -> 17.8 us
  other arithmetic: 11.4 us -> 36.3 us
    reduce_scatter x5 -> x1, waiting for transfers between devices: 686 us -> 65.3 us  [reduce_pieces(): part = lax.psum_scatter(local, SEQ_AXES, scatter_dimension=0, tiled=False)]
    psum x1 -> x0, blocking collectives: 324 us -> none  [body(): lax.psum((shards[0], shards[1], shards[2], shards[3], shards[4], shards[5...]
    all_gather x6 -> x4, waiting for transfers between devices: 369 us -> 45.5 us  [the longest x1 25.1 us: body(): do_all = lax.all_gather(after(do_aug, q_all), SEQ_AXES, axis=0, tiled=False)]
    ppermute x0 -> x45, waiting for transfers between devices: none -> 131 us  [the longest x27 72.6 us: to_rank(): return lax.ppermute(values, TP, [(a, a ^ offset) for a in range(4)])]
    dynamic_update_slice x32 -> x0, local copies, waits for them, and re-layouts: 98.1 us -> none  [body(): lax.scan(back_step, zero_query, (key_blocks, value_blocks, jnp.arange(spa...]
    pallas_call x0 -> x6, Pallas kernels: none -> 94.9 us  [the longest x1 29.7 us: key_grad(): pl.pallas_call(key_grad_kernel, out_shape=jax.ShapeDtypeStruct((4, 128, 3...]
    unnamed x138 -> x108, local copies, waits for them, and re-layouts: 89.3 us -> 12.2 us
    ppermute x0 -> x45, starting transfers between devices: none -> 73.5 us  [the longest x27 42.2 us: to_rank(): return lax.ppermute(values, TP, [(a, a ^ offset) for a in range(4)])]
  transfers between devices with their start and end apart: 11 -> 50, of which waited for: 11 -> 30; matrix products, arithmetic and copies ran while one was open for 4% -> 15% of each run, Pallas kernels for 0% -> 16%
where the time goes in v1:
time: 543 us; the launch traced here: 533 us
  waiting for transfers between devices  242 us (45%)
  Pallas kernels  94.9 us (17%)
  starting transfers between devices  74.1 us (14%)
  local copies, waits for them, and re-layouts  52.1 us (10%)
  other arithmetic  36.3 us (7%)
  matrix products  17.8 us (3%)
  between operations  15.4 us (3%)
    ppermute x27, waiting for transfers between devices, to_rank(): return lax.ppermute(values, TP, [(a, a ^ offset) for a in range(4)])  72.6 us
    reduce_scatter x1, waiting for transfers between devices, reduce_pieces(): part = lax.psum_scatter(local, SEQ_AXES, scatter_dimension=0, tiled=False)  65.3 us
    ppermute x18, waiting for transfers between devices, swap(): return lax.ppermute(values, axis, [(0, 1), (1, 0)])  58.4 us
    ppermute x27, starting transfers between devices, to_rank(): return lax.ppermute(values, TP, [(a, a ^ offset) for a in range(4)])  42.2 us
    ppermute x18, starting transfers between devices, swap(): return lax.ppermute(values, axis, [(0, 1), (1, 0)])  31.3 us
    pallas_call x1, Pallas kernels, key_grad(): pl.pallas_call(key_grad_kernel, out_shape=jax.ShapeDtypeStruct((4, 128, 3...  29.7 us
    all_gather x1, waiting for transfers between devices, body(): do_all = lax.all_gather(after(do_aug, q_all), SEQ_AXES, axis=0, tiled=False)  25.1 us
    all_gather x1, waiting for transfers between devices, body(): kv_all = lax.all_gather(kv_own, SEQ_AXES, axis=0, tiled=False)  20.5 us
  transfers between devices with their start and end apart: 50, of which 30 were waited for; matrix products, arithmetic and copies ran while one was open for 15% of the time, Pallas kernels for 16%

profile of v1, /device:TPU:1, one launch (start us, length us, event | category | flops | bytes accessed | tf_op | source)
XLA Modules:
  0.0 532.5 jit_solution(5531917955099533941)
XLA Ops:
  7.2 5.0 collective-permute-start.2
  20.2 3.3 collective-permute-start.3
  28.9 10.7 %collective-permute-done.4 = bf16[384,640]{1,0:T(8,128)(2,1)S(1)} collective-permute-done((bf16[384,640]{1,0:T(8,128)(2,1)S(1)}, bf16[384,640]{1,0:T(8,128)(2,1)S(1)}, u32[]{:S(2)}, u32[]{:S(2)}) %collective-permute-start.4) | collective-permute-done | bytes 491552 | tf_op jit(solution)/shard_map/ppermute | solution.py:365
  41.8 3.2 collective-permute-start.14
  46.8 5.6 %reshape.343 = bf16[384,2,1536]{2,1,0:T(2,128)(2,1)S(1)} reshape(bf16[384,3072]{1,0:T(8,128)(2,1)} %param.26) | data formatting | bytes 4718592 | tf_op jit(solution)/shard_map/reshape | solution.py:517
  53.0 2.8 collective-permute-start.10
  60.9 2.9 collective-permute-start.9
  65.5 20.5 %all-gather.8.cloned.1.call-done.kv_ref = bf16[16,4,128,384]{3,2,1,0:T(8,128)(2,1)} async-done(((bf16[1,4,128,384]{3,2,1,0:T(8,128)(2,1)}), bf16[16,4,128,384]{3,2,1,0:T(8,128)(2,1)}) %all-gather.8.cloned.1.call-update) | async-done | bytes 6291472 | tf_op jit(solution)/shard_map/all_gather | solution.py:529
  85.9 20.1 %attention_forward.1 = (bf16[4,128,256]{2,1,0:T(8,128)(2,1)}, bf16[4,128,256]{2,1,0:T(8,128)(2,1)}, f32[4,384,128]{2,1,0:T(8,128)}) custom-call(s32[2]{0:T(128)} %pad_add_fusion.pos_ref, bf16[4,128,256]{2,1,0:T(8,128)(2,1)} %bitcast.262, bf16[16,4,128,384]{3,2,1,0:T(8,128)(2,1)} %all-gather.8.cloned.1.call-done.kv_ref), custom_call_target="tpu_custom_call" | custom-call | flops 3221225472 | bytes 8388608 | tf_op jit(solution)/shard_map/attention_forward/pallas_call | solution.py:132
  106.2 2.8 collective-permute-start.12
  115.8 8.1 %collective-permute-done.7 = bf16[4,128,256]{2,1,0:T(8,128)(2,1)S(1)} collective-permute-done((bf16[4,128,256]{2,1,0:T(8,128)(2,1)S(1)}, bf16[4,128,256]{2,1,0:T(8,128)(2,1)S(1)}, u32[]{:S(2)}, u32[]{:S(2)}) %collective-permute-start.7) | collective-permute-done | bytes 262176 | tf_op jit(solution)/shard_map/ppermute | solution.py:369
  124.3 4.4 collective-permute-done.6
  128.7 9.1 %collective-permute-done.5 = bf16[4,128,256]{2,1,0:T(8,128)(2,1)S(1)} collective-permute-done((bf16[4,128,256]{2,1,0:T(8,128)(2,1)S(1)}, bf16[4,128,256]{2,1,0:T(8,128)(2,1)S(1)}, u32[]{:S(2)}, u32[]{:S(2)}) %collective-permute-start.5) | collective-permute-done | bytes 262176 | tf_op jit(solution)/shard_map/ppermute | solution.py:369
  142.0 2.6 fusion.89
  147.0 2.8 collective-permute-start.17
  149.8 11.6 %collective-permute-done.19 = f32[128,768]{1,0:T(8,128)S(1)} collective-permute-done((f32[128,768]{1,0:T(8,128)S(1)}, f32[128,768]{1,0:T(8,128)S(1)}, u32[]{:S(2)}, u32[]{:S(2)}) %collective-permute-start.19) | collective-permute-done | bytes 393248 | tf_op jit(solution)/shard_map/ppermute | solution.py:369
  162.8 7.5 %collective-permute-done.17 = f32[128,768]{1,0:T(8,128)S(1)} collective-permute-done((f32[128,768]{1,0:T(8,128)S(1)}, f32[128,768]{1,0:T(8,128)S(1)}, u32[]{:S(2)}, u32[]{:S(2)}) %collective-permute-start.17) | collective-permute-done | bytes 393248 | tf_op jit(solution)/shard_map/ppermute | solution.py:369
  173.3 2.7 collective-permute-start.20
  176.0 3.1 collective-permute-done.22
  182.8 2.9 attention_grad_rows.1
  187.0 20.1 %attention_query_grad.1 = f32[4,128,256]{2,1,0:T(8,128)} custom-call(s32[2]{0:T(128)} %pad_add_fusion.pos_ref, bf16[4,128,256]{2,1,0:T(8,128)(2,1)} %get-tuple-element.30.q_ref, bf16[4,128,256]{2,1,0:T(8,128)(2,1)} %get-tuple-element.34.do_ref, f32[4,384,128]{2,1,0:T(8,128)} %get-tuple-element.32.lse_ref, f32[4,384,128]{2,1,0:T(8,128)} %get-tuple-element.33.delta_ref, ...), custom_call_target="tpu_custom_call" | custom-call | flops 4831838208 | bytes 8388608 | tf_op jit(solution)/shard_map/attention_query_grad/pallas_call | solution.py:226
  207.1 25.1 %all-gather.12.cloned.1.call-done = bf16[64,128,256]{2,1,0:T(8,128)(2,1)} async-done(((bf16[4,128,256]{2,1,0:T(8,128)(2,1)}), bf16[64,128,256]{2,1,0:T(8,128)(2,1)}) %all-gather.12.cloned.1.call-update) | async-done | bytes 4194320 | tf_op jit(solution)/shard_map/all_gather | solution.py:564
  240.7 3.1 maximum_maximum_fusion
  243.8 65.3 %reduce-scatter.2.cloned.1.call-done = f32[1,112,768]{2,1,0:T(8,128)} async-done(((f32[16,112,768]{2,1,0:T(8,128)}), f32[1,112,768]{2,1,0:T(8,128)}) %reduce-scatter.2.cloned.1.call-update) | async-done | bytes 344080 | tf_op jit(solution)/shard_map/reduce_scatter | solution.py:447
  311.0 2.9 collective-permute-start.41
  313.8 3.2 collective-permute-done.41
  317.1 3.6 collective-permute-start.44
  326.8 29.7 %attention_key_grad.1 = f32[4,128,384]{2,1,0:T(8,128)} custom-call(s32[2]{0:T(128)} %pad_add_fusion.pos_ref, bf16[4,128,384]{2,1,0:T(8,128)(2,1)} %bitcast.255, bf16[16,4,128,256]{3,2,1,0:T(8,128)(2,1)} %bitcast.279, bf16[16,4,128,256]{3,2,1,0:T(8,128)(2,1)} %bitcast.280), custom_call_target="tpu_custom_call" | custom-call | flops 6442450944 | bytes 10485760 | tf_op jit(solution)/shard_map/attention_key_grad/pallas_call | solution.py:295
  359.9 2.5 multiply_reduce_fusion
  362.4 2.3 copy.72
  370.9 8.5 %collective-permute-start.29 = (f32[2,2,2,49,640]{4,2,3,1,0:T(2,128)}, f32[2,2,2,49,640]{4,2,3,1,0:T(2,128)}, u32[]{:S(2)}, u32[]{:S(2)}) collective-permute-start(f32[2,2,2,49,640]{4,2,3,1,0:T(2,128)} %bitcast.213), channel_id=1, source_target_pairs={{0,2},{2,0},{1,3},{3,1},{4,6},{6,4},{5,7},{7,5},{8,10},{10,8},{9,1... | collective-permute-start | bytes 3010568 | tf_op jit(solution)/shard_map/ppermute | solution.py:365
  379.4 2.6 collective-permute-done.29
  386.9 13.0 %collective-permute-done.30 = f32[2,2,49,640]{3,1,2,0:T(2,128)} collective-permute-done((f32[2,2,49,640]{3,1,2,0:T(2,128)}, f32[2,2,49,640]{3,1,2,0:T(2,128)}, u32[]{:S(2)}, u32[]{:S(2)}) %collective-permute-start.30) | collective-permute-done | bytes 501792 | tf_op jit(solution)/shard_map/ppermute | solution.py:365
  403.3 8.2 %collective-permute-done.31 = f32[2,49,640]{2,0,1:T(2,128)} collective-permute-done((f32[2,49,640]{2,0,1:T(2,128)}, f32[2,49,640]{2,0,1:T(2,128)}, u32[]{:S(2)}, u32[]{:S(2)}) %collective-permute-start.31) | collective-permute-done | bytes 250912 | tf_op jit(solution)/shard_map/ppermute | solution.py:365
  414.3 4.3 collective-permute-done.32
  419.6 3.8 collective-permute-start.33
  426.5 3.0 collective-permute-start.34
  432.4 4.9 collective-permute-done.37
  438.8 2.3 fusion.97
  441.0 4.8 collective-permute-done.38
  447.2 2.7 collective-permute-start.25
  452.8 3.3 collective-permute-done.39
  456.0 3.3 collective-permute-start.26
  461.1 2.5 collective-permute-start.23
  463.6 18.7 %collective-permute-done.27 = f32[128,768]{1,0:T(8,128)S(1)} collective-permute-done((f32[128,768]{1,0:T(8,128)S(1)}, f32[128,768]{1,0:T(8,128)S(1)}, u32[]{:S(2)}, u32[]{:S(2)}) %collective-permute-start.27) | collective-permute-done | bytes 393248 | tf_op jit(solution)/shard_map/ppermute | solution.py:369
  482.2 4.4 collective-permute-start.40
  493.4 10.2 %unpack_qkv.1 = f32[16,24,2304]{2,1,0:T(8,128)} custom-call(bf16[16,4,25,640]{3,2,1,0:T(8,128)(2,1)} %bitcast.224), custom_call_target="tpu_custom_call" | custom-call | tf_op jit(solution)/shard_map/unpack_qkv/pallas_call | solution.py:354
  509.3 11.8 %unpack_mlp.1 = (f32[4,8,48,768]{3,2,1,0:T(8,128)}, f32[8,48,3072]{2,1,0:T(8,128)}) custom-call(bf16[16,4,64,768]{3,2,1,0:T(8,128)(2,1)} %bitcast.227), custom_call_target="tpu_custom_call" | custom-call | tf_op jit(solution)/shard_map/unpack_mlp/pallas_call | solution.py:326
  (358 shorter events, 115.5 us)
Async XLA Ops:
  7.2 78.8 %all-gather.8.cloned.1.call-start = ((), (), s32[]{:S(2)}) async-start(), calls=%async_computation.1 | async-start | bytes 6684672 | tf_op jit(solution)/shard_map/all_gather | solution.py:529
  7.2 21.1 %collective-permute-start.2 = (bf16[128,768]{1,0:T(8,128)(2,1)}, bf16[128,768]{1,0:T(8,128)(2,1)S(1)}, u32[]{:S(2)}, u32[]{:S(2)}) collective-permute-start(bf16[128,768]{1,0:T(8,128)(2,1)} %bitcast.246), channel_id=1, source_target_pairs={{0,96},{32,64},{64,32},{96,0},{1,97},{33,65},{65,33},{97,1},{2,98}... | collective-permute-start | bytes 589832 | tf_op jit(solution)/shard_map/ppermute | solution.py:369
  12.2 16.1 %collective-permute-start.1 = (bf16[128,768]{1,0:T(8,128)(2,1)}, bf16[128,768]{1,0:T(8,128)(2,1)S(1)}, u32[]{:S(2)}, u32[]{:S(2)}) collective-permute-start(bf16[128,768]{1,0:T(8,128)(2,1)} %bitcast.247), channel_id=1, source_target_pairs={{0,64},{32,96},{64,0},{96,32},{1,65},{33,97},{65,1},{97,33},{2,66}... | collective-permute-start | bytes 589832 | tf_op jit(solution)/shard_map/ppermute | solution.py:369
  12.2 16.1 %collective-permute-start = (bf16[128,768]{1,0:T(8,128)(2,1)}, bf16[128,768]{1,0:T(8,128)(2,1)S(1)}, u32[]{:S(2)}, u32[]{:S(2)}) collective-permute-start(bf16[128,768]{1,0:T(8,128)(2,1)} %bitcast.248), channel_id=1, source_target_pairs={{0,32},{32,0},{64,96},{96,64},{1,33},{33,1},{65,97},{97,65},{2,34}... | collective-permute-start | bytes 589832 | tf_op jit(solution)/shard_map/ppermute | solution.py:369
  20.2 7.1 %collective-permute-start.3 = (bf16[36,128]{1,0:T(8,128)(2,1)S(1)}, bf16[36,128]{1,0:T(8,128)(2,1)S(1)}, u32[]{:S(2)}, u32[]{:S(2)}) collective-permute-start(bf16[36,128]{1,0:T(8,128)(2,1)S(1)} %bitcast.276), channel_id=1, source_target_pairs={{0,1},{1,0},{2,3},{3,2},{4,5},{5,4},{6,7},{7,6},{8,9},{9,8},{10,11... | collective-permute-start | bytes 27656 | tf_op jit(solution)/shard_map/ppermute | solution.py:365
  27.1 12.5 %collective-permute-start.4 = (bf16[384,640]{1,0:T(8,128)(2,1)S(1)}, bf16[384,640]{1,0:T(8,128)(2,1)S(1)}, u32[]{:S(2)}, u32[]{:S(2)}) collective-permute-start(bf16[384,640]{1,0:T(8,128)(2,1)S(1)} %concatenate.115), channel_id=1, source_target_pairs={{0,1},{1,0},{2,3},{3,2},{4,5},{5,4},{6,7},{7,6},{8,9},{9,8},{10,11... | collective-permute-start | bytes 1474568 | tf_op jit(solution)/shard_map/ppermute | solution.py:365
  41.8 143.9 %all-gather.10.cloned.1.call-start = ((), (), s32[]{:S(2)}) async-start(), calls=%async_computation.3 | async-start | bytes 4456448 | tf_op jit(solution)/shard_map/all_gather | solution.py:531
  41.8 100.1 %collective-permute-start.14 = (bf16[128,768]{1,0:T(8,128)(2,1)}, bf16[128,768]{1,0:T(8,128)(2,1)}, u32[]{:S(2)}, u32[]{:S(2)}) collective-permute-start(bf16[128,768]{1,0:T(8,128)(2,1)} %bitcast.37), channel_id=1, source_target_pairs={{0,96},{32,64},{64,32},{96,0},{1,97},{33,65},{65,33},{97,1},{2,98}... | collective-permute-start | bytes 589832 | tf_op jit(solution)/shard_map/ppermute | solution.py:369
  45.0 96.9 %collective-permute-start.13 = (bf16[128,768]{1,0:T(8,128)(2,1)}, bf16[128,768]{1,0:T(8,128)(2,1)}, u32[]{:S(2)}, u32[]{:S(2)}) collective-permute-start(bf16[128,768]{1,0:T(8,128)(2,1)} %bitcast.37), channel_id=1, source_target_pairs={{0,64},{32,96},{64,0},{96,32},{1,65},{33,97},{65,1},{97,33},{2,66}... | collective-permute-start | bytes 589832 | tf_op jit(solution)/shard_map/ppermute | solution.py:369
  46.5 14.4 %collective-permute-start.8 = (bf16[192,768]{1,0:T(8,128)(2,1)}, bf16[192,768]{1,0:T(8,128)(2,1)}, u32[]{:S(2)}, u32[]{:S(2)}) collective-permute-start(bf16[192,768]{1,0:T(8,128)(2,1)} %constant_dynamic-slice_fusion.27), channel_id=1, source_target_pairs={{0,1},{1,0},{2,3},{3,2},{4,5},{5,4},{6,7},{7,6},{8,9},{9,8},{10,11... | collective-permute-start | bytes 884744 | tf_op jit(solution)/shard_map/ppermute | solution.py:365
  53.0 53.2 %collective-permute-start.10 = (bf16[192,768]{1,0:T(8,128)(2,1)S(1)}, bf16[192,768]{1,0:T(8,128)(2,1)S(1)}, u32[]{:S(2)}, u32[]{:S(2)}) collective-permute-start(bf16[192,768]{1,0:T(8,128)(2,1)S(1)} %constant_dynamic-slice_fusion.25), channel_id=1, source_target_pairs={{0,1},{1,0},{2,3},{3,2},{4,5},{5,4},{6,7},{7,6},{8,9},{9,8},{10,11... | collective-permute-start | bytes 884744 | tf_op jit(solution)/shard_map/ppermute | solution.py:365
  56.8 52.2 %collective-permute-start.15 = (bf16[192,768]{1,0:T(8,128)(2,1)S(1)}, bf16[192,768]{1,0:T(8,128)(2,1)S(1)}, u32[]{:S(2)}, u32[]{:S(2)}) collective-permute-start(bf16[192,768]{1,0:T(8,128)(2,1)S(1)} %constant_dynamic-slice_fusion.23), channel_id=1, source_target_pairs={{0,1},{1,0},{2,3},{3,2},{4,5},{5,4},{6,7},{7,6},{8,9},{9,8},{10,11... | collective-permute-start | bytes 884744 | tf_op jit(solution)/shard_map/ppermute | solution.py:365
  60.9 48.5 %collective-permute-start.9 = (bf16[192,768]{1,0:T(8,128)(2,1)}, bf16[192,768]{1,0:T(8,128)(2,1)S(1)}, u32[]{:S(2)}, u32[]{:S(2)}) collective-permute-start(bf16[192,768]{1,0:T(8,128)(2,1)} %collective-permute-done.8), channel_id=1, source_target_pairs={{0,2},{2,0},{1,3},{3,1},{4,6},{6,4},{5,7},{7,5},{8,10},{10,8},{9,1... | collective-permute-start | bytes 884744 | tf_op jit(solution)/shard_map/ppermute | solution.py:365
  106.1 126.1 %all-gather.12.cloned.1.call-start = ((), (), s32[]{:S(2)}) async-start(), calls=%async_computation.4 | async-start | bytes 4456448 | tf_op jit(solution)/shard_map/all_gather | solution.py:564
  106.2 35.8 %collective-permute-start.12 = (bf16[128,768]{1,0:T(8,128)(2,1)}, bf16[128,768]{1,0:T(8,128)(2,1)S(1)}, u32[]{:S(2)}, u32[]{:S(2)}) collective-permute-start(bf16[128,768]{1,0:T(8,128)(2,1)} %bitcast.37), channel_id=1, source_target_pairs={{0,32},{32,0},{64,96},{96,64},{1,33},{33,1},{65,97},{97,65},{2,34}... | collective-permute-start | bytes 589832 | tf_op jit(solution)/shard_map/ppermute | solution.py:369
  114.1 9.9 %collective-permute-start.7 = (bf16[4,128,256]{2,1,0:T(8,128)(2,1)S(1)}, bf16[4,128,256]{2,1,0:T(8,128)(2,1)S(1)}, u32[]{:S(2)}, u32[]{:S(2)}) collective-permute-start(bf16[4,128,256]{2,1,0:T(8,128)(2,1)S(1)} %copy-done.6), channel_id=1, source_target_pairs={{0,96},{32,64},{64,32},{96,0},{1,97},{33,65},{65,33},{97,1},{2,98}... | collective-permute-start | bytes 786440 | tf_op jit(solution)/shard_map/ppermute | solution.py:369
  115.6 13.1 %collective-permute-start.6 = (bf16[4,128,256]{2,1,0:T(8,128)(2,1)S(1)}, bf16[4,128,256]{2,1,0:T(8,128)(2,1)S(1)}, u32[]{:S(2)}, u32[]{:S(2)}) collective-permute-start(bf16[4,128,256]{2,1,0:T(8,128)(2,1)S(1)} %copy-done.6), channel_id=1, source_target_pairs={{0,64},{32,96},{64,0},{96,32},{1,65},{33,97},{65,1},{97,33},{2,66}... | collective-permute-start | bytes 786440 | tf_op jit(solution)/shard_map/ppermute | solution.py:369
  124.0 13.9 %collective-permute-start.5 = (bf16[4,128,256]{2,1,0:T(8,128)(2,1)S(1)}, bf16[4,128,256]{2,1,0:T(8,128)(2,1)S(1)}, u32[]{:S(2)}, u32[]{:S(2)}) collective-permute-start(bf16[4,128,256]{2,1,0:T(8,128)(2,1)S(1)} %copy-done.6), channel_id=1, source_target_pairs={{0,32},{32,0},{64,96},{96,64},{1,33},{33,1},{65,97},{97,65},{2,34}... | collective-permute-start | bytes 786440 | tf_op jit(solution)/shard_map/ppermute | solution.py:369
  145.6 15.9 %collective-permute-start.19 = (f32[128,768]{1,0:T(8,128)S(1)}, f32[128,768]{1,0:T(8,128)S(1)}, u32[]{:S(2)}, u32[]{:S(2)}) collective-permute-start(f32[128,768]{1,0:T(8,128)S(1)} %get-tuple-element.82), channel_id=1, source_target_pairs={{0,96},{32,64},{64,32},{96,0},{1,97},{33,65},{65,33},{97,1},{2,98}... | collective-permute-start | bytes 1179656 | tf_op jit(solution)/shard_map/ppermute | solution.py:369
  146.7 16.1 %collective-permute-start.18 = (f32[128,768]{1,0:T(8,128)S(1)}, f32[128,768]{1,0:T(8,128)S(1)}, u32[]{:S(2)}, u32[]{:S(2)}) collective-permute-start(f32[128,768]{1,0:T(8,128)S(1)} %get-tuple-element.83), channel_id=1, source_target_pairs={{0,64},{32,96},{64,0},{96,32},{1,65},{33,97},{65,1},{97,33},{2,66}... | collective-permute-start | bytes 1179656 | tf_op jit(solution)/shard_map/ppermute | solution.py:369
  147.0 23.3 %collective-permute-start.17 = (f32[128,768]{1,0:T(8,128)S(1)}, f32[128,768]{1,0:T(8,128)S(1)}, u32[]{:S(2)}, u32[]{:S(2)}) collective-permute-start(f32[128,768]{1,0:T(8,128)S(1)} %get-tuple-element.81), channel_id=1, source_target_pairs={{0,32},{32,0},{64,96},{96,64},{1,33},{33,1},{65,97},{97,65},{2,34}... | collective-permute-start | bytes 1179656 | tf_op jit(solution)/shard_map/ppermute | solution.py:369
  171.7 7.3 %collective-permute-start.22 = (bf16[128,768]{1,0:T(8,128)(2,1)S(1)}, bf16[128,768]{1,0:T(8,128)(2,1)S(1)}, u32[]{:S(2)}, u32[]{:S(2)}) collective-permute-start(bf16[128,768]{1,0:T(8,128)(2,1)S(1)} %convert_element_type.53), channel_id=1, source_target_pairs={{0,96},{32,64},{64,32},{96,0},{1,97},{33,65},{65,33},{97,1},{2,98}... | collective-permute-start | bytes 589832 | tf_op jit(solution)/shard_map/ppermute | solution.py:369
  171.8 9.3 %collective-permute-start.21 = (bf16[128,768]{1,0:T(8,128)(2,1)S(1)}, bf16[128,768]{1,0:T(8,128)(2,1)S(1)}, u32[]{:S(2)}, u32[]{:S(2)}) collective-permute-start(bf16[128,768]{1,0:T(8,128)(2,1)S(1)} %convert_element_type.53), channel_id=1, source_target_pairs={{0,64},{32,96},{64,0},{96,32},{1,65},{33,97},{65,1},{97,33},{2,66}... | collective-permute-start | bytes 589832 | tf_op jit(solution)/shard_map/ppermute | solution.py:369
  173.3 8.5 %collective-permute-start.20 = (bf16[128,768]{1,0:T(8,128)(2,1)S(1)}, bf16[128,768]{1,0:T(8,128)(2,1)S(1)}, u32[]{:S(2)}, u32[]{:S(2)}) collective-permute-start(bf16[128,768]{1,0:T(8,128)(2,1)S(1)} %convert_element_type.53), channel_id=1, source_target_pairs={{0,32},{32,0},{64,96},{96,64},{1,33},{33,1},{65,97},{97,65},{2,34}... | collective-permute-start | bytes 589832 | tf_op jit(solution)/shard_map/ppermute | solution.py:369
  185.7 123.5 %reduce-scatter.2.cloned.1.call-start = ((), (), s32[]{:S(2)}) async-start(), calls=%async_computation.2 | async-start | bytes 5849088 | tf_op jit(solution)/shard_map/reduce_scatter | solution.py:447
  243.8 263.7 %all-gather.14.cloned.1.call-start = ((), (), s32[]{:S(2)}) async-start(), calls=%async_computation.5 | async-start | bytes 6684672 | tf_op jit(solution)/shard_map/all_gather | solution.py:467
  311.0 6.1 %collective-permute-start.41 = (f32[64,768]{1,0:T(8,128)S(1)}, f32[64,768]{1,0:T(8,128)S(1)}, u32[]{:S(2)}, u32[]{:S(2)}) collective-permute-start(f32[64,768]{1,0:T(8,128)S(1)} %pad_maximum_fusion.18), channel_id=1, source_target_pairs={{0,1},{1,0},{2,3},{3,2},{4,5},{5,4},{6,7},{7,6},{8,9},{9,8},{10,11... | collective-permute-start | bytes 589832 | tf_op jit(solution)/shard_map/ppermute | solution.py:365
  317.1 6.1 %collective-permute-start.44 = (bf16[64,768]{1,0:T(8,128)(2,1)S(1)}, bf16[64,768]{1,0:T(8,128)(2,1)S(1)}, u32[]{:S(2)}, u32[]{:S(2)}) collective-permute-start(bf16[64,768]{1,0:T(8,128)(2,1)S(1)} %fusion.67), channel_id=1, source_target_pairs={{0,96},{32,64},{64,32},{96,0},{1,97},{33,65},{65,33},{97,1},{2,98}... | collective-permute-start | bytes 294920 | tf_op jit(solution)/shard_map/ppermute | solution.py:369
  320.7 3.6 collective-permute-start.43
  320.9 5.0 collective-permute-start.42
  370.9 11.1 %collective-permute-start.29 = (f32[2,2,2,49,640]{4,2,3,1,0:T(2,128)}, f32[2,2,2,49,640]{4,2,3,1,0:T(2,128)}, u32[]{:S(2)}, u32[]{:S(2)}) collective-permute-start(f32[2,2,2,49,640]{4,2,3,1,0:T(2,128)} %bitcast.213), channel_id=1, source_target_pairs={{0,2},{2,0},{1,3},{3,1},{4,6},{6,4},{5,7},{7,5},{8,10},{10,8},{9,1... | collective-permute-start | bytes 3010568 | tf_op jit(solution)/shard_map/ppermute | solution.py:365
  386.9 13.0 %collective-permute-start.30 = (f32[2,2,49,640]{3,1,2,0:T(2,128)}, f32[2,2,49,640]{3,1,2,0:T(2,128)}, u32[]{:S(2)}, u32[]{:S(2)}) collective-permute-start(f32[2,2,49,640]{3,1,2,0:T(2,128)} %bitcast.214), channel_id=1, source_target_pairs={{0,4},{4,0},{1,5},{5,1},{2,6},{6,2},{3,7},{7,3},{8,12},{12,8},{9,1... | collective-permute-start | bytes 1505288 | tf_op jit(solution)/shard_map/ppermute | solution.py:365
  403.3 8.2 %collective-permute-start.31 = (f32[2,49,640]{2,0,1:T(2,128)}, f32[2,49,640]{2,0,1:T(2,128)}, u32[]{:S(2)}, u32[]{:S(2)}) collective-permute-start(f32[2,49,640]{2,0,1:T(2,128)} %bitcast.215), channel_id=1, source_target_pairs={{0,8},{8,0},{1,9},{9,1},{2,10},{10,2},{3,11},{11,3},{4,12},{12,4},... | collective-permute-start | bytes 752648 | tf_op jit(solution)/shard_map/ppermute | solution.py:365
  414.3 4.3 collective-permute-start.32
  419.6 5.6 %collective-permute-start.33 = (f32[25,640]{1,0:T(8,128)S(1)}, f32[25,640]{1,0:T(8,128)S(1)}, u32[]{:S(2)}, u32[]{:S(2)}) collective-permute-start(f32[25,640]{1,0:T(8,128)S(1)} %pad_maximum_fusion.23), channel_id=1, source_target_pairs={{0,1},{1,0},{2,3},{3,2},{4,5},{5,4},{6,7},{7,6},{8,9},{9,8},{10,11... | collective-permute-start | bytes 192008 | tf_op jit(solution)/shard_map/ppermute | solution.py:365
  425.3 5.3 %collective-permute-start.36 = (bf16[25,640]{1,0:T(8,128)(2,1)S(1)}, bf16[25,640]{1,0:T(8,128)(2,1)S(1)}, u32[]{:S(2)}, u32[]{:S(2)}) collective-permute-start(bf16[25,640]{1,0:T(8,128)(2,1)S(1)} %fusion.71), channel_id=1, source_target_pairs={{0,96},{32,64},{64,32},{96,0},{1,97},{33,65},{65,33},{97,1},{2,98}... | collective-permute-start | bytes 96008 | tf_op jit(solution)/shard_map/ppermute | solution.py:369
  425.4 5.2 collective-permute-start.35
  426.5 4.4 collective-permute-start.34
  432.3 5.0 collective-permute-start.37
  438.4 7.5 %collective-permute-start.38 = (bf16[2,4,25,640]{3,2,1,0:T(8,128)(2,1)S(1)}, bf16[2,4,25,640]{3,2,1,0:T(8,128)(2,1)S(1)}, u32[]{:S(2)}, u32[]{:S(2)}) collective-permute-start(bf16[2,4,25,640]{3,2,1,0:T(8,128)(2,1)S(1)} %maximum_bitcast_fusion.3), channel_id=1, source_target_pairs={{0,8},{8,0},{1,9},{9,1},{2,10},{10,2},{3,11},{11,3},{4,12},{12,4},... | collective-permute-start | bytes 768008 | tf_op jit(solution)/shard_map/ppermute | solution.py:365
  446.4 9.7 %collective-permute-start.39 = (bf16[4,4,25,640]{3,1,2,0:T(4,128)(2,1)S(1)}, bf16[4,4,25,640]{3,1,2,0:T(4,128)(2,1)S(1)}, u32[]{:S(2)}, u32[]{:S(2)}) collective-permute-start(bf16[4,4,25,640]{3,1,2,0:T(4,128)(2,1)S(1)} %bitcast.245), channel_id=1, source_target_pairs={{0,4},{4,0},{1,5},{5,1},{2,6},{6,2},{3,7},{7,3},{8,12},{12,8},{9,1... | collective-permute-start | bytes 1536008 | tf_op jit(solution)/shard_map/ppermute | solution.py:365
  447.2 40.7 %collective-permute-start.25 = (f32[128,768]{1,0:T(8,128)S(1)}, f32[128,768]{1,0:T(8,128)S(1)}, u32[]{:S(2)}, u32[]{:S(2)}) collective-permute-start(f32[128,768]{1,0:T(8,128)S(1)} %get-tuple-element.79), channel_id=1, source_target_pairs={{0,96},{32,64},{64,32},{96,0},{1,97},{33,65},{65,33},{97,1},{2,98}... | collective-permute-start | bytes 1179656 | tf_op jit(solution)/shard_map/ppermute | solution.py:369
  449.9 37.9 %collective-permute-start.24 = (f32[128,768]{1,0:T(8,128)S(1)}, f32[128,768]{1,0:T(8,128)S(1)}, u32[]{:S(2)}, u32[]{:S(2)}) collective-permute-start(f32[128,768]{1,0:T(8,128)S(1)} %get-tuple-element.80), channel_id=1, source_target_pairs={{0,64},{32,96},{64,0},{96,32},{1,65},{33,97},{65,1},{97,33},{2,66}... | collective-permute-start | bytes 1179656 | tf_op jit(solution)/shard_map/ppermute | solution.py:369
  451.5 9.6 %collective-permute-start.28 = (f32[128,768]{1,0:T(8,128)S(1)}, f32[128,768]{1,0:T(8,128)S(1)}, u32[]{:S(2)}, u32[]{:S(2)}) collective-permute-start(f32[128,768]{1,0:T(8,128)S(1)} %get-tuple-element.76), channel_id=1, source_target_pairs={{0,96},{32,64},{64,32},{96,0},{1,97},{33,65},{65,33},{97,1},{2,98}... | collective-permute-start | bytes 1179656 | tf_op jit(solution)/shard_map/ppermute | solution.py:369
  451.7 30.5 %collective-permute-start.27 = (f32[128,768]{1,0:T(8,128)S(1)}, f32[128,768]{1,0:T(8,128)S(1)}, u32[]{:S(2)}, u32[]{:S(2)}) collective-permute-start(f32[128,768]{1,0:T(8,128)S(1)} %get-tuple-element.77), channel_id=1, source_target_pairs={{0,64},{32,96},{64,0},{96,32},{1,65},{33,97},{65,1},{97,33},{2,66}... | collective-permute-start | bytes 1179656 | tf_op jit(solution)/shard_map/ppermute | solution.py:369
  456.0 30.6 %collective-permute-start.26 = (f32[128,768]{1,0:T(8,128)S(1)}, f32[128,768]{1,0:T(8,128)S(1)}, u32[]{:S(2)}, u32[]{:S(2)}) collective-permute-start(f32[128,768]{1,0:T(8,128)S(1)} %get-tuple-element.75), channel_id=1, source_target_pairs={{0,32},{32,0},{64,96},{96,64},{1,33},{33,1},{65,97},{97,65},{2,34}... | collective-permute-start | bytes 1179656 | tf_op jit(solution)/shard_map/ppermute | solution.py:369
  461.1 26.8 %collective-permute-start.23 = (f32[128,768]{1,0:T(8,128)S(1)}, f32[128,768]{1,0:T(8,128)S(1)}, u32[]{:S(2)}, u32[]{:S(2)}) collective-permute-start(f32[128,768]{1,0:T(8,128)S(1)} %get-tuple-element.78), channel_id=1, source_target_pairs={{0,32},{32,0},{64,96},{96,64},{1,33},{33,1},{65,97},{97,65},{2,34}... | collective-permute-start | bytes 1179656 | tf_op jit(solution)/shard_map/ppermute | solution.py:369
  482.2 6.7 %collective-permute-start.40 = (bf16[8,4,25,640]{3,0,2,1:T(8,128)(2,1)S(1)}, bf16[8,4,25,640]{3,0,2,1:T(8,128)(2,1)S(1)}, u32[]{:S(2)}, u32[]{:S(2)}) collective-permute-start(bf16[8,4,25,640]{3,0,2,1:T(8,128)(2,1)S(1)} %copy.83), channel_id=1, source_target_pairs={{0,2},{2,0},{1,3},{3,1},{4,6},{6,4},{5,7},{7,5},{8,10},{10,8},{9,1... | collective-permute-start | bytes 3072008 | tf_op jit(solution)/shard_map/ppermute | solution.py:365
  (52 other events, 650.3 us)
Sparse Core Ops, SparseCore 0:
  41.9 43.9 all-gather.7
  106.2 51.0 all-gather.9
  185.8 46.3 all-gather.11
  243.9 65.1 reduce-scatter.1
  327.0 47.5 all-gather.13

commit v2 on v1

--- a/solution.py
+++ b/solution.py
@@ -7,6 +7,7 @@
 
 TP = ("zl", "xh")
 SEQ_AXES = ("xl", "yh", "yl", "core")
+BLOCKS = ("xl", "yh", "yl")
 CTX = TP + SEQ_AXES
 EPS = 1e-05
 GELU_F = 0.7978845608028654
@@ -178,7 +179,9 @@
     )(dr_low, w_rows, attn)
 
 
-def query_grad_kernel(pos_ref, q_ref, do_ref, lse_ref, delta_ref, kv_ref, dq_ref, acc_ref):
+def query_grad_kernel(
+    pos_ref, q_ref, do_ref, lse_ref, delta_ref, kv_ref, dq_ref, sum_ref, acc_ref
+):
     seq = pos_ref[0]
     rank = pos_ref[1]
 
@@ -215,19 +218,28 @@
         step(last, True)
         lane = lax.broadcasted_iota(jnp.int32, (128, 128), 1)
         acc = acc_ref[...] * 0.125
-        dq_ref[slot, :, :128] = jnp.where(lane < 64, acc[:128], acc[128:256])
-        dq_ref[slot, :, 128:] = jnp.where(lane < 64, acc[256:], 0.0)
-        return carry
-
-    lax.fori_loop(0, 4, tile, 0)
+        rows = jnp.concatenate(
+            [
+                jnp.where(lane < 64, acc[:128], acc[128:256]),
+                jnp.where(lane < 64, acc[256:], 0.0),
+            ],
+            axis=1,
+        )
+        dq_ref[slot] = rows.astype(BF16)
+        return carry + jnp.sum(rows, axis=0, keepdims=True)
+
+    sum_ref[...] = lax.fori_loop(0, 4, tile, jnp.zeros((1, 256), F32))
 
 
 def query_grad(pos, q, do, lse, delta, kv):
     return pl.pallas_call(
         query_grad_kernel,
-        out_shape=jax.ShapeDtypeStruct((4, 128, 256), F32),
+        out_shape=(
+            jax.ShapeDtypeStruct((4, 128, 256), BF16),
+            jax.ShapeDtypeStruct((1, 256), F32),
+        ),
         in_specs=[pl.BlockSpec(memory_space=pltpu.SMEM)] + [vmem_spec()] * 5,
-        out_specs=vmem_spec(),
+        out_specs=(vmem_spec(), vmem_spec()),
         scratch_shapes=[pltpu.VMEM((384, 128), F32)],
         compiler_params=pltpu.CompilerParams(vmem_limit_bytes=VMEM_LIMIT),
         cost_estimate=pl.CostEstimate(
@@ -237,7 +249,7 @@
     )(pos, q, do, lse, delta, kv)
 
 
-def key_grad_kernel(pos_ref, kv_ref, qg_ref, dog_ref, dkv_ref, dk_ref, dv_ref):
+def key_grad_kernel(pos_ref, kv_ref, qg_ref, dog_ref, dkv_ref, sum_ref, dk_ref, dv_ref):
     seq = pos_ref[0]
     rank = pos_ref[1]
 
@@ -283,20 +295,29 @@
         step(first, True)
         lax.fori_loop(first + 1, 16, full, 0)
         half = lax.broadcasted_iota(jnp.int32, (128, 128), 1) < 64
-        dkv_ref[slot, :, :128] = jnp.where(half, dk_ref[:128], dk_ref[128:256])
-        dkv_ref[slot, :, 128:256] = jnp.where(half, dk_ref[256:], dv_ref[256:])
-        dkv_ref[slot, :, 256:] = jnp.where(half, dv_ref[:128], dv_ref[128:256])
-        return carry
-
-    lax.fori_loop(0, 4, tile, 0)
+        grads = jnp.concatenate(
+            [
+                jnp.where(half, dk_ref[:128], dk_ref[128:256]),
+                jnp.where(half, dk_ref[256:], dv_ref[256:]),
+                jnp.where(half, dv_ref[:128], dv_ref[128:256]),
+            ],
+            axis=1,
+        )
+        dkv_ref[slot] = grads.astype(BF16)
+        return carry + jnp.sum(grads, axis=0, keepdims=True)
+
+    sum_ref[...] = lax.fori_loop(0, 4, tile, jnp.zeros((1, 384), F32))
 
 
 def key_grad(pos, kv_own, q_all, do_all):
     return pl.pallas_call(
         key_grad_kernel,
-        out_shape=jax.ShapeDtypeStruct((4, 128, 384), F32),
+        out_shape=(
+            jax.ShapeDtypeStruct((4, 128, 384), BF16),
+            jax.ShapeDtypeStruct((1, 384), F32),
+        ),
         in_specs=[pl.BlockSpec(memory_space=pltpu.SMEM)] + [vmem_spec()] * 3,
-        out_specs=vmem_spec(),
+        out_specs=(vmem_spec(), vmem_spec()),
         scratch_shapes=[pltpu.VMEM((384, 128), F32), pltpu.VMEM((384, 128), F32)],
         compiler_params=pltpu.CompilerParams(vmem_limit_bytes=VMEM_LIMIT),
         cost_estimate=pl.CostEstimate(
@@ -306,59 +327,80 @@
     )(pos, kv_own, q_all, do_all)
 
 
-def unpack_mlp_kernel(in_ref, out_w_ref, fc_w_ref):
+def unpack_mlp_kernel(pos_ref, in_ref, out_w_ref, fc_w_ref):
     step = pl.program_id(0)
+    rank = pos_ref[0]
 
     @pl.when(step < 8)
     def _():
         for g in range(4):
-            out_w_ref[g, 0] = in_ref[0, g, :48].astype(F32)
+            out_w_ref[g, 0] = in_ref[0, rank ^ g, :48].astype(F32)
 
     @pl.when(step >= 8)
     def _():
         for g in range(4):
-            rows = in_ref[0, g, :48].astype(F32)
+            rows = in_ref[0, rank ^ g, :48].astype(F32)
             fc_w_ref[0, :, 384 * g : 384 * g + 384] = rows[:, :384]
             fc_w_ref[0, :, 1536 + 384 * g : 1920 + 384 * g] = rows[:, 384:]
 
 
-def unpack_mlp(early):
+def unpack_mlp(pos, early):
     out_w, fc_w = pl.pallas_call(
         unpack_mlp_kernel,
-        grid=(16,),
+        grid_spec=pltpu.PrefetchScalarGridSpec(
+            num_scalar_prefetch=1,
+            grid=(16,),
+            in_specs=[pl.BlockSpec((1, 4, 64, 768), lambda s, pos: (s, 0, 0, 0))],
+            out_specs=(
+                pl.BlockSpec((4, 1, 48, 768), lambda s, pos: (0, jnp.minimum(s, 7), 0, 0)),
+                pl.BlockSpec((1, 48, 3072), lambda s, pos: (jnp.maximum(s - 8, 0), 0, 0)),
+            ),
+        ),
         out_shape=(
             jax.ShapeDtypeStruct((4, 8, 48, 768), F32),
             jax.ShapeDtypeStruct((8, 48, 3072), F32),
         ),
-        in_specs=[pl.BlockSpec((1, 4, 64, 768), lambda s: (s, 0, 0, 0))],
-        out_specs=(
-            pl.BlockSpec((4, 1, 48, 768), lambda s: (0, jnp.minimum(s, 7), 0, 0)),
-            pl.BlockSpec((1, 48, 3072), lambda s: (jnp.maximum(s - 8, 0), 0, 0)),
-        ),
         name="unpack_mlp",
-    )(early)
+    )(pos, early)
     return out_w.reshape(1536, 768), fc_w.reshape(384, 3072)
 
 
-def unpack_qkv_kernel(in_ref, out_ref):
-    rows = [in_ref[0, g, :24].astype(F32) for g in range(4)]
-    out_ref[0, :, :768] = jnp.concatenate([r[:, :192] for r in rows], axis=1)
-    out_ref[0, :, 768:1536] = jnp.concatenate([r[:, 256:448] for r in rows], axis=1)
+def unpack_qkv_kernel(pos_ref, in_ref, out_ref, extra_ref):
+    rank = pos_ref[0]
+    rows = [in_ref[0, 0, rank ^ g].astype(F32) for g in range(4)]
+    out_ref[0, :, :768] = jnp.concatenate([r[:24, :192] for r in rows], axis=1)
+    out_ref[0, :, 768:1536] = jnp.concatenate([r[:24, 256:448] for r in rows], axis=1)
     out_ref[0, :, 1536:] = jnp.concatenate(
-        [part for r in rows for part in (r[:, 512:], r[:, 448:512])], axis=1
-    )
-
-
-def unpack_qkv(late):
-    rows = late.shape[2]
-    return pl.pallas_call(
+        [part for r in rows for part in (r[:24, 512:], r[:24, 448:512])], axis=1
+    )
+    for g in range(4):
+        extra_ref[0, g] = rows[g][24:]
+
+
+def unpack_qkv(pos, late):
+    grads, extra = pl.pallas_call(
         unpack_qkv_kernel,
-        grid=(16,),
-        out_shape=jax.ShapeDtypeStruct((16, 24, 2304), F32),
-        in_specs=[pl.BlockSpec((1, 4, rows, 640), lambda s: (s, 0, 0, 0))],
-        out_specs=pl.BlockSpec((1, 24, 2304), lambda s: (s, 0, 0)),
+        grid_spec=pltpu.PrefetchScalarGridSpec(
+            num_scalar_prefetch=1,
+            grid=(16,),
+            in_specs=[
+                pl.BlockSpec(
+                    (1, 1, 4, 32, 640),
+                    lambda s, pos: (lax.rem(s, 2) ^ pos[2], (s // 2) ^ pos[1], 0, 0, 0),
+                )
+            ],
+            out_specs=(
+                pl.BlockSpec((1, 24, 2304), lambda s, pos: (s, 0, 0)),
+                pl.BlockSpec((1, 4, 8, 640), lambda s, pos: (s, 0, 0, 0)),
+            ),
+        ),
+        out_shape=(
+            jax.ShapeDtypeStruct((16, 24, 2304), F32),
+            jax.ShapeDtypeStruct((16, 4, 8, 640), F32),
+        ),
         name="unpack_qkv",
-    )(late).reshape(384, 2304)
+    )(pos, late)
+    return grads.reshape(384, 2304), extra
 
 
 def swap(values, axis):
@@ -434,37 +476,30 @@
     return lax.optimization_barrier((values, *earlier))[0]
 
 
-def reduce_pieces(blocks, shared, fs, by_permute):
-    half = blocks.shape[1] // 2
-    local = jnp.concatenate([blocks, shared], axis=1)
-    rows, width = local.shape[1:]
-    if by_permute:
-        part = local.reshape(2, 2, 2, 2, rows, width)
-        for axis, dim in (("core", 3), ("yl", 2), ("yh", 1), ("xl", 0)):
-            bit = lax.axis_index(axis)
-            part = pick(part, bit, dim) + swap(pick(part, 1 - bit, dim), axis)
-    else:
-        part = lax.psum_scatter(local, SEQ_AXES, scatter_dimension=0, tiled=False)
-    part = part.reshape(rows, width)
+def to_block(values, offset):
+    return lax.ppermute(values, BLOCKS, [(a, a ^ offset) for a in range(8)])
+
+
+def add_sequences(part, half, fs):
     rest = part[2 * half :]
     own = lax.dynamic_slice_in_dim(part, fs * half, half, 0)
     other = lax.dynamic_slice_in_dim(part, (1 - fs) * half, half, 0)
     total = jnp.concatenate([own, rest], axis=0) + swap(
         jnp.concatenate([other, rest], axis=0), "fsdp"
     )
-    total = total.astype(BF16)
-    rank = lax.axis_index(TP)
-    ranks = jnp.stack(gather_ranks(total))
-    ranks = jnp.stack([pick(ranks, rank ^ k) for k in range(4)])
-    if by_permute:
-        out = ranks[None]
-        for axis in ("xl", "yh", "yl", "core"):
-            peer = swap(out, axis)
-            bit = lax.axis_index(axis)
-            pair = jnp.stack([jnp.where(bit == 0, out, peer), jnp.where(bit == 0, peer, out)])
-            out = jnp.moveaxis(pair, 0, 1).reshape((-1,) + ranks.shape)
-        return out
-    return lax.all_gather(ranks, SEQ_AXES, axis=0, tiled=False)
+    return total.astype(BF16)
+
+
+def reduce_by_permute(local):
+    core = lax.axis_index("core")
+    block = lax.axis_index(BLOCKS)
+    pair = local.reshape((8, 2) + local.shape[1:])
+    pair = pick(pair, core, 1) + swap(pick(pair, 1 - core, 1), "core")
+    moved = [to_block(pick(pair, block ^ r), r) for r in range(1, 8)]
+    total = pick(pair, block)
+    for values in moved:
+        total = total + values
+    return total
 
 
 def body(
@@ -497,13 +532,15 @@
         [w_q, jnp.zeros((384, 64), BF16), w_k, w_v[:, 128:], w_v[:, :128]], axis=1
     )
     w_cols = both_shards(qkv_shard, fs).reshape(768, 640)
-    small = jnp.concatenate(
-        [ln1_gain, ln1_bias, q_bias, v_bias, b_proj, ln2_gain, ln2_bias, b_out, b_fc]
-    )
-    small = both_shards(small.reshape(36, 128), fs).reshape(2, 4608).astype(F32)
-    wide = small[:, :3072].reshape(2, 8, 384).transpose(1, 0, 2).reshape(8, 768)
-    gain_one, shift_one, query_bias, value_bias, proj_bias, gain_two, shift_two, out_bias = wide
-    fc_bias = lax.dynamic_slice_in_dim(small[:, 3072:], 384 * rank, 384, 1).reshape(768)
+    vectors = (ln1_gain, ln1_bias, q_bias, v_bias, b_proj, ln2_gain, ln2_bias, b_out, b_fc)
+    vectors = lax.optimization_barrier((qkv_shard,) + vectors)[1:]
+    small = jnp.stack([v.astype(F32) for v in vectors[:8]])
+    small = jnp.concatenate([small, vectors[8].astype(F32).reshape(4, 384)], axis=0)
+    small = both_shards(small, fs)
+    wide_vectors = small[:, :8].transpose(1, 0, 2).reshape(8, 768)
+    gain_one, shift_one, query_bias, value_bias = wide_vectors[:4]
+    proj_bias, gain_two, shift_two, out_bias = wide_vectors[4:]
+    fc_bias = pick(small[:, 8:], rank, 1).reshape(768)
     q_own = lax.dynamic_slice_in_dim(query_bias, 192 * rank, 192, 0)
     v_own = lax.dynamic_slice_in_dim(value_bias, 192 * rank, 192, 0)
     qkv_bias = jnp.concatenate(
@@ -513,9 +550,14 @@
     proj_rows = jnp.concatenate(
         [proj_rows[:, :2], jnp.zeros((4, 1, 64, 768), BF16), proj_rows[:, 2:]], axis=1
     ).reshape(4, 256, 768)
-    proj_ranks = [pick(proj_rows, rank ^ r) for r in range(4)]
-    fc_halves = w_fc.reshape(384, 2, 1536)
-    fc_shard = lax.dynamic_slice_in_dim(fc_halves, 384 * rank, 384, 2).reshape(384, 768)
+    proj_ranks = jnp.stack([pick(proj_rows, rank ^ r) for r in range(4)])
+    fc_shard = jnp.concatenate(
+        [
+            lax.dynamic_slice_in_dim(w_fc, 384 * rank, 384, 1),
+            lax.dynamic_slice_in_dim(w_fc, 1536 + 384 * rank, 384, 1),
+        ],
+        axis=1,
+    )
     fc_cols = both_shards_by_core(fc_shard, fs).reshape(768, 768)
     out_shard = lax.dynamic_slice_in_dim(w_out, 384 * rank, 384, 0)
     out_rows = both_shards_by_core(out_shard, fs).reshape(768, 768)
@@ -527,10 +569,13 @@
     q_scaled = (projected[:, :256].astype(BF16) * 0.125).astype(BF16).reshape(4, 128, 256)
     kv_own = projected[:, 256:].astype(BF16).reshape(4, 128, 384)
     kv_all = lax.all_gather(kv_own, SEQ_AXES, axis=0, tiled=False)
+    kv_all, proj_ranks, fc_cols, out_rows, cot_low = lax.optimization_barrier(
+        (kv_all, proj_ranks, fc_cols, out_rows, jnp.concatenate(gather_ranks(out_grad[0]), axis=0))
+    )
     attn, q_aug, lse = forward_attention(pos, q_scaled, kv_all)
-    q_all = lax.all_gather(q_aug, SEQ_AXES, axis=0, tiled=False)
 
     attn_ranks = gather_ranks(attn)
+    q_all = lax.all_gather(after(q_aug, *attn_ranks[1:]), SEQ_AXES, axis=0, tiled=False)
     residual = x + proj_bias
     attn_full = jnp.concatenate(
         [
@@ -538,12 +583,11 @@
         ],
         axis=1,
     )
-    residual = residual + dot(attn_full, jnp.concatenate(proj_ranks, axis=0))
+    residual = residual + dot(attn_full, proj_ranks.reshape(1024, 768))
 
     r_normed, r_scale = normalize(residual)
     normed_two = (r_normed * gain_two + shift_two).astype(BF16)
     hidden = dot(normed_two, fc_cols) + fc_bias
-    cot_low = jnp.concatenate(gather_ranks(out_grad[0]), axis=0)
     grad_act = dot_nt(cot_low, out_rows)
     inner = GELU_F * (hidden + GELU_C * hidden * hidden * hidden)
     tanh = jnp.tanh(inner)
@@ -562,14 +606,12 @@
     grad_residual_low = jnp.concatenate(gather_ranks(grad_residual.astype(BF16)), axis=0)
     do_aug, delta = grad_rows(grad_residual_low, proj_ranks[0], attn)
     do_all = lax.all_gather(after(do_aug, q_all), SEQ_AXES, axis=0, tiled=False)
-    grad_q = query_grad(pos, q_aug, do_aug, lse, delta, kv_all)
-
-    activated, normed_two, grad_hidden_low, attn_late, grad_q, do_all = lax.optimization_barrier(
-        (activated, normed_two, grad_hidden_low, attn, grad_q, do_all)
-    )
-    output = (
-        sum_ranks(dot(activated, out_rows).reshape(4, 128, 768)) + out_bias + residual[:128]
-    ).astype(BF16)
+    grad_q, grad_q_sum = query_grad(pos, q_aug, do_aug, lse, delta, kv_all)
+
+    activated, normed_two, grad_hidden_low, attn_late, grad_q = lax.optimization_barrier(
+        (activated, normed_two, grad_hidden_low, attn, grad_q)
+    )
+    out_partial = dot(activated, out_rows).reshape(4, 128, 768)
     grad_out_w = dot_tn(activated, cot_low).reshape(2, 384, 768)
     grad_fc_w = dot_tn(normed_two, grad_hidden_low).reshape(2, 384, 768)
     grad_proj_w = dot_tn(attn_late.reshape(512, 256), grad_residual_low)
@@ -584,56 +626,84 @@
         ]
         + [jnp.zeros((768,), F32)] * 11
     )
-    early = reduce_pieces(
-        jnp.concatenate([grad_out_w, grad_fc_w], axis=1)
-        .reshape(2, 16, 48, 768)
-        .transpose(1, 0, 2, 3)
-        .reshape(16, 96, 768),
-        jnp.concatenate(
-            [grad_proj_w.reshape(16, 12, 768), extra[:, None], jnp.zeros((16, 3, 768), F32)], axis=1
-        ),
-        fs,
-        False,
-    )
-
-    grad_kv = key_grad(pos, kv_own, q_all, do_all)
+    local = jnp.concatenate(
+        [
+            jnp.concatenate([grad_out_w, grad_fc_w], axis=1)
+            .reshape(2, 16, 48, 768)
+            .transpose(1, 0, 2, 3)
+            .reshape(16, 96, 768),
+            grad_proj_w.reshape(16, 12, 768),
+            extra[:, None],
+            jnp.zeros((16, 3, 768), F32),
+        ],
+        axis=1,
+    )
+    local, do_all, out_partial = lax.optimization_barrier((local, do_all, out_partial))
+    early = lax.psum_scatter(local, SEQ_AXES, scatter_dimension=0, tiled=False)
+    out_moved = [to_rank(out_partial[r], r) for r in (1, 2, 3)]
+
+    grad_kv, grad_kv_sum = key_grad(pos, kv_own, q_all, do_all)
+    out_moved = after(tuple(out_moved), grad_kv)
+    output = (
+        out_partial[0] + out_moved[0] + out_moved[1] + out_moved[2] + out_bias + residual[:128]
+    ).astype(BF16)
+
     grad_cols = jnp.concatenate([grad_q, grad_kv], axis=2).reshape(512, 640)
-    grad_cols_low = grad_cols.astype(BF16)
-    grad_qkv_w = dot_tn(normed_one, grad_cols_low).reshape(2, 16, 24, 640)
-    partial_one = dot_nt(grad_cols_low, w_cols)
+    grad_qkv_w = dot_tn(normed_one, grad_cols).reshape(2, 16, 24, 640)
+    partial_one = dot_nt(grad_cols, w_cols)
     late_extra = jnp.concatenate(
         [
-            jnp.sum(grad_cols, axis=0),
+            grad_q_sum[0],
+            grad_kv_sum[0],
             jnp.sum(partial_one * x_normed, axis=0),
             jnp.sum(partial_one, axis=0),
             jnp.zeros((640 * 15 - 1536,), F32),
         ]
     ).reshape(16, 1, 640)
-    late = reduce_pieces(
-        grad_qkv_w.transpose(1, 0, 2, 3).reshape(16, 48, 640), late_extra, fs, True
+    late_local = jnp.concatenate(
+        [
+            grad_qkv_w.transpose(1, 0, 2, 3).reshape(16, 48, 640),
+            late_extra,
+            jnp.zeros((16, 7, 640), F32),
+        ],
+        axis=1,
+    )
+    late = add_sequences(reduce_by_permute(late_local), 24, fs)
+
+    early, late, partial_one = lax.optimization_barrier((early, late, partial_one))
+    early = add_sequences(early, 48, fs)
+    early_ranks = gather_ranks(early)
+    late_ranks = gather_ranks(late)
+    early = lax.all_gather(jnp.stack(early_ranks), SEQ_AXES, axis=0, tiled=False)
+    late = jnp.stack(late_ranks)
+    late = jnp.stack([late] + [to_block(late, r) for r in range(1, 8)])
+    late = jnp.stack([late, swap(late, "core")])
+    g_w_qkv, late_extra = unpack_qkv(
+        jnp.stack([rank, lax.axis_index(BLOCKS), lax.axis_index("core")]).astype(jnp.int32), late
     )
     grad_normed_one = sum_ranks(partial_one.reshape(4, 128, 768))
     input_grad = (
         norm_back(grad_normed_one, x_normed[:128], x_scale[:128], gain_one) + grad_residual
     )
+    early, g_w_qkv, input_grad = lax.optimization_barrier((early, g_w_qkv, input_grad))
 
     def own_half(values):
         return lax.dynamic_slice_in_dim(values, 384 * fs, 384, 0)
 
-    g_w_out, g_w_fc = unpack_mlp(early)
+    g_w_out, g_w_fc = unpack_mlp(jnp.stack([rank]).astype(jnp.int32), early)
     early = early[:, :, 48:61].astype(F32)
+    early = jnp.stack([pick(early, rank ^ g, 1) for g in range(4)], axis=1)
     g_w_proj = lax.dynamic_slice_in_dim(early[:, :, :12], 2 * fs, 2, 1)
     g_w_proj = g_w_proj.transpose(1, 0, 2, 3).reshape(384, 768)
     sums = jnp.sum(early[:4, :, 12], axis=1)
     g_b_fc = pick(early[4, :, 12].reshape(4, 2, 384), fs, 1).reshape(1536)
-    g_w_qkv = unpack_qkv(late)
-    late = late[:4, :, 24].astype(F32)
-    bias_row = late[0]
+    late_rows = late_extra[:4, :, 0]
+    bias_row = late_rows[0]
     g_q_bias = own_half(bias_row[:, :192].reshape(768))
     g_v_bias = own_half(
         jnp.concatenate([bias_row[:, 512:], bias_row[:, 448:512]], axis=1).reshape(768)
     )
-    ln_one = jnp.sum(late[1:4], axis=1).reshape(1920)
+    ln_one = jnp.sum(late_rows[1:], axis=1).reshape(1920)
     return (
         output[None],
         input_grad[None],

time: 543 us -> 511 us (0.941)
  the two profiles are of different devices: /device:TPU:1 before, /device:TPU:0 now
where the time goes in v2:
time: 511 us; the launch traced here: 502 us
  waiting for transfers between devices  184 us (36%)
  Pallas kernels  95.5 us (19%)
  starting transfers between devices  81.8 us (16%)
  local copies, waits for them, and re-layouts  65.1 us (13%)
  other arithmetic  43.8 us (9%)
  matrix products  16.2 us (3%)
  between operations  15.3 us (3%)
    ppermute x14, waiting for transfers between devices, to_block(): return lax.ppermute(values, BLOCKS, [(a, a ^ offset) for a in range(8)])  81.2 us
    ppermute x27, waiting for transfers between devices, to_rank(): return lax.ppermute(values, TP, [(a, a ^ offset) for a in range(4)])  72.3 us
    ppermute x27, starting transfers between devices, to_rank(): return lax.ppermute(values, TP, [(a, a ^ offset) for a in range(4)])  44.3 us
    pallas_call x1, Pallas kernels, key_grad(): pl.pallas_call(key_grad_kernel, out_shape=(jax.ShapeDtypeStruct((4, 128,...  29.6 us
    ppermute x12, waiting for transfers between devices, swap(): return lax.ppermute(values, axis, [(0, 1), (1, 0)])  25.8 us
    pallas_call x1, Pallas kernels, forward_attention(): pl.pallas_call(forward_kernel, out_shape=(jax.ShapeDtypeStruct((4, 128, 2...  20.2 us
    pallas_call x1, Pallas kernels, query_grad(): pl.pallas_call(query_grad_kernel, out_shape=(jax.ShapeDtypeStruct((4, 128...  20.1 us
    ppermute x14, starting transfers between devices, to_block(): return lax.ppermute(values, BLOCKS, [(a, a ^ offset) for a in range(8)])  19.3 us
  transfers between devices with their start and end apart: 58, of which 33 were waited for; matrix products, arithmetic and copies ran while one was open for 20% of the time, Pallas kernels for 13%

profile of v2, /device:TPU:0, one launch (start us, length us, event | category | flops | bytes accessed | tf_op | source)
XLA Modules:
  0.0 501.7 jit_solution(10192372700799924219)
XLA Ops:
  11.3 4.0 collective-permute-start.3
  15.5 3.9 collective-permute-start.2
  21.4 3.4 collective-permute-done.2
  24.8 11.5 %collective-permute-done.1 = bf16[128,768]{1,0:T(8,128)(2,1)S(1)} collective-permute-done((bf16[128,768]{1,0:T(8,128)(2,1)S(1)}, bf16[128,768]{1,0:T(8,128)(2,1)S(1)}, u32[]{:S(2)}, u32[]{:S(2)}) %collective-permute-start.1) | collective-permute-done | bytes 196640 | tf_op jit(solution)/shard_map/ppermute | solution.py:411
  39.3 3.5 collective-permute-start.13
  45.1 3.3 collective-permute-start.5
  51.6 3.3 collective-permute-start.9
  55.6 4.2 collective-permute-done.5
  61.0 5.1 %collective-permute-done.7 = bf16[192,768]{1,0:T(8,128)(2,1)} collective-permute-done((bf16[192,768]{1,0:T(8,128)(2,1)S(1)}, bf16[192,768]{1,0:T(8,128)(2,1)}, u32[]{:S(2)}, u32[]{:S(2)}) %collective-permute-start.7) | collective-permute-done | bytes 294944 | tf_op jit(solution)/shard_map/ppermute | solution.py:407
  66.1 6.1 %collective-permute-done.9 = bf16[192,768]{1,0:T(8,128)(2,1)} collective-permute-done((bf16[192,768]{1,0:T(8,128)(2,1)}, bf16[192,768]{1,0:T(8,128)(2,1)}, u32[]{:S(2)}, u32[]{:S(2)}) %collective-permute-start.9) | collective-permute-done | bytes 294944 | tf_op jit(solution)/shard_map/ppermute | solution.py:407
  83.3 20.2 %attention_forward.1 = (bf16[4,128,256]{2,1,0:T(8,128)(2,1)}, bf16[4,128,256]{2,1,0:T(8,128)(2,1)}, f32[4,384,128]{2,1,0:T(8,128)}) custom-call(s32[2]{0:T(128)} %pad_add_fusion.pos_ref, bf16[4,128,256]{2,1,0:T(8,128)(2,1)} %bitcast.256, bf16[16,4,128,384]{3,2,1,0:T(8,128)(2,1)} %all-gather.8.cloned.1.call-done.kv_ref), custom_call_target="tpu_custom_call" | custom-call | flops 3221225472 | bytes 8388608 | tf_op jit(solution)/shard_map/attention_forward/pallas_call | solution.py:133
  103.5 3.9 collective-permute-start.16
  108.5 6.8 %collective-permute-done.16 = bf16[4,128,256]{2,1,0:T(8,128)(2,1)S(1)} collective-permute-done((bf16[4,128,256]{2,1,0:T(8,128)(2,1)}, bf16[4,128,256]{2,1,0:T(8,128)(2,1)S(1)}, u32[]{:S(2)}, u32[]{:S(2)}) %collective-permute-start.16) | collective-permute-done | bytes 262176 | tf_op jit(solution)/shard_map/ppermute | solution.py:411
  115.3 4.9 collective-permute-done.15
  131.3 3.0 collective-permute-start.19
  136.4 14.9 %collective-permute-done.19 = f32[128,768]{1,0:T(8,128)S(1)} collective-permute-done((f32[128,768]{1,0:T(8,128)S(1)}, f32[128,768]{1,0:T(8,128)S(1)}, u32[]{:S(2)}, u32[]{:S(2)}) %collective-permute-start.19) | collective-permute-done | bytes 393248 | tf_op jit(solution)/shard_map/ppermute | solution.py:411
  152.9 14.4 %collective-permute-done.17 = f32[128,768]{1,0:T(8,128)S(1)} collective-permute-done((f32[128,768]{1,0:T(8,128)S(1)}, f32[128,768]{1,0:T(8,128)S(1)}, u32[]{:S(2)}, u32[]{:S(2)}) %collective-permute-start.17) | collective-permute-done | bytes 393248 | tf_op jit(solution)/shard_map/ppermute | solution.py:411
  168.3 3.9 collective-permute-start.22
  175.1 4.5 collective-permute-done.22
  182.3 2.9 attention_grad_rows.1
  190.3 2.7 stack.229
  194.5 20.1 %attention_query_grad.1 = (bf16[4,128,256]{2,1,0:T(8,128)(2,1)}, f32[1,256]{1,0:T(1,128)}) custom-call(s32[2]{0:T(128)} %pad_add_fusion.pos_ref, bf16[4,128,256]{2,1,0:T(8,128)(2,1)} %get-tuple-element.85.q_ref, bf16[4,128,256]{2,1,0:T(8,128)(2,1)} %get-tuple-element.86.do_ref, f32[4,384,128]{2,1,0:T(8,128)} %get-tuple-element.78.lse_ref, ...), custom_call_target="tpu_custom_call" | custom-call | flops 4831838208 | bytes 8388608 | tf_op jit(solution)/shard_map/attention_query_grad/pallas_call | solution.py:235
  224.5 3.1 maximum_maximum_fusion
  227.6 3.1 all-gather.12.cloned.1.call-done
  232.7 29.6 %attention_key_grad.1 = (bf16[4,128,384]{2,1,0:T(8,128)(2,1)}, f32[1,384]{1,0:T(1,128)}) custom-call(s32[2]{0:T(128)} %pad_add_fusion.pos_ref, bf16[4,128,384]{2,1,0:T(8,128)(2,1)} %bitcast.239, bf16[16,4,128,256]{3,2,1,0:T(8,128)(2,1)} %bitcast.273, bf16[16,4,128,256]{3,2,1,0:T(8,128)(2,1)} %bitcast.274), custom_call_target="tpu_custom_call" | custom-call | flops 6442450944 | bytes 10485760 | tf_op jit(solution)/shard_map/attention_key_grad/pallas_call | solution.py:313
  283.0 2.9 collective-permute-done.26
  289.5 8.1 %collective-permute-start.33 = (f32[56,640]{1,0:T(8,128)S(1)}, f32[56,640]{1,0:T(8,128)}, u32[]{:S(2)}, u32[]{:S(2)}) collective-permute-start(f32[56,640]{1,0:T(8,128)S(1)} %get-tuple-element.159), channel_id=1, source_target_pairs={{0,28},{4,24},{8,20},{12,16},{16,12},{20,8},{24,4},{28,0},{1,29},{... | collective-permute-start | bytes 430088 | tf_op jit(solution)/shard_map/ppermute | solution.py:480
  302.6 3.7 collective-permute-done.33
  306.3 4.6 collective-permute-done.32
  310.9 4.7 collective-permute-done.31
  315.6 3.0 collective-permute-done.30
  321.3 3.0 collective-permute-start.34
  324.3 3.3 collective-permute-done.34
  331.0 3.3 collective-permute-start.35
  334.3 4.2 collective-permute-done.35
  338.5 3.3 collective-permute-start.38
  365.3 5.3 %collective-permute-done.42 = bf16[4,32,640]{2,1,0:T(8,128)(2,1)S(1)} collective-permute-done((bf16[4,32,640]{2,1,0:T(8,128)(2,1)S(1)}, bf16[4,32,640]{2,1,0:T(8,128)(2,1)S(1)}, u32[]{:S(2)}, u32[]{:S(2)}) %collective-permute-start.42) | collective-permute-done | bytes 163872 | tf_op jit(solution)/shard_map/ppermute | solution.py:480
  373.4 7.3 %collective-permute-done.43 = bf16[4,32,640]{2,1,0:T(8,128)(2,1)S(1)} collective-permute-done((bf16[4,32,640]{2,1,0:T(8,128)(2,1)S(1)}, bf16[4,32,640]{2,1,0:T(8,128)(2,1)S(1)}, u32[]{:S(2)}, u32[]{:S(2)}) %collective-permute-start.43) | collective-permute-done | bytes 163872 | tf_op jit(solution)/shard_map/ppermute | solution.py:480
  382.4 4.8 collective-permute-done.44
  387.2 3.0 collective-permute-start.45
  390.9 27.1 %collective-permute-done.45 = bf16[4,32,640]{2,1,0:T(8,128)(2,1)S(1)} collective-permute-done((bf16[4,32,640]{2,1,0:T(8,128)(2,1)S(1)}, bf16[4,32,640]{2,1,0:T(8,128)(2,1)S(1)}, u32[]{:S(2)}, u32[]{:S(2)}) %collective-permute-start.45) | collective-permute-done | bytes 163872 | tf_op jit(solution)/shard_map/ppermute | solution.py:480
  418.6 5.5 %collective-permute-done.46 = bf16[4,32,640]{2,1,0:T(8,128)(2,1)S(1)} collective-permute-done((bf16[4,32,640]{2,1,0:T(8,128)(2,1)S(1)}, bf16[4,32,640]{2,1,0:T(8,128)(2,1)S(1)}, u32[]{:S(2)}, u32[]{:S(2)}) %collective-permute-start.46) | collective-permute-done | bytes 163872 | tf_op jit(solution)/shard_map/ppermute | solution.py:480
  424.8 8.9 %collective-permute-done.47 = bf16[4,32,640]{2,1,0:T(8,128)(2,1)S(1)} collective-permute-done((bf16[4,32,640]{2,1,0:T(8,128)(2,1)S(1)}, bf16[4,32,640]{2,1,0:T(8,128)(2,1)S(1)}, u32[]{:S(2)}, u32[]{:S(2)}) %collective-permute-start.47) | collective-permute-done | bytes 163872 | tf_op jit(solution)/shard_map/ppermute | solution.py:480
  434.8 6.3 %collective-permute-done.48 = bf16[4,32,640]{2,1,0:T(8,128)(2,1)S(1)} collective-permute-done((bf16[4,32,640]{2,1,0:T(8,128)(2,1)S(1)}, bf16[4,32,640]{2,1,0:T(8,128)(2,1)S(1)}, u32[]{:S(2)}, u32[]{:S(2)}) %collective-permute-start.48) | collective-permute-done | bytes 163872 | tf_op jit(solution)/shard_map/ppermute | solution.py:480
  446.8 3.9 collective-permute-done.50
  453.1 3.5 pad_maximum_fusion.2.in_ref
  456.5 11.0 %unpack_qkv.1 = (f32[16,24,2304]{2,1,0:T(8,128)}, f32[16,4,8,640]{3,2,1,0:T(8,128)}) custom-call(s32[3]{0:T(128)} %pad_add_fusion.1.pos_ref, bf16[2,8,4,32,640]{4,3,2,1,0:T(8,128)(2,1)} %pad_maximum_fusion.2.in_ref), custom_call_target="tpu_custom_call" | custom-call | tf_op jit(solution)/shard_map/unpack_qkv/pallas_call | solution.py:381
  476.5 11.8 %unpack_mlp.1 = (f32[4,8,48,768]{3,2,1,0:T(8,128)}, f32[8,48,3072]{2,1,0:T(8,128)}) custom-call(s32[1]{0:T(128)} %bitcast.5.pos_ref, bf16[16,4,64,768]{3,2,1,0:T(8,128)(2,1)} %bitcast.215), custom_call_target="tpu_custom_call" | custom-call | tf_op jit(solution)/shard_map/unpack_mlp/pallas_call | solution.py:348
  (381 shorter events, 157.8 us)
Async XLA Ops:
  7.3 76.0 %all-gather.8.cloned.1.call-start = ((), (), s32[]{:S(2)}) async-start(), calls=%async_computation.1 | async-start | bytes 6684672 | tf_op jit(solution)/shard_map/all_gather | solution.py:571
  11.3 9.1 %collective-permute-start.3 = (f32[12,384]{1,0:T(8,128)S(1)}, f32[12,384]{1,0:T(8,128)S(1)}, u32[]{:S(2)}, u32[]{:S(2)}) collective-permute-start(f32[12,384]{1,0:T(8,128)S(1)} %concatenate.130), channel_id=1, source_target_pairs={{0,1},{1,0},{2,3},{3,2},{4,5},{5,4},{6,7},{7,6},{8,9},{9,8},{10,11... | collective-permute-start | bytes 55304 | tf_op jit(solution)/shard_map/ppermute | solution.py:407
  15.4 21.5 %collective-permute-start.4 = (bf16[384,640]{1,0:T(8,128)(2,1)S(1)}, bf16[384,640]{1,0:T(8,128)(2,1)S(1)}, u32[]{:S(2)}, u32[]{:S(2)}) collective-permute-start(bf16[384,640]{1,0:T(8,128)(2,1)S(1)} %concatenate.128), channel_id=1, source_target_pairs={{0,1},{1,0},{2,3},{3,2},{4,5},{5,4},{6,7},{7,6},{8,9},{9,8},{10,11... | collective-permute-start | bytes 1474568 | tf_op jit(solution)/shard_map/ppermute | solution.py:407
  15.5 9.3 %collective-permute-start.2 = (bf16[128,768]{1,0:T(8,128)(2,1)S(1)}, bf16[128,768]{1,0:T(8,128)(2,1)S(1)}, u32[]{:S(2)}, u32[]{:S(2)}) collective-permute-start(bf16[128,768]{1,0:T(8,128)(2,1)S(1)} %bitcast.230), channel_id=1, source_target_pairs={{0,96},{32,64},{64,32},{96,0},{1,97},{33,65},{65,33},{97,1},{2,98}... | collective-permute-start | bytes 589832 | tf_op jit(solution)/shard_map/ppermute | solution.py:411
  19.4 16.9 %collective-permute-start.1 = (bf16[128,768]{1,0:T(8,128)(2,1)S(1)}, bf16[128,768]{1,0:T(8,128)(2,1)S(1)}, u32[]{:S(2)}, u32[]{:S(2)}) collective-permute-start(bf16[128,768]{1,0:T(8,128)(2,1)S(1)} %bitcast.231), channel_id=1, source_target_pairs={{0,64},{32,96},{64,0},{96,32},{1,65},{33,97},{65,1},{97,33},{2,66}... | collective-permute-start | bytes 589832 | tf_op jit(solution)/shard_map/ppermute | solution.py:411
  19.9 16.3 %collective-permute-start = (bf16[128,768]{1,0:T(8,128)(2,1)S(1)}, bf16[128,768]{1,0:T(8,128)(2,1)S(1)}, u32[]{:S(2)}, u32[]{:S(2)}) collective-permute-start(bf16[128,768]{1,0:T(8,128)(2,1)S(1)} %bitcast.232), channel_id=1, source_target_pairs={{0,32},{32,0},{64,96},{96,64},{1,33},{33,1},{65,97},{97,65},{2,34}... | collective-permute-start | bytes 589832 | tf_op jit(solution)/shard_map/ppermute | solution.py:411
  39.2 145.9 %all-gather.10.cloned.1.call-start = ((), (), s32[]{:S(2)}) async-start(), calls=%async_computation.3 | async-start | bytes 4456448 | tf_op jit(solution)/shard_map/all_gather | solution.py:578
  39.3 12.4 %collective-permute-start.13 = (bf16[128,768]{1,0:T(8,128)(2,1)S(1)}, bf16[128,768]{1,0:T(8,128)(2,1)S(1)}, u32[]{:S(2)}, u32[]{:S(2)}) collective-permute-start(bf16[128,768]{1,0:T(8,128)(2,1)S(1)} %bitcast.246), channel_id=1, source_target_pairs={{0,96},{32,64},{64,32},{96,0},{1,97},{33,65},{65,33},{97,1},{2,98}... | collective-permute-start | bytes 589832 | tf_op jit(solution)/shard_map/ppermute | solution.py:411
  42.8 17.0 %collective-permute-start.12 = (bf16[128,768]{1,0:T(8,128)(2,1)S(1)}, bf16[128,768]{1,0:T(8,128)(2,1)}, u32[]{:S(2)}, u32[]{:S(2)}) collective-permute-start(bf16[128,768]{1,0:T(8,128)(2,1)S(1)} %bitcast.247), channel_id=1, source_target_pairs={{0,64},{32,96},{64,0},{96,32},{1,65},{33,97},{65,1},{97,33},{2,66}... | collective-permute-start | bytes 589832 | tf_op jit(solution)/shard_map/ppermute | solution.py:411
  43.8 16.0 %collective-permute-start.11 = (bf16[128,768]{1,0:T(8,128)(2,1)S(1)}, bf16[128,768]{1,0:T(8,128)(2,1)}, u32[]{:S(2)}, u32[]{:S(2)}) collective-permute-start(bf16[128,768]{1,0:T(8,128)(2,1)S(1)} %bitcast.248), channel_id=1, source_target_pairs={{0,32},{32,0},{64,96},{96,64},{1,33},{33,1},{65,97},{97,65},{2,34}... | collective-permute-start | bytes 589832 | tf_op jit(solution)/shard_map/ppermute | solution.py:411
  45.1 14.7 %collective-permute-start.5 = (bf16[192,768]{1,0:T(8,128)(2,1)}, bf16[192,768]{1,0:T(8,128)(2,1)}, u32[]{:S(2)}, u32[]{:S(2)}) collective-permute-start(bf16[192,768]{1,0:T(8,128)(2,1)} %constant_dynamic-slice_fusion.21), channel_id=1, source_target_pairs={{0,1},{1,0},{2,3},{3,2},{4,5},{5,4},{6,7},{7,6},{8,9},{9,8},{10,11... | collective-permute-start | bytes 884744 | tf_op jit(solution)/shard_map/ppermute | solution.py:407
  49.6 16.6 %collective-permute-start.7 = (bf16[192,768]{1,0:T(8,128)(2,1)S(1)}, bf16[192,768]{1,0:T(8,128)(2,1)}, u32[]{:S(2)}, u32[]{:S(2)}) collective-permute-start(bf16[192,768]{1,0:T(8,128)(2,1)S(1)} %fusion.51), channel_id=1, source_target_pairs={{0,1},{1,0},{2,3},{3,2},{4,5},{5,4},{6,7},{7,6},{8,9},{9,8},{10,11... | collective-permute-start | bytes 884744 | tf_op jit(solution)/shard_map/ppermute | solution.py:407
  51.6 20.5 %collective-permute-start.9 = (bf16[192,768]{1,0:T(8,128)(2,1)}, bf16[192,768]{1,0:T(8,128)(2,1)}, u32[]{:S(2)}, u32[]{:S(2)}) collective-permute-start(bf16[192,768]{1,0:T(8,128)(2,1)} %constant_dynamic-slice_fusion.14), channel_id=1, source_target_pairs={{0,1},{1,0},{2,3},{3,2},{4,5},{5,4},{6,7},{7,6},{8,9},{9,8},{10,11... | collective-permute-start | bytes 884744 | tf_op jit(solution)/shard_map/ppermute | solution.py:407
  59.8 13.1 %collective-permute-start.6 = (bf16[192,768]{1,0:T(8,128)(2,1)}, bf16[192,768]{1,0:T(8,128)(2,1)S(1)}, u32[]{:S(2)}, u32[]{:S(2)}) collective-permute-start(bf16[192,768]{1,0:T(8,128)(2,1)} %collective-permute-done.5), channel_id=1, source_target_pairs={{0,2},{2,0},{1,3},{3,1},{4,6},{6,4},{5,7},{7,5},{8,10},{10,8},{9,1... | collective-permute-start | bytes 884744 | tf_op jit(solution)/shard_map/ppermute | solution.py:407
  66.1 7.8 %collective-permute-start.8 = (bf16[192,768]{1,0:T(8,128)(2,1)}, bf16[192,768]{1,0:T(8,128)(2,1)S(1)}, u32[]{:S(2)}, u32[]{:S(2)}) collective-permute-start(bf16[192,768]{1,0:T(8,128)(2,1)} %collective-permute-done.7), channel_id=1, source_target_pairs={{0,2},{2,0},{1,3},{3,1},{4,6},{6,4},{5,7},{7,5},{8,10},{10,8},{9,1... | collective-permute-start | bytes 884744 | tf_op jit(solution)/shard_map/ppermute | solution.py:407
  103.5 11.8 %collective-permute-start.16 = (bf16[4,128,256]{2,1,0:T(8,128)(2,1)}, bf16[4,128,256]{2,1,0:T(8,128)(2,1)S(1)}, u32[]{:S(2)}, u32[]{:S(2)}) collective-permute-start(bf16[4,128,256]{2,1,0:T(8,128)(2,1)} %get-tuple-element.84.attn_ref), channel_id=1, source_target_pairs={{0,96},{32,64},{64,32},{96,0},{1,97},{33,65},{65,33},{97,1},{2,98}... | collective-permute-start | bytes 786440 | tf_op jit(solution)/shard_map/ppermute | solution.py:411
  107.4 12.7 %collective-permute-start.15 = (bf16[4,128,256]{2,1,0:T(8,128)(2,1)}, bf16[4,128,256]{2,1,0:T(8,128)(2,1)S(1)}, u32[]{:S(2)}, u32[]{:S(2)}) collective-permute-start(bf16[4,128,256]{2,1,0:T(8,128)(2,1)} %get-tuple-element.84.attn_ref), channel_id=1, source_target_pairs={{0,64},{32,96},{64,0},{96,32},{1,65},{33,97},{65,1},{97,33},{2,66}... | collective-permute-start | bytes 786440 | tf_op jit(solution)/shard_map/ppermute | solution.py:411
  107.9 12.4 %collective-permute-start.14 = (bf16[4,128,256]{2,1,0:T(8,128)(2,1)}, bf16[4,128,256]{2,1,0:T(8,128)(2,1)S(1)}, u32[]{:S(2)}, u32[]{:S(2)}) collective-permute-start(bf16[4,128,256]{2,1,0:T(8,128)(2,1)} %get-tuple-element.84.attn_ref), channel_id=1, source_target_pairs={{0,32},{32,0},{64,96},{96,64},{1,33},{33,1},{65,97},{97,65},{2,34}... | collective-permute-start | bytes 786440 | tf_op jit(solution)/shard_map/ppermute | solution.py:411
  120.3 110.4 %all-gather.12.cloned.1.call-start = ((), (), s32[]{:S(2)}) async-start(), calls=%async_computation.4 | async-start | bytes 4456448 | tf_op jit(solution)/shard_map/all_gather | solution.py:608
  131.3 19.9 %collective-permute-start.19 = (f32[128,768]{1,0:T(8,128)S(1)}, f32[128,768]{1,0:T(8,128)S(1)}, u32[]{:S(2)}, u32[]{:S(2)}) collective-permute-start(f32[128,768]{1,0:T(8,128)S(1)} %get-tuple-element.148), channel_id=1, source_target_pairs={{0,96},{32,64},{64,32},{96,0},{1,97},{33,65},{65,33},{97,1},{2,98}... | collective-permute-start | bytes 1179656 | tf_op jit(solution)/shard_map/ppermute | solution.py:411
  134.3 18.6 %collective-permute-start.18 = (f32[128,768]{1,0:T(8,128)S(1)}, f32[128,768]{1,0:T(8,128)S(1)}, u32[]{:S(2)}, u32[]{:S(2)}) collective-permute-start(f32[128,768]{1,0:T(8,128)S(1)} %get-tuple-element.149), channel_id=1, source_target_pairs={{0,64},{32,96},{64,0},{96,32},{1,65},{33,97},{65,1},{97,33},{2,66}... | collective-permute-start | bytes 1179656 | tf_op jit(solution)/shard_map/ppermute | solution.py:411
  135.8 31.4 %collective-permute-start.17 = (f32[128,768]{1,0:T(8,128)S(1)}, f32[128,768]{1,0:T(8,128)S(1)}, u32[]{:S(2)}, u32[]{:S(2)}) collective-permute-start(f32[128,768]{1,0:T(8,128)S(1)} %get-tuple-element.147), channel_id=1, source_target_pairs={{0,32},{32,0},{64,96},{96,64},{1,33},{33,1},{65,97},{97,65},{2,34}... | collective-permute-start | bytes 1179656 | tf_op jit(solution)/shard_map/ppermute | solution.py:411
  168.3 11.3 %collective-permute-start.22 = (bf16[128,768]{1,0:T(8,128)(2,1)S(1)}, bf16[128,768]{1,0:T(8,128)(2,1)S(1)}, u32[]{:S(2)}, u32[]{:S(2)}) collective-permute-start(bf16[128,768]{1,0:T(8,128)(2,1)S(1)} %get-tuple-element.124), channel_id=1, source_target_pairs={{0,96},{32,64},{64,32},{96,0},{1,97},{33,65},{65,33},{97,1},{2,98}... | collective-permute-start | bytes 589832 | tf_op jit(solution)/shard_map/ppermute | solution.py:411
  173.0 8.4 %collective-permute-start.20 = (bf16[128,768]{1,0:T(8,128)(2,1)S(1)}, bf16[128,768]{1,0:T(8,128)(2,1)S(1)}, u32[]{:S(2)}, u32[]{:S(2)}) collective-permute-start(bf16[128,768]{1,0:T(8,128)(2,1)S(1)} %get-tuple-element.124), channel_id=1, source_target_pairs={{0,32},{32,0},{64,96},{96,64},{1,33},{33,1},{65,97},{97,65},{2,34}... | collective-permute-start | bytes 589832 | tf_op jit(solution)/shard_map/ppermute | solution.py:411
  185.2 144.0 %reduce-scatter.2.cloned.1.call-start = ((), (), s32[]{:S(2)}) async-start(), calls=%async_computation.2 | async-start | bytes 5849088 | tf_op jit(solution)/shard_map/reduce_scatter | solution.py:642
  230.7 241.6 %all-gather.14.cloned.1.call-start = ((), (), s32[]{:S(2)}) async-start(), calls=%async_computation.5 | async-start | bytes 6684672 | tf_op jit(solution)/shard_map/all_gather | solution.py:677
  289.5 16.7 %collective-permute-start.33 = (f32[56,640]{1,0:T(8,128)S(1)}, f32[56,640]{1,0:T(8,128)}, u32[]{:S(2)}, u32[]{:S(2)}) collective-permute-start(f32[56,640]{1,0:T(8,128)S(1)} %get-tuple-element.159), channel_id=1, source_target_pairs={{0,28},{4,24},{8,20},{12,16},{16,12},{20,8},{24,4},{28,0},{1,29},{... | collective-permute-start | bytes 430088 | tf_op jit(solution)/shard_map/ppermute | solution.py:480
  297.6 13.3 %collective-permute-start.32 = (f32[56,640]{1,0:T(8,128)S(1)}, f32[56,640]{1,0:T(8,128)}, u32[]{:S(2)}, u32[]{:S(2)}) collective-permute-start(f32[56,640]{1,0:T(8,128)S(1)} %get-tuple-element.160), channel_id=1, source_target_pairs={{0,24},{4,28},{8,16},{12,20},{16,8},{20,12},{24,0},{28,4},{1,25},{... | collective-permute-start | bytes 430088 | tf_op jit(solution)/shard_map/ppermute | solution.py:480
  297.6 18.0 %collective-permute-start.31 = (f32[56,640]{1,0:T(8,128)}, f32[56,640]{1,0:T(8,128)}, u32[]{:S(2)}, u32[]{:S(2)}) collective-permute-start(f32[56,640]{1,0:T(8,128)} %get-tuple-element.161), channel_id=1, source_target_pairs={{0,20},{4,16},{8,28},{12,24},{16,4},{20,0},{24,12},{28,8},{1,21},{... | collective-permute-start | bytes 430088 | tf_op jit(solution)/shard_map/ppermute | solution.py:480
  298.1 20.5 %collective-permute-start.30 = (f32[56,640]{1,0:T(8,128)}, f32[56,640]{1,0:T(8,128)}, u32[]{:S(2)}, u32[]{:S(2)}) collective-permute-start(f32[56,640]{1,0:T(8,128)} %get-tuple-element.162), channel_id=1, source_target_pairs={{0,16},{4,20},{8,24},{12,28},{16,0},{20,4},{24,8},{28,12},{1,17},{... | collective-permute-start | bytes 430088 | tf_op jit(solution)/shard_map/ppermute | solution.py:480
  299.9 18.7 %collective-permute-start.29 = (f32[56,640]{1,0:T(8,128)}, f32[56,640]{1,0:T(8,128)}, u32[]{:S(2)}, u32[]{:S(2)}) collective-permute-start(f32[56,640]{1,0:T(8,128)} %get-tuple-element.163), channel_id=1, source_target_pairs={{0,12},{4,8},{8,4},{12,0},{16,28},{20,24},{24,20},{28,16},{1,13},{... | collective-permute-start | bytes 430088 | tf_op jit(solution)/shard_map/ppermute | solution.py:480
  306.3 12.4 %collective-permute-start.28 = (f32[56,640]{1,0:T(8,128)}, f32[56,640]{1,0:T(8,128)}, u32[]{:S(2)}, u32[]{:S(2)}) collective-permute-start(f32[56,640]{1,0:T(8,128)} %get-tuple-element.164), channel_id=1, source_target_pairs={{0,8},{4,12},{8,0},{12,4},{16,24},{20,28},{24,16},{28,20},{1,9},{5... | collective-permute-start | bytes 430088 | tf_op jit(solution)/shard_map/ppermute | solution.py:480
  310.9 7.8 %collective-permute-start.27 = (f32[56,640]{1,0:T(8,128)}, f32[56,640]{1,0:T(8,128)}, u32[]{:S(2)}, u32[]{:S(2)}) collective-permute-start(f32[56,640]{1,0:T(8,128)} %get-tuple-element.158), channel_id=1, source_target_pairs={{0,4},{4,0},{8,12},{12,8},{16,20},{20,16},{24,28},{28,24},{1,5},{5... | collective-permute-start | bytes 430088 | tf_op jit(solution)/shard_map/ppermute | solution.py:480
  331.0 7.5 %collective-permute-start.35 = (f32[64,768]{1,0:T(8,128)S(1)}, f32[64,768]{1,0:T(8,128)S(1)}, u32[]{:S(2)}, u32[]{:S(2)}) collective-permute-start(f32[64,768]{1,0:T(8,128)S(1)} %pad_maximum_fusion.18), channel_id=1, source_target_pairs={{0,1},{1,0},{2,3},{3,2},{4,5},{5,4},{6,7},{7,6},{8,9},{9,8},{10,11... | collective-permute-start | bytes 589832 | tf_op jit(solution)/shard_map/ppermute | solution.py:407
  349.1 9.9 %collective-permute-start.41 = (bf16[32,640]{1,0:T(8,128)(2,1)}, bf16[32,640]{1,0:T(8,128)(2,1)S(1)}, u32[]{:S(2)}, u32[]{:S(2)}) collective-permute-start(bf16[32,640]{1,0:T(8,128)(2,1)} %fusion.63), channel_id=1, source_target_pairs={{0,96},{32,64},{64,32},{96,0},{1,97},{33,65},{65,33},{97,1},{2,98}... | collective-permute-start | bytes 122888 | tf_op jit(solution)/shard_map/ppermute | solution.py:411
  351.3 9.9 %collective-permute-start.40 = (bf16[32,640]{1,0:T(8,128)(2,1)}, bf16[32,640]{1,0:T(8,128)(2,1)S(1)}, u32[]{:S(2)}, u32[]{:S(2)}) collective-permute-start(bf16[32,640]{1,0:T(8,128)(2,1)} %fusion.63), channel_id=1, source_target_pairs={{0,64},{32,96},{64,0},{96,32},{1,65},{33,97},{65,1},{97,33},{2,66}... | collective-permute-start | bytes 122888 | tf_op jit(solution)/shard_map/ppermute | solution.py:411
  352.1 9.1 %collective-permute-start.39 = (bf16[32,640]{1,0:T(8,128)(2,1)}, bf16[32,640]{1,0:T(8,128)(2,1)S(1)}, u32[]{:S(2)}, u32[]{:S(2)}) collective-permute-start(bf16[32,640]{1,0:T(8,128)(2,1)} %fusion.63), channel_id=1, source_target_pairs={{0,32},{32,0},{64,96},{96,64},{1,33},{33,1},{65,97},{97,65},{2,34}... | collective-permute-start | bytes 122888 | tf_op jit(solution)/shard_map/ppermute | solution.py:411
  356.2 78.2 %collective-permute-start.23 = (f32[128,768]{1,0:T(8,128)S(1)}, f32[128,768]{1,0:T(8,128)S(1)}, u32[]{:S(2)}, u32[]{:S(2)}) collective-permute-start(f32[128,768]{1,0:T(8,128)S(1)} %get-tuple-element.144), channel_id=1, source_target_pairs={{0,32},{32,0},{64,96},{96,64},{1,33},{33,1},{65,97},{97,65},{2,34}... | collective-permute-start | bytes 1179656 | tf_op jit(solution)/shard_map/ppermute | solution.py:411
  357.7 85.5 %collective-permute-start.24 = (f32[128,768]{1,0:T(8,128)S(1)}, f32[128,768]{1,0:T(8,128)S(1)}, u32[]{:S(2)}, u32[]{:S(2)}) collective-permute-start(f32[128,768]{1,0:T(8,128)S(1)} %get-tuple-element.143), channel_id=1, source_target_pairs={{0,64},{32,96},{64,0},{96,32},{1,65},{33,97},{65,1},{97,33},{2,66}... | collective-permute-start | bytes 1179656 | tf_op jit(solution)/shard_map/ppermute | solution.py:411
  358.9 85.6 %collective-permute-start.25 = (f32[128,768]{1,0:T(8,128)}, f32[128,768]{1,0:T(8,128)}, u32[]{:S(2)}, u32[]{:S(2)}) collective-permute-start(f32[128,768]{1,0:T(8,128)} %get-tuple-element.142), channel_id=1, source_target_pairs={{0,96},{32,64},{64,32},{96,0},{1,97},{33,65},{65,33},{97,1},{2,98}... | collective-permute-start | bytes 1179656 | tf_op jit(solution)/shard_map/ppermute | solution.py:411
  361.2 9.4 %collective-permute-start.42 = (bf16[4,32,640]{2,1,0:T(8,128)(2,1)S(1)}, bf16[4,32,640]{2,1,0:T(8,128)(2,1)S(1)}, u32[]{:S(2)}, u32[]{:S(2)}) collective-permute-start(bf16[4,32,640]{2,1,0:T(8,128)(2,1)S(1)} %pad_maximum_fusion.20), channel_id=1, source_target_pairs={{0,4},{4,0},{8,12},{12,8},{16,20},{20,16},{24,28},{28,24},{1,5},{5... | collective-permute-start | bytes 491528 | tf_op jit(solution)/shard_map/ppermute | solution.py:480
  362.4 84.4 %collective-permute-start.52 = (f32[128,768]{1,0:T(8,128)}, f32[128,768]{1,0:T(8,128)}, u32[]{:S(2)}, u32[]{:S(2)}) collective-permute-start(f32[128,768]{1,0:T(8,128)} %get-tuple-element.140), channel_id=1, source_target_pairs={{0,96},{32,64},{64,32},{96,0},{1,97},{33,65},{65,33},{97,1},{2,98}... | collective-permute-start | bytes 1179656 | tf_op jit(solution)/shard_map/ppermute | solution.py:411
  370.6 10.1 %collective-permute-start.43 = (bf16[4,32,640]{2,1,0:T(8,128)(2,1)S(1)}, bf16[4,32,640]{2,1,0:T(8,128)(2,1)S(1)}, u32[]{:S(2)}, u32[]{:S(2)}) collective-permute-start(bf16[4,32,640]{2,1,0:T(8,128)(2,1)S(1)} %pad_maximum_fusion.20), channel_id=1, source_target_pairs={{0,8},{4,12},{8,0},{12,4},{16,24},{20,28},{24,16},{28,20},{1,9},{5... | collective-permute-start | bytes 491528 | tf_op jit(solution)/shard_map/ppermute | solution.py:480
  387.2 30.7 %collective-permute-start.45 = (bf16[4,32,640]{2,1,0:T(8,128)(2,1)S(1)}, bf16[4,32,640]{2,1,0:T(8,128)(2,1)S(1)}, u32[]{:S(2)}, u32[]{:S(2)}) collective-permute-start(bf16[4,32,640]{2,1,0:T(8,128)(2,1)S(1)} %pad_maximum_fusion.20), channel_id=1, source_target_pairs={{0,16},{4,20},{8,24},{12,28},{16,0},{20,4},{24,8},{28,12},{1,17},{... | collective-permute-start | bytes 491528 | tf_op jit(solution)/shard_map/ppermute | solution.py:480
  424.2 9.5 %collective-permute-start.47 = (bf16[4,32,640]{2,1,0:T(8,128)(2,1)S(1)}, bf16[4,32,640]{2,1,0:T(8,128)(2,1)S(1)}, u32[]{:S(2)}, u32[]{:S(2)}) collective-permute-start(bf16[4,32,640]{2,1,0:T(8,128)(2,1)S(1)} %pad_maximum_fusion.20), channel_id=1, source_target_pairs={{0,24},{4,28},{8,16},{12,20},{16,8},{20,12},{24,0},{28,4},{1,25},{... | collective-permute-start | bytes 491528 | tf_op jit(solution)/shard_map/ppermute | solution.py:480
  434.4 12.4 %collective-permute-start.51 = (f32[128,768]{1,0:T(8,128)}, f32[128,768]{1,0:T(8,128)}, u32[]{:S(2)}, u32[]{:S(2)}) collective-permute-start(f32[128,768]{1,0:T(8,128)} %get-tuple-element.141), channel_id=1, source_target_pairs={{0,64},{32,96},{64,0},{96,32},{1,65},{33,97},{65,1},{97,33},{2,66}... | collective-permute-start | bytes 1179656 | tf_op jit(solution)/shard_map/ppermute | solution.py:411
  441.1 9.6 %collective-permute-start.50 = (f32[128,768]{1,0:T(8,128)}, f32[128,768]{1,0:T(8,128)}, u32[]{:S(2)}, u32[]{:S(2)}) collective-permute-start(f32[128,768]{1,0:T(8,128)} %get-tuple-element.139), channel_id=1, source_target_pairs={{0,32},{32,0},{64,96},{96,64},{1,33},{33,1},{65,97},{97,65},{2,34}... | collective-permute-start | bytes 1179656 | tf_op jit(solution)/shard_map/ppermute | solution.py:411
  443.2 9.8 %collective-permute-start.49 = (bf16[8,4,32,640]{3,2,1,0:T(8,128)(2,1)}, bf16[8,4,32,640]{3,2,1,0:T(8,128)(2,1)}, u32[]{:S(2)}, u32[]{:S(2)}) collective-permute-start(bf16[8,4,32,640]{3,2,1,0:T(8,128)(2,1)} %bitcast_dynamic-update-slice_fusion), channel_id=1, source_target_pairs={{0,2},{2,0},{1,3},{3,1},{4,6},{6,4},{5,7},{7,5},{8,10},{10,8},{9,1... | collective-permute-start | bytes 3932168 | tf_op jit(solution)/shard_map/ppermute | solution.py:407
  (68 other events, 735.5 us)
Sparse Core Ops, SparseCore 0:
  39.3 43.9 all-gather.7
  120.4 56.2 all-gather.9
  185.3 45.3 all-gather.11
  233.0 85.4 reduce-scatter.1
  349.2 70.6 all-gather.13

commit v3 on v2

--- a/solution.py
+++ b/solution.py
@@ -66,7 +66,7 @@
     return jnp.concatenate([product[:256, :128], product[256:, 128:]], axis=0)
 
 
-def forward_kernel(pos_ref, q_ref, kv_ref, attn_ref, qaug_ref, lse_ref, m_ref, l_ref, acc_ref):
+def forward_kernel(pos_ref, q_ref, kv_ref, attn_ref, lse_ref, m_ref, l_ref, acc_ref):
     seq = pos_ref[0]
     rank = pos_ref[1]
 
@@ -106,20 +106,12 @@
         lax.fori_loop(0, last, full, 0)
         step(last, True)
         lane = lax.broadcasted_iota(jnp.int32, (128, 128), 1)
-        extra = jnp.zeros((128, 128), BF16)
         total = jnp.sum(l_ref[...], axis=1, keepdims=True)
         log_sum = m_ref[...] + jnp.log(total)
         lse_ref[slot] = log_sum
         outs = acc_ref[...] / total
-        for p, part in enumerate(pieces(-log_sum)):
-            for h in range(3):
-                extra = jnp.where(
-                    lane == 64 + 3 * h + p, part[128 * h : 128 * h + 128], extra
-                )
         attn_ref[slot, :, :128] = jnp.where(lane < 64, outs[:128], outs[128:256]).astype(BF16)
         attn_ref[slot, :, 128:] = jnp.where(lane < 64, 0.0, outs[256:]).astype(BF16)
-        qaug_ref[slot, :, :128] = q_rows[:, :128]
-        qaug_ref[slot, :, 128:] = jnp.where(lane < 64, q_rows[:, 128:], extra)
         return carry
 
     lax.fori_loop(0, 4, tile, 0)
@@ -134,11 +126,10 @@
         forward_kernel,
         out_shape=(
             jax.ShapeDtypeStruct((4, 128, 256), BF16),
-            jax.ShapeDtypeStruct((4, 128, 256), BF16),
             jax.ShapeDtypeStruct((4, 384, 128), F32),
         ),
         in_specs=[pl.BlockSpec(memory_space=pltpu.SMEM), vmem_spec(), vmem_spec()],
-        out_specs=(vmem_spec(), vmem_spec(), vmem_spec()),
+        out_specs=(vmem_spec(), vmem_spec()),
         scratch_shapes=[pltpu.VMEM((384, 128), F32)] * 3,
         compiler_params=pltpu.CompilerParams(vmem_limit_bytes=VMEM_LIMIT),
         cost_estimate=pl.CostEstimate(
@@ -148,7 +139,7 @@
     )(pos, q, kv)
 
 
-def grad_rows_kernel(dr_ref, w_ref, attn_ref, do_ref, delta_ref):
+def grad_rows_kernel(dr_ref, w_ref, attn_ref, lse_ref, do_ref, delta_ref):
     lane = lax.broadcasted_iota(jnp.int32, (512, 128), 1)
     grads = lax.dot_general(dr_ref[...], w_ref[...], NT, preferred_element_type=F32).astype(BF16)
     attn = attn_ref[...].reshape(512, 256).astype(F32)
@@ -159,24 +150,26 @@
         delta = jnp.broadcast_to(delta, (512, 128))
         for k in range(4):
             delta_ref[k, 128 * h : 128 * h + 128] = delta[128 * k : 128 * k + 128]
-        for p, piece in enumerate(pieces(-delta)):
+        log_sum = jnp.concatenate([lse_ref[k, 128 * h : 128 * h + 128] for k in range(4)], axis=0)
+        for p, (piece, other) in enumerate(zip(pieces(-delta), pieces(-log_sum))):
             extra = jnp.where(lane == 3 * h + p, piece, extra)
+            extra = jnp.where(lane == 16 + 3 * h + p, other, extra)
     do_ref[:, :, :128] = grads[:, :128].reshape(4, 128, 128)
     do_ref[:, :, 128:] = jnp.where(lane < 64, extra, grads[:, 128:]).reshape(4, 128, 128)
 
 
-def grad_rows(dr_low, w_rows, attn):
+def grad_rows(dr_low, w_rows, attn, lse):
     return pl.pallas_call(
         grad_rows_kernel,
         out_shape=(
             jax.ShapeDtypeStruct((4, 128, 256), BF16),
             jax.ShapeDtypeStruct((4, 384, 128), F32),
         ),
-        in_specs=[vmem_spec(), vmem_spec(), vmem_spec()],
+        in_specs=[vmem_spec()] * 4,
         out_specs=(vmem_spec(), vmem_spec()),
         compiler_params=pltpu.CompilerParams(vmem_limit_bytes=VMEM_LIMIT),
         name="attention_grad_rows",
-    )(dr_low, w_rows, attn)
+    )(dr_low, w_rows, attn, lse)
 
 
 def query_grad_kernel(
@@ -249,9 +242,19 @@
     )(pos, q, do, lse, delta, kv)
 
 
-def key_grad_kernel(pos_ref, kv_ref, qg_ref, dog_ref, dkv_ref, sum_ref, dk_ref, dv_ref):
+def key_grad_kernel(
+    pos_ref, kv_ref, qg_ref, dog_ref, dkv_ref, sum_ref, dk_ref, dv_ref, join_ref
+):
     seq = pos_ref[0]
     rank = pos_ref[1]
+
+    def join(chunk, carry):
+        q_rows = chunk_rows(qg_ref, rank, chunk)[:, 128:]
+        do_rows = chunk_rows(dog_ref, rank, chunk)[:, 128:]
+        join_ref[chunk] = jnp.concatenate([q_rows[:, :64], do_rows[:, :64]], axis=1)
+        return carry
+
+    lax.fori_loop(seq // 4, 16, join, 0)
 
     def tile(k, carry):
         slot = rank ^ k
@@ -263,7 +266,7 @@
         keys = []
         values = []
         for h, run in enumerate((0, 1, 3)):
-            key_ones = jnp.logical_and(lane >= 192 + 3 * h, lane < 195 + 3 * h)
+            key_ones = jnp.logical_and(lane >= 208 + 3 * h, lane < 211 + 3 * h)
             value_ones = jnp.logical_and(lane >= 128 + 3 * h, lane < 131 + 3 * h)
             keys.append(jnp.where(key_ones, 1.0, slot_only(key_rows, h)).astype(BF16))
             values.append(jnp.where(value_ones, 1.0, slot_only(value_rows, run)).astype(BF16))
@@ -273,7 +276,8 @@
         dv_ref[...] = jnp.zeros(dv_ref.shape, F32)
 
         def step(chunk, masked):
-            q_rows = chunk_rows(qg_ref, rank, chunk)
+            q_rows = chunk_rows(qg_ref, rank, chunk)[:, :128]
+            q_rows = jnp.concatenate([q_rows, join_ref[chunk]], axis=1)
             do_rows = chunk_rows(dog_ref, rank, chunk)
             scores = lax.dot_general(keys, q_rows, NT, preferred_element_type=F32)
             if masked:
@@ -318,7 +322,11 @@
         ),
         in_specs=[pl.BlockSpec(memory_space=pltpu.SMEM)] + [vmem_spec()] * 3,
         out_specs=(vmem_spec(), vmem_spec()),
-        scratch_shapes=[pltpu.VMEM((384, 128), F32), pltpu.VMEM((384, 128), F32)],
+        scratch_shapes=[
+            pltpu.VMEM((384, 128), F32),
+            pltpu.VMEM((384, 128), F32),
+            pltpu.VMEM((16, 512, 128), BF16),
+        ],
         compiler_params=pltpu.CompilerParams(vmem_limit_bytes=VMEM_LIMIT),
         cost_estimate=pl.CostEstimate(
             flops=3 * 512 * 4096 * 1024, transcendentals=3 * 512 * 4096, bytes_accessed=10 * 2**20
@@ -327,7 +335,55 @@
     )(pos, kv_own, q_all, do_all)
 
 
-def unpack_mlp_kernel(pos_ref, in_ref, out_w_ref, fc_w_ref):
+def first_grads_kernel(
+    norm_ref, hat_ref, q_ref, kv_ref, w_ref, q_sum_ref, kv_sum_ref, local_ref, dh_ref
+):
+    cols = jnp.concatenate([q_ref[...].reshape(512, 256), kv_ref[...].reshape(512, 384)], axis=1)
+    for half in range(2):
+        grads = jnp.dot(
+            norm_ref[384 * half : 384 * half + 384], cols, preferred_element_type=F32
+        )
+        for block in range(16):
+            local_ref[block % 2, block // 2, 24 * half : 24 * half + 24] = grads[
+                24 * block : 24 * block + 24
+            ]
+    gain = jnp.zeros((1, 768), F32)
+    shift = jnp.zeros((1, 768), F32)
+    for k in range(4):
+        rows = slice(128 * k, 128 * k + 128)
+        part = lax.dot_general(cols[rows], w_ref[...], NT, preferred_element_type=F32)
+        dh_ref[k] = part
+        gain = gain + jnp.sum(part * hat_ref[rows], axis=0, keepdims=True)
+        shift = shift + jnp.sum(part, axis=0, keepdims=True)
+    extra = (
+        jnp.concatenate([q_sum_ref[...], kv_sum_ref[...]], axis=1),
+        gain[:, :640],
+        jnp.concatenate([gain[:, 640:], shift[:, :512]], axis=1),
+        jnp.concatenate([shift[:, 512:], jnp.zeros((1, 384), F32)], axis=1),
+    )
+    top = lax.broadcasted_iota(jnp.int32, (8, 640), 0) == 0
+    for block in range(16):
+        rows = jnp.zeros((8, 640), F32)
+        if block < 4:
+            rows = jnp.where(top, extra[block], rows)
+        local_ref[block % 2, block // 2, 48:] = rows
+
+
+def first_grads(norm_t, hat, dq, dkv, w_cols, q_sum, kv_sum):
+    return pl.pallas_call(
+        first_grads_kernel,
+        out_shape=(
+            jax.ShapeDtypeStruct((2, 8, 56, 640), F32),
+            jax.ShapeDtypeStruct((4, 128, 768), F32),
+        ),
+        in_specs=[vmem_spec()] * 7,
+        out_specs=(vmem_spec(), vmem_spec()),
+        compiler_params=pltpu.CompilerParams(vmem_limit_bytes=VMEM_LIMIT),
+        name="first_grads",
+    )(norm_t, hat, dq, dkv, w_cols, q_sum, kv_sum)
+
+
+def unpack_kernel(pos_ref, in_ref, out_w_ref, fc_w_ref, qkv_ref, extra_ref):
     step = pl.program_id(0)
     rank = pos_ref[0]
 
@@ -343,64 +399,39 @@
             fc_w_ref[0, :, 384 * g : 384 * g + 384] = rows[:, :384]
             fc_w_ref[0, :, 1536 + 384 * g : 1920 + 384 * g] = rows[:, 384:]
 
-
-def unpack_mlp(pos, early):
-    out_w, fc_w = pl.pallas_call(
-        unpack_mlp_kernel,
+    rows = [in_ref[0, rank ^ g, 48:].astype(F32) for g in range(4)]
+    qkv_ref[0, :, :768] = jnp.concatenate([r[:24, :192] for r in rows], axis=1)
+    qkv_ref[0, :, 768:1536] = jnp.concatenate([r[:24, 256:448] for r in rows], axis=1)
+    qkv_ref[0, :, 1536:] = jnp.concatenate(
+        [part for r in rows for part in (r[:24, 512:640], r[:24, 448:512])], axis=1
+    )
+    for g in range(4):
+        extra_ref[0, g] = rows[g][24:]
+
+
+def unpack(pos, totals):
+    out_w, fc_w, qkv_w, extra = pl.pallas_call(
+        unpack_kernel,
         grid_spec=pltpu.PrefetchScalarGridSpec(
             num_scalar_prefetch=1,
             grid=(16,),
-            in_specs=[pl.BlockSpec((1, 4, 64, 768), lambda s, pos: (s, 0, 0, 0))],
+            in_specs=[pl.BlockSpec((1, 4, 96, 768), lambda s, pos: (s, 0, 0, 0))],
             out_specs=(
                 pl.BlockSpec((4, 1, 48, 768), lambda s, pos: (0, jnp.minimum(s, 7), 0, 0)),
                 pl.BlockSpec((1, 48, 3072), lambda s, pos: (jnp.maximum(s - 8, 0), 0, 0)),
+                pl.BlockSpec((1, 24, 2304), lambda s, pos: (s, 0, 0)),
+                pl.BlockSpec((1, 4, 24, 768), lambda s, pos: (s, 0, 0, 0)),
             ),
         ),
         out_shape=(
             jax.ShapeDtypeStruct((4, 8, 48, 768), F32),
             jax.ShapeDtypeStruct((8, 48, 3072), F32),
-        ),
-        name="unpack_mlp",
-    )(pos, early)
-    return out_w.reshape(1536, 768), fc_w.reshape(384, 3072)
-
-
-def unpack_qkv_kernel(pos_ref, in_ref, out_ref, extra_ref):
-    rank = pos_ref[0]
-    rows = [in_ref[0, 0, rank ^ g].astype(F32) for g in range(4)]
-    out_ref[0, :, :768] = jnp.concatenate([r[:24, :192] for r in rows], axis=1)
-    out_ref[0, :, 768:1536] = jnp.concatenate([r[:24, 256:448] for r in rows], axis=1)
-    out_ref[0, :, 1536:] = jnp.concatenate(
-        [part for r in rows for part in (r[:24, 512:], r[:24, 448:512])], axis=1
-    )
-    for g in range(4):
-        extra_ref[0, g] = rows[g][24:]
-
-
-def unpack_qkv(pos, late):
-    grads, extra = pl.pallas_call(
-        unpack_qkv_kernel,
-        grid_spec=pltpu.PrefetchScalarGridSpec(
-            num_scalar_prefetch=1,
-            grid=(16,),
-            in_specs=[
-                pl.BlockSpec(
-                    (1, 1, 4, 32, 640),
-                    lambda s, pos: (lax.rem(s, 2) ^ pos[2], (s // 2) ^ pos[1], 0, 0, 0),
-                )
-            ],
-            out_specs=(
-                pl.BlockSpec((1, 24, 2304), lambda s, pos: (s, 0, 0)),
-                pl.BlockSpec((1, 4, 8, 640), lambda s, pos: (s, 0, 0, 0)),
-            ),
-        ),
-        out_shape=(
             jax.ShapeDtypeStruct((16, 24, 2304), F32),
-            jax.ShapeDtypeStruct((16, 4, 8, 640), F32),
-        ),
-        name="unpack_qkv",
-    )(pos, late)
-    return grads.reshape(384, 2304), extra
+            jax.ShapeDtypeStruct((16, 4, 24, 768), F32),
+        ),
+        name="unpack_grads",
+    )(pos, totals)
+    return out_w.reshape(1536, 768), fc_w.reshape(384, 3072), qkv_w.reshape(384, 2304), extra
 
 
 def swap(values, axis):
@@ -480,21 +511,10 @@
     return lax.ppermute(values, BLOCKS, [(a, a ^ offset) for a in range(8)])
 
 
-def add_sequences(part, half, fs):
-    rest = part[2 * half :]
-    own = lax.dynamic_slice_in_dim(part, fs * half, half, 0)
-    other = lax.dynamic_slice_in_dim(part, (1 - fs) * half, half, 0)
-    total = jnp.concatenate([own, rest], axis=0) + swap(
-        jnp.concatenate([other, rest], axis=0), "fsdp"
-    )
-    return total.astype(BF16)
-
-
 def reduce_by_permute(local):
     core = lax.axis_index("core")
     block = lax.axis_index(BLOCKS)
-    pair = local.reshape((8, 2) + local.shape[1:])
-    pair = pick(pair, core, 1) + swap(pick(pair, 1 - core, 1), "core")
+    pair = pick(local, core) + swap(pick(local, 1 - core), "core")
     moved = [to_block(pick(pair, block ^ r), r) for r in range(1, 8)]
     total = pick(pair, block)
     for values in moved:
@@ -569,13 +589,21 @@
     q_scaled = (projected[:, :256].astype(BF16) * 0.125).astype(BF16).reshape(4, 128, 256)
     kv_own = projected[:, 256:].astype(BF16).reshape(4, 128, 384)
     kv_all = lax.all_gather(kv_own, SEQ_AXES, axis=0, tiled=False)
-    kv_all, proj_ranks, fc_cols, out_rows, cot_low = lax.optimization_barrier(
-        (kv_all, proj_ranks, fc_cols, out_rows, jnp.concatenate(gather_ranks(out_grad[0]), axis=0))
-    )
-    attn, q_aug, lse = forward_attention(pos, q_scaled, kv_all)
+    q_all = lax.all_gather(after(q_scaled, kv_all), SEQ_AXES, axis=0, tiled=False)
+    normed_one_t = normed_one.T
+    kv_all, proj_ranks, fc_cols, out_rows, cot_low, normed_one_t = lax.optimization_barrier(
+        (
+            kv_all,
+            proj_ranks,
+            fc_cols,
+            out_rows,
+            jnp.concatenate(gather_ranks(out_grad[0]), axis=0),
+            normed_one_t,
+        )
+    )
+    attn, lse = forward_attention(pos, q_scaled, kv_all)
 
     attn_ranks = gather_ranks(attn)
-    q_all = lax.all_gather(after(q_aug, *attn_ranks[1:]), SEQ_AXES, axis=0, tiled=False)
     residual = x + proj_bias
     attn_full = jnp.concatenate(
         [
@@ -597,23 +625,36 @@
     )
     grad_hidden = grad_act * slope
     grad_hidden_low = grad_hidden.astype(BF16)
-    grad_normed_two = sum_ranks(dot_nt(grad_hidden_low, fc_cols).reshape(4, 128, 768))
+    partial_two = dot_nt(grad_hidden_low, fc_cols).reshape(4, 128, 768)
+    moved_two = tuple(to_rank(partial_two[r], r) for r in (1, 2, 3))
+    grad_out_w = dot_tn(activated, cot_low).reshape(2, 384, 768)
+    grad_fc_w = dot_tn(normed_two, grad_hidden_low).reshape(2, 384, 768)
+    moved_two, grad_out_w, grad_fc_w = lax.optimization_barrier(
+        (moved_two, grad_out_w, grad_fc_w)
+    )
+    grad_normed_two = partial_two[0] + moved_two[0] + moved_two[1] + moved_two[2]
 
     cot_own = out_grad[0].astype(F32)
     grad_residual = (
         norm_back(grad_normed_two, r_normed[:128], r_scale[:128], gain_two) + cot_own
     )
     grad_residual_low = jnp.concatenate(gather_ranks(grad_residual.astype(BF16)), axis=0)
-    do_aug, delta = grad_rows(grad_residual_low, proj_ranks[0], attn)
+    do_aug, delta = grad_rows(grad_residual_low, proj_ranks[0], attn, lse)
     do_all = lax.all_gather(after(do_aug, q_all), SEQ_AXES, axis=0, tiled=False)
-    grad_q, grad_q_sum = query_grad(pos, q_aug, do_aug, lse, delta, kv_all)
-
-    activated, normed_two, grad_hidden_low, attn_late, grad_q = lax.optimization_barrier(
-        (activated, normed_two, grad_hidden_low, attn, grad_q)
+    grad_q, grad_q_sum = query_grad(pos, q_scaled, do_aug, lse, delta, kv_all)
+
+    (
+        activated,
+        attn_late,
+        grad_q,
+        grad_normed_two,
+        grad_residual,
+        grad_hidden,
+        cot_own,
+    ) = lax.optimization_barrier(
+        (activated, attn, grad_q, grad_normed_two, grad_residual, grad_hidden, cot_own)
     )
     out_partial = dot(activated, out_rows).reshape(4, 128, 768)
-    grad_out_w = dot_tn(activated, cot_low).reshape(2, 384, 768)
-    grad_fc_w = dot_tn(normed_two, grad_hidden_low).reshape(2, 384, 768)
     grad_proj_w = dot_tn(attn_late.reshape(512, 256), grad_residual_low)
     grad_proj_w = jnp.concatenate([grad_proj_w[:128], grad_proj_w[192:]], axis=0)
     extra = jnp.stack(
@@ -648,56 +689,44 @@
         out_partial[0] + out_moved[0] + out_moved[1] + out_moved[2] + out_bias + residual[:128]
     ).astype(BF16)
 
-    grad_cols = jnp.concatenate([grad_q, grad_kv], axis=2).reshape(512, 640)
-    grad_qkv_w = dot_tn(normed_one, grad_cols).reshape(2, 16, 24, 640)
-    partial_one = dot_nt(grad_cols, w_cols)
-    late_extra = jnp.concatenate(
-        [
-            grad_q_sum[0],
-            grad_kv_sum[0],
-            jnp.sum(partial_one * x_normed, axis=0),
-            jnp.sum(partial_one, axis=0),
-            jnp.zeros((640 * 15 - 1536,), F32),
-        ]
-    ).reshape(16, 1, 640)
-    late_local = jnp.concatenate(
-        [
-            grad_qkv_w.transpose(1, 0, 2, 3).reshape(16, 48, 640),
-            late_extra,
-            jnp.zeros((16, 7, 640), F32),
-        ],
-        axis=1,
-    )
-    late = add_sequences(reduce_by_permute(late_local), 24, fs)
+    late_local, partial_one = first_grads(
+        normed_one_t, x_normed, grad_q, grad_kv, w_cols, grad_q_sum, grad_kv_sum
+    )
+    late = reduce_by_permute(late_local)
 
     early, late, partial_one = lax.optimization_barrier((early, late, partial_one))
-    early = add_sequences(early, 48, fs)
-    early_ranks = gather_ranks(early)
-    late_ranks = gather_ranks(late)
-    early = lax.all_gather(jnp.stack(early_ranks), SEQ_AXES, axis=0, tiled=False)
-    late = jnp.stack(late_ranks)
-    late = jnp.stack([late] + [to_block(late, r) for r in range(1, 8)])
-    late = jnp.stack([late, swap(late, "core")])
-    g_w_qkv, late_extra = unpack_qkv(
-        jnp.stack([rank, lax.axis_index(BLOCKS), lax.axis_index("core")]).astype(jnp.int32), late
-    )
-    grad_normed_one = sum_ranks(partial_one.reshape(4, 128, 768))
+    late = jnp.concatenate([late, jnp.zeros((56, 128), F32)], axis=1)
+
+    def rows_of(which):
+        return jnp.concatenate(
+            [
+                lax.dynamic_slice_in_dim(early, 48 * which, 48, 0),
+                lax.dynamic_slice_in_dim(late, 24 * which, 24, 0),
+                late[48:],
+                early[96:],
+            ],
+            axis=0,
+        )
+
+    totals = (rows_of(fs) + swap(rows_of(1 - fs), "fsdp")).astype(BF16)
+    totals = jnp.stack(gather_ranks(totals))
+    totals = lax.all_gather(totals, SEQ_AXES, axis=0, tiled=False)
+    grad_normed_one = sum_ranks(partial_one)
     input_grad = (
         norm_back(grad_normed_one, x_normed[:128], x_scale[:128], gain_one) + grad_residual
     )
-    early, g_w_qkv, input_grad = lax.optimization_barrier((early, g_w_qkv, input_grad))
+    totals, input_grad, output = lax.optimization_barrier((totals, input_grad, output))
+    g_w_out, g_w_fc, g_w_qkv, extra = unpack(jnp.stack([rank]).astype(jnp.int32), totals)
 
     def own_half(values):
         return lax.dynamic_slice_in_dim(values, 384 * fs, 384, 0)
 
-    g_w_out, g_w_fc = unpack_mlp(jnp.stack([rank]).astype(jnp.int32), early)
-    early = early[:, :, 48:61].astype(F32)
-    early = jnp.stack([pick(early, rank ^ g, 1) for g in range(4)], axis=1)
+    early = extra[:, :, 8:]
+    late_rows = extra[:4, :, 0, :640]
     g_w_proj = lax.dynamic_slice_in_dim(early[:, :, :12], 2 * fs, 2, 1)
     g_w_proj = g_w_proj.transpose(1, 0, 2, 3).reshape(384, 768)
     sums = jnp.sum(early[:4, :, 12], axis=1)
     g_b_fc = pick(early[4, :, 12].reshape(4, 2, 384), fs, 1).reshape(1536)
-    late_rows = late_extra[:4, :, 0]
     bias_row = late_rows[0]
     g_q_bias = own_half(bias_row[:, :192].reshape(768))
     g_v_bias = own_half(

time: 511 us -> 441 us (0.86)
  the two profiles are of different devices: /device:TPU:0 before, /device:TPU:1 now
where the time goes in v3:
time: 441 us; the launch traced here: 436 us
  waiting for transfers between devices  178 us (40%)
  Pallas kernels  96.2 us (22%)
  starting transfers between devices  60.6 us (14%)
  local copies, waits for them, and re-layouts  39.6 us (9%)
  other arithmetic  33.9 us (8%)
  between operations  14.9 us (3%)
  matrix products  11.9 us (3%)
    ppermute x24, waiting for transfers between devices, to_rank(): return lax.ppermute(values, TP, [(a, a ^ offset) for a in range(4)])  87.3 us
    ppermute x24, starting transfers between devices, to_rank(): return lax.ppermute(values, TP, [(a, a ^ offset) for a in range(4)])  34.4 us
    all_gather x1, waiting for transfers between devices, body(): totals = lax.all_gather(totals, SEQ_AXES, axis=0, tiled=False)  31.7 us
    pallas_call x1, Pallas kernels, key_grad(): pl.pallas_call(key_grad_kernel, out_shape=(jax.ShapeDtypeStruct((4, 128,...  31.3 us
    ppermute x10, waiting for transfers between devices, swap(): return lax.ppermute(values, axis, [(0, 1), (1, 0)])  22.6 us
    pallas_call x1, Pallas kernels, forward_attention(): pl.pallas_call(forward_kernel, out_shape=(jax.ShapeDtypeStruct((4, 128, 2...  20.6 us
    pallas_call x1, Pallas kernels, query_grad(): pl.pallas_call(query_grad_kernel, out_shape=(jax.ShapeDtypeStruct((4, 128...  20.1 us
    ppermute x10, starting transfers between devices, swap(): return lax.ppermute(values, axis, [(0, 1), (1, 0)])  16.6 us
  transfers between devices with their start and end apart: 46, of which 30 were waited for; matrix products, arithmetic and copies ran while one was open for 14% of the time, Pallas kernels for 19%

profile of v3, /device:TPU:1, one launch (start us, length us, event | category | flops | bytes accessed | tf_op | source)
XLA Modules:
  0.0 435.6 jit_solution(8057442943023959035)
XLA Ops:
  11.3 4.5 %collective-permute-start.3 = (f32[12,384]{1,0:T(8,128)S(1)}, f32[12,384]{1,0:T(8,128)S(1)}, u32[]{:S(2)}, u32[]{:S(2)}) collective-permute-start(f32[12,384]{1,0:T(8,128)S(1)} %concatenate.113), channel_id=1, source_target_pairs={{0,1},{1,0},{2,3},{3,2},{4,5},{5,4},{6,7},{7,6},{8,9},{9,8},{10,11... | collective-permute-start | bytes 55304 | tf_op jit(solution)/shard_map/ppermute | solution.py:438
  15.9 3.4 collective-permute-start.2
  21.0 2.7 collective-permute-done.2
  23.8 12.3 %collective-permute-done.1 = bf16[128,768]{1,0:T(8,128)(2,1)S(1)} collective-permute-done((bf16[128,768]{1,0:T(8,128)(2,1)S(1)}, bf16[128,768]{1,0:T(8,128)(2,1)S(1)}, u32[]{:S(2)}, u32[]{:S(2)}) %collective-permute-start.1) | collective-permute-done | bytes 196640 | tf_op jit(solution)/shard_map/ppermute | solution.py:442
  38.8 3.3 collective-permute-start.13
  43.1 2.9 collective-permute-start.5
  49.1 2.8 collective-permute-start.9
  53.7 6.4 %collective-permute-done.5 = bf16[192,768]{1,0:T(8,128)(2,1)} collective-permute-done((bf16[192,768]{1,0:T(8,128)(2,1)S(1)}, bf16[192,768]{1,0:T(8,128)(2,1)}, u32[]{:S(2)}, u32[]{:S(2)}) %collective-permute-start.5) | collective-permute-done | bytes 294944 | tf_op jit(solution)/shard_map/ppermute | solution.py:438
  62.2 4.2 collective-permute-done.7
  67.3 5.4 %collective-permute-done.9 = bf16[192,768]{1,0:T(8,128)(2,1)} collective-permute-done((bf16[192,768]{1,0:T(8,128)(2,1)S(1)}, bf16[192,768]{1,0:T(8,128)(2,1)}, u32[]{:S(2)}, u32[]{:S(2)}) %collective-permute-start.9) | collective-permute-done | bytes 294944 | tf_op jit(solution)/shard_map/ppermute | solution.py:438
  76.3 7.9 %all-gather.8.cloned.1.call-done.kv_ref = bf16[16,4,128,384]{3,2,1,0:T(8,128)(2,1)} async-done(((bf16[1,4,128,384]{3,2,1,0:T(8,128)(2,1)}), bf16[16,4,128,384]{3,2,1,0:T(8,128)(2,1)}) %all-gather.8.cloned.1.call-update) | async-done | bytes 6291472 | tf_op jit(solution)/shard_map/all_gather | solution.py:591
  89.9 20.6 %attention_forward.1 = (bf16[4,128,256]{2,1,0:T(8,128)(2,1)}, f32[4,384,128]{2,1,0:T(8,128)}) custom-call(s32[2]{0:T(128)} %pad_add_fusion.pos_ref, bf16[4,128,256]{2,1,0:T(8,128)(2,1)} %bitcast.213, bf16[16,4,128,384]{3,2,1,0:T(8,128)(2,1)} %all-gather.8.cloned.1.call-done.kv_ref), custom_call_target="tpu_custom_call" | custom-call | flops 3221225472 | bytes 8388608 | tf_op jit(solution)/shard_map/attention_forward/pallas_call | solution.py:125
  110.6 3.7 collective-permute-start.16
  119.0 8.1 %collective-permute-done.16 = bf16[4,128,256]{2,1,0:T(8,128)(2,1)} collective-permute-done((bf16[4,128,256]{2,1,0:T(8,128)(2,1)}, bf16[4,128,256]{2,1,0:T(8,128)(2,1)}, u32[]{:S(2)}, u32[]{:S(2)}) %collective-permute-start.16) | collective-permute-done | bytes 262176 | tf_op jit(solution)/shard_map/ppermute | solution.py:442
  128.9 4.1 collective-permute-done.14
  141.2 2.5 collective-permute-start.19
  144.6 2.2 fusion.54
  146.8 4.5 %collective-permute-done.17 = f32[128,768]{1,0:T(8,128)S(1)} collective-permute-done((f32[128,768]{1,0:T(8,128)S(1)}, f32[128,768]{1,0:T(8,128)S(1)}, u32[]{:S(2)}, u32[]{:S(2)}) %collective-permute-start.17) | collective-permute-done | bytes 393248 | tf_op jit(solution)/shard_map/ppermute | solution.py:442
  151.3 9.4 %collective-permute-done.19 = f32[128,768]{1,0:T(8,128)S(1)} collective-permute-done((f32[128,768]{1,0:T(8,128)S(1)}, f32[128,768]{1,0:T(8,128)S(1)}, u32[]{:S(2)}, u32[]{:S(2)}) %collective-permute-start.19) | collective-permute-done | bytes 393248 | tf_op jit(solution)/shard_map/ppermute | solution.py:442
  162.4 2.9 collective-permute-start.20
  168.8 3.0 collective-permute-done.20
  172.8 3.3 attention_grad_rows.1
  179.3 2.6 copy.35
  181.9 20.1 %attention_query_grad.1 = (bf16[4,128,256]{2,1,0:T(8,128)(2,1)}, f32[1,256]{1,0:T(1,128)}) custom-call(s32[2]{0:T(128)} %pad_add_fusion.pos_ref, bf16[4,128,256]{2,1,0:T(8,128)(2,1)} %bitcast.214, bf16[4,128,256]{2,1,0:T(8,128)(2,1)} %get-tuple-element.100.do_ref, f32[4,384,128]{2,1,0:T(8,128)} %get-tuple-element.90.lse_ref, ...), custom_call_target="tpu_custom_call" | custom-call | flops 4831838208 | bytes 8388608 | tf_op jit(solution)/shard_map/attention_query_grad/pallas_call | solution.py:228
  205.4 3.3 fusion.90
  208.6 5.5 %maximum_maximum_fusion = f32[16,112,768]{2,1,0:T(8,128)} fusion(f32[16,1,768]{2,1,0:T(1,128)S(1)} %broadcast_in_dim.34, f32[16,12,768]{2,1,0:T(8,128)S(1)} %reshape.335, f32[16,96,768]{2,1,0:T(8,128)} %bitcast.179, f32[112]{0:T(128)S(1)} %pad.18.clone), kind=kLoop, calls=%fused_computation | loop fusion | flops 4128768 | bytes 10863040 | tf_op jit(solution)/shard_map/concatenate | solution.py:670
  214.1 2.9 all-gather.12.cloned.1.call-done
  219.3 31.3 %attention_key_grad.1 = (bf16[4,128,384]{2,1,0:T(8,128)(2,1)}, f32[1,384]{1,0:T(1,128)}) custom-call(s32[2]{0:T(128)} %pad_add_fusion.pos_ref, bf16[4,128,384]{2,1,0:T(8,128)(2,1)} %bitcast.207, bf16[16,4,128,256]{3,2,1,0:T(8,128)(2,1)} %bitcast.228, bf16[16,4,128,256]{3,2,1,0:T(8,128)(2,1)} %bitcast.229), custom_call_target="tpu_custom_call" | custom-call | flops 6442450944 | bytes 10485760 | tf_op jit(solution)/shard_map/attention_key_grad/pallas_call | solution.py:317
  250.6 6.0 %first_grads.1 = (f32[2,8,56,640]{3,2,1,0:T(8,128)}, f32[4,128,768]{2,1,0:T(8,128)}) custom-call(bf16[768,512]{1,0:T(8,128)(2,1)} %copy.36.norm_ref, f32[512,768]{1,0:T(8,128)} %get-tuple-element.175.hat_ref, bf16[4,128,256]{2,1,0:T(8,128)(2,1)} %get-tuple-element.104.q_ref, bf16[4,128,384]{2,1,0:T(8,128)(2,1)} %get-tuple-element.106.kv_ref, ...), custom_call_target="tpu_custom_call" | custom-call | tf_op jit(solution)/shard_map/first_grads/pallas_call | solution.py:373
  258.3 2.5 collective-permute-done.23
  268.6 4.1 collective-permute-done.30
  274.4 2.9 collective-permute-start.24
  277.3 4.1 collective-permute-done.27
  281.4 3.9 collective-permute-done.26
  285.4 12.2 %reduce-scatter.2.cloned.1.call-done = f32[1,112,768]{2,1,0:T(8,128)} async-done(((f32[16,112,768]{2,1,0:T(8,128)}), f32[1,112,768]{2,1,0:T(8,128)}) %reduce-scatter.2.cloned.1.call-update) | async-done | bytes 344080 | tf_op jit(solution)/shard_map/reduce_scatter | solution.py:683
  299.4 3.2 collective-permute-start.31
  302.6 4.1 collective-permute-done.31
  306.8 4.0 collective-permute-start.34
  311.2 2.2 collective-permute-done.34
  321.2 2.7 collective-permute-start.40
  327.6 2.2 collective-permute-start.35
  329.9 9.0 %collective-permute-done.40 = f32[128,768]{1,0:T(8,128)} collective-permute-done((f32[128,768]{1,0:T(8,128)}, f32[128,768]{1,0:T(8,128)}, u32[]{:S(2)}, u32[]{:S(2)}) %collective-permute-start.40) | collective-permute-done | bytes 393248 | tf_op jit(solution)/shard_map/ppermute | solution.py:442
  338.9 2.1 fusion.45
  341.0 15.0 %collective-permute-done.37 = f32[128,768]{1,0:T(8,128)} collective-permute-done((f32[128,768]{1,0:T(8,128)}, f32[128,768]{1,0:T(8,128)}, u32[]{:S(2)}, u32[]{:S(2)}) %collective-permute-start.37) | collective-permute-done | bytes 393248 | tf_op jit(solution)/shard_map/ppermute | solution.py:442
  356.0 10.4 %collective-permute-done.35 = f32[128,768]{1,0:T(8,128)} collective-permute-done((f32[128,768]{1,0:T(8,128)}, f32[128,768]{1,0:T(8,128)}, u32[]{:S(2)}, u32[]{:S(2)}) %collective-permute-start.35) | collective-permute-done | bytes 393248 | tf_op jit(solution)/shard_map/ppermute | solution.py:442
  368.9 31.7 %all-gather.14.cloned.1.call-done = bf16[64,96,768]{2,1,0:T(8,128)(2,1)} async-done(((bf16[4,96,768]{2,1,0:T(8,128)(2,1)}), bf16[64,96,768]{2,1,0:T(8,128)(2,1)}) %all-gather.14.cloned.1.call-update) | async-done | bytes 9437200 | tf_op jit(solution)/shard_map/all_gather | solution.py:713
  400.6 15.0 %unpack_grads.1 = (f32[4,8,48,768]{3,2,1,0:T(8,128)}, f32[8,48,3072]{2,1,0:T(8,128)}, f32[16,24,2304]{2,1,0:T(8,128)}, f32[16,4,24,768]{3,2,1,0:T(8,128)}) custom-call(s32[1]{0:T(128)} %bitcast.23.pos_ref, bf16[16,4,96,768]{3,2,1,0:T(8,128)(2,1)} %bitcast.181), custom_call_target="tpu_custom_call" | custom-call | tf_op jit(solution)/shard_map/unpack_grads/pallas_call | solution.py:413
  417.6 2.2 slice.281
  (313 shorter events, 95.4 us)
Async XLA Ops:
  7.3 76.9 %all-gather.8.cloned.1.call-start = ((), (), s32[]{:S(2)}) async-start(), calls=%async_computation.1 | async-start | bytes 6684672 | tf_op jit(solution)/shard_map/all_gather | solution.py:591
  11.3 8.7 %collective-permute-start.3 = (f32[12,384]{1,0:T(8,128)S(1)}, f32[12,384]{1,0:T(8,128)S(1)}, u32[]{:S(2)}, u32[]{:S(2)}) collective-permute-start(f32[12,384]{1,0:T(8,128)S(1)} %concatenate.113), channel_id=1, source_target_pairs={{0,1},{1,0},{2,3},{3,2},{4,5},{5,4},{6,7},{7,6},{8,9},{9,8},{10,11... | collective-permute-start | bytes 55304 | tf_op jit(solution)/shard_map/ppermute | solution.py:438
  15.8 20.9 %collective-permute-start.4 = (bf16[384,640]{1,0:T(8,128)(2,1)S(1)}, bf16[384,640]{1,0:T(8,128)(2,1)S(1)}, u32[]{:S(2)}, u32[]{:S(2)}) collective-permute-start(bf16[384,640]{1,0:T(8,128)(2,1)S(1)} %concatenate.111), channel_id=1, source_target_pairs={{0,1},{1,0},{2,3},{3,2},{4,5},{5,4},{6,7},{7,6},{8,9},{9,8},{10,11... | collective-permute-start | bytes 1474568 | tf_op jit(solution)/shard_map/ppermute | solution.py:438
  15.9 7.9 %collective-permute-start.2 = (bf16[128,768]{1,0:T(8,128)(2,1)S(1)}, bf16[128,768]{1,0:T(8,128)(2,1)S(1)}, u32[]{:S(2)}, u32[]{:S(2)}) collective-permute-start(bf16[128,768]{1,0:T(8,128)(2,1)S(1)} %bitcast.198), channel_id=1, source_target_pairs={{0,96},{32,64},{64,32},{96,0},{1,97},{33,65},{65,33},{97,1},{2,98}... | collective-permute-start | bytes 589832 | tf_op jit(solution)/shard_map/ppermute | solution.py:442
  19.3 16.8 %collective-permute-start.1 = (bf16[128,768]{1,0:T(8,128)(2,1)S(1)}, bf16[128,768]{1,0:T(8,128)(2,1)S(1)}, u32[]{:S(2)}, u32[]{:S(2)}) collective-permute-start(bf16[128,768]{1,0:T(8,128)(2,1)S(1)} %bitcast.199), channel_id=1, source_target_pairs={{0,64},{32,96},{64,0},{96,32},{1,65},{33,97},{65,1},{97,33},{2,66}... | collective-permute-start | bytes 589832 | tf_op jit(solution)/shard_map/ppermute | solution.py:442
  19.8 16.3 %collective-permute-start = (bf16[128,768]{1,0:T(8,128)(2,1)S(1)}, bf16[128,768]{1,0:T(8,128)(2,1)S(1)}, u32[]{:S(2)}, u32[]{:S(2)}) collective-permute-start(bf16[128,768]{1,0:T(8,128)(2,1)S(1)} %bitcast.200), channel_id=1, source_target_pairs={{0,32},{32,0},{64,96},{96,64},{1,33},{33,1},{65,97},{97,65},{2,34}... | collective-permute-start | bytes 589832 | tf_op jit(solution)/shard_map/ppermute | solution.py:442
  38.8 137.4 %all-gather.10.cloned.1.call-start = ((), (), s32[]{:S(2)}) async-start(), calls=%async_computation.3 | async-start | bytes 4456448 | tf_op jit(solution)/shard_map/all_gather | solution.py:592
  38.8 10.3 %collective-permute-start.13 = (bf16[128,768]{1,0:T(8,128)(2,1)S(1)}, bf16[128,768]{1,0:T(8,128)(2,1)S(1)}, u32[]{:S(2)}, u32[]{:S(2)}) collective-permute-start(bf16[128,768]{1,0:T(8,128)(2,1)S(1)} %bitcast.194), channel_id=1, source_target_pairs={{0,96},{32,64},{64,32},{96,0},{1,97},{33,65},{65,33},{97,1},{2,98}... | collective-permute-start | bytes 589832 | tf_op jit(solution)/shard_map/ppermute | solution.py:442
  42.2 18.8 %collective-permute-start.12 = (bf16[128,768]{1,0:T(8,128)(2,1)S(1)}, bf16[128,768]{1,0:T(8,128)(2,1)}, u32[]{:S(2)}, u32[]{:S(2)}) collective-permute-start(bf16[128,768]{1,0:T(8,128)(2,1)S(1)} %bitcast.195), channel_id=1, source_target_pairs={{0,64},{32,96},{64,0},{96,32},{1,65},{33,97},{65,1},{97,33},{2,66}... | collective-permute-start | bytes 589832 | tf_op jit(solution)/shard_map/ppermute | solution.py:442
  42.8 18.1 %collective-permute-start.11 = (bf16[128,768]{1,0:T(8,128)(2,1)S(1)}, bf16[128,768]{1,0:T(8,128)(2,1)}, u32[]{:S(2)}, u32[]{:S(2)}) collective-permute-start(bf16[128,768]{1,0:T(8,128)(2,1)S(1)} %bitcast.196), channel_id=1, source_target_pairs={{0,32},{32,0},{64,96},{96,64},{1,33},{33,1},{65,97},{97,65},{2,34}... | collective-permute-start | bytes 589832 | tf_op jit(solution)/shard_map/ppermute | solution.py:442
  43.1 16.9 %collective-permute-start.5 = (bf16[192,768]{1,0:T(8,128)(2,1)S(1)}, bf16[192,768]{1,0:T(8,128)(2,1)}, u32[]{:S(2)}, u32[]{:S(2)}) collective-permute-start(bf16[192,768]{1,0:T(8,128)(2,1)S(1)} %constant_dynamic-slice_fusion.15), channel_id=1, source_target_pairs={{0,1},{1,0},{2,3},{3,2},{4,5},{5,4},{6,7},{7,6},{8,9},{9,8},{10,11... | collective-permute-start | bytes 884744 | tf_op jit(solution)/shard_map/ppermute | solution.py:438
  47.1 19.2 %collective-permute-start.7 = (bf16[192,768]{1,0:T(8,128)(2,1)S(1)}, bf16[192,768]{1,0:T(8,128)(2,1)}, u32[]{:S(2)}, u32[]{:S(2)}) collective-permute-start(bf16[192,768]{1,0:T(8,128)(2,1)S(1)} %fusion.60), channel_id=1, source_target_pairs={{0,1},{1,0},{2,3},{3,2},{4,5},{5,4},{6,7},{7,6},{8,9},{9,8},{10,11... | collective-permute-start | bytes 884744 | tf_op jit(solution)/shard_map/ppermute | solution.py:438
  49.1 23.6 %collective-permute-start.9 = (bf16[192,768]{1,0:T(8,128)(2,1)S(1)}, bf16[192,768]{1,0:T(8,128)(2,1)}, u32[]{:S(2)}, u32[]{:S(2)}) collective-permute-start(bf16[192,768]{1,0:T(8,128)(2,1)S(1)} %constant_dynamic-slice_fusion.8), channel_id=1, source_target_pairs={{0,1},{1,0},{2,3},{3,2},{4,5},{5,4},{6,7},{7,6},{8,9},{9,8},{10,11... | collective-permute-start | bytes 884744 | tf_op jit(solution)/shard_map/ppermute | solution.py:438
  60.0 15.0 %collective-permute-start.6 = (bf16[192,768]{1,0:T(8,128)(2,1)}, bf16[192,768]{1,0:T(8,128)(2,1)S(1)}, u32[]{:S(2)}, u32[]{:S(2)}) collective-permute-start(bf16[192,768]{1,0:T(8,128)(2,1)} %collective-permute-done.5), channel_id=1, source_target_pairs={{0,2},{2,0},{1,3},{3,1},{4,6},{6,4},{5,7},{7,5},{8,10},{10,8},{9,1... | collective-permute-start | bytes 884744 | tf_op jit(solution)/shard_map/ppermute | solution.py:438
  66.4 17.9 %collective-permute-start.8 = (bf16[192,768]{1,0:T(8,128)(2,1)}, bf16[192,768]{1,0:T(8,128)(2,1)}, u32[]{:S(2)}, u32[]{:S(2)}) collective-permute-start(bf16[192,768]{1,0:T(8,128)(2,1)} %collective-permute-done.7), channel_id=1, source_target_pairs={{0,2},{2,0},{1,3},{3,1},{4,6},{6,4},{5,7},{7,5},{8,10},{10,8},{9,1... | collective-permute-start | bytes 884744 | tf_op jit(solution)/shard_map/ppermute | solution.py:438
  72.7 13.3 %collective-permute-start.10 = (bf16[192,768]{1,0:T(8,128)(2,1)}, bf16[192,768]{1,0:T(8,128)(2,1)S(1)}, u32[]{:S(2)}, u32[]{:S(2)}) collective-permute-start(bf16[192,768]{1,0:T(8,128)(2,1)} %collective-permute-done.9), channel_id=1, source_target_pairs={{0,2},{2,0},{1,3},{3,1},{4,6},{6,4},{5,7},{7,5},{8,10},{10,8},{9,1... | collective-permute-start | bytes 884744 | tf_op jit(solution)/shard_map/ppermute | solution.py:438
  84.2 132.8 %all-gather.12.cloned.1.call-start = ((), (), s32[]{:S(2)}) async-start(), calls=%async_computation.4 | async-start | bytes 4456448 | tf_op jit(solution)/shard_map/all_gather | solution.py:643
  89.9 43.2 %copy-start.8 = (bf16[4,256,768]{2,1,0:T(8,128)(2,1)}, bf16[4,256,768]{2,1,0:T(8,128)(2,1)S(1)}, u32[]{:S(2)}) copy-start(bf16[4,256,768]{2,1,0:T(8,128)(2,1)S(1)} %pad_maximum_fusion.2) | copy-start | bytes 4718596
  110.6 16.5 %collective-permute-start.16 = (bf16[4,128,256]{2,1,0:T(8,128)(2,1)}, bf16[4,128,256]{2,1,0:T(8,128)(2,1)}, u32[]{:S(2)}, u32[]{:S(2)}) collective-permute-start(bf16[4,128,256]{2,1,0:T(8,128)(2,1)} %get-tuple-element.94.attn_ref), channel_id=1, source_target_pairs={{0,96},{32,64},{64,32},{96,0},{1,97},{33,65},{65,33},{97,1},{2,98}... | collective-permute-start | bytes 786440 | tf_op jit(solution)/shard_map/ppermute | solution.py:442
  117.4 11.5 %collective-permute-start.15 = (bf16[4,128,256]{2,1,0:T(8,128)(2,1)}, bf16[4,128,256]{2,1,0:T(8,128)(2,1)S(1)}, u32[]{:S(2)}, u32[]{:S(2)}) collective-permute-start(bf16[4,128,256]{2,1,0:T(8,128)(2,1)} %get-tuple-element.94.attn_ref), channel_id=1, source_target_pairs={{0,64},{32,96},{64,0},{96,32},{1,65},{33,97},{65,1},{97,33},{2,66}... | collective-permute-start | bytes 786440 | tf_op jit(solution)/shard_map/ppermute | solution.py:442
  117.7 15.4 %collective-permute-start.14 = (bf16[4,128,256]{2,1,0:T(8,128)(2,1)}, bf16[4,128,256]{2,1,0:T(8,128)(2,1)S(1)}, u32[]{:S(2)}, u32[]{:S(2)}) collective-permute-start(bf16[4,128,256]{2,1,0:T(8,128)(2,1)} %get-tuple-element.94.attn_ref), channel_id=1, source_target_pairs={{0,32},{32,0},{64,96},{96,64},{1,33},{33,1},{65,97},{97,65},{2,34}... | collective-permute-start | bytes 786440 | tf_op jit(solution)/shard_map/ppermute | solution.py:442
  139.5 11.8 %collective-permute-start.17 = (f32[128,768]{1,0:T(8,128)S(1)}, f32[128,768]{1,0:T(8,128)S(1)}, u32[]{:S(2)}, u32[]{:S(2)}) collective-permute-start(f32[128,768]{1,0:T(8,128)S(1)} %get-tuple-element.157), channel_id=1, source_target_pairs={{0,32},{32,0},{64,96},{96,64},{1,33},{33,1},{65,97},{97,65},{2,34}... | collective-permute-start | bytes 1179656 | tf_op jit(solution)/shard_map/ppermute | solution.py:442
  140.1 11.2 %collective-permute-start.18 = (f32[128,768]{1,0:T(8,128)S(1)}, f32[128,768]{1,0:T(8,128)S(1)}, u32[]{:S(2)}, u32[]{:S(2)}) collective-permute-start(f32[128,768]{1,0:T(8,128)S(1)} %get-tuple-element.156), channel_id=1, source_target_pairs={{0,64},{32,96},{64,0},{96,32},{1,65},{33,97},{65,1},{97,33},{2,66}... | collective-permute-start | bytes 1179656 | tf_op jit(solution)/shard_map/ppermute | solution.py:442
  141.2 19.5 %collective-permute-start.19 = (f32[128,768]{1,0:T(8,128)S(1)}, f32[128,768]{1,0:T(8,128)S(1)}, u32[]{:S(2)}, u32[]{:S(2)}) collective-permute-start(f32[128,768]{1,0:T(8,128)S(1)} %get-tuple-element.155), channel_id=1, source_target_pairs={{0,96},{32,64},{64,32},{96,0},{1,97},{33,65},{65,33},{97,1},{2,98}... | collective-permute-start | bytes 1179656 | tf_op jit(solution)/shard_map/ppermute | solution.py:442
  161.1 7.6 %collective-permute-start.22 = (bf16[128,768]{1,0:T(8,128)(2,1)S(1)}, bf16[128,768]{1,0:T(8,128)(2,1)S(1)}, u32[]{:S(2)}, u32[]{:S(2)}) collective-permute-start(bf16[128,768]{1,0:T(8,128)(2,1)S(1)} %get-tuple-element.140), channel_id=1, source_target_pairs={{0,96},{32,64},{64,32},{96,0},{1,97},{33,65},{65,33},{97,1},{2,98}... | collective-permute-start | bytes 589832 | tf_op jit(solution)/shard_map/ppermute | solution.py:442
  161.6 7.3 %collective-permute-start.21 = (bf16[128,768]{1,0:T(8,128)(2,1)S(1)}, bf16[128,768]{1,0:T(8,128)(2,1)S(1)}, u32[]{:S(2)}, u32[]{:S(2)}) collective-permute-start(bf16[128,768]{1,0:T(8,128)(2,1)S(1)} %get-tuple-element.140), channel_id=1, source_target_pairs={{0,64},{32,96},{64,0},{96,32},{1,65},{33,97},{65,1},{97,33},{2,66}... | collective-permute-start | bytes 589832 | tf_op jit(solution)/shard_map/ppermute | solution.py:442
  162.4 9.4 %collective-permute-start.20 = (bf16[128,768]{1,0:T(8,128)(2,1)S(1)}, bf16[128,768]{1,0:T(8,128)(2,1)S(1)}, u32[]{:S(2)}, u32[]{:S(2)}) collective-permute-start(bf16[128,768]{1,0:T(8,128)(2,1)S(1)} %get-tuple-element.140), channel_id=1, source_target_pairs={{0,32},{32,0},{64,96},{96,64},{1,33},{33,1},{65,97},{97,65},{2,34}... | collective-permute-start | bytes 589832 | tf_op jit(solution)/shard_map/ppermute | solution.py:442
  176.2 121.4 %reduce-scatter.2.cloned.1.call-start = ((), (), s32[]{:S(2)}) async-start(), calls=%async_computation.2 | async-start | bytes 5849088 | tf_op jit(solution)/shard_map/reduce_scatter | solution.py:683
  217.1 183.5 %all-gather.14.cloned.1.call-start = ((), (), s32[]{:S(2)}) async-start(), calls=%async_computation.5 | async-start | bytes 10027008 | tf_op jit(solution)/shard_map/all_gather | solution.py:713
  258.0 2.9 collective-permute-start.23
  262.3 10.4 %collective-permute-start.30 = (f32[56,640]{1,0:T(8,128)S(1)}, f32[56,640]{1,0:T(8,128)S(1)}, u32[]{:S(2)}, u32[]{:S(2)}) collective-permute-start(f32[56,640]{1,0:T(8,128)S(1)} %get-tuple-element.167), channel_id=1, source_target_pairs={{0,28},{4,24},{8,20},{12,16},{16,12},{20,8},{24,4},{28,0},{1,29},{... | collective-permute-start | bytes 430088 | tf_op jit(solution)/shard_map/ppermute | solution.py:511
  264.4 9.9 %collective-permute-start.29 = (f32[56,640]{1,0:T(8,128)S(1)}, f32[56,640]{1,0:T(8,128)S(1)}, u32[]{:S(2)}, u32[]{:S(2)}) collective-permute-start(f32[56,640]{1,0:T(8,128)S(1)} %get-tuple-element.168), channel_id=1, source_target_pairs={{0,24},{4,28},{8,16},{12,20},{16,8},{20,12},{24,0},{28,4},{1,25},{... | collective-permute-start | bytes 430088 | tf_op jit(solution)/shard_map/ppermute | solution.py:511
  266.1 11.3 %collective-permute-start.28 = (f32[56,640]{1,0:T(8,128)S(1)}, f32[56,640]{1,0:T(8,128)S(1)}, u32[]{:S(2)}, u32[]{:S(2)}) collective-permute-start(f32[56,640]{1,0:T(8,128)S(1)} %get-tuple-element.169), channel_id=1, source_target_pairs={{0,20},{4,16},{8,28},{12,24},{16,4},{20,0},{24,12},{28,8},{1,21},{... | collective-permute-start | bytes 430088 | tf_op jit(solution)/shard_map/ppermute | solution.py:511
  266.1 15.3 %collective-permute-start.27 = (f32[56,640]{1,0:T(8,128)S(1)}, f32[56,640]{1,0:T(8,128)S(1)}, u32[]{:S(2)}, u32[]{:S(2)}) collective-permute-start(f32[56,640]{1,0:T(8,128)S(1)} %get-tuple-element.170), channel_id=1, source_target_pairs={{0,16},{4,20},{8,24},{12,28},{16,0},{20,4},{24,8},{28,12},{1,17},{... | collective-permute-start | bytes 430088 | tf_op jit(solution)/shard_map/ppermute | solution.py:511
  267.8 17.5 %collective-permute-start.26 = (f32[56,640]{1,0:T(8,128)S(1)}, f32[56,640]{1,0:T(8,128)S(1)}, u32[]{:S(2)}, u32[]{:S(2)}) collective-permute-start(f32[56,640]{1,0:T(8,128)S(1)} %get-tuple-element.171), channel_id=1, source_target_pairs={{0,12},{4,8},{8,4},{12,0},{16,28},{20,24},{24,20},{28,16},{1,13},{... | collective-permute-start | bytes 430088 | tf_op jit(solution)/shard_map/ppermute | solution.py:511
  272.7 12.6 %collective-permute-start.25 = (f32[56,640]{1,0:T(8,128)S(1)}, f32[56,640]{1,0:T(8,128)S(1)}, u32[]{:S(2)}, u32[]{:S(2)}) collective-permute-start(f32[56,640]{1,0:T(8,128)S(1)} %get-tuple-element.172), channel_id=1, source_target_pairs={{0,8},{4,12},{8,0},{12,4},{16,24},{20,28},{24,16},{28,20},{1,9},{5... | collective-permute-start | bytes 430088 | tf_op jit(solution)/shard_map/ppermute | solution.py:511
  274.4 10.9 %collective-permute-start.24 = (f32[56,640]{1,0:T(8,128)S(1)}, f32[56,640]{1,0:T(8,128)S(1)}, u32[]{:S(2)}, u32[]{:S(2)}) collective-permute-start(f32[56,640]{1,0:T(8,128)S(1)} %get-tuple-element.166), channel_id=1, source_target_pairs={{0,4},{4,0},{8,12},{12,8},{16,20},{20,16},{24,28},{28,24},{1,5},{5... | collective-permute-start | bytes 430088 | tf_op jit(solution)/shard_map/ppermute | solution.py:511
  299.4 7.3 %collective-permute-start.31 = (f32[96,768]{1,0:T(8,128)S(1)}, f32[96,768]{1,0:T(8,128)S(1)}, u32[]{:S(2)}, u32[]{:S(2)}) collective-permute-start(f32[96,768]{1,0:T(8,128)S(1)} %pad_maximum_fusion.18), channel_id=1, source_target_pairs={{0,1},{1,0},{2,3},{3,2},{4,5},{5,4},{6,7},{7,6},{8,9},{9,8},{10,11... | collective-permute-start | bytes 884744 | tf_op jit(solution)/shard_map/ppermute | solution.py:438
  306.8 6.6 %collective-permute-start.34 = (bf16[96,768]{1,0:T(8,128)(2,1)S(1)}, bf16[96,768]{1,0:T(8,128)(2,1)S(1)}, u32[]{:S(2)}, u32[]{:S(2)}) collective-permute-start(bf16[96,768]{1,0:T(8,128)(2,1)S(1)} %fusion.59), channel_id=1, source_target_pairs={{0,96},{32,64},{64,32},{96,0},{1,97},{33,65},{65,33},{97,1},{2,98}... | collective-permute-start | bytes 442376 | tf_op jit(solution)/shard_map/ppermute | solution.py:442
  310.8 4.1 collective-permute-start.33
  311.0 5.8 %collective-permute-start.32 = (bf16[96,768]{1,0:T(8,128)(2,1)S(1)}, bf16[96,768]{1,0:T(8,128)(2,1)S(1)}, u32[]{:S(2)}, u32[]{:S(2)}) collective-permute-start(bf16[96,768]{1,0:T(8,128)(2,1)S(1)} %fusion.59), channel_id=1, source_target_pairs={{0,32},{32,0},{64,96},{96,64},{1,33},{33,1},{65,97},{97,65},{2,34}... | collective-permute-start | bytes 442376 | tf_op jit(solution)/shard_map/ppermute | solution.py:442
  318.7 8.1 %collective-permute-start.38 = (f32[128,768]{1,0:T(8,128)S(1)}, f32[128,768]{1,0:T(8,128)S(1)}, u32[]{:S(2)}, u32[]{:S(2)}) collective-permute-start(f32[128,768]{1,0:T(8,128)S(1)} %get-tuple-element.151), channel_id=1, source_target_pairs={{0,32},{32,0},{64,96},{96,64},{1,33},{33,1},{65,97},{97,65},{2,34}... | collective-permute-start | bytes 1179656 | tf_op jit(solution)/shard_map/ppermute | solution.py:442
  319.8 10.0 %collective-permute-start.39 = (f32[128,768]{1,0:T(8,128)}, f32[128,768]{1,0:T(8,128)}, u32[]{:S(2)}, u32[]{:S(2)}) collective-permute-start(f32[128,768]{1,0:T(8,128)} %get-tuple-element.150), channel_id=1, source_target_pairs={{0,64},{32,96},{64,0},{96,32},{1,65},{33,97},{65,1},{97,33},{2,66}... | collective-permute-start | bytes 1179656 | tf_op jit(solution)/shard_map/ppermute | solution.py:442
  321.2 17.7 %collective-permute-start.40 = (f32[128,768]{1,0:T(8,128)}, f32[128,768]{1,0:T(8,128)}, u32[]{:S(2)}, u32[]{:S(2)}) collective-permute-start(f32[128,768]{1,0:T(8,128)} %get-tuple-element.149), channel_id=1, source_target_pairs={{0,96},{32,64},{64,32},{96,0},{1,97},{33,65},{65,33},{97,1},{2,98}... | collective-permute-start | bytes 1179656 | tf_op jit(solution)/shard_map/ppermute | solution.py:442
  324.9 41.5 %copy-start.3 = (f32[512,768]{1,0:T(8,128)S(1)}, f32[512,768]{1,0:T(8,128)}, u32[]{:S(2)}) copy-start(f32[512,768]{1,0:T(8,128)} %get-tuple-element.175.hat_ref) | copy-start | bytes 4718596
  324.9 31.1 %collective-permute-start.37 = (f32[128,768]{1,0:T(8,128)}, f32[128,768]{1,0:T(8,128)}, u32[]{:S(2)}, u32[]{:S(2)}) collective-permute-start(f32[128,768]{1,0:T(8,128)} %get-tuple-element.153), channel_id=1, source_target_pairs={{0,96},{32,64},{64,32},{96,0},{1,97},{33,65},{65,33},{97,1},{2,98}... | collective-permute-start | bytes 1179656 | tf_op jit(solution)/shard_map/ppermute | solution.py:442
  326.1 29.9 %collective-permute-start.36 = (f32[128,768]{1,0:T(8,128)}, f32[128,768]{1,0:T(8,128)}, u32[]{:S(2)}, u32[]{:S(2)}) collective-permute-start(f32[128,768]{1,0:T(8,128)} %get-tuple-element.154), channel_id=1, source_target_pairs={{0,64},{32,96},{64,0},{96,32},{1,65},{33,97},{65,1},{97,33},{2,66}... | collective-permute-start | bytes 1179656 | tf_op jit(solution)/shard_map/ppermute | solution.py:442
  327.6 38.8 %collective-permute-start.35 = (f32[128,768]{1,0:T(8,128)}, f32[128,768]{1,0:T(8,128)}, u32[]{:S(2)}, u32[]{:S(2)}) collective-permute-start(f32[128,768]{1,0:T(8,128)} %get-tuple-element.152), channel_id=1, source_target_pairs={{0,32},{32,0},{64,96},{96,64},{1,33},{33,1},{65,97},{97,65},{2,34}... | collective-permute-start | bytes 1179656 | tf_op jit(solution)/shard_map/ppermute | solution.py:442
  (47 other events, 479.9 us)
Sparse Core Ops, SparseCore 0:
  38.9 45.2 all-gather.7
  85.9 41.4 all-gather.9
  176.3 40.7 all-gather.11
  219.3 78.1 reduce-scatter.1
  317.9 82.6 all-gather.13

commit v4 on v3

--- a/solution.py
+++ b/solution.py
@@ -336,7 +336,7 @@
 
 
 def first_grads_kernel(
-    norm_ref, hat_ref, q_ref, kv_ref, w_ref, q_sum_ref, kv_sum_ref, local_ref, dh_ref
+    norm_ref, hat_ref, q_ref, kv_ref, w_ref, q_sum_ref, kv_sum_ref, local_ref, own_ref, other_ref
 ):
     cols = jnp.concatenate([q_ref[...].reshape(512, 256), kv_ref[...].reshape(512, 384)], axis=1)
     for half in range(2):
@@ -352,7 +352,10 @@
     for k in range(4):
         rows = slice(128 * k, 128 * k + 128)
         part = lax.dot_general(cols[rows], w_ref[...], NT, preferred_element_type=F32)
-        dh_ref[k] = part
+        if k == 0:
+            own_ref[...] = part
+        else:
+            other_ref[k - 1] = part.astype(BF16)
         gain = gain + jnp.sum(part * hat_ref[rows], axis=0, keepdims=True)
         shift = shift + jnp.sum(part, axis=0, keepdims=True)
     extra = (
@@ -374,16 +377,17 @@
         first_grads_kernel,
         out_shape=(
             jax.ShapeDtypeStruct((2, 8, 56, 640), F32),
-            jax.ShapeDtypeStruct((4, 128, 768), F32),
+            jax.ShapeDtypeStruct((128, 768), F32),
+            jax.ShapeDtypeStruct((3, 128, 768), BF16),
         ),
         in_specs=[vmem_spec()] * 7,
-        out_specs=(vmem_spec(), vmem_spec()),
+        out_specs=(vmem_spec(), vmem_spec(), vmem_spec()),
         compiler_params=pltpu.CompilerParams(vmem_limit_bytes=VMEM_LIMIT),
         name="first_grads",
     )(norm_t, hat, dq, dkv, w_cols, q_sum, kv_sum)
 
 
-def unpack_kernel(pos_ref, in_ref, out_w_ref, fc_w_ref, qkv_ref, extra_ref):
+def unpack_kernel(pos_ref, in_ref, out_w_ref, fc_w_ref, qkv_ref, proj_ref, sum_ref):
     step = pl.program_id(0)
     rank = pos_ref[0]
 
@@ -405,12 +409,24 @@
     qkv_ref[0, :, 1536:] = jnp.concatenate(
         [part for r in rows for part in (r[:24, 512:640], r[:24, 448:512])], axis=1
     )
-    for g in range(4):
-        extra_ref[0, g] = rows[g][24:]
+    for g in range(2):
+        proj_ref[g, 0] = in_ref[0, rank ^ (2 * pos_ref[1] + g), 80:].astype(F32)[:12]
+    first = [r[24:25] for r in rows]
+    second = [r[44:45] for r in rows]
+    sum_ref[0] = jnp.concatenate(
+        [
+            (first[0] + first[1]) + (first[2] + first[3]),
+            (second[0] + second[1]) + (second[2] + second[3]),
+            jnp.zeros((6, 768), F32),
+        ]
+        + first
+        + second,
+        axis=0,
+    )
 
 
 def unpack(pos, totals):
-    out_w, fc_w, qkv_w, extra = pl.pallas_call(
+    out_w, fc_w, qkv_w, proj_w, sums = pl.pallas_call(
         unpack_kernel,
         grid_spec=pltpu.PrefetchScalarGridSpec(
             num_scalar_prefetch=1,
@@ -420,18 +436,26 @@
                 pl.BlockSpec((4, 1, 48, 768), lambda s, pos: (0, jnp.minimum(s, 7), 0, 0)),
                 pl.BlockSpec((1, 48, 3072), lambda s, pos: (jnp.maximum(s - 8, 0), 0, 0)),
                 pl.BlockSpec((1, 24, 2304), lambda s, pos: (s, 0, 0)),
-                pl.BlockSpec((1, 4, 24, 768), lambda s, pos: (s, 0, 0, 0)),
+                pl.BlockSpec((2, 1, 12, 768), lambda s, pos: (0, s, 0, 0)),
+                pl.BlockSpec((1, 16, 768), lambda s, pos: (s, 0, 0)),
             ),
         ),
         out_shape=(
             jax.ShapeDtypeStruct((4, 8, 48, 768), F32),
             jax.ShapeDtypeStruct((8, 48, 3072), F32),
             jax.ShapeDtypeStruct((16, 24, 2304), F32),
-            jax.ShapeDtypeStruct((16, 4, 24, 768), F32),
+            jax.ShapeDtypeStruct((2, 16, 12, 768), F32),
+            jax.ShapeDtypeStruct((16, 16, 768), F32),
         ),
         name="unpack_grads",
     )(pos, totals)
-    return out_w.reshape(1536, 768), fc_w.reshape(384, 3072), qkv_w.reshape(384, 2304), extra
+    return (
+        out_w.reshape(1536, 768),
+        fc_w.reshape(384, 3072),
+        qkv_w.reshape(384, 2304),
+        proj_w.reshape(384, 768),
+        sums,
+    )
 
 
 def swap(values, axis):
@@ -444,13 +468,6 @@
 
 def gather_ranks(values):
     return [values] + [to_rank(values, r) for r in (1, 2, 3)]
-
-
-def sum_ranks(partial):
-    total = partial[0]
-    for r in (1, 2, 3):
-        total = total + to_rank(partial[r], r)
-    return total
 
 
 def pick(values, index, axis=0):
@@ -490,11 +507,16 @@
     return jnp.stack([first, second])
 
 
-def both_shards_by_core(own, fs):
+def fetch_by_core(own):
     core = lax.axis_index("core")
     half = own.shape[0] // 2
     part = swap(lax.dynamic_slice_in_dim(own, half * core, half, 0), "fsdp")
-    other = swap(part, "core")
+    return (part, swap(part, "core"))
+
+
+def join_shards(own, fetched, fs):
+    core = lax.axis_index("core")
+    part, other = fetched
     peer = jnp.concatenate(
         [jnp.where(core == 0, part, other), jnp.where(core == 0, other, part)], axis=0
     )
@@ -566,11 +588,6 @@
     qkv_bias = jnp.concatenate(
         [q_own, jnp.zeros((64 + 192,), F32), v_own[128:], v_own[:128]], axis=0
     )
-    proj_rows = both_shards_by_core(w_proj, fs).reshape(4, 3, 64, 768)
-    proj_rows = jnp.concatenate(
-        [proj_rows[:, :2], jnp.zeros((4, 1, 64, 768), BF16), proj_rows[:, 2:]], axis=1
-    ).reshape(4, 256, 768)
-    proj_ranks = jnp.stack([pick(proj_rows, rank ^ r) for r in range(4)])
     fc_shard = jnp.concatenate(
         [
             lax.dynamic_slice_in_dim(w_fc, 384 * rank, 384, 1),
@@ -578,9 +595,8 @@
         ],
         axis=1,
     )
-    fc_cols = both_shards_by_core(fc_shard, fs).reshape(768, 768)
     out_shard = lax.dynamic_slice_in_dim(w_out, 384 * rank, 384, 0)
-    out_rows = both_shards_by_core(out_shard, fs).reshape(768, 768)
+    fetched = (fetch_by_core(w_proj), fetch_by_core(fc_shard), fetch_by_core(out_shard))
 
     x = x_low.astype(F32)
     x_normed, x_scale = normalize(x)
@@ -591,19 +607,21 @@
     kv_all = lax.all_gather(kv_own, SEQ_AXES, axis=0, tiled=False)
     q_all = lax.all_gather(after(q_scaled, kv_all), SEQ_AXES, axis=0, tiled=False)
     normed_one_t = normed_one.T
-    kv_all, proj_ranks, fc_cols, out_rows, cot_low, normed_one_t = lax.optimization_barrier(
-        (
-            kv_all,
-            proj_ranks,
-            fc_cols,
-            out_rows,
-            jnp.concatenate(gather_ranks(out_grad[0]), axis=0),
-            normed_one_t,
-        )
+    cot_ranks = tuple(gather_ranks(out_grad[0]))
+    kv_all, fetched, cot_ranks, normed_one_t = lax.optimization_barrier(
+        (kv_all, fetched, cot_ranks, normed_one_t)
     )
     attn, lse = forward_attention(pos, q_scaled, kv_all)
 
     attn_ranks = gather_ranks(attn)
+    proj_rows = join_shards(w_proj, fetched[0], fs).reshape(4, 3, 64, 768)
+    proj_rows = jnp.concatenate(
+        [proj_rows[:, :2], jnp.zeros((4, 1, 64, 768), BF16), proj_rows[:, 2:]], axis=1
+    ).reshape(4, 256, 768)
+    proj_ranks = jnp.stack([pick(proj_rows, rank ^ r) for r in range(4)])
+    fc_cols = join_shards(fc_shard, fetched[1], fs).reshape(768, 768)
+    out_rows = join_shards(out_shard, fetched[2], fs).reshape(768, 768)
+    cot_low = jnp.concatenate(cot_ranks, axis=0)
     residual = x + proj_bias
     attn_full = jnp.concatenate(
         [
@@ -638,7 +656,16 @@
     grad_residual = (
         norm_back(grad_normed_two, r_normed[:128], r_scale[:128], gain_two) + cot_own
     )
-    grad_residual_low = jnp.concatenate(gather_ranks(grad_residual.astype(BF16)), axis=0)
+    residual_ranks = tuple(gather_ranks(grad_residual.astype(BF16)))
+    local = jnp.pad(
+        jnp.concatenate([grad_out_w, grad_fc_w], axis=1)
+        .reshape(2, 16, 48, 768)
+        .transpose(1, 0, 2, 3)
+        .reshape(16, 96, 768),
+        ((0, 0), (0, 16), (0, 0)),
+    )
+    residual_ranks, local = lax.optimization_barrier((residual_ranks, local))
+    grad_residual_low = jnp.concatenate(residual_ranks, axis=0)
     do_aug, delta = grad_rows(grad_residual_low, proj_ranks[0], attn, lse)
     do_all = lax.all_gather(after(do_aug, q_all), SEQ_AXES, axis=0, tiled=False)
     grad_q, grad_q_sum = query_grad(pos, q_scaled, do_aug, lse, delta, kv_all)
@@ -667,34 +694,26 @@
         ]
         + [jnp.zeros((768,), F32)] * 11
     )
-    local = jnp.concatenate(
-        [
-            jnp.concatenate([grad_out_w, grad_fc_w], axis=1)
-            .reshape(2, 16, 48, 768)
-            .transpose(1, 0, 2, 3)
-            .reshape(16, 96, 768),
-            grad_proj_w.reshape(16, 12, 768),
-            extra[:, None],
-            jnp.zeros((16, 3, 768), F32),
-        ],
-        axis=1,
-    )
-    local, do_all, out_partial = lax.optimization_barrier((local, do_all, out_partial))
+    shared = jnp.concatenate(
+        [grad_proj_w.reshape(16, 12, 768), extra[:, None], jnp.zeros((16, 3, 768), F32)], axis=1
+    )
+    local = lax.dynamic_update_slice(local, shared, (0, 96, 0))
+    out_low = out_partial[1:].astype(BF16)
+    out_low = (None,) + tuple(out_low)
+    local, do_all, out_low = lax.optimization_barrier((local, do_all, out_low))
     early = lax.psum_scatter(local, SEQ_AXES, scatter_dimension=0, tiled=False)
-    out_moved = [to_rank(out_partial[r], r) for r in (1, 2, 3)]
+    out_moved = tuple(to_rank(out_low[r], r) for r in (1, 2, 3))
 
     grad_kv, grad_kv_sum = key_grad(pos, kv_own, q_all, do_all)
-    out_moved = after(tuple(out_moved), grad_kv)
-    output = (
-        out_partial[0] + out_moved[0] + out_moved[1] + out_moved[2] + out_bias + residual[:128]
-    ).astype(BF16)
-
-    late_local, partial_one = first_grads(
+    grad_kv, out_moved = lax.optimization_barrier((grad_kv, out_moved))
+    late_local, partial_one, partial_low = first_grads(
         normed_one_t, x_normed, grad_q, grad_kv, w_cols, grad_q_sum, grad_kv_sum
     )
     late = reduce_by_permute(late_local)
-
-    early, late, partial_one = lax.optimization_barrier((early, late, partial_one))
+    low_one, late = lax.optimization_barrier((partial_low, late))
+    one_moved = tuple(to_rank(low_one[r - 1], r) for r in (1, 2, 3))
+
+    early, late, one_moved = lax.optimization_barrier((early, late, one_moved))
     late = jnp.concatenate([late, jnp.zeros((56, 128), F32)], axis=1)
 
     def rows_of(which):
@@ -711,44 +730,55 @@
     totals = (rows_of(fs) + swap(rows_of(1 - fs), "fsdp")).astype(BF16)
     totals = jnp.stack(gather_ranks(totals))
     totals = lax.all_gather(totals, SEQ_AXES, axis=0, tiled=False)
-    grad_normed_one = sum_ranks(partial_one)
+    output = (
+        out_partial[0]
+        + out_moved[0].astype(F32)
+        + out_moved[1].astype(F32)
+        + out_moved[2].astype(F32)
+        + out_bias
+        + residual[:128]
+    ).astype(BF16)
+    grad_normed_one = (
+        partial_one
+        + one_moved[0].astype(F32)
+        + one_moved[1].astype(F32)
+        + one_moved[2].astype(F32)
+    )
     input_grad = (
         norm_back(grad_normed_one, x_normed[:128], x_scale[:128], gain_one) + grad_residual
     )
     totals, input_grad, output = lax.optimization_barrier((totals, input_grad, output))
-    g_w_out, g_w_fc, g_w_qkv, extra = unpack(jnp.stack([rank]).astype(jnp.int32), totals)
+    g_w_out, g_w_fc, g_w_qkv, g_w_proj, sums = unpack(
+        jnp.stack([rank, fs]).astype(jnp.int32), totals
+    )
 
     def own_half(values):
-        return lax.dynamic_slice_in_dim(values, 384 * fs, 384, 0)
-
-    early = extra[:, :, 8:]
-    late_rows = extra[:4, :, 0, :640]
-    g_w_proj = lax.dynamic_slice_in_dim(early[:, :, :12], 2 * fs, 2, 1)
-    g_w_proj = g_w_proj.transpose(1, 0, 2, 3).reshape(384, 768)
-    sums = jnp.sum(early[:4, :, 12], axis=1)
-    g_b_fc = pick(early[4, :, 12].reshape(4, 2, 384), fs, 1).reshape(1536)
-    bias_row = late_rows[0]
+        return lax.dynamic_slice_in_dim(values, 384 * fs, 384, values.ndim - 1)
+
+    mlp_sums = own_half(sums[:4, 1])
+    g_b_fc = pick(sums[4, 12:].reshape(4, 2, 384), fs, 1).reshape(1536)
+    bias_row = sums[0, 8:12]
     g_q_bias = own_half(bias_row[:, :192].reshape(768))
     g_v_bias = own_half(
-        jnp.concatenate([bias_row[:, 512:], bias_row[:, 448:512]], axis=1).reshape(768)
-    )
-    ln_one = jnp.sum(late_rows[1:], axis=1).reshape(1920)
+        jnp.concatenate([bias_row[:, 512:640], bias_row[:, 448:512]], axis=1).reshape(768)
+    )
+    ln_one = own_half(sums[1:4, 0, :640].reshape(1920)[:1536].reshape(2, 768))
     return (
         output[None],
         input_grad[None],
-        own_half(ln_one[:768]),
-        own_half(ln_one[768:1536]),
+        ln_one[0],
+        ln_one[1],
         g_w_qkv,
         g_q_bias,
         g_v_bias,
         g_w_proj,
-        own_half(sums[2]),
-        own_half(sums[0]),
-        own_half(sums[1]),
+        mlp_sums[2],
+        mlp_sums[0],
+        mlp_sums[1],
         g_w_fc,
         g_b_fc,
         g_w_out,
-        own_half(sums[3]),
+        mlp_sums[3],
     )
 
 

time: 441 us -> 431 us (0.977)
  other arithmetic: 33.9 us -> 23.1 us
  starting transfers between devices: 60.6 us -> 68.1 us
    all_gather x1, waiting for transfers between devices: 31.7 us -> 54.8 us  [body(): totals = lax.all_gather(totals, SEQ_AXES, axis=0, tiled=False)]
    ppermute x10, waiting for transfers between devices: 22.6 us -> 9.48 us  [swap(): return lax.ppermute(values, axis, [(0, 1), (1, 0)])]
    reduce_scatter x1, waiting for transfers between devices: 12.2 us -> 0.01 us  [body(): early = lax.psum_scatter(local, SEQ_AXES, scatter_dimension=0, tiled=False)]
    ppermute x24, waiting for transfers between devices: 87.3 us -> 76.9 us  [to_rank(): return lax.ppermute(values, TP, [(a, a ^ offset) for a in range(4)])]
    ppermute x10, starting transfers between devices: 16.6 us -> 24.7 us  [swap(): return lax.ppermute(values, axis, [(0, 1), (1, 0)])]
    concatenate x5 -> x2, other arithmetic: 8.72 us -> 1.1 us  [the longest x1 1.09 us: join_shards(): jnp.concatenate([jnp.where(core == 0, part, other), jnp.where(core == 0,...]
    all_gather x1, waiting for transfers between devices: 2.93 us -> 8.97 us  [body(): do_all = lax.all_gather(after(do_aug, q_all), SEQ_AXES, axis=0, tiled=False)]
    unnamed x95 -> x108, local copies, waits for them, and re-layouts: 4.58 us -> 9.23 us
  transfers between devices with their start and end apart: 46 -> 46, of which waited for: 30 -> 23; matrix products, arithmetic and copies ran while one was open for 14% -> 11% of each run, Pallas kernels for 19% -> 14%
where the time goes in v4:
time: 431 us; the launch traced here: 430 us
  waiting for transfers between devices  176 us (41%)
  Pallas kernels  96 us (22%)
  starting transfers between devices  68.1 us (16%)
  local copies, waits for them, and re-layouts  42.1 us (10%)
  other arithmetic  23.1 us (5%)
  between operations  15 us (3%)
  matrix products  9.2 us (2%)
    ppermute x24, waiting for transfers between devices, to_rank(): return lax.ppermute(values, TP, [(a, a ^ offset) for a in range(4)])  76.9 us
    all_gather x1, waiting for transfers between devices, body(): totals = lax.all_gather(totals, SEQ_AXES, axis=0, tiled=False)  54.8 us
    ppermute x24, starting transfers between devices, to_rank(): return lax.ppermute(values, TP, [(a, a ^ offset) for a in range(4)])  35.5 us
    pallas_call x1, Pallas kernels, key_grad(): pl.pallas_call(key_grad_kernel, out_shape=(jax.ShapeDtypeStruct((4, 128,...  31.3 us
    ppermute x10, starting transfers between devices, swap(): return lax.ppermute(values, axis, [(0, 1), (1, 0)])  24.7 us
    pallas_call x1, Pallas kernels, query_grad(): pl.pallas_call(query_grad_kernel, out_shape=(jax.ShapeDtypeStruct((4, 128...  20.1 us
    pallas_call x1, Pallas kernels, forward_attention(): pl.pallas_call(forward_kernel, out_shape=(jax.ShapeDtypeStruct((4, 128, 2...  20 us
    pallas_call x1, Pallas kernels, unpack(): pl.pallas_call(unpack_kernel, grid_spec=pltpu.PrefetchScalarGridSpec(num_...  15.5 us
  transfers between devices with their start and end apart: 46, of which 23 were waited for; matrix products, arithmetic and copies ran while one was open for 11% of the time, Pallas kernels for 14%

profile of v4, /device:TPU:1, one launch (start us, length us, event | category | flops | bytes accessed | tf_op | source)
XLA Modules:
  0.0 429.8 jit_solution(15776646769490181027)
XLA Ops:
  11.3 4.5 %collective-permute-start.3 = (f32[12,384]{1,0:T(8,128)S(1)}, f32[12,384]{1,0:T(8,128)S(1)}, u32[]{:S(2)}, u32[]{:S(2)}) collective-permute-start(f32[12,384]{1,0:T(8,128)S(1)} %concatenate.113), channel_id=1, source_target_pairs={{0,1},{1,0},{2,3},{3,2},{4,5},{5,4},{6,7},{7,6},{8,9},{9,8},{10,11... | collective-permute-start | bytes 55304 | tf_op jit(solution)/shard_map/ppermute | solution.py:462
  15.9 3.4 collective-permute-start.2
  20.5 3.3 collective-permute-done.2
  23.8 12.3 %collective-permute-done.1 = bf16[128,768]{1,0:T(8,128)(2,1)S(1)} collective-permute-done((bf16[128,768]{1,0:T(8,128)(2,1)S(1)}, bf16[128,768]{1,0:T(8,128)(2,1)S(1)}, u32[]{:S(2)}, u32[]{:S(2)}) %collective-permute-start.1) | collective-permute-done | bytes 196640 | tf_op jit(solution)/shard_map/ppermute | solution.py:466
  39.5 2.8 collective-permute-start.5
  45.5 2.8 collective-permute-start.9
  48.3 2.7 collective-permute-start.11
  53.4 3.0 collective-permute-start.6
  56.4 2.8 collective-permute-start.8
  60.9 4.6 %collective-permute-start.10 = (bf16[192,768]{1,0:T(8,128)(2,1)}, bf16[192,768]{1,0:T(8,128)(2,1)}, u32[]{:S(2)}, u32[]{:S(2)}) collective-permute-start(bf16[192,768]{1,0:T(8,128)(2,1)} %collective-permute-done.9), channel_id=1, source_target_pairs={{0,2},{2,0},{1,3},{3,1},{4,6},{6,4},{5,7},{7,5},{8,10},{10,8},{9,1... | collective-permute-start | bytes 884744 | tf_op jit(solution)/shard_map/ppermute | solution.py:462
  65.5 1.8 fusion
  67.3 3.2 collective-permute-start.13
  71.2 9.4 %collective-permute-done.13 = bf16[128,768]{1,0:T(8,128)(2,1)S(1)} collective-permute-done((bf16[128,768]{1,0:T(8,128)(2,1)S(1)}, bf16[128,768]{1,0:T(8,128)(2,1)S(1)}, u32[]{:S(2)}, u32[]{:S(2)}) %collective-permute-start.13) | collective-permute-done | bytes 196640 | tf_op jit(solution)/shard_map/ppermute | solution.py:466
  81.4 10.8 %all-gather.8.cloned.1.call-done.kv_ref = bf16[16,4,128,384]{3,2,1,0:T(8,128)(2,1)} async-done(((bf16[1,4,128,384]{3,2,1,0:T(8,128)(2,1)}), bf16[16,4,128,384]{3,2,1,0:T(8,128)(2,1)}) %all-gather.8.cloned.1.call-update) | async-done | bytes 6291472 | tf_op jit(solution)/shard_map/all_gather | solution.py:607
  96.9 20.0 %attention_forward.1 = (bf16[4,128,256]{2,1,0:T(8,128)(2,1)}, f32[4,384,128]{2,1,0:T(8,128)}) custom-call(s32[2]{0:T(128)} %pad_add_fusion.pos_ref, bf16[4,128,256]{2,1,0:T(8,128)(2,1)} %bitcast.183, bf16[16,4,128,384]{3,2,1,0:T(8,128)(2,1)} %all-gather.8.cloned.1.call-done.kv_ref), custom_call_target="tpu_custom_call" | custom-call | flops 3221225472 | bytes 8388608 | tf_op jit(solution)/shard_map/attention_forward/pallas_call | solution.py:125
  129.7 2.0 collective-permute-done.15
  140.9 2.0 collective-permute-start.18
  145.2 14.4 %collective-permute-done.17 = f32[128,768]{1,0:T(8,128)S(1)} collective-permute-done((f32[128,768]{1,0:T(8,128)S(1)}, f32[128,768]{1,0:T(8,128)S(1)}, u32[]{:S(2)}, u32[]{:S(2)}) %collective-permute-start.17) | collective-permute-done | bytes 393248 | tf_op jit(solution)/shard_map/ppermute | solution.py:466
  159.6 17.9 %collective-permute-done.19 = f32[128,768]{1,0:T(8,128)S(1)} collective-permute-done((f32[128,768]{1,0:T(8,128)S(1)}, f32[128,768]{1,0:T(8,128)S(1)}, u32[]{:S(2)}, u32[]{:S(2)}) %collective-permute-start.19) | collective-permute-done | bytes 393248 | tf_op jit(solution)/shard_map/ppermute | solution.py:466
  178.2 4.0 collective-permute-start.22
  182.9 2.9 pad.5
  185.9 2.7 collective-permute-done.22
  189.6 3.4 attention_grad_rows.1
  195.1 20.1 %attention_query_grad.1 = (bf16[4,128,256]{2,1,0:T(8,128)(2,1)}, f32[1,256]{1,0:T(1,128)}) custom-call(s32[2]{0:T(128)} %pad_add_fusion.pos_ref, bf16[4,128,256]{2,1,0:T(8,128)(2,1)} %bitcast.185, bf16[4,128,256]{2,1,0:T(8,128)(2,1)} %get-tuple-element.131.do_ref, f32[4,384,128]{2,1,0:T(8,128)} %get-tuple-element.121.lse_ref, ...), custom_call_target="tpu_custom_call" | custom-call | flops 4831838208 | bytes 8388608 | tf_op jit(solution)/shard_map/attention_query_grad/pallas_call | solution.py:228
  219.9 1.9 fusion.85
  223.0 9.0 %all-gather.12.cloned.1.call-done = bf16[64,128,256]{2,1,0:T(8,128)(2,1)} async-done(((bf16[4,128,256]{2,1,0:T(8,128)(2,1)}), bf16[64,128,256]{2,1,0:T(8,128)(2,1)}) %all-gather.12.cloned.1.call-update) | async-done | bytes 4194320 | tf_op jit(solution)/shard_map/all_gather | solution.py:670
  234.2 2.4 collective-permute-start.23
  238.4 31.3 %attention_key_grad.1 = (bf16[4,128,384]{2,1,0:T(8,128)(2,1)}, f32[1,384]{1,0:T(1,128)}) custom-call(s32[2]{0:T(128)} %pad_add_fusion.pos_ref, bf16[4,128,384]{2,1,0:T(8,128)(2,1)} %bitcast.182, bf16[16,4,128,256]{3,2,1,0:T(8,128)(2,1)} %bitcast.197, bf16[16,4,128,256]{3,2,1,0:T(8,128)(2,1)} %bitcast.198), custom_call_target="tpu_custom_call" | custom-call | flops 6442450944 | bytes 10485760 | tf_op jit(solution)/shard_map/attention_key_grad/pallas_call | solution.py:317
  269.7 5.8 %first_grads.1 = (f32[2,8,56,640]{3,2,1,0:T(8,128)}, f32[128,768]{1,0:T(8,128)}, bf16[3,128,768]{2,1,0:T(8,128)(2,1)}) custom-call(bf16[768,512]{1,0:T(8,128)(2,1)} %copy.35.norm_ref, f32[512,768]{1,0:T(8,128)} %get-tuple-element.215.hat_ref, bf16[4,128,256]{2,1,0:T(8,128)(2,1)} %get-tuple-element.135.q_ref, bf16[4,128,384]{2,1,0:T(8,128)(2,1)} %get-tuple-element.141.kv_ref, ...), custom_call_target="tpu_custom_call" | custom-call | tf_op jit(solution)/shard_map/first_grads/pallas_call | solution.py:376
  278.0 2.4 collective-permute-done.26
  282.6 3.6 collective-permute-start.32
  287.9 3.5 collective-permute-done.33
  291.4 2.7 collective-permute-done.32
  294.1 2.0 collective-permute-start.27
  296.1 5.7 %collective-permute-done.30 = f32[56,640]{1,0:T(8,128)} collective-permute-done((f32[56,640]{1,0:T(8,128)S(1)}, f32[56,640]{1,0:T(8,128)}, u32[]{:S(2)}, u32[]{:S(2)}) %collective-permute-start.30) | collective-permute-done | bytes 143392 | tf_op jit(solution)/shard_map/ppermute | solution.py:533
  301.8 3.3 collective-permute-done.29
  306.4 2.6 collective-permute-start.34
  310.6 3.2 collective-permute-done.34
  314.3 4.2 collective-permute-done.36
  320.4 2.8 collective-permute-start.37
  323.2 5.4 %collective-permute-done.37 = f32[96,768]{1,0:T(8,128)S(1)} collective-permute-done((f32[96,768]{1,0:T(8,128)S(1)}, f32[96,768]{1,0:T(8,128)S(1)}, u32[]{:S(2)}, u32[]{:S(2)}) %collective-permute-start.37) | collective-permute-done | bytes 294944 | tf_op jit(solution)/shard_map/ppermute | solution.py:462
  328.6 3.2 collective-permute-start.40
  333.0 2.2 collective-permute-done.40
  336.7 3.1 collective-permute-done.38
  341.3 2.0 fusion.45
  344.5 54.8 %all-gather.14.cloned.1.call-done = bf16[64,96,768]{2,1,0:T(8,128)(2,1)} async-done(((bf16[4,96,768]{2,1,0:T(8,128)(2,1)}), bf16[64,96,768]{2,1,0:T(8,128)(2,1)}) %all-gather.14.cloned.1.call-update) | async-done | bytes 9437200 | tf_op jit(solution)/shard_map/all_gather | solution.py:732
  399.3 15.5 %unpack_grads.1 = (f32[4,8,48,768]{3,2,1,0:T(8,128)}, f32[8,48,3072]{2,1,0:T(8,128)}, f32[16,24,2304]{2,1,0:T(8,128)}, f32[2,16,12,768]{3,2,1,0:T(8,128)}, f32[16,16,768]{2,1,0:T(8,128)}) custom-call(s32[2]{0:T(128)} %pad_add_fusion.1.pos_ref, bf16[16,4,96,768]{3,2,1,0:T(8,128)(2,1)} %bitcast.153), custom_call_target="tpu_custom_call" | custom-call | tf_op jit(solution)/shard_map/unpack_grads/pallas_call | solution.py:429
  418.9 2.4 reshape.351
  (320 shorter events, 83.1 us)
Async XLA Ops:
  7.3 84.9 %all-gather.8.cloned.1.call-start = ((), (), s32[]{:S(2)}) async-start(), calls=%async_computation.1 | async-start | bytes 6684672 | tf_op jit(solution)/shard_map/all_gather | solution.py:607
  11.3 8.7 %collective-permute-start.3 = (f32[12,384]{1,0:T(8,128)S(1)}, f32[12,384]{1,0:T(8,128)S(1)}, u32[]{:S(2)}, u32[]{:S(2)}) collective-permute-start(f32[12,384]{1,0:T(8,128)S(1)} %concatenate.113), channel_id=1, source_target_pairs={{0,1},{1,0},{2,3},{3,2},{4,5},{5,4},{6,7},{7,6},{8,9},{9,8},{10,11... | collective-permute-start | bytes 55304 | tf_op jit(solution)/shard_map/ppermute | solution.py:462
  15.8 20.8 %collective-permute-start.4 = (bf16[384,640]{1,0:T(8,128)(2,1)S(1)}, bf16[384,640]{1,0:T(8,128)(2,1)S(1)}, u32[]{:S(2)}, u32[]{:S(2)}) collective-permute-start(bf16[384,640]{1,0:T(8,128)(2,1)S(1)} %concatenate.111), channel_id=1, source_target_pairs={{0,1},{1,0},{2,3},{3,2},{4,5},{5,4},{6,7},{7,6},{8,9},{9,8},{10,11... | collective-permute-start | bytes 1474568 | tf_op jit(solution)/shard_map/ppermute | solution.py:462
  15.9 7.9 %collective-permute-start.2 = (bf16[128,768]{1,0:T(8,128)(2,1)S(1)}, bf16[128,768]{1,0:T(8,128)(2,1)S(1)}, u32[]{:S(2)}, u32[]{:S(2)}) collective-permute-start(bf16[128,768]{1,0:T(8,128)(2,1)S(1)} %bitcast.172), channel_id=1, source_target_pairs={{0,96},{32,64},{64,32},{96,0},{1,97},{33,65},{65,33},{97,1},{2,98}... | collective-permute-start | bytes 589832 | tf_op jit(solution)/shard_map/ppermute | solution.py:466
  19.3 16.8 %collective-permute-start.1 = (bf16[128,768]{1,0:T(8,128)(2,1)S(1)}, bf16[128,768]{1,0:T(8,128)(2,1)S(1)}, u32[]{:S(2)}, u32[]{:S(2)}) collective-permute-start(bf16[128,768]{1,0:T(8,128)(2,1)S(1)} %bitcast.173), channel_id=1, source_target_pairs={{0,64},{32,96},{64,0},{96,32},{1,65},{33,97},{65,1},{97,33},{2,66}... | collective-permute-start | bytes 589832 | tf_op jit(solution)/shard_map/ppermute | solution.py:466
  19.8 16.3 %collective-permute-start = (bf16[128,768]{1,0:T(8,128)(2,1)S(1)}, bf16[128,768]{1,0:T(8,128)(2,1)S(1)}, u32[]{:S(2)}, u32[]{:S(2)}) collective-permute-start(bf16[128,768]{1,0:T(8,128)(2,1)S(1)} %bitcast.174), channel_id=1, source_target_pairs={{0,32},{32,0},{64,96},{96,64},{1,33},{33,1},{65,97},{97,65},{2,34}... | collective-permute-start | bytes 589832 | tf_op jit(solution)/shard_map/ppermute | solution.py:466
  38.7 154.3 %all-gather.10.cloned.1.call-start = ((), (), s32[]{:S(2)}) async-start(), calls=%async_computation.3 | async-start | bytes 4456448 | tf_op jit(solution)/shard_map/all_gather | solution.py:608
  39.5 13.9 %collective-permute-start.5 = (bf16[192,768]{1,0:T(8,128)(2,1)}, bf16[192,768]{1,0:T(8,128)(2,1)}, u32[]{:S(2)}, u32[]{:S(2)}) collective-permute-start(bf16[192,768]{1,0:T(8,128)(2,1)} %constant_dynamic-slice_fusion.16), channel_id=1, source_target_pairs={{0,1},{1,0},{2,3},{3,2},{4,5},{5,4},{6,7},{7,6},{8,9},{9,8},{10,11... | collective-permute-start | bytes 884744 | tf_op jit(solution)/shard_map/ppermute | solution.py:462
  43.5 13.0 %collective-permute-start.7 = (bf16[192,768]{1,0:T(8,128)(2,1)S(1)}, bf16[192,768]{1,0:T(8,128)(2,1)}, u32[]{:S(2)}, u32[]{:S(2)}) collective-permute-start(bf16[192,768]{1,0:T(8,128)(2,1)S(1)} %fusion.57), channel_id=1, source_target_pairs={{0,1},{1,0},{2,3},{3,2},{4,5},{5,4},{6,7},{7,6},{8,9},{9,8},{10,11... | collective-permute-start | bytes 884744 | tf_op jit(solution)/shard_map/ppermute | solution.py:462
  45.5 15.4 %collective-permute-start.9 = (bf16[192,768]{1,0:T(8,128)(2,1)}, bf16[192,768]{1,0:T(8,128)(2,1)}, u32[]{:S(2)}, u32[]{:S(2)}) collective-permute-start(bf16[192,768]{1,0:T(8,128)(2,1)} %constant_dynamic-slice_fusion.13), channel_id=1, source_target_pairs={{0,1},{1,0},{2,3},{3,2},{4,5},{5,4},{6,7},{7,6},{8,9},{9,8},{10,11... | collective-permute-start | bytes 884744 | tf_op jit(solution)/shard_map/ppermute | solution.py:462
  48.3 19.0 %collective-permute-start.11 = (bf16[128,768]{1,0:T(8,128)(2,1)S(1)}, bf16[128,768]{1,0:T(8,128)(2,1)}, u32[]{:S(2)}, u32[]{:S(2)}) collective-permute-start(bf16[128,768]{1,0:T(8,128)(2,1)S(1)} %bitcast.168), channel_id=1, source_target_pairs={{0,32},{32,0},{64,96},{96,64},{1,33},{33,1},{65,97},{97,65},{2,34}... | collective-permute-start | bytes 589832 | tf_op jit(solution)/shard_map/ppermute | solution.py:466
  51.0 20.2 %collective-permute-start.12 = (bf16[128,768]{1,0:T(8,128)(2,1)S(1)}, bf16[128,768]{1,0:T(8,128)(2,1)S(1)}, u32[]{:S(2)}, u32[]{:S(2)}) collective-permute-start(bf16[128,768]{1,0:T(8,128)(2,1)S(1)} %bitcast.169), channel_id=1, source_target_pairs={{0,64},{32,96},{64,0},{96,32},{1,65},{33,97},{65,1},{97,33},{2,66}... | collective-permute-start | bytes 589832 | tf_op jit(solution)/shard_map/ppermute | solution.py:466
  53.4 27.2 %collective-permute-start.6 = (bf16[192,768]{1,0:T(8,128)(2,1)}, bf16[192,768]{1,0:T(8,128)(2,1)S(1)}, u32[]{:S(2)}, u32[]{:S(2)}) collective-permute-start(bf16[192,768]{1,0:T(8,128)(2,1)} %collective-permute-done.5), channel_id=1, source_target_pairs={{0,2},{2,0},{1,3},{3,1},{4,6},{6,4},{5,7},{7,5},{8,10},{10,8},{9,1... | collective-permute-start | bytes 884744 | tf_op jit(solution)/shard_map/ppermute | solution.py:462
  56.4 24.2 %collective-permute-start.8 = (bf16[192,768]{1,0:T(8,128)(2,1)}, bf16[192,768]{1,0:T(8,128)(2,1)S(1)}, u32[]{:S(2)}, u32[]{:S(2)}) collective-permute-start(bf16[192,768]{1,0:T(8,128)(2,1)} %collective-permute-done.7), channel_id=1, source_target_pairs={{0,2},{2,0},{1,3},{3,1},{4,6},{6,4},{5,7},{7,5},{8,10},{10,8},{9,1... | collective-permute-start | bytes 884744 | tf_op jit(solution)/shard_map/ppermute | solution.py:462
  60.9 20.5 %collective-permute-start.10 = (bf16[192,768]{1,0:T(8,128)(2,1)}, bf16[192,768]{1,0:T(8,128)(2,1)}, u32[]{:S(2)}, u32[]{:S(2)}) collective-permute-start(bf16[192,768]{1,0:T(8,128)(2,1)} %collective-permute-done.9), channel_id=1, source_target_pairs={{0,2},{2,0},{1,3},{3,1},{4,6},{6,4},{5,7},{7,5},{8,10},{10,8},{9,1... | collective-permute-start | bytes 884744 | tf_op jit(solution)/shard_map/ppermute | solution.py:462
  67.3 13.4 %collective-permute-start.13 = (bf16[128,768]{1,0:T(8,128)(2,1)S(1)}, bf16[128,768]{1,0:T(8,128)(2,1)S(1)}, u32[]{:S(2)}, u32[]{:S(2)}) collective-permute-start(bf16[128,768]{1,0:T(8,128)(2,1)S(1)} %bitcast.170), channel_id=1, source_target_pairs={{0,96},{32,64},{64,32},{96,0},{1,97},{33,65},{65,33},{97,1},{2,98}... | collective-permute-start | bytes 589832 | tf_op jit(solution)/shard_map/ppermute | solution.py:466
  117.0 11.5 %collective-permute-start.16 = (bf16[4,128,256]{2,1,0:T(8,128)(2,1)}, bf16[4,128,256]{2,1,0:T(8,128)(2,1)}, u32[]{:S(2)}, u32[]{:S(2)}) collective-permute-start(bf16[4,128,256]{2,1,0:T(8,128)(2,1)} %get-tuple-element.125.attn_ref), channel_id=1, source_target_pairs={{0,96},{32,64},{64,32},{96,0},{1,97},{33,65},{65,33},{97,1},{2,98}... | collective-permute-start | bytes 786440 | tf_op jit(solution)/shard_map/ppermute | solution.py:466
  118.5 13.3 %collective-permute-start.15 = (bf16[4,128,256]{2,1,0:T(8,128)(2,1)}, bf16[4,128,256]{2,1,0:T(8,128)(2,1)}, u32[]{:S(2)}, u32[]{:S(2)}) collective-permute-start(bf16[4,128,256]{2,1,0:T(8,128)(2,1)} %get-tuple-element.125.attn_ref), channel_id=1, source_target_pairs={{0,64},{32,96},{64,0},{96,32},{1,65},{33,97},{65,1},{97,33},{2,66}... | collective-permute-start | bytes 786440 | tf_op jit(solution)/shard_map/ppermute | solution.py:466
  119.9 12.8 %collective-permute-start.14 = (bf16[4,128,256]{2,1,0:T(8,128)(2,1)}, bf16[4,128,256]{2,1,0:T(8,128)(2,1)}, u32[]{:S(2)}, u32[]{:S(2)}) collective-permute-start(bf16[4,128,256]{2,1,0:T(8,128)(2,1)} %get-tuple-element.125.attn_ref), channel_id=1, source_target_pairs={{0,32},{32,0},{64,96},{96,64},{1,33},{33,1},{65,97},{97,65},{2,34}... | collective-permute-start | bytes 786440 | tf_op jit(solution)/shard_map/ppermute | solution.py:466
  121.8 110.1 %all-gather.12.cloned.1.call-start = ((), (), s32[]{:S(2)}) async-start(), calls=%async_computation.4 | async-start | bytes 4456448 | tf_op jit(solution)/shard_map/all_gather | solution.py:670
  139.3 20.3 %collective-permute-start.17 = (f32[128,768]{1,0:T(8,128)S(1)}, f32[128,768]{1,0:T(8,128)S(1)}, u32[]{:S(2)}, u32[]{:S(2)}) collective-permute-start(f32[128,768]{1,0:T(8,128)S(1)} %get-tuple-element.197), channel_id=1, source_target_pairs={{0,32},{32,0},{64,96},{96,64},{1,33},{33,1},{65,97},{97,65},{2,34}... | collective-permute-start | bytes 1179656 | tf_op jit(solution)/shard_map/ppermute | solution.py:466
  140.9 18.8 %collective-permute-start.18 = (f32[128,768]{1,0:T(8,128)S(1)}, f32[128,768]{1,0:T(8,128)S(1)}, u32[]{:S(2)}, u32[]{:S(2)}) collective-permute-start(f32[128,768]{1,0:T(8,128)S(1)} %get-tuple-element.196), channel_id=1, source_target_pairs={{0,64},{32,96},{64,0},{96,32},{1,65},{33,97},{65,1},{97,33},{2,66}... | collective-permute-start | bytes 1179656 | tf_op jit(solution)/shard_map/ppermute | solution.py:466
  142.9 34.6 %collective-permute-start.19 = (f32[128,768]{1,0:T(8,128)S(1)}, f32[128,768]{1,0:T(8,128)S(1)}, u32[]{:S(2)}, u32[]{:S(2)}) collective-permute-start(f32[128,768]{1,0:T(8,128)S(1)} %get-tuple-element.195), channel_id=1, source_target_pairs={{0,96},{32,64},{64,32},{96,0},{1,97},{33,65},{65,33},{97,1},{2,98}... | collective-permute-start | bytes 1179656 | tf_op jit(solution)/shard_map/ppermute | solution.py:466
  145.2 32.6 %copy-start.17 = (bf16[1,128,768]{2,1,0:T(8,128)(2,1)S(1)}, bf16[1,128,768]{2,1,0:T(8,128)(2,1)}, u32[]{:S(2)}) copy-start(bf16[1,128,768]{2,1,0:T(8,128)(2,1)} %param.16) | copy-start | bytes 589828
  145.2 32.6 %slice-start.3 = ((f32[512]{0:T(512)}), f32[128]{0:T(128)S(1)}, s32[]{:S(2)}) async-start(f32[512]{0:T(512)} %copy-done.38), calls=%async_computation.9 | async-start | bytes 1024 | tf_op jit(solution)/shard_map/slice | solution.py:657
  177.9 7.9 %collective-permute-start.20 = (bf16[128,768]{1,0:T(8,128)(2,1)S(1)}, bf16[128,768]{1,0:T(8,128)(2,1)S(1)}, u32[]{:S(2)}, u32[]{:S(2)}) collective-permute-start(bf16[128,768]{1,0:T(8,128)(2,1)S(1)} %get-tuple-element.117), channel_id=1, source_target_pairs={{0,32},{32,0},{64,96},{96,64},{1,33},{33,1},{65,97},{97,65},{2,34}... | collective-permute-start | bytes 589832 | tf_op jit(solution)/shard_map/ppermute | solution.py:466
  178.1 7.7 %collective-permute-start.21 = (bf16[128,768]{1,0:T(8,128)(2,1)S(1)}, bf16[128,768]{1,0:T(8,128)(2,1)S(1)}, u32[]{:S(2)}, u32[]{:S(2)}) collective-permute-start(bf16[128,768]{1,0:T(8,128)(2,1)S(1)} %get-tuple-element.117), channel_id=1, source_target_pairs={{0,64},{32,96},{64,0},{96,32},{1,65},{33,97},{65,1},{97,33},{2,66}... | collective-permute-start | bytes 589832 | tf_op jit(solution)/shard_map/ppermute | solution.py:466
  178.2 10.4 %collective-permute-start.22 = (bf16[128,768]{1,0:T(8,128)(2,1)S(1)}, bf16[128,768]{1,0:T(8,128)(2,1)S(1)}, u32[]{:S(2)}, u32[]{:S(2)}) collective-permute-start(bf16[128,768]{1,0:T(8,128)(2,1)S(1)} %get-tuple-element.117), channel_id=1, source_target_pairs={{0,96},{32,64},{64,32},{96,0},{1,97},{33,65},{65,33},{97,1},{2,98}... | collective-permute-start | bytes 589832 | tf_op jit(solution)/shard_map/ppermute | solution.py:466
  193.0 125.5 %reduce-scatter.2.cloned.1.call-start = ((), (), s32[]{:S(2)}) async-start(), calls=%async_computation.2 | async-start | bytes 5849088 | tf_op jit(solution)/shard_map/reduce_scatter | solution.py:704
  232.0 167.3 %all-gather.14.cloned.1.call-start = ((), (), s32[]{:S(2)}) async-start(), calls=%async_computation.5 | async-start | bytes 10027008 | tf_op jit(solution)/shard_map/all_gather | solution.py:732
  234.2 35.4 %collective-permute-start.23 = (bf16[128,768]{1,0:T(8,128)(2,1)S(1)}, bf16[128,768]{1,0:T(8,128)(2,1)S(1)}, u32[]{:S(2)}, u32[]{:S(2)}) collective-permute-start(bf16[128,768]{1,0:T(8,128)(2,1)S(1)} %get-tuple-element.138), channel_id=1, source_target_pairs={{0,32},{32,0},{64,96},{96,64},{1,33},{33,1},{65,97},{97,65},{2,34}... | collective-permute-start | bytes 589832 | tf_op jit(solution)/shard_map/ppermute | solution.py:466
  236.7 33.0 %collective-permute-start.24 = (bf16[128,768]{1,0:T(8,128)(2,1)S(1)}, bf16[128,768]{1,0:T(8,128)(2,1)S(1)}, u32[]{:S(2)}, u32[]{:S(2)}) collective-permute-start(bf16[128,768]{1,0:T(8,128)(2,1)S(1)} %get-tuple-element.139), channel_id=1, source_target_pairs={{0,64},{32,96},{64,0},{96,32},{1,65},{33,97},{65,1},{97,33},{2,66}... | collective-permute-start | bytes 589832 | tf_op jit(solution)/shard_map/ppermute | solution.py:466
  237.9 31.8 %collective-permute-start.25 = (bf16[128,768]{1,0:T(8,128)(2,1)S(1)}, bf16[128,768]{1,0:T(8,128)(2,1)S(1)}, u32[]{:S(2)}, u32[]{:S(2)}) collective-permute-start(bf16[128,768]{1,0:T(8,128)(2,1)S(1)} %get-tuple-element.140), channel_id=1, source_target_pairs={{0,96},{32,64},{64,32},{96,0},{1,97},{33,65},{65,33},{97,1},{2,98}... | collective-permute-start | bytes 589832 | tf_op jit(solution)/shard_map/ppermute | solution.py:466
  276.9 3.6 collective-permute-start.26
  282.6 8.8 %collective-permute-start.33 = (f32[56,640]{1,0:T(8,128)S(1)}, f32[56,640]{1,0:T(8,128)S(1)}, u32[]{:S(2)}, u32[]{:S(2)}) collective-permute-start(f32[56,640]{1,0:T(8,128)S(1)} %get-tuple-element.207), channel_id=1, source_target_pairs={{0,28},{4,24},{8,20},{12,16},{16,12},{20,8},{24,4},{28,0},{1,29},{... | collective-permute-start | bytes 430088 | tf_op jit(solution)/shard_map/ppermute | solution.py:533
  282.6 11.6 %collective-permute-start.32 = (f32[56,640]{1,0:T(8,128)S(1)}, f32[56,640]{1,0:T(8,128)S(1)}, u32[]{:S(2)}, u32[]{:S(2)}) collective-permute-start(f32[56,640]{1,0:T(8,128)S(1)} %get-tuple-element.208), channel_id=1, source_target_pairs={{0,24},{4,28},{8,16},{12,20},{16,8},{20,12},{24,0},{28,4},{1,25},{... | collective-permute-start | bytes 430088 | tf_op jit(solution)/shard_map/ppermute | solution.py:533
  286.2 9.9 %collective-permute-start.31 = (f32[56,640]{1,0:T(8,128)}, f32[56,640]{1,0:T(8,128)S(1)}, u32[]{:S(2)}, u32[]{:S(2)}) collective-permute-start(f32[56,640]{1,0:T(8,128)} %get-tuple-element.209), channel_id=1, source_target_pairs={{0,20},{4,16},{8,28},{12,24},{16,4},{20,0},{24,12},{28,8},{1,21},{... | collective-permute-start | bytes 430088 | tf_op jit(solution)/shard_map/ppermute | solution.py:533
  286.2 15.6 %collective-permute-start.30 = (f32[56,640]{1,0:T(8,128)S(1)}, f32[56,640]{1,0:T(8,128)}, u32[]{:S(2)}, u32[]{:S(2)}) collective-permute-start(f32[56,640]{1,0:T(8,128)S(1)} %get-tuple-element.210), channel_id=1, source_target_pairs={{0,16},{4,20},{8,24},{12,28},{16,0},{20,4},{24,8},{28,12},{1,17},{... | collective-permute-start | bytes 430088 | tf_op jit(solution)/shard_map/ppermute | solution.py:533
  287.9 17.2 %collective-permute-start.29 = (f32[56,640]{1,0:T(8,128)S(1)}, f32[56,640]{1,0:T(8,128)}, u32[]{:S(2)}, u32[]{:S(2)}) collective-permute-start(f32[56,640]{1,0:T(8,128)S(1)} %get-tuple-element.211), channel_id=1, source_target_pairs={{0,12},{4,8},{8,4},{12,0},{16,28},{20,24},{24,20},{28,16},{1,13},{... | collective-permute-start | bytes 430088 | tf_op jit(solution)/shard_map/ppermute | solution.py:533
  291.4 13.7 %collective-permute-start.28 = (f32[56,640]{1,0:T(8,128)S(1)}, f32[56,640]{1,0:T(8,128)}, u32[]{:S(2)}, u32[]{:S(2)}) collective-permute-start(f32[56,640]{1,0:T(8,128)S(1)} %get-tuple-element.212), channel_id=1, source_target_pairs={{0,8},{4,12},{8,0},{12,4},{16,24},{20,28},{24,16},{28,20},{1,9},{5... | collective-permute-start | bytes 430088 | tf_op jit(solution)/shard_map/ppermute | solution.py:533
  294.1 11.0 %collective-permute-start.27 = (f32[56,640]{1,0:T(8,128)S(1)}, f32[56,640]{1,0:T(8,128)}, u32[]{:S(2)}, u32[]{:S(2)}) collective-permute-start(f32[56,640]{1,0:T(8,128)S(1)} %get-tuple-element.206), channel_id=1, source_target_pairs={{0,4},{4,0},{8,12},{12,8},{16,20},{20,16},{24,28},{28,24},{1,5},{5... | collective-permute-start | bytes 430088 | tf_op jit(solution)/shard_map/ppermute | solution.py:533
  306.4 7.4 %collective-permute-start.34 = (bf16[128,768]{1,0:T(8,128)(2,1)S(1)}, bf16[128,768]{1,0:T(8,128)(2,1)S(1)}, u32[]{:S(2)}, u32[]{:S(2)}) collective-permute-start(bf16[128,768]{1,0:T(8,128)(2,1)S(1)} %get-tuple-element.224), channel_id=1, source_target_pairs={{0,32},{32,0},{64,96},{96,64},{1,33},{33,1},{65,97},{97,65},{2,34}... | collective-permute-start | bytes 589832 | tf_op jit(solution)/shard_map/ppermute | solution.py:466
  308.9 5.4 %collective-permute-start.35 = (bf16[128,768]{1,0:T(8,128)(2,1)S(1)}, bf16[128,768]{1,0:T(8,128)(2,1)S(1)}, u32[]{:S(2)}, u32[]{:S(2)}) collective-permute-start(bf16[128,768]{1,0:T(8,128)(2,1)S(1)} %get-tuple-element.223), channel_id=1, source_target_pairs={{0,64},{32,96},{64,0},{96,32},{1,65},{33,97},{65,1},{97,33},{2,66}... | collective-permute-start | bytes 589832 | tf_op jit(solution)/shard_map/ppermute | solution.py:466
  310.3 8.2 %collective-permute-start.36 = (bf16[128,768]{1,0:T(8,128)(2,1)S(1)}, bf16[128,768]{1,0:T(8,128)(2,1)S(1)}, u32[]{:S(2)}, u32[]{:S(2)}) collective-permute-start(bf16[128,768]{1,0:T(8,128)(2,1)S(1)} %get-tuple-element.222), channel_id=1, source_target_pairs={{0,96},{32,64},{64,32},{96,0},{1,97},{33,65},{65,33},{97,1},{2,98}... | collective-permute-start | bytes 589832 | tf_op jit(solution)/shard_map/ppermute | solution.py:466
  320.4 8.1 %collective-permute-start.37 = (f32[96,768]{1,0:T(8,128)S(1)}, f32[96,768]{1,0:T(8,128)S(1)}, u32[]{:S(2)}, u32[]{:S(2)}) collective-permute-start(f32[96,768]{1,0:T(8,128)S(1)} %pad_maximum_fusion.16), channel_id=1, source_target_pairs={{0,1},{1,0},{2,3},{3,2},{4,5},{5,4},{6,7},{7,6},{8,9},{9,8},{10,11... | collective-permute-start | bytes 884744 | tf_op jit(solution)/shard_map/ppermute | solution.py:462
  328.6 6.6 %collective-permute-start.40 = (bf16[96,768]{1,0:T(8,128)(2,1)S(1)}, bf16[96,768]{1,0:T(8,128)(2,1)S(1)}, u32[]{:S(2)}, u32[]{:S(2)}) collective-permute-start(bf16[96,768]{1,0:T(8,128)(2,1)S(1)} %fusion.56), channel_id=1, source_target_pairs={{0,96},{32,64},{64,32},{96,0},{1,97},{33,65},{65,33},{97,1},{2,98}... | collective-permute-start | bytes 442376 | tf_op jit(solution)/shard_map/ppermute | solution.py:466
  331.8 4.9 %collective-permute-start.39 = (bf16[96,768]{1,0:T(8,128)(2,1)S(1)}, bf16[96,768]{1,0:T(8,128)(2,1)S(1)}, u32[]{:S(2)}, u32[]{:S(2)}) collective-permute-start(bf16[96,768]{1,0:T(8,128)(2,1)S(1)} %fusion.56), channel_id=1, source_target_pairs={{0,64},{32,96},{64,0},{96,32},{1,65},{33,97},{65,1},{97,33},{2,66}... | collective-permute-start | bytes 442376 | tf_op jit(solution)/shard_map/ppermute | solution.py:466
  333.0 6.8 %collective-permute-start.38 = (bf16[96,768]{1,0:T(8,128)(2,1)S(1)}, bf16[96,768]{1,0:T(8,128)(2,1)S(1)}, u32[]{:S(2)}, u32[]{:S(2)}) collective-permute-start(bf16[96,768]{1,0:T(8,128)(2,1)S(1)} %fusion.56), channel_id=1, source_target_pairs={{0,32},{32,0},{64,96},{96,64},{1,33},{33,1},{65,97},{97,65},{2,34}... | collective-permute-start | bytes 442376 | tf_op jit(solution)/shard_map/ppermute | solution.py:466
  (53 other events, 353.1 us)
Sparse Core Ops, SparseCore 0:
  38.8 53.3 all-gather.7
  122.0 51.8 all-gather.9
  193.1 38.7 all-gather.11
  234.2 73.8 reduce-scatter.1
  340.8 58.4 all-gather.13

commit v5 on v4

--- a/solution.py
+++ b/solution.py
@@ -410,9 +410,9 @@
         [part for r in rows for part in (r[:24, 512:640], r[:24, 448:512])], axis=1
     )
     for g in range(2):
-        proj_ref[g, 0] = in_ref[0, rank ^ (2 * pos_ref[1] + g), 80:].astype(F32)[:12]
-    first = [r[24:25] for r in rows]
-    second = [r[44:45] for r in rows]
+        proj_ref[g, 0] = in_ref[0, rank ^ (2 * pos_ref[1] + g), 48:].astype(F32)[24:36]
+    first = [r[37:38] for r in rows]
+    second = [r[36:37] for r in rows]
     sum_ref[0] = jnp.concatenate(
         [
             (first[0] + first[1]) + (first[2] + first[3]),
@@ -431,7 +431,7 @@
         grid_spec=pltpu.PrefetchScalarGridSpec(
             num_scalar_prefetch=1,
             grid=(16,),
-            in_specs=[pl.BlockSpec((1, 4, 96, 768), lambda s, pos: (s, 0, 0, 0))],
+            in_specs=[pl.BlockSpec((1, 4, 88, 768), lambda s, pos: (s, 0, 0, 0))],
             out_specs=(
                 pl.BlockSpec((4, 1, 48, 768), lambda s, pos: (0, jnp.minimum(s, 7), 0, 0)),
                 pl.BlockSpec((1, 48, 3072), lambda s, pos: (jnp.maximum(s - 8, 0), 0, 0)),
@@ -537,10 +537,11 @@
     core = lax.axis_index("core")
     block = lax.axis_index(BLOCKS)
     pair = pick(local, core) + swap(pick(local, 1 - core), "core")
-    moved = [to_block(pick(pair, block ^ r), r) for r in range(1, 8)]
+    low = pair.astype(BF16)
+    moved = [to_block(pick(low, block ^ r), r) for r in range(1, 8)]
     total = pick(pair, block)
     for values in moved:
-        total = total + values
+        total = total + values.astype(F32)
     return total
 
 
@@ -567,18 +568,26 @@
     pos = jnp.stack([seq, rank]).astype(jnp.int32)
 
     x_low = jnp.concatenate(gather_ranks(block_in[0]), axis=0)
-    w_q = lax.dynamic_slice_in_dim(w_qkv, 192 * rank, 192, 1)
-    w_k = lax.dynamic_slice_in_dim(w_qkv, 768 + 192 * rank, 192, 1)
-    w_v = lax.dynamic_slice_in_dim(w_qkv, 1536 + 192 * rank, 192, 1)
-    qkv_shard = jnp.concatenate(
-        [w_q, jnp.zeros((384, 64), BF16), w_k, w_v[:, 128:], w_v[:, :128]], axis=1
-    )
-    w_cols = both_shards(qkv_shard, fs).reshape(768, 640)
+
+    def head_columns(which):
+        w_q = lax.dynamic_slice_in_dim(w_qkv, 192 * which, 192, 1)
+        w_k = lax.dynamic_slice_in_dim(w_qkv, 768 + 192 * which, 192, 1)
+        w_v = lax.dynamic_slice_in_dim(w_qkv, 1536 + 192 * which, 192, 1)
+        return jnp.concatenate(
+            [w_q, jnp.zeros((384, 64), BF16), w_k, w_v[:, 128:], w_v[:, :128]], axis=1
+        )
+
+    qkv_shard = head_columns(rank ^ 2)
+    qkv_peer = lax.ppermute(qkv_shard, ("zl", "fsdp"), [(a, 3 - a) for a in range(4)])
     vectors = (ln1_gain, ln1_bias, q_bias, v_bias, b_proj, ln2_gain, ln2_bias, b_out, b_fc)
     vectors = lax.optimization_barrier((qkv_shard,) + vectors)[1:]
     small = jnp.stack([v.astype(F32) for v in vectors[:8]])
     small = jnp.concatenate([small, vectors[8].astype(F32).reshape(4, 384)], axis=0)
     small = both_shards(small, fs)
+    qkv_own = head_columns(rank)
+    w_cols = jnp.concatenate(
+        [jnp.where(fs == 0, qkv_own, qkv_peer), jnp.where(fs == 0, qkv_peer, qkv_own)], axis=0
+    )
     wide_vectors = small[:, :8].transpose(1, 0, 2).reshape(8, 768)
     gain_one, shift_one, query_bias, value_bias = wide_vectors[:4]
     proj_bias, gain_two, shift_two, out_bias = wide_vectors[4:]
@@ -613,7 +622,7 @@
     )
     attn, lse = forward_attention(pos, q_scaled, kv_all)
 
-    attn_ranks = gather_ranks(attn)
+    attn_ranks, q_all = lax.optimization_barrier((tuple(gather_ranks(attn)), q_all))
     proj_rows = join_shards(w_proj, fetched[0], fs).reshape(4, 3, 64, 768)
     proj_rows = jnp.concatenate(
         [proj_rows[:, :2], jnp.zeros((4, 1, 64, 768), BF16), proj_rows[:, 2:]], axis=1
@@ -721,13 +730,14 @@
             [
                 lax.dynamic_slice_in_dim(early, 48 * which, 48, 0),
                 lax.dynamic_slice_in_dim(late, 24 * which, 24, 0),
-                late[48:],
-                early[96:],
+                early[96:109],
+                late[48:51],
             ],
             axis=0,
         )
 
-    totals = (rows_of(fs) + swap(rows_of(1 - fs), "fsdp")).astype(BF16)
+    totals = rows_of(fs) + swap(rows_of(1 - fs).astype(BF16), "fsdp").astype(F32)
+    totals = totals.astype(BF16)
     totals = jnp.stack(gather_ranks(totals))
     totals = lax.all_gather(totals, SEQ_AXES, axis=0, tiled=False)
     output = (

time: 431 us -> 431 us (level)
    all_gather x1, waiting for transfers between devices: 10.8 us -> 42.7 us  [body(): kv_all = lax.all_gather(kv_own, SEQ_AXES, axis=0, tiled=False)]
    ppermute x24, waiting for transfers between devices: 76.9 us -> 48.6 us  [to_rank(): return lax.ppermute(values, TP, [(a, a ^ offset) for a in range(4)])]
    ppermute x7, waiting for transfers between devices: 15.2 us -> 5.7 us  [to_block(): return lax.ppermute(values, BLOCKS, [(a, a ^ offset) for a in range(8)])]
    all_gather x1, waiting for transfers between devices: 8.97 us -> 15.9 us  [body(): do_all = lax.all_gather(after(do_aug, q_all), SEQ_AXES, axis=0, tiled=False)]
    ppermute x10 -> x9, starting transfers between devices: 24.7 us -> 19.4 us  [swap(): return lax.ppermute(values, axis, [(0, 1), (1, 0)])]
    ppermute x10 -> x9, waiting for transfers between devices: 9.48 us -> 12 us  [swap(): return lax.ppermute(values, axis, [(0, 1), (1, 0)])]
    unnamed x108 -> x114, local copies, waits for them, and re-layouts: 9.23 us -> 7.19 us
  transfers between devices with their start and end apart: 46 -> 46, of which waited for: 23 -> 23; matrix products, arithmetic and copies ran while one was open for 11% -> 10% of each run, Pallas kernels for 14% -> 18%
where the time goes in v5:
time: 431 us; the launch traced here: 429 us
  waiting for transfers between devices  178 us (41%)
  Pallas kernels  95.6 us (22%)
  starting transfers between devices  66.5 us (15%)
  local copies, waits for them, and re-layouts  38.4 us (9%)
  other arithmetic  26.4 us (6%)
  between operations  15.1 us (4%)
  matrix products  9.15 us (2%)
    all_gather x1, waiting for transfers between devices, body(): totals = lax.all_gather(totals, SEQ_AXES, axis=0, tiled=False)  53.2 us
    ppermute x24, waiting for transfers between devices, to_rank(): return lax.ppermute(values, TP, [(a, a ^ offset) for a in range(4)])  48.6 us
    all_gather x1, waiting for transfers between devices, body(): kv_all = lax.all_gather(kv_own, SEQ_AXES, axis=0, tiled=False)  42.7 us
    ppermute x24, starting transfers between devices, to_rank(): return lax.ppermute(values, TP, [(a, a ^ offset) for a in range(4)])  38.5 us
    pallas_call x1, Pallas kernels, key_grad(): pl.pallas_call(key_grad_kernel, out_shape=(jax.ShapeDtypeStruct((4, 128,...  31.5 us
    pallas_call x1, Pallas kernels, query_grad(): pl.pallas_call(query_grad_kernel, out_shape=(jax.ShapeDtypeStruct((4, 128...  20.1 us
    pallas_call x1, Pallas kernels, forward_attention(): pl.pallas_call(forward_kernel, out_shape=(jax.ShapeDtypeStruct((4, 128, 2...  20.1 us
    ppermute x9, starting transfers between devices, swap(): return lax.ppermute(values, axis, [(0, 1), (1, 0)])  19.4 us
  transfers between devices with their start and end apart: 46, of which 23 were waited for; matrix products, arithmetic and copies ran while one was open for 10% of the time, Pallas kernels for 18%

profile of v5, /device:TPU:1, one launch (start us, length us, event | category | flops | bytes accessed | tf_op | source)
XLA Modules:
  0.0 429.2 jit_solution(5131191515286685369)
XLA Ops:
  9.6 1.6 constant_dynamic-slice_fusion.18
  11.9 4.5 %collective-permute-start.3 = (f32[12,384]{1,0:T(8,128)S(1)}, f32[12,384]{1,0:T(8,128)S(1)}, u32[]{:S(2)}, u32[]{:S(2)}) collective-permute-start(f32[12,384]{1,0:T(8,128)S(1)} %concatenate.120), channel_id=1, source_target_pairs={{0,1},{1,0},{2,3},{3,2},{4,5},{5,4},{6,7},{7,6},{8,9},{9,8},{10,11... | collective-permute-start | bytes 55304 | tf_op jit(solution)/shard_map/ppermute | solution.py:462
  16.9 2.8 collective-permute-start.2
  21.8 2.7 collective-permute-done.2
  24.4 5.9 %collective-permute-done.1 = bf16[128,768]{1,0:T(8,128)(2,1)S(1)} collective-permute-done((bf16[128,768]{1,0:T(8,128)(2,1)S(1)}, bf16[128,768]{1,0:T(8,128)(2,1)S(1)}, u32[]{:S(2)}, u32[]{:S(2)}) %collective-permute-start.1) | collective-permute-done | bytes 196640 | tf_op jit(solution)/shard_map/ppermute | solution.py:466
  33.6 42.7 %all-gather.8.cloned.1.call-done.kv_ref = bf16[16,4,128,384]{3,2,1,0:T(8,128)(2,1)} async-done(((bf16[1,4,128,384]{3,2,1,0:T(8,128)(2,1)}), bf16[16,4,128,384]{3,2,1,0:T(8,128)(2,1)}) %all-gather.8.cloned.1.call-update) | async-done | bytes 6291472 | tf_op jit(solution)/shard_map/all_gather | solution.py:616
  76.5 3.0 collective-permute-start.5
  81.8 3.0 collective-permute-start.9
  84.8 2.7 collective-permute-start.11
  87.8 1.7 collective-permute-start.6
  89.5 3.3 collective-permute-done.7
  92.8 1.7 collective-permute-start.8
  94.5 4.6 %collective-permute-done.9 = bf16[192,768]{1,0:T(8,128)(2,1)} collective-permute-done((bf16[192,768]{1,0:T(8,128)(2,1)S(1)}, bf16[192,768]{1,0:T(8,128)(2,1)}, u32[]{:S(2)}, u32[]{:S(2)}) %collective-permute-start.9) | collective-permute-done | bytes 294944 | tf_op jit(solution)/shard_map/ppermute | solution.py:462
  99.2 1.8 collective-permute-start.10
  101.7 3.7 collective-permute-start.13
  105.4 1.8 fusion
  107.2 6.8 %collective-permute-done.13 = bf16[128,768]{1,0:T(8,128)(2,1)S(1)} collective-permute-done((bf16[128,768]{1,0:T(8,128)(2,1)S(1)}, bf16[128,768]{1,0:T(8,128)(2,1)S(1)}, u32[]{:S(2)}, u32[]{:S(2)}) %collective-permute-start.13) | collective-permute-done | bytes 196640 | tf_op jit(solution)/shard_map/ppermute | solution.py:466
  117.9 20.1 %attention_forward.1 = (bf16[4,128,256]{2,1,0:T(8,128)(2,1)}, f32[4,384,128]{2,1,0:T(8,128)}) custom-call(s32[2]{0:T(128)} %get-tuple-element.275.pos_ref, bf16[4,128,256]{2,1,0:T(8,128)(2,1)} %bitcast.177, bf16[16,4,128,384]{3,2,1,0:T(8,128)(2,1)} %all-gather.8.cloned.1.call-done.kv_ref), custom_call_target="tpu_custom_call" | custom-call | flops 3221225472 | bytes 8388608 | tf_op jit(solution)/shard_map/attention_forward/pallas_call | solution.py:125
  137.9 3.7 collective-permute-start.14
  149.2 5.7 %collective-permute-done.16 = bf16[4,128,256]{2,1,0:T(8,128)(2,1)} collective-permute-done((bf16[4,128,256]{2,1,0:T(8,128)(2,1)}, bf16[4,128,256]{2,1,0:T(8,128)(2,1)}, u32[]{:S(2)}, u32[]{:S(2)}) %collective-permute-start.16) | collective-permute-done | bytes 262176 | tf_op jit(solution)/shard_map/ppermute | solution.py:466
  168.4 4.9 %collective-permute-done.17 = f32[128,768]{1,0:T(8,128)S(1)} collective-permute-done((f32[128,768]{1,0:T(8,128)S(1)}, f32[128,768]{1,0:T(8,128)S(1)}, u32[]{:S(2)}, u32[]{:S(2)}) %collective-permute-start.17) | collective-permute-done | bytes 393248 | tf_op jit(solution)/shard_map/ppermute | solution.py:466
  173.3 6.8 %collective-permute-done.19 = f32[128,768]{1,0:T(8,128)S(1)} collective-permute-done((f32[128,768]{1,0:T(8,128)S(1)}, f32[128,768]{1,0:T(8,128)S(1)}, u32[]{:S(2)}, u32[]{:S(2)}) %collective-permute-start.19) | collective-permute-done | bytes 393248 | tf_op jit(solution)/shard_map/ppermute | solution.py:466
  180.5 4.0 collective-permute-start.20
  186.9 2.9 pad.5
  189.8 3.4 collective-permute-done.22
  194.2 3.3 attention_grad_rows.1
  198.4 1.7 bitcast_convert_fusion
  200.1 20.1 %attention_query_grad.1 = (bf16[4,128,256]{2,1,0:T(8,128)(2,1)}, f32[1,256]{1,0:T(1,128)}) custom-call(s32[2]{0:T(128)} %get-tuple-element.275.pos_ref, bf16[4,128,256]{2,1,0:T(8,128)(2,1)} %bitcast.178, bf16[4,128,256]{2,1,0:T(8,128)(2,1)} %get-tuple-element.141.do_ref, f32[4,384,128]{2,1,0:T(8,128)} %get-tuple-element.131.lse_ref, ...), custom_call_target="tpu_custom_call" | custom-call | flops 4831838208 | bytes 8388608 | tf_op jit(solution)/shard_map/attention_query_grad/pallas_call | solution.py:228
  225.0 1.9 fusion.87
  228.8 15.9 %all-gather.12.cloned.1.call-done = bf16[64,128,256]{2,1,0:T(8,128)(2,1)} async-done(((bf16[4,128,256]{2,1,0:T(8,128)(2,1)}), bf16[64,128,256]{2,1,0:T(8,128)(2,1)}) %all-gather.12.cloned.1.call-update) | async-done | bytes 4194320 | tf_op jit(solution)/shard_map/all_gather | solution.py:679
  248.1 2.2 collective-permute-start.23
  252.2 31.5 %attention_key_grad.1 = (bf16[4,128,384]{2,1,0:T(8,128)(2,1)}, f32[1,384]{1,0:T(1,128)}) custom-call(s32[2]{0:T(128)} %get-tuple-element.275.pos_ref, bf16[4,128,384]{2,1,0:T(8,128)(2,1)} %bitcast.175, bf16[16,4,128,256]{3,2,1,0:T(8,128)(2,1)} %bitcast.192, bf16[16,4,128,256]{3,2,1,0:T(8,128)(2,1)} %bitcast.193), custom_call_target="tpu_custom_call" | custom-call | flops 6442450944 | bytes 10485760 | tf_op jit(solution)/shard_map/attention_key_grad/pallas_call | solution.py:317
  283.7 5.8 %first_grads.1 = (f32[2,8,56,640]{3,2,1,0:T(8,128)}, f32[128,768]{1,0:T(8,128)}, bf16[3,128,768]{2,1,0:T(8,128)(2,1)}) custom-call(bf16[768,512]{1,0:T(8,128)(2,1)} %copy.35.norm_ref, f32[512,768]{1,0:T(8,128)} %get-tuple-element.228.hat_ref, bf16[4,128,256]{2,1,0:T(8,128)(2,1)} %get-tuple-element.145.q_ref, bf16[4,128,384]{2,1,0:T(8,128)(2,1)} %get-tuple-element.151.kv_ref, ...), custom_call_target="tpu_custom_call" | custom-call | tf_op jit(solution)/shard_map/first_grads/pallas_call | solution.py:376
  289.6 2.5 dynamic-slice_bitcast_fusion
  293.3 2.8 collective-permute-done.26
  296.0 2.4 fusion.80
  298.6 3.2 collective-permute-start.32
  301.9 2.1 collective-permute-start.30
  313.0 2.3 collective-permute-start.34
  317.2 4.6 %collective-permute-done.34 = bf16[128,768]{1,0:T(8,128)(2,1)S(1)} collective-permute-done((bf16[128,768]{1,0:T(8,128)(2,1)S(1)}, bf16[128,768]{1,0:T(8,128)(2,1)S(1)}, u32[]{:S(2)}, u32[]{:S(2)}) %collective-permute-start.34) | collective-permute-done | bytes 196640 | tf_op jit(solution)/shard_map/ppermute | solution.py:466
  321.9 4.8 %collective-permute-done.36 = bf16[128,768]{1,0:T(8,128)(2,1)S(1)} collective-permute-done((bf16[128,768]{1,0:T(8,128)(2,1)S(1)}, bf16[128,768]{1,0:T(8,128)(2,1)S(1)}, u32[]{:S(2)}, u32[]{:S(2)}) %collective-permute-start.36) | collective-permute-done | bytes 196640 | tf_op jit(solution)/shard_map/ppermute | solution.py:466
  328.5 2.5 collective-permute-start.37
  335.7 2.6 collective-permute-start.38
  338.3 2.1 collective-permute-done.40
  342.2 1.9 fusion.45
  346.2 53.2 %all-gather.14.cloned.1.call-done = bf16[64,88,768]{2,1,0:T(8,128)(2,1)} async-done(((bf16[4,88,768]{2,1,0:T(8,128)(2,1)}), bf16[64,88,768]{2,1,0:T(8,128)(2,1)}) %all-gather.14.cloned.1.call-update) | async-done | bytes 8650768 | tf_op jit(solution)/shard_map/all_gather | solution.py:742
  399.4 14.8 %unpack_grads.1 = (f32[4,8,48,768]{3,2,1,0:T(8,128)}, f32[8,48,3072]{2,1,0:T(8,128)}, f32[16,24,2304]{2,1,0:T(8,128)}, f32[2,16,12,768]{3,2,1,0:T(8,128)}, f32[16,16,768]{2,1,0:T(8,128)}) custom-call(s32[2]{0:T(128)} %get-tuple-element.276.pos_ref, bf16[16,4,88,768]{3,2,1,0:T(8,128)(2,1)} %bitcast.149), custom_call_target="tpu_custom_call" | custom-call | tf_op jit(solution)/shard_map/unpack_grads/pallas_call | solution.py:429
  418.3 2.4 reshape.347
  (329 shorter events, 81.7 us)
Async XLA Ops:
  7.2 69.2 %all-gather.8.cloned.1.call-start = ((), (), s32[]{:S(2)}) async-start(), calls=%async_computation.1 | async-start | bytes 6684672 | tf_op jit(solution)/shard_map/all_gather | solution.py:616
  11.9 9.4 %collective-permute-start.3 = (f32[12,384]{1,0:T(8,128)S(1)}, f32[12,384]{1,0:T(8,128)S(1)}, u32[]{:S(2)}, u32[]{:S(2)}) collective-permute-start(f32[12,384]{1,0:T(8,128)S(1)} %concatenate.120), channel_id=1, source_target_pairs={{0,1},{1,0},{2,3},{3,2},{4,5},{5,4},{6,7},{7,6},{8,9},{9,8},{10,11... | collective-permute-start | bytes 55304 | tf_op jit(solution)/shard_map/ppermute | solution.py:462
  16.4 14.5 %collective-permute-start.4 = (bf16[384,640]{1,0:T(8,128)(2,1)S(1)}, bf16[384,640]{1,0:T(8,128)(2,1)S(1)}, u32[]{:S(2)}, u32[]{:S(2)}) collective-permute-start(bf16[384,640]{1,0:T(8,128)(2,1)S(1)} %concatenate.118), channel_id=1, source_target_pairs={{0,65},{1,64},{64,1},{65,0},{2,67},{3,66},{66,3},{67,2},{4,69},{5,... | collective-permute-start | bytes 1474568 | tf_op jit(solution)/shard_map/ppermute | solution.py:581
  16.9 7.6 %collective-permute-start.2 = (bf16[128,768]{1,0:T(8,128)(2,1)S(1)}, bf16[128,768]{1,0:T(8,128)(2,1)S(1)}, u32[]{:S(2)}, u32[]{:S(2)}) collective-permute-start(bf16[128,768]{1,0:T(8,128)(2,1)S(1)} %bitcast.165), channel_id=1, source_target_pairs={{0,96},{32,64},{64,32},{96,0},{1,97},{33,65},{65,33},{97,1},{2,98}... | collective-permute-start | bytes 589832 | tf_op jit(solution)/shard_map/ppermute | solution.py:466
  19.6 10.7 %collective-permute-start.1 = (bf16[128,768]{1,0:T(8,128)(2,1)S(1)}, bf16[128,768]{1,0:T(8,128)(2,1)S(1)}, u32[]{:S(2)}, u32[]{:S(2)}) collective-permute-start(bf16[128,768]{1,0:T(8,128)(2,1)S(1)} %bitcast.166), channel_id=1, source_target_pairs={{0,64},{32,96},{64,0},{96,32},{1,65},{33,97},{65,1},{97,33},{2,66}... | collective-permute-start | bytes 589832 | tf_op jit(solution)/shard_map/ppermute | solution.py:466
  20.8 9.5 %collective-permute-start = (bf16[128,768]{1,0:T(8,128)(2,1)S(1)}, bf16[128,768]{1,0:T(8,128)(2,1)S(1)}, u32[]{:S(2)}, u32[]{:S(2)}) collective-permute-start(bf16[128,768]{1,0:T(8,128)(2,1)S(1)} %bitcast.167), channel_id=1, source_target_pairs={{0,32},{32,0},{64,96},{96,64},{1,33},{33,1},{65,97},{97,65},{2,34}... | collective-permute-start | bytes 589832 | tf_op jit(solution)/shard_map/ppermute | solution.py:466
  30.9 311.3 %copy-start.42 = (f32[512]{0:T(512)}, f32[512]{0:T(512)S(1)}, u32[]{:S(2)}) copy-start(f32[512]{0:T(512)S(1)} %add_rsqrt_fusion.1) | copy-start | bytes 6148
  32.0 44.4 %copy-start.26 = (bf16[384,768]{1,0:T(8,128)(2,1)S(1)}, bf16[384,768]{1,0:T(8,128)(2,1)}, u32[]{:S(2)}) copy-start(bf16[384,768]{1,0:T(8,128)(2,1)} %param.22) | copy-start | bytes 1769476
  32.8 122.1 %all-gather.10.cloned.1.call-start = ((), (), s32[]{:S(2)}) async-start(), calls=%async_computation.3 | async-start | bytes 4456448 | tf_op jit(solution)/shard_map/all_gather | solution.py:617
  76.4 168.3 %all-gather.12.cloned.1.call-start = ((), (), s32[]{:S(2)}) async-start(), calls=%async_computation.4 | async-start | bytes 4456448 | tf_op jit(solution)/shard_map/all_gather | solution.py:679
  76.5 11.3 %collective-permute-start.5 = (bf16[192,768]{1,0:T(8,128)(2,1)S(1)}, bf16[192,768]{1,0:T(8,128)(2,1)}, u32[]{:S(2)}, u32[]{:S(2)}) collective-permute-start(bf16[192,768]{1,0:T(8,128)(2,1)S(1)} %constant_dynamic-slice_fusion.16), channel_id=1, source_target_pairs={{0,1},{1,0},{2,3},{3,2},{4,5},{5,4},{6,7},{7,6},{8,9},{9,8},{10,11... | collective-permute-start | bytes 884744 | tf_op jit(solution)/shard_map/ppermute | solution.py:462
  80.6 12.2 %collective-permute-start.7 = (bf16[192,768]{1,0:T(8,128)(2,1)S(1)}, bf16[192,768]{1,0:T(8,128)(2,1)S(1)}, u32[]{:S(2)}, u32[]{:S(2)}) collective-permute-start(bf16[192,768]{1,0:T(8,128)(2,1)S(1)} %fusion.55), channel_id=1, source_target_pairs={{0,1},{1,0},{2,3},{3,2},{4,5},{5,4},{6,7},{7,6},{8,9},{9,8},{10,11... | collective-permute-start | bytes 884744 | tf_op jit(solution)/shard_map/ppermute | solution.py:462
  81.8 17.3 %collective-permute-start.9 = (bf16[192,768]{1,0:T(8,128)(2,1)S(1)}, bf16[192,768]{1,0:T(8,128)(2,1)}, u32[]{:S(2)}, u32[]{:S(2)}) collective-permute-start(bf16[192,768]{1,0:T(8,128)(2,1)S(1)} %constant_dynamic-slice_fusion.13), channel_id=1, source_target_pairs={{0,1},{1,0},{2,3},{3,2},{4,5},{5,4},{6,7},{7,6},{8,9},{9,8},{10,11... | collective-permute-start | bytes 884744 | tf_op jit(solution)/shard_map/ppermute | solution.py:462
  84.8 16.9 %collective-permute-start.11 = (bf16[128,768]{1,0:T(8,128)(2,1)S(1)}, bf16[128,768]{1,0:T(8,128)(2,1)}, u32[]{:S(2)}, u32[]{:S(2)}) collective-permute-start(bf16[128,768]{1,0:T(8,128)(2,1)S(1)} %bitcast.161), channel_id=1, source_target_pairs={{0,32},{32,0},{64,96},{96,64},{1,33},{33,1},{65,97},{97,65},{2,34}... | collective-permute-start | bytes 589832 | tf_op jit(solution)/shard_map/ppermute | solution.py:466
  87.5 19.8 %collective-permute-start.12 = (bf16[128,768]{1,0:T(8,128)(2,1)S(1)}, bf16[128,768]{1,0:T(8,128)(2,1)}, u32[]{:S(2)}, u32[]{:S(2)}) collective-permute-start(bf16[128,768]{1,0:T(8,128)(2,1)S(1)} %bitcast.162), channel_id=1, source_target_pairs={{0,64},{32,96},{64,0},{96,32},{1,65},{33,97},{65,1},{97,33},{2,66}... | collective-permute-start | bytes 589832 | tf_op jit(solution)/shard_map/ppermute | solution.py:466
  87.8 26.2 %collective-permute-start.6 = (bf16[192,768]{1,0:T(8,128)(2,1)}, bf16[192,768]{1,0:T(8,128)(2,1)S(1)}, u32[]{:S(2)}, u32[]{:S(2)}) collective-permute-start(bf16[192,768]{1,0:T(8,128)(2,1)} %collective-permute-done.5), channel_id=1, source_target_pairs={{0,2},{2,0},{1,3},{3,1},{4,6},{6,4},{5,7},{7,5},{8,10},{10,8},{9,1... | collective-permute-start | bytes 884744 | tf_op jit(solution)/shard_map/ppermute | solution.py:462
  92.8 21.2 %collective-permute-start.8 = (bf16[192,768]{1,0:T(8,128)(2,1)S(1)}, bf16[192,768]{1,0:T(8,128)(2,1)S(1)}, u32[]{:S(2)}, u32[]{:S(2)}) collective-permute-start(bf16[192,768]{1,0:T(8,128)(2,1)S(1)} %collective-permute-done.7), channel_id=1, source_target_pairs={{0,2},{2,0},{1,3},{3,1},{4,6},{6,4},{5,7},{7,5},{8,10},{10,8},{9,1... | collective-permute-start | bytes 884744 | tf_op jit(solution)/shard_map/ppermute | solution.py:462
  99.2 14.9 %collective-permute-start.10 = (bf16[192,768]{1,0:T(8,128)(2,1)}, bf16[192,768]{1,0:T(8,128)(2,1)S(1)}, u32[]{:S(2)}, u32[]{:S(2)}) collective-permute-start(bf16[192,768]{1,0:T(8,128)(2,1)} %collective-permute-done.9), channel_id=1, source_target_pairs={{0,2},{2,0},{1,3},{3,1},{4,6},{6,4},{5,7},{7,5},{8,10},{10,8},{9,1... | collective-permute-start | bytes 884744 | tf_op jit(solution)/shard_map/ppermute | solution.py:462
  101.7 12.4 %collective-permute-start.13 = (bf16[128,768]{1,0:T(8,128)(2,1)S(1)}, bf16[128,768]{1,0:T(8,128)(2,1)S(1)}, u32[]{:S(2)}, u32[]{:S(2)}) collective-permute-start(bf16[128,768]{1,0:T(8,128)(2,1)S(1)} %bitcast.163), channel_id=1, source_target_pairs={{0,96},{32,64},{64,32},{96,0},{1,97},{33,65},{65,33},{97,1},{2,98}... | collective-permute-start | bytes 589832 | tf_op jit(solution)/shard_map/ppermute | solution.py:466
  137.9 11.3 %collective-permute-start.14 = (bf16[4,128,256]{2,1,0:T(8,128)(2,1)}, bf16[4,128,256]{2,1,0:T(8,128)(2,1)S(1)}, u32[]{:S(2)}, u32[]{:S(2)}) collective-permute-start(bf16[4,128,256]{2,1,0:T(8,128)(2,1)} %get-tuple-element.135.attn_ref), channel_id=1, source_target_pairs={{0,32},{32,0},{64,96},{96,64},{1,33},{33,1},{65,97},{97,65},{2,34}... | collective-permute-start | bytes 786440 | tf_op jit(solution)/shard_map/ppermute | solution.py:466
  141.6 7.6 %collective-permute-start.15 = (bf16[4,128,256]{2,1,0:T(8,128)(2,1)}, bf16[4,128,256]{2,1,0:T(8,128)(2,1)S(1)}, u32[]{:S(2)}, u32[]{:S(2)}) collective-permute-start(bf16[4,128,256]{2,1,0:T(8,128)(2,1)} %get-tuple-element.135.attn_ref), channel_id=1, source_target_pairs={{0,64},{32,96},{64,0},{96,32},{1,65},{33,97},{65,1},{97,33},{2,66}... | collective-permute-start | bytes 786440 | tf_op jit(solution)/shard_map/ppermute | solution.py:466
  142.4 12.6 %collective-permute-start.16 = (bf16[4,128,256]{2,1,0:T(8,128)(2,1)}, bf16[4,128,256]{2,1,0:T(8,128)(2,1)}, u32[]{:S(2)}, u32[]{:S(2)}) collective-permute-start(bf16[4,128,256]{2,1,0:T(8,128)(2,1)} %get-tuple-element.135.attn_ref), channel_id=1, source_target_pairs={{0,96},{32,64},{64,32},{96,0},{1,97},{33,65},{65,33},{97,1},{2,98}... | collective-permute-start | bytes 786440 | tf_op jit(solution)/shard_map/ppermute | solution.py:466
  162.5 10.8 %collective-permute-start.17 = (f32[128,768]{1,0:T(8,128)S(1)}, f32[128,768]{1,0:T(8,128)S(1)}, u32[]{:S(2)}, u32[]{:S(2)}) collective-permute-start(f32[128,768]{1,0:T(8,128)S(1)} %get-tuple-element.217), channel_id=1, source_target_pairs={{0,32},{32,0},{64,96},{96,64},{1,33},{33,1},{65,97},{97,65},{2,34}... | collective-permute-start | bytes 1179656 | tf_op jit(solution)/shard_map/ppermute | solution.py:466
  163.8 9.5 %collective-permute-start.18 = (f32[128,768]{1,0:T(8,128)S(1)}, f32[128,768]{1,0:T(8,128)S(1)}, u32[]{:S(2)}, u32[]{:S(2)}) collective-permute-start(f32[128,768]{1,0:T(8,128)S(1)} %get-tuple-element.216), channel_id=1, source_target_pairs={{0,64},{32,96},{64,0},{96,32},{1,65},{33,97},{65,1},{97,33},{2,66}... | collective-permute-start | bytes 1179656 | tf_op jit(solution)/shard_map/ppermute | solution.py:466
  165.2 14.9 %collective-permute-start.19 = (f32[128,768]{1,0:T(8,128)S(1)}, f32[128,768]{1,0:T(8,128)S(1)}, u32[]{:S(2)}, u32[]{:S(2)}) collective-permute-start(f32[128,768]{1,0:T(8,128)S(1)} %get-tuple-element.215), channel_id=1, source_target_pairs={{0,96},{32,64},{64,32},{96,0},{1,97},{33,65},{65,33},{97,1},{2,98}... | collective-permute-start | bytes 1179656 | tf_op jit(solution)/shard_map/ppermute | solution.py:466
  180.5 9.3 %collective-permute-start.20 = (bf16[128,768]{1,0:T(8,128)(2,1)S(1)}, bf16[128,768]{1,0:T(8,128)(2,1)S(1)}, u32[]{:S(2)}, u32[]{:S(2)}) collective-permute-start(bf16[128,768]{1,0:T(8,128)(2,1)S(1)} %get-tuple-element.127), channel_id=1, source_target_pairs={{0,32},{32,0},{64,96},{96,64},{1,33},{33,1},{65,97},{97,65},{2,34}... | collective-permute-start | bytes 589832 | tf_op jit(solution)/shard_map/ppermute | solution.py:466
  184.5 5.3 %collective-permute-start.21 = (bf16[128,768]{1,0:T(8,128)(2,1)S(1)}, bf16[128,768]{1,0:T(8,128)(2,1)S(1)}, u32[]{:S(2)}, u32[]{:S(2)}) collective-permute-start(bf16[128,768]{1,0:T(8,128)(2,1)S(1)} %get-tuple-element.127), channel_id=1, source_target_pairs={{0,64},{32,96},{64,0},{96,32},{1,65},{33,97},{65,1},{97,33},{2,66}... | collective-permute-start | bytes 589832 | tf_op jit(solution)/shard_map/ppermute | solution.py:466
  184.5 8.7 %collective-permute-start.22 = (bf16[128,768]{1,0:T(8,128)(2,1)S(1)}, bf16[128,768]{1,0:T(8,128)(2,1)S(1)}, u32[]{:S(2)}, u32[]{:S(2)}) collective-permute-start(bf16[128,768]{1,0:T(8,128)(2,1)S(1)} %get-tuple-element.127), channel_id=1, source_target_pairs={{0,96},{32,64},{64,32},{96,0},{1,97},{33,65},{65,33},{97,1},{2,98}... | collective-permute-start | bytes 589832 | tf_op jit(solution)/shard_map/ppermute | solution.py:466
  197.5 129.2 %reduce-scatter.2.cloned.1.call-start = ((), (), s32[]{:S(2)}) async-start(), calls=%async_computation.2 | async-start | bytes 5849088 | tf_op jit(solution)/shard_map/reduce_scatter | solution.py:713
  244.7 154.7 %all-gather.14.cloned.1.call-start = ((), (), s32[]{:S(2)}) async-start(), calls=%async_computation.5 | async-start | bytes 9191424 | tf_op jit(solution)/shard_map/all_gather | solution.py:742
  248.1 35.6 %collective-permute-start.23 = (bf16[128,768]{1,0:T(8,128)(2,1)S(1)}, bf16[128,768]{1,0:T(8,128)(2,1)S(1)}, u32[]{:S(2)}, u32[]{:S(2)}) collective-permute-start(bf16[128,768]{1,0:T(8,128)(2,1)S(1)} %copy-done.39), channel_id=1, source_target_pairs={{0,32},{32,0},{64,96},{96,64},{1,33},{33,1},{65,97},{97,65},{2,34}... | collective-permute-start | bytes 589832 | tf_op jit(solution)/shard_map/ppermute | solution.py:466
  250.3 33.4 %collective-permute-start.24 = (bf16[128,768]{1,0:T(8,128)(2,1)S(1)}, bf16[128,768]{1,0:T(8,128)(2,1)S(1)}, u32[]{:S(2)}, u32[]{:S(2)}) collective-permute-start(bf16[128,768]{1,0:T(8,128)(2,1)S(1)} %copy-done.38), channel_id=1, source_target_pairs={{0,64},{32,96},{64,0},{96,32},{1,65},{33,97},{65,1},{97,33},{2,66}... | collective-permute-start | bytes 589832 | tf_op jit(solution)/shard_map/ppermute | solution.py:466
  251.6 32.2 %collective-permute-start.25 = (bf16[128,768]{1,0:T(8,128)(2,1)S(1)}, bf16[128,768]{1,0:T(8,128)(2,1)S(1)}, u32[]{:S(2)}, u32[]{:S(2)}) collective-permute-start(bf16[128,768]{1,0:T(8,128)(2,1)S(1)} %get-tuple-element.150), channel_id=1, source_target_pairs={{0,96},{32,64},{64,32},{96,0},{1,97},{33,65},{65,33},{97,1},{2,98}... | collective-permute-start | bytes 589832 | tf_op jit(solution)/shard_map/ppermute | solution.py:466
  292.1 4.0 collective-permute-start.26
  298.5 6.9 %collective-permute-start.33 = (bf16[56,640]{1,0:T(8,128)(2,1)S(1)}, bf16[56,640]{1,0:T(8,128)(2,1)S(1)}, u32[]{:S(2)}, u32[]{:S(2)}) collective-permute-start(bf16[56,640]{1,0:T(8,128)(2,1)S(1)} %get-tuple-element.245), channel_id=1, source_target_pairs={{0,28},{4,24},{8,20},{12,16},{16,12},{20,8},{24,4},{28,0},{1,29},{... | collective-permute-start | bytes 215048 | tf_op jit(solution)/shard_map/ppermute | solution.py:533
  298.6 7.7 %collective-permute-start.32 = (bf16[56,640]{1,0:T(8,128)(2,1)S(1)}, bf16[56,640]{1,0:T(8,128)(2,1)S(1)}, u32[]{:S(2)}, u32[]{:S(2)}) collective-permute-start(bf16[56,640]{1,0:T(8,128)(2,1)S(1)} %get-tuple-element.246), channel_id=1, source_target_pairs={{0,24},{4,28},{8,16},{12,20},{16,8},{20,12},{24,0},{28,4},{1,25},{... | collective-permute-start | bytes 215048 | tf_op jit(solution)/shard_map/ppermute | solution.py:533
  301.9 5.8 %collective-permute-start.31 = (bf16[56,640]{1,0:T(8,128)(2,1)S(1)}, bf16[56,640]{1,0:T(8,128)(2,1)S(1)}, u32[]{:S(2)}, u32[]{:S(2)}) collective-permute-start(bf16[56,640]{1,0:T(8,128)(2,1)S(1)} %get-tuple-element.247), channel_id=1, source_target_pairs={{0,20},{4,16},{8,28},{12,24},{16,4},{20,0},{24,12},{28,8},{1,21},{... | collective-permute-start | bytes 215048 | tf_op jit(solution)/shard_map/ppermute | solution.py:533
  301.9 6.7 %collective-permute-start.30 = (bf16[56,640]{1,0:T(8,128)(2,1)S(1)}, bf16[56,640]{1,0:T(8,128)(2,1)S(1)}, u32[]{:S(2)}, u32[]{:S(2)}) collective-permute-start(bf16[56,640]{1,0:T(8,128)(2,1)S(1)} %get-tuple-element.248), channel_id=1, source_target_pairs={{0,16},{4,20},{8,24},{12,28},{16,0},{20,4},{24,8},{28,12},{1,17},{... | collective-permute-start | bytes 215048 | tf_op jit(solution)/shard_map/ppermute | solution.py:533
  303.9 5.2 %collective-permute-start.29 = (bf16[56,640]{1,0:T(8,128)(2,1)S(1)}, bf16[56,640]{1,0:T(8,128)(2,1)S(1)}, u32[]{:S(2)}, u32[]{:S(2)}) collective-permute-start(bf16[56,640]{1,0:T(8,128)(2,1)S(1)} %get-tuple-element.249), channel_id=1, source_target_pairs={{0,12},{4,8},{8,4},{12,0},{16,28},{20,24},{24,20},{28,16},{1,13},{... | collective-permute-start | bytes 215048 | tf_op jit(solution)/shard_map/ppermute | solution.py:533
  305.4 5.2 %collective-permute-start.28 = (bf16[56,640]{1,0:T(8,128)(2,1)S(1)}, bf16[56,640]{1,0:T(8,128)(2,1)S(1)}, u32[]{:S(2)}, u32[]{:S(2)}) collective-permute-start(bf16[56,640]{1,0:T(8,128)(2,1)S(1)} %get-tuple-element.250), channel_id=1, source_target_pairs={{0,8},{4,12},{8,0},{12,4},{16,24},{20,28},{24,16},{28,20},{1,9},{5... | collective-permute-start | bytes 215048 | tf_op jit(solution)/shard_map/ppermute | solution.py:533
  306.3 5.6 %collective-permute-start.27 = (bf16[56,640]{1,0:T(8,128)(2,1)S(1)}, bf16[56,640]{1,0:T(8,128)(2,1)S(1)}, u32[]{:S(2)}, u32[]{:S(2)}) collective-permute-start(bf16[56,640]{1,0:T(8,128)(2,1)S(1)} %get-tuple-element.244), channel_id=1, source_target_pairs={{0,4},{4,0},{8,12},{12,8},{16,20},{20,16},{24,28},{28,24},{1,5},{5... | collective-permute-start | bytes 215048 | tf_op jit(solution)/shard_map/ppermute | solution.py:533
  313.0 8.9 %collective-permute-start.34 = (bf16[128,768]{1,0:T(8,128)(2,1)S(1)}, bf16[128,768]{1,0:T(8,128)(2,1)S(1)}, u32[]{:S(2)}, u32[]{:S(2)}) collective-permute-start(bf16[128,768]{1,0:T(8,128)(2,1)S(1)} %get-tuple-element.237), channel_id=1, source_target_pairs={{0,32},{32,0},{64,96},{96,64},{1,33},{33,1},{65,97},{97,65},{2,34}... | collective-permute-start | bytes 589832 | tf_op jit(solution)/shard_map/ppermute | solution.py:466
  315.3 6.6 %collective-permute-start.35 = (bf16[128,768]{1,0:T(8,128)(2,1)S(1)}, bf16[128,768]{1,0:T(8,128)(2,1)S(1)}, u32[]{:S(2)}, u32[]{:S(2)}) collective-permute-start(bf16[128,768]{1,0:T(8,128)(2,1)S(1)} %get-tuple-element.236), channel_id=1, source_target_pairs={{0,64},{32,96},{64,0},{96,32},{1,65},{33,97},{65,1},{97,33},{2,66}... | collective-permute-start | bytes 589832 | tf_op jit(solution)/shard_map/ppermute | solution.py:466
  316.6 10.1 %collective-permute-start.36 = (bf16[128,768]{1,0:T(8,128)(2,1)S(1)}, bf16[128,768]{1,0:T(8,128)(2,1)S(1)}, u32[]{:S(2)}, u32[]{:S(2)}) collective-permute-start(bf16[128,768]{1,0:T(8,128)(2,1)S(1)} %get-tuple-element.235), channel_id=1, source_target_pairs={{0,96},{32,64},{64,32},{96,0},{1,97},{33,65},{65,33},{97,1},{2,98}... | collective-permute-start | bytes 589832 | tf_op jit(solution)/shard_map/ppermute | solution.py:466
  328.5 5.4 %collective-permute-start.37 = (bf16[88,768]{1,0:T(8,128)(2,1)S(1)}, bf16[88,768]{1,0:T(8,128)(2,1)S(1)}, u32[]{:S(2)}, u32[]{:S(2)}) collective-permute-start(bf16[88,768]{1,0:T(8,128)(2,1)S(1)} %pad_maximum_fusion.14), channel_id=1, source_target_pairs={{0,1},{1,0},{2,3},{3,2},{4,5},{5,4},{6,7},{7,6},{8,9},{9,8},{10,11... | collective-permute-start | bytes 405512 | tf_op jit(solution)/shard_map/ppermute | solution.py:462
  334.0 6.3 %collective-permute-start.40 = (bf16[88,768]{1,0:T(8,128)(2,1)S(1)}, bf16[88,768]{1,0:T(8,128)(2,1)S(1)}, u32[]{:S(2)}, u32[]{:S(2)}) collective-permute-start(bf16[88,768]{1,0:T(8,128)(2,1)S(1)} %fusion.56), channel_id=1, source_target_pairs={{0,96},{32,64},{64,32},{96,0},{1,97},{33,65},{65,33},{97,1},{2,98}... | collective-permute-start | bytes 405512 | tf_op jit(solution)/shard_map/ppermute | solution.py:466
  334.7 5.7 %collective-permute-start.39 = (bf16[88,768]{1,0:T(8,128)(2,1)S(1)}, bf16[88,768]{1,0:T(8,128)(2,1)S(1)}, u32[]{:S(2)}, u32[]{:S(2)}) collective-permute-start(bf16[88,768]{1,0:T(8,128)(2,1)S(1)} %fusion.56), channel_id=1, source_target_pairs={{0,64},{32,96},{64,0},{96,32},{1,65},{33,97},{65,1},{97,33},{2,66}... | collective-permute-start | bytes 405512 | tf_op jit(solution)/shard_map/ppermute | solution.py:466
  335.7 5.6 %collective-permute-start.38 = (bf16[88,768]{1,0:T(8,128)(2,1)S(1)}, bf16[88,768]{1,0:T(8,128)(2,1)S(1)}, u32[]{:S(2)}, u32[]{:S(2)}) collective-permute-start(bf16[88,768]{1,0:T(8,128)(2,1)S(1)} %fusion.56), channel_id=1, source_target_pairs={{0,32},{32,0},{64,96},{96,64},{1,33},{33,1},{65,97},{97,65},{2,34}... | collective-permute-start | bytes 405512 | tf_op jit(solution)/shard_map/ppermute | solution.py:466
  (56 other events, 282.2 us)
Sparse Core Ops, SparseCore 0:
  33.0 43.3 all-gather.7
  78.1 42.7 all-gather.9
  197.6 46.9 all-gather.11
  246.9 70.9 reduce-scatter.1
  342.2 57.1 all-gather.13

commit v6 on v5

--- a/solution.py
+++ b/solution.py
@@ -537,11 +537,10 @@
     core = lax.axis_index("core")
     block = lax.axis_index(BLOCKS)
     pair = pick(local, core) + swap(pick(local, 1 - core), "core")
-    low = pair.astype(BF16)
-    moved = [to_block(pick(low, block ^ r), r) for r in range(1, 8)]
+    moved = [to_block(pick(pair, block ^ r), r) for r in range(1, 8)]
     total = pick(pair, block)
     for values in moved:
-        total = total + values.astype(F32)
+        total = total + values
     return total
 
 
@@ -614,7 +613,7 @@
     q_scaled = (projected[:, :256].astype(BF16) * 0.125).astype(BF16).reshape(4, 128, 256)
     kv_own = projected[:, 256:].astype(BF16).reshape(4, 128, 384)
     kv_all = lax.all_gather(kv_own, SEQ_AXES, axis=0, tiled=False)
-    q_all = lax.all_gather(after(q_scaled, kv_all), SEQ_AXES, axis=0, tiled=False)
+    q_all = lax.all_gather(q_scaled, SEQ_AXES, axis=0, tiled=False)
     normed_one_t = normed_one.T
     cot_ranks = tuple(gather_ranks(out_grad[0]))
     kv_all, fetched, cot_ranks, normed_one_t = lax.optimization_barrier(
@@ -736,8 +735,7 @@
             axis=0,
         )
 
-    totals = rows_of(fs) + swap(rows_of(1 - fs).astype(BF16), "fsdp").astype(F32)
-    totals = totals.astype(BF16)
+    totals = (rows_of(fs) + swap(rows_of(1 - fs), "fsdp")).astype(BF16)
     totals = jnp.stack(gather_ranks(totals))
     totals = lax.all_gather(totals, SEQ_AXES, axis=0, tiled=False)
     output = (

time: 431 us -> 410 us (0.951)
  waiting for transfers between devices: 178 us -> 164 us
  starting transfers between devices: 66.5 us -> 61.7 us
    all_gather x1, waiting for transfers between devices: 42.7 us -> 11.4 us  [body(): kv_all = lax.all_gather(kv_own, SEQ_AXES, axis=0, tiled=False)]
    ppermute x7, waiting for transfers between devices: 5.7 us -> 15 us  [to_block(): return lax.ppermute(values, BLOCKS, [(a, a ^ offset) for a in range(8)])]
    all_gather x1, waiting for transfers between devices: 15.9 us -> 6.77 us  [body(): do_all = lax.all_gather(after(do_aug, q_all), SEQ_AXES, axis=0, tiled=False)]
    all_gather x1, waiting for transfers between devices: 0.01 us -> 6.96 us  [body(): q_all = lax.all_gather(q_scaled, SEQ_AXES, axis=0, tiled=False)]
    ppermute x24, waiting for transfers between devices: 48.6 us -> 55.3 us  [to_rank(): return lax.ppermute(values, TP, [(a, a ^ offset) for a in range(4)])]
    ppermute x9, waiting for transfers between devices: 12 us -> 17.9 us  [swap(): return lax.ppermute(values, axis, [(0, 1), (1, 0)])]
    ppermute x24, starting transfers between devices: 38.5 us -> 32.9 us  [to_rank(): return lax.ppermute(values, TP, [(a, a ^ offset) for a in range(4)])]
  transfers between devices with their start and end apart: 46 -> 46, of which waited for: 23 -> 26; matrix products, arithmetic and copies ran while one was open for 10% -> 10% of each run, Pallas kernels for 18% -> 19%
where the time goes in v6:
time: 410 us; the launch traced here: 408 us
  waiting for transfers between devices  164 us (40%)
  Pallas kernels  95.3 us (23%)
  starting transfers between devices  61.7 us (15%)
  local copies, waits for them, and re-layouts  37.5 us (9%)
  other arithmetic  25.4 us (6%)
  between operations  15 us (4%)
  matrix products  9.17 us (2%)
    ppermute x24, waiting for transfers between devices, to_rank(): return lax.ppermute(values, TP, [(a, a ^ offset) for a in range(4)])  55.3 us
    all_gather x1, waiting for transfers between devices, body(): totals = lax.all_gather(totals, SEQ_AXES, axis=0, tiled=False)  50.8 us
    ppermute x24, starting transfers between devices, to_rank(): return lax.ppermute(values, TP, [(a, a ^ offset) for a in range(4)])  32.9 us
    pallas_call x1, Pallas kernels, key_grad(): pl.pallas_call(key_grad_kernel, out_shape=(jax.ShapeDtypeStruct((4, 128,...  31.4 us
    pallas_call x1, Pallas kernels, query_grad(): pl.pallas_call(query_grad_kernel, out_shape=(jax.ShapeDtypeStruct((4, 128...  20 us
    ppermute x9, starting transfers between devices, swap(): return lax.ppermute(values, axis, [(0, 1), (1, 0)])  20 us
    pallas_call x1, Pallas kernels, forward_attention(): pl.pallas_call(forward_kernel, out_shape=(jax.ShapeDtypeStruct((4, 128, 2...  20 us
    ppermute x9, waiting for transfers between devices, swap(): return lax.ppermute(values, axis, [(0, 1), (1, 0)])  17.9 us
  transfers between devices with their start and end apart: 46, of which 26 were waited for; matrix products, arithmetic and copies ran while one was open for 10% of the time, Pallas kernels for 19%

profile of v6, /device:TPU:1, one launch (start us, length us, event | category | flops | bytes accessed | tf_op | source)
XLA Modules:
  0.0 408.3 jit_solution(6439580200742591032)
XLA Ops:
  11.9 4.5 %collective-permute-start.3 = (f32[12,384]{1,0:T(8,128)S(1)}, f32[12,384]{1,0:T(8,128)S(1)}, u32[]{:S(2)}, u32[]{:S(2)}) collective-permute-start(f32[12,384]{1,0:T(8,128)S(1)} %concatenate.119), channel_id=1, source_target_pairs={{0,1},{1,0},{2,3},{3,2},{4,5},{5,4},{6,7},{7,6},{8,9},{9,8},{10,11... | collective-permute-start | bytes 55304 | tf_op jit(solution)/shard_map/ppermute | solution.py:462
  16.9 2.8 collective-permute-start.2
  21.8 2.7 collective-permute-done.2
  24.4 5.9 %collective-permute-done.1 = bf16[128,768]{1,0:T(8,128)(2,1)S(1)} collective-permute-done((bf16[128,768]{1,0:T(8,128)(2,1)S(1)}, bf16[128,768]{1,0:T(8,128)(2,1)S(1)}, u32[]{:S(2)}, u32[]{:S(2)}) %collective-permute-start.1) | collective-permute-done | bytes 196640 | tf_op jit(solution)/shard_map/ppermute | solution.py:466
  33.7 2.2 collective-permute-start.5
  39.1 2.2 collective-permute-start.9
  43.5 2.3 collective-permute-start.6
  45.8 4.0 collective-permute-done.7
  49.8 2.2 collective-permute-start.8
  52.0 4.1 %collective-permute-done.9 = bf16[192,768]{1,0:T(8,128)(2,1)} collective-permute-done((bf16[192,768]{1,0:T(8,128)(2,1)S(1)}, bf16[192,768]{1,0:T(8,128)(2,1)}, u32[]{:S(2)}, u32[]{:S(2)}) %collective-permute-start.9) | collective-permute-done | bytes 294944 | tf_op jit(solution)/shard_map/ppermute | solution.py:462
  56.1 2.3 collective-permute-start.10
  59.2 2.3 collective-permute-start.13
  63.3 9.3 %collective-permute-done.13 = bf16[128,768]{1,0:T(8,128)(2,1)S(1)} collective-permute-done((bf16[128,768]{1,0:T(8,128)(2,1)S(1)}, bf16[128,768]{1,0:T(8,128)(2,1)S(1)}, u32[]{:S(2)}, u32[]{:S(2)}) %collective-permute-start.13) | collective-permute-done | bytes 196640 | tf_op jit(solution)/shard_map/ppermute | solution.py:466
  73.3 11.4 %all-gather.7.cloned.1.call-done.kv_ref = bf16[16,4,128,384]{3,2,1,0:T(8,128)(2,1)} async-done(((bf16[1,4,128,384]{3,2,1,0:T(8,128)(2,1)}), bf16[16,4,128,384]{3,2,1,0:T(8,128)(2,1)}) %all-gather.7.cloned.1.call-update) | async-done | bytes 6291472 | tf_op jit(solution)/shard_map/all_gather | solution.py:615
  88.4 20.0 %attention_forward.1 = (bf16[4,128,256]{2,1,0:T(8,128)(2,1)}, f32[4,384,128]{2,1,0:T(8,128)}) custom-call(s32[2]{0:T(128)} %get-tuple-element.273.pos_ref, bf16[4,128,256]{2,1,0:T(8,128)(2,1)} %bitcast.176, bf16[16,4,128,384]{3,2,1,0:T(8,128)(2,1)} %all-gather.7.cloned.1.call-done.kv_ref), custom_call_target="tpu_custom_call" | custom-call | flops 3221225472 | bytes 8388608 | tf_op jit(solution)/shard_map/attention_forward/pallas_call | solution.py:125
  108.4 2.2 collective-permute-start.14
  119.6 7.0 %all-gather.9.cloned.1.call-done.qg_ref = bf16[16,4,128,256]{3,2,1,0:T(8,128)(2,1)} async-done(((bf16[1,4,128,256]{3,2,1,0:T(8,128)(2,1)}), bf16[16,4,128,256]{3,2,1,0:T(8,128)(2,1)}) %all-gather.9.cloned.1.call-update) | async-done | bytes 4194320 | tf_op jit(solution)/shard_map/all_gather | solution.py:616
  126.6 5.2 %collective-permute-done.16 = bf16[4,128,256]{2,1,0:T(8,128)(2,1)} collective-permute-done((bf16[4,128,256]{2,1,0:T(8,128)(2,1)}, bf16[4,128,256]{2,1,0:T(8,128)(2,1)}, u32[]{:S(2)}, u32[]{:S(2)}) %collective-permute-start.16) | collective-permute-done | bytes 262176 | tf_op jit(solution)/shard_map/ppermute | solution.py:466
  140.2 2.8 collective-permute-start.19
  144.7 5.9 %collective-permute-done.17 = f32[128,768]{1,0:T(8,128)S(1)} collective-permute-done((f32[128,768]{1,0:T(8,128)S(1)}, f32[128,768]{1,0:T(8,128)S(1)}, u32[]{:S(2)}, u32[]{:S(2)}) %collective-permute-start.17) | collective-permute-done | bytes 393248 | tf_op jit(solution)/shard_map/ppermute | solution.py:466
  150.6 8.7 %collective-permute-done.19 = f32[128,768]{1,0:T(8,128)S(1)} collective-permute-done((f32[128,768]{1,0:T(8,128)S(1)}, f32[128,768]{1,0:T(8,128)S(1)}, u32[]{:S(2)}, u32[]{:S(2)}) %collective-permute-start.19) | collective-permute-done | bytes 393248 | tf_op jit(solution)/shard_map/ppermute | solution.py:466
  161.6 2.4 collective-permute-start.22
  164.7 2.9 pad.5
  167.7 3.5 collective-permute-done.22
  172.1 3.3 attention_grad_rows.1
  178.1 20.0 %attention_query_grad.1 = (bf16[4,128,256]{2,1,0:T(8,128)(2,1)}, f32[1,256]{1,0:T(1,128)}) custom-call(s32[2]{0:T(128)} %get-tuple-element.273.pos_ref, bf16[4,128,256]{2,1,0:T(8,128)(2,1)} %bitcast.177, bf16[4,128,256]{2,1,0:T(8,128)(2,1)} %get-tuple-element.139.do_ref, f32[4,384,128]{2,1,0:T(8,128)} %get-tuple-element.129.lse_ref, ...), custom_call_target="tpu_custom_call" | custom-call | flops 4831838208 | bytes 8388608 | tf_op jit(solution)/shard_map/attention_query_grad/pallas_call | solution.py:228
  202.9 1.9 fusion.85
  206.6 6.8 %all-gather.11.cloned.1.call-done = bf16[64,128,256]{2,1,0:T(8,128)(2,1)} async-done(((bf16[4,128,256]{2,1,0:T(8,128)(2,1)}), bf16[64,128,256]{2,1,0:T(8,128)(2,1)}) %all-gather.11.cloned.1.call-update) | async-done | bytes 4194320 | tf_op jit(solution)/shard_map/all_gather | solution.py:678
  216.8 2.4 collective-permute-start.23
  221.0 31.4 %attention_key_grad.1 = (bf16[4,128,384]{2,1,0:T(8,128)(2,1)}, f32[1,384]{1,0:T(1,128)}) custom-call(s32[2]{0:T(128)} %get-tuple-element.273.pos_ref, bf16[4,128,384]{2,1,0:T(8,128)(2,1)} %bitcast.174, bf16[16,4,128,256]{3,2,1,0:T(8,128)(2,1)} %all-gather.9.cloned.1.call-done.qg_ref, bf16[16,4,128,256]{3,2,1,0:T(8,128)(2,1)} %bitcast.189), custom_call_target="tpu_custom_call" | custom-call | flops 6442450944 | bytes 10485760 | tf_op jit(solution)/shard_map/attention_key_grad/pallas_call | solution.py:317
  252.4 5.7 %first_grads.1 = (f32[2,8,56,640]{3,2,1,0:T(8,128)}, f32[128,768]{1,0:T(8,128)}, bf16[3,128,768]{2,1,0:T(8,128)(2,1)}) custom-call(bf16[768,512]{1,0:T(8,128)(2,1)} %copy.35.norm_ref, f32[512,768]{1,0:T(8,128)} %get-tuple-element.229.hat_ref, bf16[4,128,256]{2,1,0:T(8,128)(2,1)} %get-tuple-element.143.q_ref, bf16[4,128,384]{2,1,0:T(8,128)(2,1)} %get-tuple-element.149.kv_ref, ...), custom_call_target="tpu_custom_call" | custom-call | tf_op jit(solution)/shard_map/first_grads/pallas_call | solution.py:376
  260.8 2.4 collective-permute-done.26
  265.4 3.7 collective-permute-start.32
  270.7 4.3 %collective-permute-done.33 = f32[56,640]{1,0:T(8,128)S(1)} collective-permute-done((f32[56,640]{1,0:T(8,128)S(1)}, f32[56,640]{1,0:T(8,128)S(1)}, u32[]{:S(2)}, u32[]{:S(2)}) %collective-permute-start.33) | collective-permute-done | bytes 143392 | tf_op jit(solution)/shard_map/ppermute | solution.py:533
  275.0 2.2 collective-permute-done.32
  277.2 2.6 collective-permute-start.27
  279.8 5.4 %collective-permute-done.30 = f32[56,640]{1,0:T(8,128)} collective-permute-done((f32[56,640]{1,0:T(8,128)}, f32[56,640]{1,0:T(8,128)}, u32[]{:S(2)}, u32[]{:S(2)}) %collective-permute-start.30) | collective-permute-done | bytes 143392 | tf_op jit(solution)/shard_map/ppermute | solution.py:533
  285.2 3.1 collective-permute-done.29
  289.7 2.4 collective-permute-start.34
  293.9 3.3 collective-permute-done.34
  297.7 4.9 %collective-permute-done.36 = bf16[128,768]{1,0:T(8,128)(2,1)S(1)} collective-permute-done((bf16[128,768]{1,0:T(8,128)(2,1)S(1)}, bf16[128,768]{1,0:T(8,128)(2,1)S(1)}, u32[]{:S(2)}, u32[]{:S(2)}) %collective-permute-start.36) | collective-permute-done | bytes 196640 | tf_op jit(solution)/shard_map/ppermute | solution.py:466
  304.5 2.2 collective-permute-start.37
  306.7 6.2 %collective-permute-done.37 = f32[88,768]{1,0:T(8,128)S(1)} collective-permute-done((f32[88,768]{1,0:T(8,128)S(1)}, f32[88,768]{1,0:T(8,128)S(1)}, u32[]{:S(2)}, u32[]{:S(2)}) %collective-permute-start.37) | collective-permute-done | bytes 270368 | tf_op jit(solution)/shard_map/ppermute | solution.py:462
  317.2 2.2 collective-permute-done.40
  320.1 2.6 collective-permute-done.38
  327.7 50.8 %all-gather.13.cloned.1.call-done = bf16[64,88,768]{2,1,0:T(8,128)(2,1)} async-done(((bf16[4,88,768]{2,1,0:T(8,128)(2,1)}), bf16[64,88,768]{2,1,0:T(8,128)(2,1)}) %all-gather.13.cloned.1.call-update) | async-done | bytes 8650768 | tf_op jit(solution)/shard_map/all_gather | solution.py:740
  378.5 14.8 %unpack_grads.1 = (f32[4,8,48,768]{3,2,1,0:T(8,128)}, f32[8,48,3072]{2,1,0:T(8,128)}, f32[16,24,2304]{2,1,0:T(8,128)}, f32[2,16,12,768]{3,2,1,0:T(8,128)}, f32[16,16,768]{2,1,0:T(8,128)}) custom-call(s32[2]{0:T(128)} %get-tuple-element.274.pos_ref, bf16[16,4,88,768]{3,2,1,0:T(8,128)(2,1)} %bitcast.148), custom_call_target="tpu_custom_call" | custom-call | tf_op jit(solution)/shard_map/unpack_grads/pallas_call | solution.py:429
  397.4 2.4 reshape.347
  (312 shorter events, 87.6 us)
Async XLA Ops:
  7.2 77.5 %all-gather.7.cloned.1.call-start = ((), (), s32[]{:S(2)}) async-start(), calls=%async_computation.1 | async-start | bytes 6684672 | tf_op jit(solution)/shard_map/all_gather | solution.py:615
  11.9 9.4 %collective-permute-start.3 = (f32[12,384]{1,0:T(8,128)S(1)}, f32[12,384]{1,0:T(8,128)S(1)}, u32[]{:S(2)}, u32[]{:S(2)}) collective-permute-start(f32[12,384]{1,0:T(8,128)S(1)} %concatenate.119), channel_id=1, source_target_pairs={{0,1},{1,0},{2,3},{3,2},{4,5},{5,4},{6,7},{7,6},{8,9},{9,8},{10,11... | collective-permute-start | bytes 55304 | tf_op jit(solution)/shard_map/ppermute | solution.py:462
  16.4 14.5 %collective-permute-start.4 = (bf16[384,640]{1,0:T(8,128)(2,1)S(1)}, bf16[384,640]{1,0:T(8,128)(2,1)S(1)}, u32[]{:S(2)}, u32[]{:S(2)}) collective-permute-start(bf16[384,640]{1,0:T(8,128)(2,1)S(1)} %concatenate.117), channel_id=1, source_target_pairs={{0,65},{1,64},{64,1},{65,0},{2,67},{3,66},{66,3},{67,2},{4,69},{5,... | collective-permute-start | bytes 1474568 | tf_op jit(solution)/shard_map/ppermute | solution.py:580
  16.9 7.6 %collective-permute-start.2 = (bf16[128,768]{1,0:T(8,128)(2,1)S(1)}, bf16[128,768]{1,0:T(8,128)(2,1)S(1)}, u32[]{:S(2)}, u32[]{:S(2)}) collective-permute-start(bf16[128,768]{1,0:T(8,128)(2,1)S(1)} %bitcast.164), channel_id=1, source_target_pairs={{0,96},{32,64},{64,32},{96,0},{1,97},{33,65},{65,33},{97,1},{2,98}... | collective-permute-start | bytes 589832 | tf_op jit(solution)/shard_map/ppermute | solution.py:466
  19.6 10.7 %collective-permute-start.1 = (bf16[128,768]{1,0:T(8,128)(2,1)S(1)}, bf16[128,768]{1,0:T(8,128)(2,1)S(1)}, u32[]{:S(2)}, u32[]{:S(2)}) collective-permute-start(bf16[128,768]{1,0:T(8,128)(2,1)S(1)} %bitcast.165), channel_id=1, source_target_pairs={{0,64},{32,96},{64,0},{96,32},{1,65},{33,97},{65,1},{97,33},{2,66}... | collective-permute-start | bytes 589832 | tf_op jit(solution)/shard_map/ppermute | solution.py:466
  20.8 9.5 %collective-permute-start = (bf16[128,768]{1,0:T(8,128)(2,1)S(1)}, bf16[128,768]{1,0:T(8,128)(2,1)S(1)}, u32[]{:S(2)}, u32[]{:S(2)}) collective-permute-start(bf16[128,768]{1,0:T(8,128)(2,1)S(1)} %bitcast.166), channel_id=1, source_target_pairs={{0,32},{32,0},{64,96},{96,64},{1,33},{33,1},{65,97},{97,65},{2,34}... | collective-permute-start | bytes 589832 | tf_op jit(solution)/shard_map/ppermute | solution.py:466
  30.9 292.7 %copy-start.35 = (f32[512]{0:T(512)}, f32[512]{0:T(512)S(1)}, u32[]{:S(2)}) copy-start(f32[512]{0:T(512)S(1)} %add_rsqrt_fusion.1) | copy-start | bytes 6148
  32.8 93.7 %all-gather.9.cloned.1.call-start = ((), (), s32[]{:S(2)}) async-start(), calls=%async_computation.2 | async-start | bytes 4456448 | tf_op jit(solution)/shard_map/all_gather | solution.py:616
  33.6 179.8 %all-gather.11.cloned.1.call-start = ((), (), s32[]{:S(2)}) async-start(), calls=%async_computation.4 | async-start | bytes 4456448 | tf_op jit(solution)/shard_map/all_gather | solution.py:678
  33.7 9.8 %collective-permute-start.5 = (bf16[192,768]{1,0:T(8,128)(2,1)S(1)}, bf16[192,768]{1,0:T(8,128)(2,1)}, u32[]{:S(2)}, u32[]{:S(2)}) collective-permute-start(bf16[192,768]{1,0:T(8,128)(2,1)S(1)} %constant_dynamic-slice_fusion.17), channel_id=1, source_target_pairs={{0,1},{1,0},{2,3},{3,2},{4,5},{5,4},{6,7},{7,6},{8,9},{9,8},{10,11... | collective-permute-start | bytes 884744 | tf_op jit(solution)/shard_map/ppermute | solution.py:462
  37.1 12.8 %collective-permute-start.7 = (bf16[192,768]{1,0:T(8,128)(2,1)S(1)}, bf16[192,768]{1,0:T(8,128)(2,1)S(1)}, u32[]{:S(2)}, u32[]{:S(2)}) collective-permute-start(bf16[192,768]{1,0:T(8,128)(2,1)S(1)} %fusion.55), channel_id=1, source_target_pairs={{0,1},{1,0},{2,3},{3,2},{4,5},{5,4},{6,7},{7,6},{8,9},{9,8},{10,11... | collective-permute-start | bytes 884744 | tf_op jit(solution)/shard_map/ppermute | solution.py:462
  39.1 17.1 %collective-permute-start.9 = (bf16[192,768]{1,0:T(8,128)(2,1)S(1)}, bf16[192,768]{1,0:T(8,128)(2,1)}, u32[]{:S(2)}, u32[]{:S(2)}) collective-permute-start(bf16[192,768]{1,0:T(8,128)(2,1)S(1)} %constant_dynamic-slice_fusion.14), channel_id=1, source_target_pairs={{0,1},{1,0},{2,3},{3,2},{4,5},{5,4},{6,7},{7,6},{8,9},{9,8},{10,11... | collective-permute-start | bytes 884744 | tf_op jit(solution)/shard_map/ppermute | solution.py:462
  41.2 17.9 %collective-permute-start.11 = (bf16[128,768]{1,0:T(8,128)(2,1)S(1)}, bf16[128,768]{1,0:T(8,128)(2,1)}, u32[]{:S(2)}, u32[]{:S(2)}) collective-permute-start(bf16[128,768]{1,0:T(8,128)(2,1)S(1)} %bitcast.160), channel_id=1, source_target_pairs={{0,32},{32,0},{64,96},{96,64},{1,33},{33,1},{65,97},{97,65},{2,34}... | collective-permute-start | bytes 589832 | tf_op jit(solution)/shard_map/ppermute | solution.py:466
  42.5 20.8 %collective-permute-start.12 = (bf16[128,768]{1,0:T(8,128)(2,1)S(1)}, bf16[128,768]{1,0:T(8,128)(2,1)}, u32[]{:S(2)}, u32[]{:S(2)}) collective-permute-start(bf16[128,768]{1,0:T(8,128)(2,1)S(1)} %bitcast.161), channel_id=1, source_target_pairs={{0,64},{32,96},{64,0},{96,32},{1,65},{33,97},{65,1},{97,33},{2,66}... | collective-permute-start | bytes 589832 | tf_op jit(solution)/shard_map/ppermute | solution.py:466
  43.5 29.1 %collective-permute-start.6 = (bf16[192,768]{1,0:T(8,128)(2,1)}, bf16[192,768]{1,0:T(8,128)(2,1)S(1)}, u32[]{:S(2)}, u32[]{:S(2)}) collective-permute-start(bf16[192,768]{1,0:T(8,128)(2,1)} %collective-permute-done.5), channel_id=1, source_target_pairs={{0,2},{2,0},{1,3},{3,1},{4,6},{6,4},{5,7},{7,5},{8,10},{10,8},{9,1... | collective-permute-start | bytes 884744 | tf_op jit(solution)/shard_map/ppermute | solution.py:462
  49.8 22.8 %collective-permute-start.8 = (bf16[192,768]{1,0:T(8,128)(2,1)S(1)}, bf16[192,768]{1,0:T(8,128)(2,1)S(1)}, u32[]{:S(2)}, u32[]{:S(2)}) collective-permute-start(bf16[192,768]{1,0:T(8,128)(2,1)S(1)} %collective-permute-done.7), channel_id=1, source_target_pairs={{0,2},{2,0},{1,3},{3,1},{4,6},{6,4},{5,7},{7,5},{8,10},{10,8},{9,1... | collective-permute-start | bytes 884744 | tf_op jit(solution)/shard_map/ppermute | solution.py:462
  56.1 17.1 %collective-permute-start.10 = (bf16[192,768]{1,0:T(8,128)(2,1)}, bf16[192,768]{1,0:T(8,128)(2,1)S(1)}, u32[]{:S(2)}, u32[]{:S(2)}) collective-permute-start(bf16[192,768]{1,0:T(8,128)(2,1)} %collective-permute-done.9), channel_id=1, source_target_pairs={{0,2},{2,0},{1,3},{3,1},{4,6},{6,4},{5,7},{7,5},{8,10},{10,8},{9,1... | collective-permute-start | bytes 884744 | tf_op jit(solution)/shard_map/ppermute | solution.py:462
  59.2 13.4 %collective-permute-start.13 = (bf16[128,768]{1,0:T(8,128)(2,1)S(1)}, bf16[128,768]{1,0:T(8,128)(2,1)S(1)}, u32[]{:S(2)}, u32[]{:S(2)}) collective-permute-start(bf16[128,768]{1,0:T(8,128)(2,1)S(1)} %bitcast.162), channel_id=1, source_target_pairs={{0,96},{32,64},{64,32},{96,0},{1,97},{33,65},{65,33},{97,1},{2,98}... | collective-permute-start | bytes 589832 | tf_op jit(solution)/shard_map/ppermute | solution.py:466
  108.4 18.1 %collective-permute-start.14 = (bf16[4,128,256]{2,1,0:T(8,128)(2,1)}, bf16[4,128,256]{2,1,0:T(8,128)(2,1)S(1)}, u32[]{:S(2)}, u32[]{:S(2)}) collective-permute-start(bf16[4,128,256]{2,1,0:T(8,128)(2,1)} %get-tuple-element.133.attn_ref), channel_id=1, source_target_pairs={{0,32},{32,0},{64,96},{96,64},{1,33},{33,1},{65,97},{97,65},{2,34}... | collective-permute-start | bytes 786440 | tf_op jit(solution)/shard_map/ppermute | solution.py:466
  110.7 15.9 %collective-permute-start.15 = (bf16[4,128,256]{2,1,0:T(8,128)(2,1)}, bf16[4,128,256]{2,1,0:T(8,128)(2,1)S(1)}, u32[]{:S(2)}, u32[]{:S(2)}) collective-permute-start(bf16[4,128,256]{2,1,0:T(8,128)(2,1)} %get-tuple-element.133.attn_ref), channel_id=1, source_target_pairs={{0,64},{32,96},{64,0},{96,32},{1,65},{33,97},{65,1},{97,33},{2,66}... | collective-permute-start | bytes 786440 | tf_op jit(solution)/shard_map/ppermute | solution.py:466
  110.7 21.1 %collective-permute-start.16 = (bf16[4,128,256]{2,1,0:T(8,128)(2,1)}, bf16[4,128,256]{2,1,0:T(8,128)(2,1)}, u32[]{:S(2)}, u32[]{:S(2)}) collective-permute-start(bf16[4,128,256]{2,1,0:T(8,128)(2,1)} %get-tuple-element.133.attn_ref), channel_id=1, source_target_pairs={{0,96},{32,64},{64,32},{96,0},{1,97},{33,65},{65,33},{97,1},{2,98}... | collective-permute-start | bytes 786440 | tf_op jit(solution)/shard_map/ppermute | solution.py:466
  138.8 11.8 %collective-permute-start.17 = (f32[128,768]{1,0:T(8,128)S(1)}, f32[128,768]{1,0:T(8,128)S(1)}, u32[]{:S(2)}, u32[]{:S(2)}) collective-permute-start(f32[128,768]{1,0:T(8,128)S(1)} %get-tuple-element.211), channel_id=1, source_target_pairs={{0,32},{32,0},{64,96},{96,64},{1,33},{33,1},{65,97},{97,65},{2,34}... | collective-permute-start | bytes 1179656 | tf_op jit(solution)/shard_map/ppermute | solution.py:466
  139.8 10.8 %collective-permute-start.18 = (f32[128,768]{1,0:T(8,128)S(1)}, f32[128,768]{1,0:T(8,128)S(1)}, u32[]{:S(2)}, u32[]{:S(2)}) collective-permute-start(f32[128,768]{1,0:T(8,128)S(1)} %get-tuple-element.210), channel_id=1, source_target_pairs={{0,64},{32,96},{64,0},{96,32},{1,65},{33,97},{65,1},{97,33},{2,66}... | collective-permute-start | bytes 1179656 | tf_op jit(solution)/shard_map/ppermute | solution.py:466
  140.2 19.1 %collective-permute-start.19 = (f32[128,768]{1,0:T(8,128)S(1)}, f32[128,768]{1,0:T(8,128)S(1)}, u32[]{:S(2)}, u32[]{:S(2)}) collective-permute-start(f32[128,768]{1,0:T(8,128)S(1)} %get-tuple-element.209), channel_id=1, source_target_pairs={{0,96},{32,64},{64,32},{96,0},{1,97},{33,65},{65,33},{97,1},{2,98}... | collective-permute-start | bytes 1179656 | tf_op jit(solution)/shard_map/ppermute | solution.py:466
  159.7 7.9 %collective-permute-start.20 = (bf16[128,768]{1,0:T(8,128)(2,1)S(1)}, bf16[128,768]{1,0:T(8,128)(2,1)S(1)}, u32[]{:S(2)}, u32[]{:S(2)}) collective-permute-start(bf16[128,768]{1,0:T(8,128)(2,1)S(1)} %get-tuple-element.125), channel_id=1, source_target_pairs={{0,32},{32,0},{64,96},{96,64},{1,33},{33,1},{65,97},{97,65},{2,34}... | collective-permute-start | bytes 589832 | tf_op jit(solution)/shard_map/ppermute | solution.py:466
  160.5 7.1 %collective-permute-start.21 = (bf16[128,768]{1,0:T(8,128)(2,1)S(1)}, bf16[128,768]{1,0:T(8,128)(2,1)S(1)}, u32[]{:S(2)}, u32[]{:S(2)}) collective-permute-start(bf16[128,768]{1,0:T(8,128)(2,1)S(1)} %get-tuple-element.125), channel_id=1, source_target_pairs={{0,64},{32,96},{64,0},{96,32},{1,65},{33,97},{65,1},{97,33},{2,66}... | collective-permute-start | bytes 589832 | tf_op jit(solution)/shard_map/ppermute | solution.py:466
  161.6 9.6 %collective-permute-start.22 = (bf16[128,768]{1,0:T(8,128)(2,1)S(1)}, bf16[128,768]{1,0:T(8,128)(2,1)S(1)}, u32[]{:S(2)}, u32[]{:S(2)}) collective-permute-start(bf16[128,768]{1,0:T(8,128)(2,1)S(1)} %get-tuple-element.125), channel_id=1, source_target_pairs={{0,96},{32,64},{64,32},{96,0},{1,97},{33,65},{65,33},{97,1},{2,98}... | collective-permute-start | bytes 589832 | tf_op jit(solution)/shard_map/ppermute | solution.py:466
  175.5 127.1 %reduce-scatter.2.cloned.1.call-start = ((), (), s32[]{:S(2)}) async-start(), calls=%async_computation.3 | async-start | bytes 5849088 | tf_op jit(solution)/shard_map/reduce_scatter | solution.py:712
  213.5 165.0 %all-gather.13.cloned.1.call-start = ((), (), s32[]{:S(2)}) async-start(), calls=%async_computation.5 | async-start | bytes 9191424 | tf_op jit(solution)/shard_map/all_gather | solution.py:740
  216.8 35.5 %collective-permute-start.23 = (bf16[128,768]{1,0:T(8,128)(2,1)S(1)}, bf16[128,768]{1,0:T(8,128)(2,1)S(1)}, u32[]{:S(2)}, u32[]{:S(2)}) collective-permute-start(bf16[128,768]{1,0:T(8,128)(2,1)S(1)} %copy-done.32), channel_id=1, source_target_pairs={{0,32},{32,0},{64,96},{96,64},{1,33},{33,1},{65,97},{97,65},{2,34}... | collective-permute-start | bytes 589832 | tf_op jit(solution)/shard_map/ppermute | solution.py:466
  219.2 33.1 %collective-permute-start.24 = (bf16[128,768]{1,0:T(8,128)(2,1)S(1)}, bf16[128,768]{1,0:T(8,128)(2,1)S(1)}, u32[]{:S(2)}, u32[]{:S(2)}) collective-permute-start(bf16[128,768]{1,0:T(8,128)(2,1)S(1)} %get-tuple-element.147), channel_id=1, source_target_pairs={{0,64},{32,96},{64,0},{96,32},{1,65},{33,97},{65,1},{97,33},{2,66}... | collective-permute-start | bytes 589832 | tf_op jit(solution)/shard_map/ppermute | solution.py:466
  220.5 31.9 %collective-permute-start.25 = (bf16[128,768]{1,0:T(8,128)(2,1)S(1)}, bf16[128,768]{1,0:T(8,128)(2,1)S(1)}, u32[]{:S(2)}, u32[]{:S(2)}) collective-permute-start(bf16[128,768]{1,0:T(8,128)(2,1)S(1)} %get-tuple-element.148), channel_id=1, source_target_pairs={{0,96},{32,64},{64,32},{96,0},{1,97},{33,65},{65,33},{97,1},{2,98}... | collective-permute-start | bytes 589832 | tf_op jit(solution)/shard_map/ppermute | solution.py:466
  259.4 3.7 collective-permute-start.26
  264.6 25.1 %copy-start.28 = (bf16[3,128,768]{2,1,0:T(8,128)(2,1)S(1)}, bf16[3,128,768]{2,1,0:T(8,128)(2,1)}, u32[]{:S(2)}) copy-start(bf16[3,128,768]{2,1,0:T(8,128)(2,1)} %get-tuple-element.155) | copy-start | bytes 1769476
  265.4 9.6 %collective-permute-start.33 = (f32[56,640]{1,0:T(8,128)S(1)}, f32[56,640]{1,0:T(8,128)S(1)}, u32[]{:S(2)}, u32[]{:S(2)}) collective-permute-start(f32[56,640]{1,0:T(8,128)S(1)} %get-tuple-element.221), channel_id=1, source_target_pairs={{0,28},{4,24},{8,20},{12,16},{16,12},{20,8},{24,4},{28,0},{1,29},{... | collective-permute-start | bytes 430088 | tf_op jit(solution)/shard_map/ppermute | solution.py:533
  265.4 11.8 %collective-permute-start.32 = (f32[56,640]{1,0:T(8,128)S(1)}, f32[56,640]{1,0:T(8,128)S(1)}, u32[]{:S(2)}, u32[]{:S(2)}) collective-permute-start(f32[56,640]{1,0:T(8,128)S(1)} %get-tuple-element.222), channel_id=1, source_target_pairs={{0,24},{4,28},{8,16},{12,20},{16,8},{20,12},{24,0},{28,4},{1,25},{... | collective-permute-start | bytes 430088 | tf_op jit(solution)/shard_map/ppermute | solution.py:533
  269.1 10.7 %collective-permute-start.31 = (f32[56,640]{1,0:T(8,128)}, f32[56,640]{1,0:T(8,128)}, u32[]{:S(2)}, u32[]{:S(2)}) collective-permute-start(f32[56,640]{1,0:T(8,128)} %get-tuple-element.223), channel_id=1, source_target_pairs={{0,20},{4,16},{8,28},{12,24},{16,4},{20,0},{24,12},{28,8},{1,21},{... | collective-permute-start | bytes 430088 | tf_op jit(solution)/shard_map/ppermute | solution.py:533
  269.1 16.2 %collective-permute-start.30 = (f32[56,640]{1,0:T(8,128)}, f32[56,640]{1,0:T(8,128)}, u32[]{:S(2)}, u32[]{:S(2)}) collective-permute-start(f32[56,640]{1,0:T(8,128)} %get-tuple-element.224), channel_id=1, source_target_pairs={{0,16},{4,20},{8,24},{12,28},{16,0},{20,4},{24,8},{28,12},{1,17},{... | collective-permute-start | bytes 430088 | tf_op jit(solution)/shard_map/ppermute | solution.py:533
  270.7 17.6 %collective-permute-start.29 = (f32[56,640]{1,0:T(8,128)S(1)}, f32[56,640]{1,0:T(8,128)}, u32[]{:S(2)}, u32[]{:S(2)}) collective-permute-start(f32[56,640]{1,0:T(8,128)S(1)} %get-tuple-element.225), channel_id=1, source_target_pairs={{0,12},{4,8},{8,4},{12,0},{16,28},{20,24},{24,20},{28,16},{1,13},{... | collective-permute-start | bytes 430088 | tf_op jit(solution)/shard_map/ppermute | solution.py:533
  275.0 13.3 %collective-permute-start.28 = (f32[56,640]{1,0:T(8,128)S(1)}, f32[56,640]{1,0:T(8,128)}, u32[]{:S(2)}, u32[]{:S(2)}) collective-permute-start(f32[56,640]{1,0:T(8,128)S(1)} %get-tuple-element.226), channel_id=1, source_target_pairs={{0,8},{4,12},{8,0},{12,4},{16,24},{20,28},{24,16},{28,20},{1,9},{5... | collective-permute-start | bytes 430088 | tf_op jit(solution)/shard_map/ppermute | solution.py:533
  277.2 11.1 %collective-permute-start.27 = (f32[56,640]{1,0:T(8,128)S(1)}, f32[56,640]{1,0:T(8,128)}, u32[]{:S(2)}, u32[]{:S(2)}) collective-permute-start(f32[56,640]{1,0:T(8,128)S(1)} %get-tuple-element.220), channel_id=1, source_target_pairs={{0,4},{4,0},{8,12},{12,8},{16,20},{20,16},{24,28},{28,24},{1,5},{5... | collective-permute-start | bytes 430088 | tf_op jit(solution)/shard_map/ppermute | solution.py:533
  289.7 7.5 %collective-permute-start.34 = (bf16[128,768]{1,0:T(8,128)(2,1)S(1)}, bf16[128,768]{1,0:T(8,128)(2,1)S(1)}, u32[]{:S(2)}, u32[]{:S(2)}) collective-permute-start(bf16[128,768]{1,0:T(8,128)(2,1)S(1)} %get-tuple-element.238), channel_id=1, source_target_pairs={{0,32},{32,0},{64,96},{96,64},{1,33},{33,1},{65,97},{97,65},{2,34}... | collective-permute-start | bytes 589832 | tf_op jit(solution)/shard_map/ppermute | solution.py:466
  292.1 5.6 %collective-permute-start.35 = (bf16[128,768]{1,0:T(8,128)(2,1)S(1)}, bf16[128,768]{1,0:T(8,128)(2,1)S(1)}, u32[]{:S(2)}, u32[]{:S(2)}) collective-permute-start(bf16[128,768]{1,0:T(8,128)(2,1)S(1)} %get-tuple-element.237), channel_id=1, source_target_pairs={{0,64},{32,96},{64,0},{96,32},{1,65},{33,97},{65,1},{97,33},{2,66}... | collective-permute-start | bytes 589832 | tf_op jit(solution)/shard_map/ppermute | solution.py:466
  293.2 9.4 %collective-permute-start.36 = (bf16[128,768]{1,0:T(8,128)(2,1)S(1)}, bf16[128,768]{1,0:T(8,128)(2,1)S(1)}, u32[]{:S(2)}, u32[]{:S(2)}) collective-permute-start(bf16[128,768]{1,0:T(8,128)(2,1)S(1)} %get-tuple-element.236), channel_id=1, source_target_pairs={{0,96},{32,64},{64,32},{96,0},{1,97},{33,65},{65,33},{97,1},{2,98}... | collective-permute-start | bytes 589832 | tf_op jit(solution)/shard_map/ppermute | solution.py:466
  304.5 8.4 %collective-permute-start.37 = (f32[88,768]{1,0:T(8,128)S(1)}, f32[88,768]{1,0:T(8,128)S(1)}, u32[]{:S(2)}, u32[]{:S(2)}) collective-permute-start(f32[88,768]{1,0:T(8,128)S(1)} %pad_maximum_fusion.14), channel_id=1, source_target_pairs={{0,1},{1,0},{2,3},{3,2},{4,5},{5,4},{6,7},{7,6},{8,9},{9,8},{10,11... | collective-permute-start | bytes 811016 | tf_op jit(solution)/shard_map/ppermute | solution.py:462
  312.9 6.5 %collective-permute-start.40 = (bf16[88,768]{1,0:T(8,128)(2,1)S(1)}, bf16[88,768]{1,0:T(8,128)(2,1)S(1)}, u32[]{:S(2)}, u32[]{:S(2)}) collective-permute-start(bf16[88,768]{1,0:T(8,128)(2,1)S(1)} %fusion.57), channel_id=1, source_target_pairs={{0,96},{32,64},{64,32},{96,0},{1,97},{33,65},{65,33},{97,1},{2,98}... | collective-permute-start | bytes 405512 | tf_op jit(solution)/shard_map/ppermute | solution.py:466
  314.8 5.3 %collective-permute-start.39 = (bf16[88,768]{1,0:T(8,128)(2,1)S(1)}, bf16[88,768]{1,0:T(8,128)(2,1)S(1)}, u32[]{:S(2)}, u32[]{:S(2)}) collective-permute-start(bf16[88,768]{1,0:T(8,128)(2,1)S(1)} %fusion.57), channel_id=1, source_target_pairs={{0,64},{32,96},{64,0},{96,32},{1,65},{33,97},{65,1},{97,33},{2,66}... | collective-permute-start | bytes 405512 | tf_op jit(solution)/shard_map/ppermute | solution.py:466
  315.9 6.8 %collective-permute-start.38 = (bf16[88,768]{1,0:T(8,128)(2,1)S(1)}, bf16[88,768]{1,0:T(8,128)(2,1)S(1)}, u32[]{:S(2)}, u32[]{:S(2)}) collective-permute-start(bf16[88,768]{1,0:T(8,128)(2,1)S(1)} %fusion.57), channel_id=1, source_target_pairs={{0,32},{32,0},{64,96},{96,64},{1,33},{33,1},{65,97},{97,65},{2,34}... | collective-permute-start | bytes 405512 | tf_op jit(solution)/shard_map/ppermute | solution.py:466
  (49 other events, 222.4 us)
Sparse Core Ops, SparseCore 0:
  32.9 51.6 all-gather.6
  86.4 40.1 all-gather.8
  175.6 37.7 all-gather.10
  215.7 75.1 reduce-scatter.1
  323.7 54.7 all-gather.12

commit v7 on v6

--- a/solution.py
+++ b/solution.py
@@ -391,38 +391,44 @@
     step = pl.program_id(0)
     rank = pos_ref[0]
 
-    @pl.when(step < 8)
+    @pl.when(step < 4)
     def _():
-        for g in range(4):
-            out_w_ref[g, 0] = in_ref[0, rank ^ g, :48].astype(F32)
-
-    @pl.when(step >= 8)
+        for t in range(2):
+            for g in range(4):
+                out_w_ref[g, t] = in_ref[t, rank ^ g, :48].astype(F32)
+
+    @pl.when(step >= 4)
     def _():
-        for g in range(4):
-            rows = in_ref[0, rank ^ g, :48].astype(F32)
-            fc_w_ref[0, :, 384 * g : 384 * g + 384] = rows[:, :384]
-            fc_w_ref[0, :, 1536 + 384 * g : 1920 + 384 * g] = rows[:, 384:]
-
-    rows = [in_ref[0, rank ^ g, 48:].astype(F32) for g in range(4)]
-    qkv_ref[0, :, :768] = jnp.concatenate([r[:24, :192] for r in rows], axis=1)
-    qkv_ref[0, :, 768:1536] = jnp.concatenate([r[:24, 256:448] for r in rows], axis=1)
-    qkv_ref[0, :, 1536:] = jnp.concatenate(
-        [part for r in rows for part in (r[:24, 512:640], r[:24, 448:512])], axis=1
-    )
+        for t in range(2):
+            for g in range(4):
+                rows = in_ref[t, rank ^ g, :48].astype(F32)
+                fc_w_ref[t, :, 384 * g : 384 * g + 384] = rows[:, :384]
+                fc_w_ref[t, :, 1536 + 384 * g : 1920 + 384 * g] = rows[:, 384:]
+
+    for t in range(2):
+        rows = [in_ref[t, rank ^ g, 48:].astype(F32) for g in range(4)]
+        qkv_ref[t, :, :768] = jnp.concatenate([r[:24, :192] for r in rows], axis=1)
+        qkv_ref[t, :, 768:1536] = jnp.concatenate([r[:24, 256:448] for r in rows], axis=1)
+        qkv_ref[t, :, 1536:] = jnp.concatenate(
+            [part for r in rows for part in (r[:24, 512:640], r[:24, 448:512])], axis=1
+        )
+        first = [r[37:38] for r in rows]
+        second = [r[36:37] for r in rows]
+        sum_ref[t] = jnp.concatenate(
+            [
+                (first[0] + first[1]) + (first[2] + first[3]),
+                (second[0] + second[1]) + (second[2] + second[3]),
+                jnp.zeros((6, 768), F32),
+            ]
+            + first
+            + second,
+            axis=0,
+        )
     for g in range(2):
-        proj_ref[g, 0] = in_ref[0, rank ^ (2 * pos_ref[1] + g), 48:].astype(F32)[24:36]
-    first = [r[37:38] for r in rows]
-    second = [r[36:37] for r in rows]
-    sum_ref[0] = jnp.concatenate(
-        [
-            (first[0] + first[1]) + (first[2] + first[3]),
-            (second[0] + second[1]) + (second[2] + second[3]),
-            jnp.zeros((6, 768), F32),
+        pieces_of = [
+            in_ref[t, rank ^ (2 * pos_ref[1] + g), 48:].astype(F32)[24:36] for t in range(2)
         ]
-        + first
-        + second,
-        axis=0,
-    )
+        proj_ref[g, 0] = jnp.concatenate(pieces_of, axis=0)
 
 
 def unpack(pos, totals):
@@ -430,23 +436,24 @@
         unpack_kernel,
         grid_spec=pltpu.PrefetchScalarGridSpec(
             num_scalar_prefetch=1,
-            grid=(16,),
-            in_specs=[pl.BlockSpec((1, 4, 88, 768), lambda s, pos: (s, 0, 0, 0))],
+            grid=(8,),
+            in_specs=[pl.BlockSpec((2, 4, 88, 768), lambda s, pos: (s, 0, 0, 0))],
             out_specs=(
-                pl.BlockSpec((4, 1, 48, 768), lambda s, pos: (0, jnp.minimum(s, 7), 0, 0)),
-                pl.BlockSpec((1, 48, 3072), lambda s, pos: (jnp.maximum(s - 8, 0), 0, 0)),
-                pl.BlockSpec((1, 24, 2304), lambda s, pos: (s, 0, 0)),
-                pl.BlockSpec((2, 1, 12, 768), lambda s, pos: (0, s, 0, 0)),
-                pl.BlockSpec((1, 16, 768), lambda s, pos: (s, 0, 0)),
+                pl.BlockSpec((4, 2, 48, 768), lambda s, pos: (0, jnp.minimum(s, 3), 0, 0)),
+                pl.BlockSpec((2, 48, 3072), lambda s, pos: (jnp.maximum(s - 4, 0), 0, 0)),
+                pl.BlockSpec((2, 24, 2304), lambda s, pos: (s, 0, 0)),
+                pl.BlockSpec((2, 1, 24, 768), lambda s, pos: (0, s, 0, 0)),
+                pl.BlockSpec((2, 16, 768), lambda s, pos: (s, 0, 0)),
             ),
         ),
         out_shape=(
             jax.ShapeDtypeStruct((4, 8, 48, 768), F32),
             jax.ShapeDtypeStruct((8, 48, 3072), F32),
             jax.ShapeDtypeStruct((16, 24, 2304), F32),
-            jax.ShapeDtypeStruct((2, 16, 12, 768), F32),
+            jax.ShapeDtypeStruct((2, 8, 24, 768), F32),
             jax.ShapeDtypeStruct((16, 16, 768), F32),
         ),
+        compiler_params=pltpu.CompilerParams(vmem_limit_bytes=VMEM_LIMIT),
         name="unpack_grads",
     )(pos, totals)
     return (
@@ -533,15 +540,16 @@
     return lax.ppermute(values, BLOCKS, [(a, a ^ offset) for a in range(8)])
 
 
-def reduce_by_permute(local):
+def reduce_by_permute(local, beside):
     core = lax.axis_index("core")
     block = lax.axis_index(BLOCKS)
     pair = pick(local, core) + swap(pick(local, 1 - core), "core")
+    pair, beside = lax.optimization_barrier((pair, beside))
     moved = [to_block(pick(pair, block ^ r), r) for r in range(1, 8)]
     total = pick(pair, block)
     for values in moved:
         total = total + values
-    return total
+    return (total, beside)
 
 
 def body(
@@ -717,9 +725,9 @@
     late_local, partial_one, partial_low = first_grads(
         normed_one_t, x_normed, grad_q, grad_kv, w_cols, grad_q_sum, grad_kv_sum
     )
-    late = reduce_by_permute(late_local)
-    low_one, late = lax.optimization_barrier((partial_low, late))
-    one_moved = tuple(to_rank(low_one[r - 1], r) for r in (1, 2, 3))
+    late, one_moved = reduce_by_permute(
+        late_local, tuple(to_rank(partial_low[r - 1], r) for r in (1, 2, 3))
+    )
 
     early, late, one_moved = lax.optimization_barrier((early, late, one_moved))
     late = jnp.concatenate([late, jnp.zeros((56, 128), F32)], axis=1)

time: 410 us -> 403 us (0.983)
    ppermute x7, waiting for transfers between devices: 15 us -> 10.4 us  [to_block(): return lax.ppermute(values, BLOCKS, [(a, a ^ offset) for a in range(8)])]
    unnamed x100 -> x112, local copies, waits for them, and re-layouts: 8.44 us -> 8.49 us
  transfers between devices with their start and end apart: 46 -> 46, of which waited for: 26 -> 23; matrix products, arithmetic and copies ran while one was open for 10% -> 10% of each run, Pallas kernels for 19% -> 19%
where the time goes in v7:
time: 403 us; the launch traced here: 402 us
  waiting for transfers between devices  160 us (40%)
  Pallas kernels  92.4 us (23%)
  starting transfers between devices  65.3 us (16%)
  local copies, waits for them, and re-layouts  34.5 us (9%)
  other arithmetic  25.5 us (6%)
  between operations  15 us (4%)
  matrix products  9.16 us (2%)
    ppermute x24, waiting for transfers between devices, to_rank(): return lax.ppermute(values, TP, [(a, a ^ offset) for a in range(4)])  58.1 us
    all_gather x1, waiting for transfers between devices, body(): totals = lax.all_gather(totals, SEQ_AXES, axis=0, tiled=False)  51.8 us
    ppermute x24, starting transfers between devices, to_rank(): return lax.ppermute(values, TP, [(a, a ^ offset) for a in range(4)])  33.3 us
    pallas_call x1, Pallas kernels, key_grad(): pl.pallas_call(key_grad_kernel, out_shape=(jax.ShapeDtypeStruct((4, 128,...  31.4 us
    ppermute x9, starting transfers between devices, swap(): return lax.ppermute(values, axis, [(0, 1), (1, 0)])  20.7 us
    pallas_call x1, Pallas kernels, query_grad(): pl.pallas_call(query_grad_kernel, out_shape=(jax.ShapeDtypeStruct((4, 128...  20.1 us
    pallas_call x1, Pallas kernels, forward_attention(): pl.pallas_call(forward_kernel, out_shape=(jax.ShapeDtypeStruct((4, 128, 2...  20.1 us
    ppermute x9, waiting for transfers between devices, swap(): return lax.ppermute(values, axis, [(0, 1), (1, 0)])  14.1 us
  transfers between devices with their start and end apart: 46, of which 23 were waited for; matrix products, arithmetic and copies ran while one was open for 10% of the time, Pallas kernels for 19%

profile of v7, /device:TPU:1, one launch (start us, length us, event | category | flops | bytes accessed | tf_op | source)
XLA Modules:
  0.0 401.6 jit_solution(13034694575650653772)
XLA Ops:
  11.9 4.5 %collective-permute-start.3 = (f32[12,384]{1,0:T(8,128)S(1)}, f32[12,384]{1,0:T(8,128)S(1)}, u32[]{:S(2)}, u32[]{:S(2)}) collective-permute-start(f32[12,384]{1,0:T(8,128)S(1)} %concatenate.119), channel_id=1, source_target_pairs={{0,1},{1,0},{2,3},{3,2},{4,5},{5,4},{6,7},{7,6},{8,9},{9,8},{10,11... | collective-permute-start | bytes 55304 | tf_op jit(solution)/shard_map/ppermute | solution.py:469
  16.9 2.8 collective-permute-start.2
  21.8 2.7 collective-permute-done.2
  24.4 5.9 %collective-permute-done.1 = bf16[128,768]{1,0:T(8,128)(2,1)S(1)} collective-permute-done((bf16[128,768]{1,0:T(8,128)(2,1)S(1)}, bf16[128,768]{1,0:T(8,128)(2,1)S(1)}, u32[]{:S(2)}, u32[]{:S(2)}) %collective-permute-start.1) | collective-permute-done | bytes 196640 | tf_op jit(solution)/shard_map/ppermute | solution.py:473
  33.8 2.2 collective-permute-start.5
  39.1 2.2 collective-permute-start.9
  43.5 2.3 collective-permute-start.6
  45.8 4.0 %collective-permute-done.7 = bf16[192,768]{1,0:T(8,128)(2,1)S(1)} collective-permute-done((bf16[192,768]{1,0:T(8,128)(2,1)S(1)}, bf16[192,768]{1,0:T(8,128)(2,1)S(1)}, u32[]{:S(2)}, u32[]{:S(2)}) %collective-permute-start.7) | collective-permute-done | bytes 294944 | tf_op jit(solution)/shard_map/ppermute | solution.py:469
  49.8 2.2 collective-permute-start.8
  52.0 4.1 %collective-permute-done.9 = bf16[192,768]{1,0:T(8,128)(2,1)} collective-permute-done((bf16[192,768]{1,0:T(8,128)(2,1)S(1)}, bf16[192,768]{1,0:T(8,128)(2,1)}, u32[]{:S(2)}, u32[]{:S(2)}) %collective-permute-start.9) | collective-permute-done | bytes 294944 | tf_op jit(solution)/shard_map/ppermute | solution.py:469
  56.2 2.3 collective-permute-start.10
  59.2 2.3 collective-permute-start.13
  61.5 1.8 fusion
  63.3 9.3 %collective-permute-done.13 = bf16[128,768]{1,0:T(8,128)(2,1)S(1)} collective-permute-done((bf16[128,768]{1,0:T(8,128)(2,1)S(1)}, bf16[128,768]{1,0:T(8,128)(2,1)S(1)}, u32[]{:S(2)}, u32[]{:S(2)}) %collective-permute-start.13) | collective-permute-done | bytes 196640 | tf_op jit(solution)/shard_map/ppermute | solution.py:473
  73.3 11.4 %all-gather.7.cloned.1.call-done.kv_ref = bf16[16,4,128,384]{3,2,1,0:T(8,128)(2,1)} async-done(((bf16[1,4,128,384]{3,2,1,0:T(8,128)(2,1)}), bf16[16,4,128,384]{3,2,1,0:T(8,128)(2,1)}) %all-gather.7.cloned.1.call-update) | async-done | bytes 6291472 | tf_op jit(solution)/shard_map/all_gather | solution.py:623
  88.4 20.1 %attention_forward.1 = (bf16[4,128,256]{2,1,0:T(8,128)(2,1)}, f32[4,384,128]{2,1,0:T(8,128)}) custom-call(s32[2]{0:T(128)} %get-tuple-element.277.pos_ref, bf16[4,128,256]{2,1,0:T(8,128)(2,1)} %bitcast.177, bf16[16,4,128,384]{3,2,1,0:T(8,128)(2,1)} %all-gather.7.cloned.1.call-done.kv_ref), custom_call_target="tpu_custom_call" | custom-call | flops 3221225472 | bytes 8388608 | tf_op jit(solution)/shard_map/attention_forward/pallas_call | solution.py:125
  108.5 2.2 collective-permute-start.14
  110.7 1.9 collective-permute-start.16
  119.7 7.3 %all-gather.9.cloned.1.call-done.qg_ref = bf16[16,4,128,256]{3,2,1,0:T(8,128)(2,1)} async-done(((bf16[1,4,128,256]{3,2,1,0:T(8,128)(2,1)}), bf16[16,4,128,256]{3,2,1,0:T(8,128)(2,1)}) %all-gather.9.cloned.1.call-update) | async-done | bytes 4194320 | tf_op jit(solution)/shard_map/all_gather | solution.py:624
  127.0 4.8 %collective-permute-done.16 = bf16[4,128,256]{2,1,0:T(8,128)(2,1)} collective-permute-done((bf16[4,128,256]{2,1,0:T(8,128)(2,1)}, bf16[4,128,256]{2,1,0:T(8,128)(2,1)}, u32[]{:S(2)}, u32[]{:S(2)}) %collective-permute-start.16) | collective-permute-done | bytes 262176 | tf_op jit(solution)/shard_map/ppermute | solution.py:473
  140.2 2.9 collective-permute-start.19
  144.8 5.9 %collective-permute-done.17 = f32[128,768]{1,0:T(8,128)S(1)} collective-permute-done((f32[128,768]{1,0:T(8,128)S(1)}, f32[128,768]{1,0:T(8,128)S(1)}, u32[]{:S(2)}, u32[]{:S(2)}) %collective-permute-start.17) | collective-permute-done | bytes 393248 | tf_op jit(solution)/shard_map/ppermute | solution.py:473
  150.6 8.6 %collective-permute-done.19 = f32[128,768]{1,0:T(8,128)S(1)} collective-permute-done((f32[128,768]{1,0:T(8,128)S(1)}, f32[128,768]{1,0:T(8,128)S(1)}, u32[]{:S(2)}, u32[]{:S(2)}) %collective-permute-start.19) | collective-permute-done | bytes 393248 | tf_op jit(solution)/shard_map/ppermute | solution.py:473
  161.6 2.3 collective-permute-start.22
  164.6 2.9 pad.5
  167.6 3.6 collective-permute-done.22
  172.2 3.3 attention_grad_rows.1
  178.1 20.1 %attention_query_grad.1 = (bf16[4,128,256]{2,1,0:T(8,128)(2,1)}, f32[1,256]{1,0:T(1,128)}) custom-call(s32[2]{0:T(128)} %get-tuple-element.277.pos_ref, bf16[4,128,256]{2,1,0:T(8,128)(2,1)} %bitcast.178, bf16[4,128,256]{2,1,0:T(8,128)(2,1)} %get-tuple-element.141.do_ref, f32[4,384,128]{2,1,0:T(8,128)} %get-tuple-element.131.lse_ref, ...), custom_call_target="tpu_custom_call" | custom-call | flops 4831838208 | bytes 8388608 | tf_op jit(solution)/shard_map/attention_query_grad/pallas_call | solution.py:228
  203.0 1.9 fusion.85
  206.8 6.6 %all-gather.11.cloned.1.call-done = bf16[64,128,256]{2,1,0:T(8,128)(2,1)} async-done(((bf16[4,128,256]{2,1,0:T(8,128)(2,1)}), bf16[64,128,256]{2,1,0:T(8,128)(2,1)}) %all-gather.11.cloned.1.call-update) | async-done | bytes 4194320 | tf_op jit(solution)/shard_map/all_gather | solution.py:686
  216.7 2.4 collective-permute-start.23
  220.9 31.4 %attention_key_grad.1 = (bf16[4,128,384]{2,1,0:T(8,128)(2,1)}, f32[1,384]{1,0:T(1,128)}) custom-call(s32[2]{0:T(128)} %get-tuple-element.277.pos_ref, bf16[4,128,384]{2,1,0:T(8,128)(2,1)} %bitcast.175, bf16[16,4,128,256]{3,2,1,0:T(8,128)(2,1)} %all-gather.9.cloned.1.call-done.qg_ref, bf16[16,4,128,256]{3,2,1,0:T(8,128)(2,1)} %bitcast.190), custom_call_target="tpu_custom_call" | custom-call | flops 6442450944 | bytes 10485760 | tf_op jit(solution)/shard_map/attention_key_grad/pallas_call | solution.py:317
  252.3 5.8 %first_grads.1 = (f32[2,8,56,640]{3,2,1,0:T(8,128)}, f32[128,768]{1,0:T(8,128)}, bf16[3,128,768]{2,1,0:T(8,128)(2,1)}) custom-call(bf16[768,512]{1,0:T(8,128)(2,1)} %copy.35.norm_ref, f32[512,768]{1,0:T(8,128)} %get-tuple-element.233.hat_ref, bf16[4,128,256]{2,1,0:T(8,128)(2,1)} %get-tuple-element.145.q_ref, bf16[4,128,384]{2,1,0:T(8,128)(2,1)} %get-tuple-element.151.kv_ref, ...), custom_call_target="tpu_custom_call" | custom-call | tf_op jit(solution)/shard_map/first_grads/pallas_call | solution.py:376
  261.0 2.4 collective-permute-start.27
  266.6 3.7 collective-permute-done.27
  270.3 7.6 %collective-permute-done.29 = bf16[128,768]{1,0:T(8,128)(2,1)S(1)} collective-permute-done((bf16[128,768]{1,0:T(8,128)(2,1)S(1)}, bf16[128,768]{1,0:T(8,128)(2,1)S(1)}, u32[]{:S(2)}, u32[]{:S(2)}) %collective-permute-start.29) | collective-permute-done | bytes 196640 | tf_op jit(solution)/shard_map/ppermute | solution.py:473
  278.4 5.0 %collective-permute-start.33 = (f32[56,640]{1,0:T(8,128)S(1)}, f32[56,640]{1,0:T(8,128)}, u32[]{:S(2)}, u32[]{:S(2)}) collective-permute-start(f32[56,640]{1,0:T(8,128)S(1)} %get-tuple-element.228), channel_id=1, source_target_pairs={{0,16},{4,20},{8,24},{12,28},{16,0},{20,4},{24,8},{28,12},{1,17},{... | collective-permute-start | bytes 430088 | tf_op jit(solution)/shard_map/ppermute | solution.py:540
  283.4 6.0 %collective-permute-done.36 = f32[56,640]{1,0:T(8,128)S(1)} collective-permute-done((f32[56,640]{1,0:T(8,128)S(1)}, f32[56,640]{1,0:T(8,128)S(1)}, u32[]{:S(2)}, u32[]{:S(2)}) %collective-permute-start.36) | collective-permute-done | bytes 143392 | tf_op jit(solution)/shard_map/ppermute | solution.py:540
  289.5 5.1 %collective-permute-start.30 = (f32[56,640]{1,0:T(8,128)S(1)}, f32[56,640]{1,0:T(8,128)}, u32[]{:S(2)}, u32[]{:S(2)}) collective-permute-start(f32[56,640]{1,0:T(8,128)S(1)} %get-tuple-element.224), channel_id=1, source_target_pairs={{0,4},{4,0},{8,12},{12,8},{16,20},{20,16},{24,28},{28,24},{1,5},{5... | collective-permute-start | bytes 430088 | tf_op jit(solution)/shard_map/ppermute | solution.py:540
  294.5 3.6 collective-permute-done.33
  302.1 2.9 collective-permute-start.37
  304.9 4.8 %collective-permute-done.37 = f32[88,768]{1,0:T(8,128)S(1)} collective-permute-done((f32[88,768]{1,0:T(8,128)S(1)}, f32[88,768]{1,0:T(8,128)S(1)}, u32[]{:S(2)}, u32[]{:S(2)}) %collective-permute-start.37) | collective-permute-done | bytes 270368 | tf_op jit(solution)/shard_map/ppermute | solution.py:469
  309.8 2.7 collective-permute-start.40
  314.4 1.9 collective-permute-done.40
  317.6 2.7 collective-permute-done.38
  321.3 1.9 fusion.45
  325.4 51.8 %all-gather.13.cloned.1.call-done = bf16[64,88,768]{2,1,0:T(8,128)(2,1)} async-done(((bf16[4,88,768]{2,1,0:T(8,128)(2,1)}), bf16[64,88,768]{2,1,0:T(8,128)(2,1)}) %all-gather.13.cloned.1.call-update) | async-done | bytes 8650768 | tf_op jit(solution)/shard_map/all_gather | solution.py:748
  377.3 11.8 %unpack_grads.1 = (f32[4,8,48,768]{3,2,1,0:T(8,128)}, f32[8,48,3072]{2,1,0:T(8,128)}, f32[16,24,2304]{2,1,0:T(8,128)}, f32[2,8,24,768]{3,2,1,0:T(8,128)}, f32[16,16,768]{2,1,0:T(8,128)}) custom-call(s32[2]{0:T(128)} %get-tuple-element.278.pos_ref, bf16[16,4,88,768]{3,2,1,0:T(8,128)(2,1)} %bitcast.149), custom_call_target="tpu_custom_call" | custom-call | tf_op jit(solution)/shard_map/unpack_grads/pallas_call | solution.py:435
  (323 shorter events, 78.6 us)
Async XLA Ops:
  7.2 77.5 %all-gather.7.cloned.1.call-start = ((), (), s32[]{:S(2)}) async-start(), calls=%async_computation.1 | async-start | bytes 6684672 | tf_op jit(solution)/shard_map/all_gather | solution.py:623
  11.9 9.4 %collective-permute-start.3 = (f32[12,384]{1,0:T(8,128)S(1)}, f32[12,384]{1,0:T(8,128)S(1)}, u32[]{:S(2)}, u32[]{:S(2)}) collective-permute-start(f32[12,384]{1,0:T(8,128)S(1)} %concatenate.119), channel_id=1, source_target_pairs={{0,1},{1,0},{2,3},{3,2},{4,5},{5,4},{6,7},{7,6},{8,9},{9,8},{10,11... | collective-permute-start | bytes 55304 | tf_op jit(solution)/shard_map/ppermute | solution.py:469
  16.4 14.5 %collective-permute-start.4 = (bf16[384,640]{1,0:T(8,128)(2,1)S(1)}, bf16[384,640]{1,0:T(8,128)(2,1)S(1)}, u32[]{:S(2)}, u32[]{:S(2)}) collective-permute-start(bf16[384,640]{1,0:T(8,128)(2,1)S(1)} %concatenate.117), channel_id=1, source_target_pairs={{0,65},{1,64},{64,1},{65,0},{2,67},{3,66},{66,3},{67,2},{4,69},{5,... | collective-permute-start | bytes 1474568 | tf_op jit(solution)/shard_map/ppermute | solution.py:588
  16.9 7.6 %collective-permute-start.2 = (bf16[128,768]{1,0:T(8,128)(2,1)S(1)}, bf16[128,768]{1,0:T(8,128)(2,1)S(1)}, u32[]{:S(2)}, u32[]{:S(2)}) collective-permute-start(bf16[128,768]{1,0:T(8,128)(2,1)S(1)} %bitcast.165), channel_id=1, source_target_pairs={{0,96},{32,64},{64,32},{96,0},{1,97},{33,65},{65,33},{97,1},{2,98}... | collective-permute-start | bytes 589832 | tf_op jit(solution)/shard_map/ppermute | solution.py:473
  19.6 10.7 %collective-permute-start.1 = (bf16[128,768]{1,0:T(8,128)(2,1)S(1)}, bf16[128,768]{1,0:T(8,128)(2,1)S(1)}, u32[]{:S(2)}, u32[]{:S(2)}) collective-permute-start(bf16[128,768]{1,0:T(8,128)(2,1)S(1)} %bitcast.166), channel_id=1, source_target_pairs={{0,64},{32,96},{64,0},{96,32},{1,65},{33,97},{65,1},{97,33},{2,66}... | collective-permute-start | bytes 589832 | tf_op jit(solution)/shard_map/ppermute | solution.py:473
  20.8 9.5 %collective-permute-start = (bf16[128,768]{1,0:T(8,128)(2,1)S(1)}, bf16[128,768]{1,0:T(8,128)(2,1)S(1)}, u32[]{:S(2)}, u32[]{:S(2)}) collective-permute-start(bf16[128,768]{1,0:T(8,128)(2,1)S(1)} %bitcast.167), channel_id=1, source_target_pairs={{0,32},{32,0},{64,96},{96,64},{1,33},{33,1},{65,97},{97,65},{2,34}... | collective-permute-start | bytes 589832 | tf_op jit(solution)/shard_map/ppermute | solution.py:473
  30.9 290.4 %copy-start.41 = (f32[512]{0:T(512)}, f32[512]{0:T(512)S(1)}, u32[]{:S(2)}) copy-start(f32[512]{0:T(512)S(1)} %add_rsqrt_fusion.1) | copy-start | bytes 6148
  32.8 94.1 %all-gather.9.cloned.1.call-start = ((), (), s32[]{:S(2)}) async-start(), calls=%async_computation.2 | async-start | bytes 4456448 | tf_op jit(solution)/shard_map/all_gather | solution.py:624
  33.6 179.7 %all-gather.11.cloned.1.call-start = ((), (), s32[]{:S(2)}) async-start(), calls=%async_computation.4 | async-start | bytes 4456448 | tf_op jit(solution)/shard_map/all_gather | solution.py:686
  33.8 9.8 %collective-permute-start.5 = (bf16[192,768]{1,0:T(8,128)(2,1)S(1)}, bf16[192,768]{1,0:T(8,128)(2,1)}, u32[]{:S(2)}, u32[]{:S(2)}) collective-permute-start(bf16[192,768]{1,0:T(8,128)(2,1)S(1)} %constant_dynamic-slice_fusion.17), channel_id=1, source_target_pairs={{0,1},{1,0},{2,3},{3,2},{4,5},{5,4},{6,7},{7,6},{8,9},{9,8},{10,11... | collective-permute-start | bytes 884744 | tf_op jit(solution)/shard_map/ppermute | solution.py:469
  37.1 12.8 %collective-permute-start.7 = (bf16[192,768]{1,0:T(8,128)(2,1)S(1)}, bf16[192,768]{1,0:T(8,128)(2,1)S(1)}, u32[]{:S(2)}, u32[]{:S(2)}) collective-permute-start(bf16[192,768]{1,0:T(8,128)(2,1)S(1)} %fusion.55), channel_id=1, source_target_pairs={{0,1},{1,0},{2,3},{3,2},{4,5},{5,4},{6,7},{7,6},{8,9},{9,8},{10,11... | collective-permute-start | bytes 884744 | tf_op jit(solution)/shard_map/ppermute | solution.py:469
  39.1 17.1 %collective-permute-start.9 = (bf16[192,768]{1,0:T(8,128)(2,1)S(1)}, bf16[192,768]{1,0:T(8,128)(2,1)}, u32[]{:S(2)}, u32[]{:S(2)}) collective-permute-start(bf16[192,768]{1,0:T(8,128)(2,1)S(1)} %constant_dynamic-slice_fusion.14), channel_id=1, source_target_pairs={{0,1},{1,0},{2,3},{3,2},{4,5},{5,4},{6,7},{7,6},{8,9},{9,8},{10,11... | collective-permute-start | bytes 884744 | tf_op jit(solution)/shard_map/ppermute | solution.py:469
  41.3 17.9 %collective-permute-start.11 = (bf16[128,768]{1,0:T(8,128)(2,1)S(1)}, bf16[128,768]{1,0:T(8,128)(2,1)}, u32[]{:S(2)}, u32[]{:S(2)}) collective-permute-start(bf16[128,768]{1,0:T(8,128)(2,1)S(1)} %bitcast.161), channel_id=1, source_target_pairs={{0,32},{32,0},{64,96},{96,64},{1,33},{33,1},{65,97},{97,65},{2,34}... | collective-permute-start | bytes 589832 | tf_op jit(solution)/shard_map/ppermute | solution.py:473
  42.5 20.8 %collective-permute-start.12 = (bf16[128,768]{1,0:T(8,128)(2,1)S(1)}, bf16[128,768]{1,0:T(8,128)(2,1)}, u32[]{:S(2)}, u32[]{:S(2)}) collective-permute-start(bf16[128,768]{1,0:T(8,128)(2,1)S(1)} %bitcast.162), channel_id=1, source_target_pairs={{0,64},{32,96},{64,0},{96,32},{1,65},{33,97},{65,1},{97,33},{2,66}... | collective-permute-start | bytes 589832 | tf_op jit(solution)/shard_map/ppermute | solution.py:473
  43.5 29.1 %collective-permute-start.6 = (bf16[192,768]{1,0:T(8,128)(2,1)}, bf16[192,768]{1,0:T(8,128)(2,1)S(1)}, u32[]{:S(2)}, u32[]{:S(2)}) collective-permute-start(bf16[192,768]{1,0:T(8,128)(2,1)} %collective-permute-done.5), channel_id=1, source_target_pairs={{0,2},{2,0},{1,3},{3,1},{4,6},{6,4},{5,7},{7,5},{8,10},{10,8},{9,1... | collective-permute-start | bytes 884744 | tf_op jit(solution)/shard_map/ppermute | solution.py:469
  49.8 22.8 %collective-permute-start.8 = (bf16[192,768]{1,0:T(8,128)(2,1)S(1)}, bf16[192,768]{1,0:T(8,128)(2,1)S(1)}, u32[]{:S(2)}, u32[]{:S(2)}) collective-permute-start(bf16[192,768]{1,0:T(8,128)(2,1)S(1)} %collective-permute-done.7), channel_id=1, source_target_pairs={{0,2},{2,0},{1,3},{3,1},{4,6},{6,4},{5,7},{7,5},{8,10},{10,8},{9,1... | collective-permute-start | bytes 884744 | tf_op jit(solution)/shard_map/ppermute | solution.py:469
  56.2 17.1 %collective-permute-start.10 = (bf16[192,768]{1,0:T(8,128)(2,1)}, bf16[192,768]{1,0:T(8,128)(2,1)S(1)}, u32[]{:S(2)}, u32[]{:S(2)}) collective-permute-start(bf16[192,768]{1,0:T(8,128)(2,1)} %collective-permute-done.9), channel_id=1, source_target_pairs={{0,2},{2,0},{1,3},{3,1},{4,6},{6,4},{5,7},{7,5},{8,10},{10,8},{9,1... | collective-permute-start | bytes 884744 | tf_op jit(solution)/shard_map/ppermute | solution.py:469
  59.2 13.4 %collective-permute-start.13 = (bf16[128,768]{1,0:T(8,128)(2,1)S(1)}, bf16[128,768]{1,0:T(8,128)(2,1)S(1)}, u32[]{:S(2)}, u32[]{:S(2)}) collective-permute-start(bf16[128,768]{1,0:T(8,128)(2,1)S(1)} %bitcast.163), channel_id=1, source_target_pairs={{0,96},{32,64},{64,32},{96,0},{1,97},{33,65},{65,33},{97,1},{2,98}... | collective-permute-start | bytes 589832 | tf_op jit(solution)/shard_map/ppermute | solution.py:473
  108.5 18.5 %collective-permute-start.14 = (bf16[4,128,256]{2,1,0:T(8,128)(2,1)}, bf16[4,128,256]{2,1,0:T(8,128)(2,1)S(1)}, u32[]{:S(2)}, u32[]{:S(2)}) collective-permute-start(bf16[4,128,256]{2,1,0:T(8,128)(2,1)} %get-tuple-element.135.attn_ref), channel_id=1, source_target_pairs={{0,32},{32,0},{64,96},{96,64},{1,33},{33,1},{65,97},{97,65},{2,34}... | collective-permute-start | bytes 786440 | tf_op jit(solution)/shard_map/ppermute | solution.py:473
  110.7 16.2 %collective-permute-start.15 = (bf16[4,128,256]{2,1,0:T(8,128)(2,1)}, bf16[4,128,256]{2,1,0:T(8,128)(2,1)S(1)}, u32[]{:S(2)}, u32[]{:S(2)}) collective-permute-start(bf16[4,128,256]{2,1,0:T(8,128)(2,1)} %get-tuple-element.135.attn_ref), channel_id=1, source_target_pairs={{0,64},{32,96},{64,0},{96,32},{1,65},{33,97},{65,1},{97,33},{2,66}... | collective-permute-start | bytes 786440 | tf_op jit(solution)/shard_map/ppermute | solution.py:473
  110.7 21.1 %collective-permute-start.16 = (bf16[4,128,256]{2,1,0:T(8,128)(2,1)}, bf16[4,128,256]{2,1,0:T(8,128)(2,1)}, u32[]{:S(2)}, u32[]{:S(2)}) collective-permute-start(bf16[4,128,256]{2,1,0:T(8,128)(2,1)} %get-tuple-element.135.attn_ref), channel_id=1, source_target_pairs={{0,96},{32,64},{64,32},{96,0},{1,97},{33,65},{65,33},{97,1},{2,98}... | collective-permute-start | bytes 786440 | tf_op jit(solution)/shard_map/ppermute | solution.py:473
  138.9 11.8 %collective-permute-start.17 = (f32[128,768]{1,0:T(8,128)S(1)}, f32[128,768]{1,0:T(8,128)S(1)}, u32[]{:S(2)}, u32[]{:S(2)}) collective-permute-start(f32[128,768]{1,0:T(8,128)S(1)} %get-tuple-element.215), channel_id=1, source_target_pairs={{0,32},{32,0},{64,96},{96,64},{1,33},{33,1},{65,97},{97,65},{2,34}... | collective-permute-start | bytes 1179656 | tf_op jit(solution)/shard_map/ppermute | solution.py:473
  139.8 10.8 %collective-permute-start.18 = (f32[128,768]{1,0:T(8,128)S(1)}, f32[128,768]{1,0:T(8,128)S(1)}, u32[]{:S(2)}, u32[]{:S(2)}) collective-permute-start(f32[128,768]{1,0:T(8,128)S(1)} %get-tuple-element.214), channel_id=1, source_target_pairs={{0,64},{32,96},{64,0},{96,32},{1,65},{33,97},{65,1},{97,33},{2,66}... | collective-permute-start | bytes 1179656 | tf_op jit(solution)/shard_map/ppermute | solution.py:473
  140.2 19.0 %collective-permute-start.19 = (f32[128,768]{1,0:T(8,128)S(1)}, f32[128,768]{1,0:T(8,128)S(1)}, u32[]{:S(2)}, u32[]{:S(2)}) collective-permute-start(f32[128,768]{1,0:T(8,128)S(1)} %get-tuple-element.213), channel_id=1, source_target_pairs={{0,96},{32,64},{64,32},{96,0},{1,97},{33,65},{65,33},{97,1},{2,98}... | collective-permute-start | bytes 1179656 | tf_op jit(solution)/shard_map/ppermute | solution.py:473
  159.7 7.9 %collective-permute-start.20 = (bf16[128,768]{1,0:T(8,128)(2,1)S(1)}, bf16[128,768]{1,0:T(8,128)(2,1)S(1)}, u32[]{:S(2)}, u32[]{:S(2)}) collective-permute-start(bf16[128,768]{1,0:T(8,128)(2,1)S(1)} %get-tuple-element.127), channel_id=1, source_target_pairs={{0,32},{32,0},{64,96},{96,64},{1,33},{33,1},{65,97},{97,65},{2,34}... | collective-permute-start | bytes 589832 | tf_op jit(solution)/shard_map/ppermute | solution.py:473
  160.6 7.0 %collective-permute-start.21 = (bf16[128,768]{1,0:T(8,128)(2,1)S(1)}, bf16[128,768]{1,0:T(8,128)(2,1)S(1)}, u32[]{:S(2)}, u32[]{:S(2)}) collective-permute-start(bf16[128,768]{1,0:T(8,128)(2,1)S(1)} %get-tuple-element.127), channel_id=1, source_target_pairs={{0,64},{32,96},{64,0},{96,32},{1,65},{33,97},{65,1},{97,33},{2,66}... | collective-permute-start | bytes 589832 | tf_op jit(solution)/shard_map/ppermute | solution.py:473
  161.6 9.6 %collective-permute-start.22 = (bf16[128,768]{1,0:T(8,128)(2,1)S(1)}, bf16[128,768]{1,0:T(8,128)(2,1)S(1)}, u32[]{:S(2)}, u32[]{:S(2)}) collective-permute-start(bf16[128,768]{1,0:T(8,128)(2,1)S(1)} %get-tuple-element.127), channel_id=1, source_target_pairs={{0,96},{32,64},{64,32},{96,0},{1,97},{33,65},{65,33},{97,1},{2,98}... | collective-permute-start | bytes 589832 | tf_op jit(solution)/shard_map/ppermute | solution.py:473
  175.5 124.6 %reduce-scatter.2.cloned.1.call-start = ((), (), s32[]{:S(2)}) async-start(), calls=%async_computation.3 | async-start | bytes 5849088 | tf_op jit(solution)/shard_map/reduce_scatter | solution.py:720
  213.4 163.9 %all-gather.13.cloned.1.call-start = ((), (), s32[]{:S(2)}) async-start(), calls=%async_computation.5 | async-start | bytes 9191424 | tf_op jit(solution)/shard_map/all_gather | solution.py:748
  216.7 35.6 %collective-permute-start.23 = (bf16[128,768]{1,0:T(8,128)(2,1)S(1)}, bf16[128,768]{1,0:T(8,128)(2,1)S(1)}, u32[]{:S(2)}, u32[]{:S(2)}) collective-permute-start(bf16[128,768]{1,0:T(8,128)(2,1)S(1)} %copy-done.38), channel_id=1, source_target_pairs={{0,32},{32,0},{64,96},{96,64},{1,33},{33,1},{65,97},{97,65},{2,34}... | collective-permute-start | bytes 589832 | tf_op jit(solution)/shard_map/ppermute | solution.py:473
  219.1 33.2 %collective-permute-start.24 = (bf16[128,768]{1,0:T(8,128)(2,1)S(1)}, bf16[128,768]{1,0:T(8,128)(2,1)S(1)}, u32[]{:S(2)}, u32[]{:S(2)}) collective-permute-start(bf16[128,768]{1,0:T(8,128)(2,1)S(1)} %copy-done.37), channel_id=1, source_target_pairs={{0,64},{32,96},{64,0},{96,32},{1,65},{33,97},{65,1},{97,33},{2,66}... | collective-permute-start | bytes 589832 | tf_op jit(solution)/shard_map/ppermute | solution.py:473
  220.5 31.9 %collective-permute-start.25 = (bf16[128,768]{1,0:T(8,128)(2,1)S(1)}, bf16[128,768]{1,0:T(8,128)(2,1)S(1)}, u32[]{:S(2)}, u32[]{:S(2)}) collective-permute-start(bf16[128,768]{1,0:T(8,128)(2,1)S(1)} %get-tuple-element.150), channel_id=1, source_target_pairs={{0,96},{32,64},{64,32},{96,0},{1,97},{33,65},{65,33},{97,1},{2,98}... | collective-permute-start | bytes 589832 | tf_op jit(solution)/shard_map/ppermute | solution.py:473
  259.6 5.6 %collective-permute-start.26 = (f32[8,56,640]{2,1,0:T(8,128)S(1)}, f32[8,56,640]{2,1,0:T(8,128)S(1)}, u32[]{:S(2)}, u32[]{:S(2)}) collective-permute-start(f32[8,56,640]{2,1,0:T(8,128)S(1)} %dynamic-slice_bitcast_fusion), channel_id=1, source_target_pairs={{0,2},{2,0},{1,3},{3,1},{4,6},{6,4},{5,7},{7,5},{8,10},{10,8},{9,1... | collective-permute-start | bytes 3440648 | tf_op jit(solution)/shard_map/ppermute | solution.py:469
  261.0 9.4 %collective-permute-start.27 = (bf16[128,768]{1,0:T(8,128)(2,1)S(1)}, bf16[128,768]{1,0:T(8,128)(2,1)S(1)}, u32[]{:S(2)}, u32[]{:S(2)}) collective-permute-start(bf16[128,768]{1,0:T(8,128)(2,1)S(1)} %get-tuple-element.242), channel_id=1, source_target_pairs={{0,32},{32,0},{64,96},{96,64},{1,33},{33,1},{65,97},{97,65},{2,34}... | collective-permute-start | bytes 589832 | tf_op jit(solution)/shard_map/ppermute | solution.py:473
  263.4 6.9 %collective-permute-start.28 = (bf16[128,768]{1,0:T(8,128)(2,1)S(1)}, bf16[128,768]{1,0:T(8,128)(2,1)S(1)}, u32[]{:S(2)}, u32[]{:S(2)}) collective-permute-start(bf16[128,768]{1,0:T(8,128)(2,1)S(1)} %get-tuple-element.241), channel_id=1, source_target_pairs={{0,64},{32,96},{64,0},{96,32},{1,65},{33,97},{65,1},{97,33},{2,66}... | collective-permute-start | bytes 589832 | tf_op jit(solution)/shard_map/ppermute | solution.py:473
  264.7 13.2 %collective-permute-start.29 = (bf16[128,768]{1,0:T(8,128)(2,1)S(1)}, bf16[128,768]{1,0:T(8,128)(2,1)S(1)}, u32[]{:S(2)}, u32[]{:S(2)}) collective-permute-start(bf16[128,768]{1,0:T(8,128)(2,1)S(1)} %get-tuple-element.240), channel_id=1, source_target_pairs={{0,96},{32,64},{64,32},{96,0},{1,97},{33,65},{65,33},{97,1},{2,98}... | collective-permute-start | bytes 589832 | tf_op jit(solution)/shard_map/ppermute | solution.py:473
  270.3 29.8 %copy-start.35 = (bf16[128,768]{1,0:T(8,128)(2,1)}, bf16[128,768]{1,0:T(8,128)(2,1)S(1)}, u32[]{:S(2)}) copy-start(bf16[128,768]{1,0:T(8,128)(2,1)S(1)} %collective-permute-done.28) | copy-start | bytes 589828
  278.0 11.4 %collective-permute-start.36 = (f32[56,640]{1,0:T(8,128)S(1)}, f32[56,640]{1,0:T(8,128)S(1)}, u32[]{:S(2)}, u32[]{:S(2)}) collective-permute-start(f32[56,640]{1,0:T(8,128)S(1)} %get-tuple-element.225), channel_id=1, source_target_pairs={{0,28},{4,24},{8,20},{12,16},{16,12},{20,8},{24,4},{28,0},{1,29},{... | collective-permute-start | bytes 430088 | tf_op jit(solution)/shard_map/ppermute | solution.py:540
  278.1 11.4 %collective-permute-start.35 = (f32[56,640]{1,0:T(8,128)S(1)}, f32[56,640]{1,0:T(8,128)S(1)}, u32[]{:S(2)}, u32[]{:S(2)}) collective-permute-start(f32[56,640]{1,0:T(8,128)S(1)} %get-tuple-element.226), channel_id=1, source_target_pairs={{0,24},{4,28},{8,16},{12,20},{16,8},{20,12},{24,0},{28,4},{1,25},{... | collective-permute-start | bytes 430088 | tf_op jit(solution)/shard_map/ppermute | solution.py:540
  278.2 16.3 %collective-permute-start.34 = (f32[56,640]{1,0:T(8,128)S(1)}, f32[56,640]{1,0:T(8,128)S(1)}, u32[]{:S(2)}, u32[]{:S(2)}) collective-permute-start(f32[56,640]{1,0:T(8,128)S(1)} %get-tuple-element.227), channel_id=1, source_target_pairs={{0,20},{4,16},{8,28},{12,24},{16,4},{20,0},{24,12},{28,8},{1,21},{... | collective-permute-start | bytes 430088 | tf_op jit(solution)/shard_map/ppermute | solution.py:540
  278.4 19.8 %collective-permute-start.33 = (f32[56,640]{1,0:T(8,128)S(1)}, f32[56,640]{1,0:T(8,128)}, u32[]{:S(2)}, u32[]{:S(2)}) collective-permute-start(f32[56,640]{1,0:T(8,128)S(1)} %get-tuple-element.228), channel_id=1, source_target_pairs={{0,16},{4,20},{8,24},{12,28},{16,0},{20,4},{24,8},{28,12},{1,17},{... | collective-permute-start | bytes 430088 | tf_op jit(solution)/shard_map/ppermute | solution.py:540
  283.4 15.5 %collective-permute-start.32 = (f32[56,640]{1,0:T(8,128)S(1)}, f32[56,640]{1,0:T(8,128)}, u32[]{:S(2)}, u32[]{:S(2)}) collective-permute-start(f32[56,640]{1,0:T(8,128)S(1)} %get-tuple-element.229), channel_id=1, source_target_pairs={{0,12},{4,8},{8,4},{12,0},{16,28},{20,24},{24,20},{28,16},{1,13},{... | collective-permute-start | bytes 430088 | tf_op jit(solution)/shard_map/ppermute | solution.py:540
  289.5 9.4 %collective-permute-start.31 = (f32[56,640]{1,0:T(8,128)S(1)}, f32[56,640]{1,0:T(8,128)}, u32[]{:S(2)}, u32[]{:S(2)}) collective-permute-start(f32[56,640]{1,0:T(8,128)S(1)} %get-tuple-element.230), channel_id=1, source_target_pairs={{0,8},{4,12},{8,0},{12,4},{16,24},{20,28},{24,16},{28,20},{1,9},{5... | collective-permute-start | bytes 430088 | tf_op jit(solution)/shard_map/ppermute | solution.py:540
  289.5 9.4 %collective-permute-start.30 = (f32[56,640]{1,0:T(8,128)S(1)}, f32[56,640]{1,0:T(8,128)}, u32[]{:S(2)}, u32[]{:S(2)}) collective-permute-start(f32[56,640]{1,0:T(8,128)S(1)} %get-tuple-element.224), channel_id=1, source_target_pairs={{0,4},{4,0},{8,12},{12,8},{16,20},{20,16},{24,28},{28,24},{1,5},{5... | collective-permute-start | bytes 430088 | tf_op jit(solution)/shard_map/ppermute | solution.py:540
  302.1 7.7 %collective-permute-start.37 = (f32[88,768]{1,0:T(8,128)S(1)}, f32[88,768]{1,0:T(8,128)S(1)}, u32[]{:S(2)}, u32[]{:S(2)}) collective-permute-start(f32[88,768]{1,0:T(8,128)S(1)} %pad_maximum_fusion.14), channel_id=1, source_target_pairs={{0,1},{1,0},{2,3},{3,2},{4,5},{5,4},{6,7},{7,6},{8,9},{9,8},{10,11... | collective-permute-start | bytes 811016 | tf_op jit(solution)/shard_map/ppermute | solution.py:469
  309.8 6.4 %collective-permute-start.40 = (bf16[88,768]{1,0:T(8,128)(2,1)S(1)}, bf16[88,768]{1,0:T(8,128)(2,1)S(1)}, u32[]{:S(2)}, u32[]{:S(2)}) collective-permute-start(bf16[88,768]{1,0:T(8,128)(2,1)S(1)} %fusion.57), channel_id=1, source_target_pairs={{0,96},{32,64},{64,32},{96,0},{1,97},{33,65},{65,33},{97,1},{2,98}... | collective-permute-start | bytes 405512 | tf_op jit(solution)/shard_map/ppermute | solution.py:473
  312.5 5.1 %collective-permute-start.39 = (bf16[88,768]{1,0:T(8,128)(2,1)S(1)}, bf16[88,768]{1,0:T(8,128)(2,1)S(1)}, u32[]{:S(2)}, u32[]{:S(2)}) collective-permute-start(bf16[88,768]{1,0:T(8,128)(2,1)S(1)} %fusion.57), channel_id=1, source_target_pairs={{0,64},{32,96},{64,0},{96,32},{1,65},{33,97},{65,1},{97,33},{2,66}... | collective-permute-start | bytes 405512 | tf_op jit(solution)/shard_map/ppermute | solution.py:473
  313.4 6.9 %collective-permute-start.38 = (bf16[88,768]{1,0:T(8,128)(2,1)S(1)}, bf16[88,768]{1,0:T(8,128)(2,1)S(1)}, u32[]{:S(2)}, u32[]{:S(2)}) collective-permute-start(bf16[88,768]{1,0:T(8,128)(2,1)S(1)} %fusion.57), channel_id=1, source_target_pairs={{0,32},{32,0},{64,96},{96,64},{1,33},{33,1},{65,97},{97,65},{2,34}... | collective-permute-start | bytes 405512 | tf_op jit(solution)/shard_map/ppermute | solution.py:473
  (55 other events, 324.9 us)
Sparse Core Ops, SparseCore 0:
  33.0 51.6 all-gather.6
  86.4 40.5 all-gather.8
  175.6 37.6 all-gather.10
  215.6 77.2 reduce-scatter.1
  321.4 55.8 all-gather.12
